TPU v7x, 256 devices: a whole 4x4x8 slice. The times are simulated.
256 devices in a mesh: inner: 32 (over z, y), cols: 8 (over x, core).
Axes of the slice: x: 4, y: 4, z: 8, core: 2. Of those that a mesh axis runs over, the one named last changes fastest.
Arguments:
- left_u: bfloat16 [256, 512, 128], P(('inner', 'cols')), may hold values from -6 to 6
- left_v: bfloat16 [256, 512, 128], P(('inner', 'cols')), may hold values from -0.0234375 to 0.0234375
- right_u: bfloat16 [32, 256, 512, 128], P('cols', 'inner'), may hold values from -6 to 6
- right_v: bfloat16 [32, 256, 512, 128], P('cols', 'inner'), may hold values from -0.09375 to 0.09375
- sketch: bfloat16 [32, 512, 128], P('cols'), may hold values from -0.25 to 0.25
- tile_index: int32 [32, 256], P('cols', 'inner'), may hold values from 0 to 255, as said below
- slot_mask: int32 [32, 256], P('cols', 'inner'), may hold values from 0 to 1, as said below
Outputs:
- basis: float32 [32, 512, 128], P('cols', 'inner')
- coeff: float32 [32, 512, 128], P('cols', 'inner')
Inputs may be any that keep to these rules, and one draw needn't show every extreme that they name: `tile_index`: slot s of an output tile belongs to inner group g = s // 8 and names a left tile of that group, g * 8 to g * 8 + 7; the tiles named by one output tile's slots of one group are distinct. `slot_mask`: in each output tile and inner group the live slots come first and there is at least one; in every output tile some group has all 8 slots live, and the others at most 4.
All inputs are finite; a program needn't handle non-finite values.
Results may differ from a plain program's by a relative error of at most 0.0045.
Values may be sent and summed in bfloat16 or wider, within the bound.
No kernel may reach another device: no remote copies, remote signals or barrier semaphores. Data moves between devices by JAX's collectives and lax.ppermute only.
A program may use at most 64 MiB of HBM per device.

v0:
```python
import functools
import math

import jax
import jax.numpy as jnp
from jax import lax
from jax.experimental import pallas as pl
from jax.experimental.pallas import tpu as pltpu
from jax.sharding import PartitionSpec as P

NB = 512
R = 128
YS = 4
BATCH = 4
HIGH = lax.Precision.HIGHEST
BF = jnp.bfloat16
F32 = jnp.float32
VMEM = pltpu.VMEM
NT = (((1,), (1,)), ((), ()))


def dot(a, b):
    return jnp.dot(a, b, preferred_element_type=F32)


def dot_nt(a, b):
    return lax.dot_general(a, b, NT, preferred_element_type=F32)


def halves(a):
    high = a.astype(BF)
    return high, (a - high.astype(F32)).astype(BF)


def in_vmem():
    return pl.BlockSpec(memory_space=VMEM)


def in_place():
    return pl.BlockSpec(memory_space=pltpu.HBM)


def in_smem():
    return pl.BlockSpec(memory_space=pltpu.SMEM)


def fetch(meta, outs, slots, source, held, sems):
    def tile(j, _):
        def one(s, _):
            pltpu.make_async_copy(source.at[j, s], held.at[j * slots + s], sems.at[j * slots + s]).start()
            return 0

        lax.fori_loop(0, meta[outs * slots + j], one, 0)
        return 0

    lax.fori_loop(0, outs, tile, 0)


def arrive(meta, outs, slots, j, s, source, held, sems):
    @pl.when(s < meta[outs * slots + j])
    def _():
        pltpu.make_async_copy(source.at[j, s], held.at[j * slots + s], sems.at[j * slots + s]).wait()


def probe_kernel(outs, slots, meta, right_v, sketch, probe_h, probe_l, held, sems):
    fetch(meta, outs, slots, right_v, held, sems)

    def tile(j, _):
        turned = sketch[j].T

        def batch(first, _):
            base = first * BATCH
            for i in range(BATCH):
                arrive(meta, outs, slots, j, base + i, right_v, held, sems)
            for i in range(BATCH):
                at = j * slots + base + i
                high, low = halves(dot(turned, held[at]))
                probe_h[at] = high
                probe_l[at] = low
            return 0

        lax.fori_loop(0, (meta[outs * slots + j] + BATCH - 1) // BATCH, batch, 0)
        return 0

    lax.fori_loop(0, outs, tile, 0)


def forward_kernel(outs, slots, meta, right_u, group, probe_h, probe_l, own, send1, send2, send3, pair_h, pair_l,
                   held, turned, acc, sems):
    fetch(meta, outs, slots, right_u, held, sems)
    y = meta[outs * slots + outs]

    def turn(k, _):
        turned[k] = group[k, 1].T
        return 0

    lax.fori_loop(0, group.shape[0], turn, 0)

    def tile(order, _):
        j = lax.rem(y + 1 + order, YS)
        count = meta[outs * slots + j]
        acc[...] = jnp.zeros_like(acc)

        def batch(first, _):
            base = first * BATCH
            for i in range(BATCH):
                arrive(meta, outs, slots, j, base + i, right_u, held, sems)
            terms = []
            for i in range(BATCH):
                at = j * slots + base + i
                k = meta[at]
                high, low = halves(dot(turned[k], held[at]))
                pair_h[at] = high
                pair_l[at] = low
                mixing = dot_nt(high, probe_h[at]) + dot_nt(high, probe_l[at]) + dot_nt(low, probe_h[at])
                mixing = jnp.where(base + i < count, mixing, 0.0).astype(BF)
                terms.append(dot(group[k, 0], mixing))
            acc[...] += (terms[0] + terms[1]) + (terms[2] + terms[3])
            return 0

        lax.fori_loop(0, (count + BATCH - 1) // BATCH, batch, 0)
        for place, out in enumerate((send1, send2, send3, own)):
            @pl.when(order == place)
            def _():
                out[...] = acc[...].astype(out.dtype)
        return 0

    lax.fori_loop(0, YS, tile, 0)


def backward_kernel(outs, slots, zs, meta, right_v, group, pair_h, pair_l, msg0, msg1, msg2, msg3,
                    own, send1, send2, send3, basis, held, turned, acc, sems):
    fetch(meta, outs, slots, right_v, held, sems)
    y = meta[outs * slots + outs]
    rows = NB // (zs * YS)
    for step, msg in enumerate((msg0, msg1, msg2, msg3)):
        j = lax.rem(y + YS - step, YS)
        turned[j] = msg[:NB].T
        kept = msg[NB:NB + rows].astype(F32) + msg[NB + rows:].astype(F32)
        basis[j] = kept * math.sqrt(NB)

    def tile(j, _):
        count = meta[outs * slots + j]
        acc[...] = jnp.zeros_like(acc)

        def batch(first, _):
            base = first * BATCH
            for i in range(BATCH):
                arrive(meta, outs, slots, j, base + i, right_v, held, sems)
            terms = []
            for i in range(BATCH):
                at = j * slots + base + i
                live = base + i < count
                high, low = halves(dot(turned[j], group[meta[at], 0]))
                back = dot(high, pair_h[at]) + dot(high, pair_l[at]) + dot(low, pair_h[at])
                back = jnp.where(live, back, 0.0).astype(BF)
                terms.append(dot_nt(jnp.where(live, held[at], jnp.zeros_like(held[at])), back))
            acc[...] += (terms[0] + terms[1]) + (terms[2] + terms[3])
            return 0

        lax.fori_loop(0, (count + BATCH - 1) // BATCH, batch, 0)
        for step, out in enumerate((own, send1, send2, send3)):
            there = lax.rem(y + step, YS)
            for block in range(zs):
                start = pl.multiple_of((block * YS + there) * rows, rows)
                out[block, j] = acc[pl.ds(start, rows)].astype(out.dtype)
        return 0

    lax.fori_loop(0, outs, tile, 0)


def shift_y(array, step, zs):
    pairs = [(z * YS + y, z * YS + (y + step) % YS) for z in range(zs) for y in range(YS)]
    return lax.ppermute(array, "inner", pairs)


def over_z(array, zs):
    groups = [[z * YS + y for z in range(zs)] for y in range(YS)]
    return lax.all_to_all(array, "inner", 0, 0, tiled=True, axis_index_groups=groups)


def params():
    return pltpu.CompilerParams(vmem_limit_bytes=20 << 20)


def body(left_u, left_v, right_u, right_v, sketch, tile_index, slot_mask):
    inner = lax.axis_index("inner")
    zs = lax.axis_size("inner") // YS
    z, y = inner // YS, inner % YS
    outs, slots = tile_index.shape
    tiles = lax.axis_size("cols")
    meta = jnp.concatenate([
        (tile_index - inner * tiles).reshape(-1), jnp.sum(slot_mask, axis=1), y[None]
    ]).astype(jnp.int32)
    shape = jax.ShapeDtypeStruct
    square = shape((outs * slots, R, R), BF)
    fetched = [VMEM((outs * slots, NB, R), BF)]
    sems = [pltpu.SemaphoreType.DMA((outs * slots,))]

    group = lax.all_gather(jnp.stack([left_u, left_v], 1), "cols", axis=0, tiled=True)
    probe_h, probe_l = pl.pallas_call(
        functools.partial(probe_kernel, outs, slots),
        out_shape=(square, square),
        in_specs=[in_smem(), in_place(), in_vmem()],
        out_specs=(in_vmem(),) * 2,
        scratch_shapes=fetched + sems,
        compiler_params=params(),
        cost_estimate=pl.CostEstimate(flops=outs * slots * 2 * NB * R * R, bytes_accessed=6 << 20, transcendentals=0),
        name="probe",
    )(meta, right_v, sketch)
    own, send1, send2, send3, pair_h, pair_l = pl.pallas_call(
        functools.partial(forward_kernel, outs, slots),
        out_shape=(shape((NB, R), F32),) + (shape((NB, R), BF),) * 3 + (square, square),
        in_specs=[in_smem(), in_place()] + [in_vmem()] * 3,
        out_specs=(in_vmem(),) * 6,
        scratch_shapes=fetched + [VMEM((tiles, R, NB), BF), VMEM((NB, R), F32)] + sems,
        compiler_params=params(),
        name="forward",
    )(meta, right_u, group, probe_h, probe_l)
    total = own
    for step, send in enumerate((send1, send2, send3)):
        total = total + shift_y(send, step + 1, zs).astype(F32)
    rows = NB // zs
    mine = jnp.sum(over_z(total.reshape(zs, rows, R), zs), axis=0)
    summed = over_z(jnp.broadcast_to(mine[None], (zs, rows, R)), zs).reshape(1, NB, R)
    gram = jnp.einsum("ona,onb->oab", summed, summed, precision=HIGH)
    factor = jnp.linalg.cholesky(gram)
    solved = jax.scipy.linalg.solve_triangular(factor, jnp.swapaxes(summed, 1, 2), lower=True)
    ortho = jnp.swapaxes(solved, 1, 2)[0]
    high, low = halves(ortho)
    out_rows = NB // (zs * YS)
    messages = []
    for step in range(YS):
        start = (z * YS + (y + step) % YS) * out_rows
        kept = [lax.dynamic_slice_in_dim(half, start, out_rows, 0) for half in (high, low)]
        message = jnp.concatenate([high] + kept)
        messages.append(shift_y(message, step, zs) if step else message)
    pieces = (zs, outs, out_rows, R)
    own, send1, send2, send3, basis = pl.pallas_call(
        functools.partial(backward_kernel, outs, slots, zs),
        out_shape=(shape(pieces, F32),) + (shape(pieces, BF),) * 3 + (shape((outs, out_rows, R), F32),),
        in_specs=[in_smem(), in_place()] + [in_vmem()] * 7,
        out_specs=(in_vmem(),) * 5,
        scratch_shapes=fetched + [VMEM((outs, R, NB), BF), VMEM((NB, R), F32)] + sems,
        compiler_params=params(),
        name="backward",
    )(meta, right_v, group, pair_h, pair_l, *messages)
    part = own
    for step, send in enumerate((send1, send2, send3)):
        part = part + shift_y(send, step + 1, zs).astype(F32)
    coeff = jnp.sum(over_z(part, zs), axis=0)
    return (basis, coeff)


def solution(mesh):
    return jax.shard_map(
        body,
        mesh=mesh,
        in_specs=(
            P(("inner", "cols"), None, None),
            P(("inner", "cols"), None, None),
            P("cols", "inner", None, None),
            P("cols", "inner", None, None),
            P("cols", None, None),
            P("cols", "inner"),
            P("cols", "inner"),
        ),
        out_specs=(P("cols", "inner", None), P("cols", "inner", None)),
        check_vma=False,
    )
```

profile of v0, /device:TPU:8, one launch (start us, length us, event | category | flops | bytes accessed | tf_op | source)
XLA Modules:
  0.0 176.7 jit_solution(6018530304419518796)
XLA Ops:
  7.2 1.7 pad_maximum_fusion
  8.9 0.8 reduce_sum.27
  10.6 2.2 %copy-done = bf16[4,8,512,128]{3,2,1,0:T(8,128)(2,1)S(1)} copy-done((bf16[4,8,512,128]{3,2,1,0:T(8,128)(2,1)S(1)}, bf16[4,8,512,128]{3,2,1,0:T(8,128)(2,1)}, u32[]{:S(2)}) %copy-start) | copy-done | bytes 4194328
  12.8 1.0 copy-done.7
  13.8 5.2 %probe.1 = (bf16[32,128,128]{2,1,0:T(8,128)(2,1)S(1)}, bf16[32,128,128]{2,1,0:T(8,128)(2,1)S(1)}) custom-call(s32[37]{0:T(128)S(1)} %pad_add_fusion.meta, bf16[4,8,512,128]{3,2,1,0:T(8,128)(2,1)S(1)} %copy-done, bf16[4,512,128]{2,1,0:T(8,128)(2,1)S(1)} %copy-done.7), custom_call_target="tpu_custom_call" | custom-call | flops 536870912 | bytes 6291456 | tf_op jit(solution)/shard_map/probe/pallas_call | solution.py:201
  19.0 21.5 %all-gather.2.cloned.1.call-done.group = bf16[8,2,512,128]{3,2,1,0:T(8,128)(2,1)} async-done(((bf16[1,2,512,128]{3,2,1,0:T(8,128)(2,1)}), bf16[8,2,512,128]{3,2,1,0:T(8,128)(2,1)}) %all-gather.2.cloned.1.call-update) | async-done | bytes 2097168 | tf_op jit(solution)/shard_map/all_gather | solution.py:200
  40.5 1.6 copy-done.2
  42.1 2.2 %copy-done.4 = bf16[4,8,512,128]{3,2,1,0:T(8,128)(2,1)S(1)} copy-done((bf16[4,8,512,128]{3,2,1,0:T(8,128)(2,1)S(1)}, bf16[4,8,512,128]{3,2,1,0:T(8,128)(2,1)}, u32[]{:S(2)}) %copy-start.4) | copy-done | bytes 4194328
  44.2 10.4 %forward.1 = (f32[512,128]{1,0:T(8,128)S(1)}, bf16[512,128]{1,0:T(8,128)(2,1)S(1)}, bf16[512,128]{1,0:T(8,128)(2,1)S(1)}, bf16[512,128]{1,0:T(8,128)(2,1)S(1)}, ...) custom-call(s32[37]{0:T(128)S(1)} %pad_add_fusion.meta, bf16[4,8,512,128]{3,2,1,0:T(8,128)(2,1)S(1)} %copy-done.4, ...), custom_call_target="tpu_custom_call" | custom-call | tf_op jit(solution)/shard_map/forward/pallas_call | solution.py:211
  54.7 1.0 copy-done.5
  55.7 3.0 %collective-permute-start.1 = (bf16[512,128]{1,0:T(8,128)(2,1)S(1)}, bf16[512,128]{1,0:T(8,128)(2,1)S(1)}, u32[]{:S(2)}, u32[]{:S(2)}) collective-permute-start(bf16[512,128]{1,0:T(8,128)(2,1)S(1)} %get-tuple-element.21), channel_id=1, source_target_pairs={{0,16},{8,24},{16,0},{24,8},{32,48},{40,56},{48,32},{56,40},{64,80... | collective-permute-start | bytes 393224 | tf_op jit(solution)/shard_map/ppermute | solution.py:174
  58.6 2.0 %collective-permute-done = bf16[512,128]{1,0:T(8,128)(2,1)S(1)} collective-permute-done((bf16[512,128]{1,0:T(8,128)(2,1)S(1)}, bf16[512,128]{1,0:T(8,128)(2,1)S(1)}, u32[]{:S(2)}, u32[]{:S(2)}) %collective-permute-start) | collective-permute-done | bytes 131104 | tf_op jit(solution)/shard_map/ppermute | solution.py:174
  60.6 2.2 %collective-permute-done.1 = bf16[512,128]{1,0:T(8,128)(2,1)S(1)} collective-permute-done((bf16[512,128]{1,0:T(8,128)(2,1)S(1)}, bf16[512,128]{1,0:T(8,128)(2,1)S(1)}, u32[]{:S(2)}, u32[]{:S(2)}) %collective-permute-start.1) | collective-permute-done | bytes 131104 | tf_op jit(solution)/shard_map/ppermute | solution.py:174
  62.8 3.0 %collective-permute-done.2 = bf16[512,128]{1,0:T(8,128)(2,1)S(1)} collective-permute-done((bf16[512,128]{1,0:T(8,128)(2,1)S(1)}, bf16[512,128]{1,0:T(8,128)(2,1)S(1)}, u32[]{:S(2)}, u32[]{:S(2)}) %collective-permute-start.2) | collective-permute-done | bytes 131104 | tf_op jit(solution)/shard_map/ppermute | solution.py:174
  65.8 17.2 %all_to_all.15 = f32[8,64,128]{2,1,0:T(8,128)S(1)} all-to-all(f32[8,64,128]{2,1,0:T(8,128)S(1)} %bitcast.31), channel_id=1, replica_groups={{0,32,64,96,128,160,192,224},{8,40,72,104,136,168,200,232},{16,48,80,11..., dimensions={0} | all-to-all | bytes 524288 | tf_op jit(solution)/shard_map/all_to_all | solution.py:179
  83.8 3.4 %all-to-all-start.1 = ((f32[8,64,128]{2,1,0:T(8,128)}), f32[8,64,128]{2,1,0:T(8,128)S(1)}, u32[]{:S(2)}, u32[]{:S(2)}) async-start(f32[8,64,128]{2,1,0:T(8,128)} %broadcast_in_dim.18), calls=%async_computation.1 | async-start | bytes 524288 | tf_op jit(solution)/shard_map/all_to_all | solution.py:179
  87.3 10.3 %all-to-all-done.1 = f32[8,64,128]{2,1,0:T(8,128)S(1)} async-done(((f32[8,64,128]{2,1,0:T(8,128)}), f32[8,64,128]{2,1,0:T(8,128)S(1)}, u32[]{:S(2)}, u32[]{:S(2)}) %all-to-all-start.1) | async-done | bytes 262176 | tf_op jit(solution)/shard_map/all_to_all | solution.py:179
  98.9 12.5 %custom-call.8 = f32[1,128,128]{2,1,0:T(8,128)S(1)} custom-call(f32[1,128,128]{2,1,0:T(8,128)} %fusion), custom_call_target="Cholesky" | custom-call | tf_op jit(solution)/shard_map/jit(cholesky)/cholesky | solution.py:227
  112.8 9.8 %custom-call.9 = f32[1,128,128]{1,2,0:T(8,128)S(1)} custom-call(f32[1,128,128]{2,1,0:T(8,128)S(1)} %select_select_fusion), custom_call_target="InvertDiagBlocksLowerTriangular" | custom-call | tf_op jit(solution)/shard_map/jit(_solve_triangular)/triangular_solve | solution.py:228
  123.4 1.7 collective-permute-start.4
  125.1 2.5 %collective-permute-start.3 = (bf16[544,128]{1,0:T(8,128)(2,1)S(1)}, bf16[544,128]{1,0:T(8,128)(2,1)S(1)}, u32[]{:S(2)}, u32[]{:S(2)}) collective-permute-start(bf16[544,128]{1,0:T(8,128)(2,1)S(1)} %get-tuple-element.33), channel_id=1, source_target_pairs={{0,8},{8,16},{16,24},{24,0},{32,40},{40,48},{48,56},{56,32},{64,72... | collective-permute-start | bytes 417800 | tf_op jit(solution)/shard_map/ppermute | solution.py:174
  127.7 0.8 collective-permute-done.5.msg3
  128.4 1.6 collective-permute-done.4.msg2
  130.0 2.0 %collective-permute-done.3.msg1 = bf16[544,128]{1,0:T(8,128)(2,1)S(1)} collective-permute-done((bf16[544,128]{1,0:T(8,128)(2,1)S(1)}, bf16[544,128]{1,0:T(8,128)(2,1)S(1)}, u32[]{:S(2)}, u32[]{:S(2)}) %collective-permute-start.3) | collective-permute-done | bytes 139296 | tf_op jit(solution)/shard_map/ppermute | solution.py:174
  132.0 2.2 %copy-done.1 = bf16[4,8,512,128]{3,2,1,0:T(8,128)(2,1)S(1)} copy-done((bf16[4,8,512,128]{3,2,1,0:T(8,128)(2,1)S(1)}, bf16[4,8,512,128]{3,2,1,0:T(8,128)(2,1)}, u32[]{:S(2)}) %copy-start.1) | copy-done | bytes 4194328
  134.2 1.2 copy-done.6
  135.4 11.1 %backward.1 = (f32[8,4,16,128]{3,2,1,0:T(8,128)S(1)}, bf16[8,4,16,128]{3,2,1,0:T(8,128)(2,1)S(1)}, bf16[8,4,16,128]{3,2,1,0:T(8,128)(2,1)S(1)}, bf16[8,4,16,128]{3,2,1,0:T(8,128)(2,1)S(1)}, f32[4,16,128]{2,1,0:T(8,128)}) custom-call(s32[37]{0:T(128)S(1)} %pad_add_fusion.meta, bf16[4,8,512,128]{3,2,1,0:T(8,128)(2,1)S(1)} %copy-done.1, ...), custom_call_target="tpu_custom_call" | custom-call | tf_op jit(solution)/shard_map/backward/pallas_call | solution.py:239
  146.6 4.7 %collective-permute-start.7 = (bf16[8,4,16,128]{3,2,1,0:T(8,128)(2,1)S(1)}, bf16[8,4,16,128]{3,2,1,0:T(8,128)(2,1)S(1)}, u32[]{:S(2)}, u32[]{:S(2)}) collective-permute-start(bf16[8,4,16,128]{3,2,1,0:T(8,128)(2,1)S(1)} %get-tuple-element.26), channel_id=1, source_target_pairs={{0,16},{8,24},{16,0},{24,8},{32,48},{40,56},{48,32},{56,40},{64,80... | collective-permute-start | bytes 393224 | tf_op jit(solution)/shard_map/ppermute | solution.py:174
  151.3 0.9 collective-permute-done.6
  152.2 2.1 %collective-permute-done.7 = bf16[8,4,16,128]{3,2,1,0:T(8,128)(2,1)S(1)} collective-permute-done((bf16[8,4,16,128]{3,2,1,0:T(8,128)(2,1)S(1)}, bf16[8,4,16,128]{3,2,1,0:T(8,128)(2,1)S(1)}, u32[]{:S(2)}, u32[]{:S(2)}) %collective-permute-start.7) | collective-permute-done | bytes 131104 | tf_op jit(solution)/shard_map/ppermute | solution.py:174
  154.2 2.0 %collective-permute-done.8 = bf16[8,4,16,128]{3,2,1,0:T(8,128)(2,1)S(1)} collective-permute-done((bf16[8,4,16,128]{3,2,1,0:T(8,128)(2,1)S(1)}, bf16[8,4,16,128]{3,2,1,0:T(8,128)(2,1)S(1)}, u32[]{:S(2)}, u32[]{:S(2)}) %collective-permute-start.8) | collective-permute-done | bytes 131104 | tf_op jit(solution)/shard_map/ppermute | solution.py:174
  156.3 12.9 %all_to_all.16 = f32[8,4,16,128]{3,2,1,0:T(8,128)S(1)} all-to-all(f32[8,4,16,128]{3,2,1,0:T(8,128)S(1)} %convert_add_fusion), channel_id=1, replica_groups={{0,32,64,96,128,160,192,224},{8,40,72,104,136,168,200,232},{16,48,80,11..., dimensions={0} | all-to-all | bytes 524288 | tf_op jit(solution)/shard_map/all_to_all | solution.py:179
  (33 shorter events, 5.9 us)
Async XLA Ops:
  7.2 33.3 %all-gather.2.cloned.1.call-start = ((), (), s32[]{:S(2)}) async-start(), calls=%async_computation.3 | async-start | bytes 2359296 | tf_op jit(solution)/shard_map/all_gather | solution.py:200
  10.6 2.2 %copy-start = (bf16[4,8,512,128]{3,2,1,0:T(8,128)(2,1)S(1)}, bf16[4,8,512,128]{3,2,1,0:T(8,128)(2,1)}, u32[]{:S(2)}) copy-start(bf16[4,8,512,128]{3,2,1,0:T(8,128)(2,1)} %right_v.3) | copy-start | bytes 12582916
  12.8 1.0 copy-start.7
  40.5 1.6 copy-start.2
  42.1 2.2 %copy-start.4 = (bf16[4,8,512,128]{3,2,1,0:T(8,128)(2,1)S(1)}, bf16[4,8,512,128]{3,2,1,0:T(8,128)(2,1)}, u32[]{:S(2)}) copy-start(bf16[4,8,512,128]{3,2,1,0:T(8,128)(2,1)} %right_u.1) | copy-start | bytes 12582916
  54.7 1.0 copy-start.5
  55.6 76.3 %copy-start.3 = (bf16[8,2,512,128]{3,2,1,0:T(8,128)(2,1)S(1)}, bf16[8,2,512,128]{3,2,1,0:T(8,128)(2,1)}, u32[]{:S(2)}) copy-start(bf16[8,2,512,128]{3,2,1,0:T(8,128)(2,1)} %all-gather.2.cloned.1.call-done.group) | copy-start | bytes 6291460
  55.7 5.0 %collective-permute-start = (bf16[512,128]{1,0:T(8,128)(2,1)S(1)}, bf16[512,128]{1,0:T(8,128)(2,1)S(1)}, u32[]{:S(2)}, u32[]{:S(2)}) collective-permute-start(bf16[512,128]{1,0:T(8,128)(2,1)S(1)} %get-tuple-element.20), channel_id=1, source_target_pairs={{0,8},{8,16},{16,24},{24,0},{32,40},{40,48},{48,56},{56,32},{64,72... | collective-permute-start | bytes 393224 | tf_op jit(solution)/shard_map/ppermute | solution.py:174
  55.7 7.2 %collective-permute-start.1 = (bf16[512,128]{1,0:T(8,128)(2,1)S(1)}, bf16[512,128]{1,0:T(8,128)(2,1)S(1)}, u32[]{:S(2)}, u32[]{:S(2)}) collective-permute-start(bf16[512,128]{1,0:T(8,128)(2,1)S(1)} %get-tuple-element.21), channel_id=1, source_target_pairs={{0,16},{8,24},{16,0},{24,8},{32,48},{40,56},{48,32},{56,40},{64,80... | collective-permute-start | bytes 393224 | tf_op jit(solution)/shard_map/ppermute | solution.py:174
  58.6 7.2 %collective-permute-start.2 = (bf16[512,128]{1,0:T(8,128)(2,1)S(1)}, bf16[512,128]{1,0:T(8,128)(2,1)S(1)}, u32[]{:S(2)}, u32[]{:S(2)}) collective-permute-start(bf16[512,128]{1,0:T(8,128)(2,1)S(1)} %get-tuple-element.22), channel_id=1, source_target_pairs={{0,24},{8,0},{16,8},{24,16},{32,56},{40,32},{48,40},{56,48},{64,88... | collective-permute-start | bytes 393224 | tf_op jit(solution)/shard_map/ppermute | solution.py:174
  83.8 13.8 %all-to-all-start.1 = ((f32[8,64,128]{2,1,0:T(8,128)}), f32[8,64,128]{2,1,0:T(8,128)S(1)}, u32[]{:S(2)}, u32[]{:S(2)}) async-start(f32[8,64,128]{2,1,0:T(8,128)} %broadcast_in_dim.18), calls=%async_computation.1 | async-start | bytes 524288 | tf_op jit(solution)/shard_map/all_to_all | solution.py:179
  123.1 5.3 %collective-permute-start.5 = (bf16[544,128]{1,0:T(8,128)(2,1)S(1)}, bf16[544,128]{1,0:T(8,128)(2,1)S(1)}, u32[]{:S(2)}, u32[]{:S(2)}) collective-permute-start(bf16[544,128]{1,0:T(8,128)(2,1)S(1)} %get-tuple-element.30), channel_id=1, source_target_pairs={{0,24},{8,0},{16,8},{24,16},{32,56},{40,32},{48,40},{56,48},{64,88... | collective-permute-start | bytes 417800 | tf_op jit(solution)/shard_map/ppermute | solution.py:174
  123.4 6.6 %collective-permute-start.4 = (bf16[544,128]{1,0:T(8,128)(2,1)S(1)}, bf16[544,128]{1,0:T(8,128)(2,1)S(1)}, u32[]{:S(2)}, u32[]{:S(2)}) collective-permute-start(bf16[544,128]{1,0:T(8,128)(2,1)S(1)} %get-tuple-element.31), channel_id=1, source_target_pairs={{0,16},{8,24},{16,0},{24,8},{32,48},{40,56},{48,32},{56,40},{64,80... | collective-permute-start | bytes 417800 | tf_op jit(solution)/shard_map/ppermute | solution.py:174
  125.1 6.9 %collective-permute-start.3 = (bf16[544,128]{1,0:T(8,128)(2,1)S(1)}, bf16[544,128]{1,0:T(8,128)(2,1)S(1)}, u32[]{:S(2)}, u32[]{:S(2)}) collective-permute-start(bf16[544,128]{1,0:T(8,128)(2,1)S(1)} %get-tuple-element.33), channel_id=1, source_target_pairs={{0,8},{8,16},{16,24},{24,0},{32,40},{40,48},{48,56},{56,32},{64,72... | collective-permute-start | bytes 417800 | tf_op jit(solution)/shard_map/ppermute | solution.py:174
  132.0 2.2 %copy-start.1 = (bf16[4,8,512,128]{3,2,1,0:T(8,128)(2,1)S(1)}, bf16[4,8,512,128]{3,2,1,0:T(8,128)(2,1)}, u32[]{:S(2)}) copy-start(bf16[4,8,512,128]{3,2,1,0:T(8,128)(2,1)} %right_v.3) | copy-start | bytes 12582916
  134.2 1.2 copy-start.6
  146.5 5.6 %collective-permute-start.6 = (bf16[8,4,16,128]{3,2,1,0:T(8,128)(2,1)S(1)}, bf16[8,4,16,128]{3,2,1,0:T(8,128)(2,1)S(1)}, u32[]{:S(2)}, u32[]{:S(2)}) collective-permute-start(bf16[8,4,16,128]{3,2,1,0:T(8,128)(2,1)S(1)} %get-tuple-element.25), channel_id=1, source_target_pairs={{0,8},{8,16},{16,24},{24,0},{32,40},{40,48},{48,56},{56,32},{64,72... | collective-permute-start | bytes 393224 | tf_op jit(solution)/shard_map/ppermute | solution.py:174
  146.6 7.6 %collective-permute-start.7 = (bf16[8,4,16,128]{3,2,1,0:T(8,128)(2,1)S(1)}, bf16[8,4,16,128]{3,2,1,0:T(8,128)(2,1)S(1)}, u32[]{:S(2)}, u32[]{:S(2)}) collective-permute-start(bf16[8,4,16,128]{3,2,1,0:T(8,128)(2,1)S(1)} %get-tuple-element.26), channel_id=1, source_target_pairs={{0,16},{8,24},{16,0},{24,8},{32,48},{40,56},{48,32},{56,40},{64,80... | collective-permute-start | bytes 393224 | tf_op jit(solution)/shard_map/ppermute | solution.py:174
  151.3 5.0 %collective-permute-start.8 = (bf16[8,4,16,128]{3,2,1,0:T(8,128)(2,1)S(1)}, bf16[8,4,16,128]{3,2,1,0:T(8,128)(2,1)S(1)}, u32[]{:S(2)}, u32[]{:S(2)}) collective-permute-start(bf16[8,4,16,128]{3,2,1,0:T(8,128)(2,1)S(1)} %get-tuple-element.27), channel_id=1, source_target_pairs={{0,24},{8,0},{16,8},{24,16},{32,56},{40,32},{48,40},{56,48},{64,88... | collective-permute-start | bytes 393224 | tf_op jit(solution)/shard_map/ppermute | solution.py:174
Sparse Core Ops, SparseCore 0:
  9.9 30.5 all-gather.1
where the time goes:
time: 179 us; the launch traced here: 177 us
  waiting for transfers between devices  48.2 us (27%)
  blocking collectives  30.1 us (17%)
  other arithmetic  28.4 us (16%)
  Pallas kernels  26.7 us (15%)
  starting transfers between devices  15.7 us (9%)
  between operations  14.3 us (8%)
  local copies, waits for them, and re-layouts  12.3 us (7%)
    all_to_all x2, blocking collectives, over_z(): lax.all_to_all(array, 'inner', 0, 0, tiled=True, axis_index_groups=groups)  30.1 us
    all_gather x1, waiting for transfers between devices, body(): lax.all_gather(jnp.stack([left_u, left_v], 1), 'cols', axis=0, tiled=True)  21.5 us
    ppermute x9, waiting for transfers between devices, shift_y(): return lax.ppermute(array, 'inner', pairs)  16.4 us
    another operation x3, other arithmetic, body(): factor = jnp.linalg.cholesky(gram)  13.2 us
    ppermute x9, starting transfers between devices, shift_y(): return lax.ppermute(array, 'inner', pairs)  12.3 us
    unnamed x16, local copies, waits for them, and re-layouts  11.4 us
    pallas_call x1, Pallas kernels, body(): pl.pallas_call(functools.partial(backward_kernel, outs, slots, zs), out_s...  11.1 us
    another operation x2, other arithmetic, body(): jax.scipy.linalg.solve_triangular(factor, jnp.swapaxes(summed, 1, 2), low...  10.5 us
  transfers between devices with their start and end apart: 11, of which 11 were waited for; matrix products, arithmetic and copies ran while one was open for 1% of the time, Pallas kernels for 3%

commit v1 on v0

--- a/solution.py
+++ b/solution.py
@@ -16,7 +16,9 @@
 BF = jnp.bfloat16
 F32 = jnp.float32
 VMEM = pltpu.VMEM
+NN = (((1,), (0,)), ((), ()))
 NT = (((1,), (1,)), ((), ()))
+TN = (((0,), (0,)), ((), ()))
 
 
 def dot(a, b):
@@ -85,40 +87,57 @@
     lax.fori_loop(0, outs, tile, 0)
 
 
-def forward_kernel(outs, slots, meta, right_u, group, probe_h, probe_l, own, send1, send2, send3, pair_h, pair_l,
-                   held, turned, acc, sems):
+def tile_ids(meta, at, tiles):
+    me = meta[at]
+    return [lax.rem(me + 2 * hop, tiles) ^ flip for flip in (0, 1) for hop in (0, tiles // 2 - 1, 1, 2)]
+
+
+def pair_kernel(outs, slots, meta, right_u, probe_h, probe_l, *rest):
+    parts, (pair_h, pair_l, mixing, held, turned, sems) = rest[:-6], rest[-6:]
     fetch(meta, outs, slots, right_u, held, sems)
+    for k, part in zip(tile_ids(meta, outs * slots + outs + 2, len(parts)), parts):
+        turned[k] = part[0].T
+
+    def tile(j, _):
+        count = meta[outs * slots + j]
+
+        def batch(first, _):
+            base = first * BATCH
+            for i in range(BATCH):
+                arrive(meta, outs, slots, j, base + i, right_u, held, sems)
+            for i in range(BATCH):
+                at = j * slots + base + i
+                high, low = halves(dot(turned[meta[at]], held[at]))
+                pair_h[at] = high
+                pair_l[at] = low
+                mixed = dot_nt(high, probe_h[at]) + dot_nt(high, probe_l[at]) + dot_nt(low, probe_h[at])
+                mixing[at] = jnp.where(base + i < count, mixed, 0.0).astype(BF)
+            return 0
+
+        lax.fori_loop(0, (count + BATCH - 1) // BATCH, batch, 0)
+        return 0
+
+    lax.fori_loop(0, outs, tile, 0)
+
+
+def sketch_kernel(outs, slots, meta, mixing, *rest):
+    parts, (own, send1, send2, send3, group, acc) = rest[:-6], rest[-6:]
+    for k, part in zip(tile_ids(meta, outs * slots + outs + 2, len(parts)), parts):
+        group[k] = part[0]
     y = meta[outs * slots + outs]
-
-    def turn(k, _):
-        turned[k] = group[k, 1].T
-        return 0
-
-    lax.fori_loop(0, group.shape[0], turn, 0)
 
     def tile(order, _):
         j = lax.rem(y + 1 + order, YS)
-        count = meta[outs * slots + j]
         acc[...] = jnp.zeros_like(acc)
 
         def batch(first, _):
             base = first * BATCH
-            for i in range(BATCH):
-                arrive(meta, outs, slots, j, base + i, right_u, held, sems)
-            terms = []
-            for i in range(BATCH):
-                at = j * slots + base + i
-                k = meta[at]
-                high, low = halves(dot(turned[k], held[at]))
-                pair_h[at] = high
-                pair_l[at] = low
-                mixing = dot_nt(high, probe_h[at]) + dot_nt(high, probe_l[at]) + dot_nt(low, probe_h[at])
-                mixing = jnp.where(base + i < count, mixing, 0.0).astype(BF)
-                terms.append(dot(group[k, 0], mixing))
+            at = [j * slots + base + i for i in range(BATCH)]
+            terms = [dot(group[meta[slot]], mixing[slot]) for slot in at]
             acc[...] += (terms[0] + terms[1]) + (terms[2] + terms[3])
             return 0
 
-        lax.fori_loop(0, (count + BATCH - 1) // BATCH, batch, 0)
+        lax.fori_loop(0, (meta[outs * slots + j] + BATCH - 1) // BATCH, batch, 0)
         for place, out in enumerate((send1, send2, send3, own)):
             @pl.when(order == place)
             def _():
@@ -126,6 +145,71 @@
         return 0
 
     lax.fori_loop(0, YS, tile, 0)
+
+
+def exact(a, b, dims):
+    return lax.dot_general(a, b, dims, precision=HIGH, preferred_element_type=F32)
+
+
+def inverse_factor(block):
+    n = block.shape[0]
+    lanes = 2 * n
+    same = lax.broadcasted_iota(jnp.int32, (n, n), 0) == lax.broadcasted_iota(jnp.int32, (n, n), 1)
+    full = jnp.concatenate([same.astype(F32), block], axis=1)
+    x = [full[8 * i:8 * i + 8] for i in range(n // 8)]
+    sub = lax.broadcasted_iota(jnp.int32, (8, lanes), 0)
+
+    def wide(v):
+        return jnp.broadcast_to(v, (8, lanes))
+
+    for k in range(0, n, 2):
+        i0, r = k // 8, k % 8
+        first, second = wide(x[i0][r:r + 1]), wide(x[i0][r + 1:r + 2])
+        a, b = wide(first[:, n + k:n + k + 1]), wide(first[:, n + k + 1:n + k + 2])
+        c = wide(second[:, n + k + 1:n + k + 2])
+        scale = 1.0 / (a * c - b * b)
+        p, q = (c * first - b * second) * scale, (a * second - b * first) * scale
+        for i in range(i0, n // 8):
+            if i == i0 and r == 6:
+                continue
+            step = wide(x[i][:, n + k:n + k + 1]) * p + wide(x[i][:, n + k + 1:n + k + 2]) * q
+            if i == i0:
+                step = jnp.where(sub > r + 1, step, 0.0)
+            x[i] = x[i] - step
+    full = jnp.concatenate(x, axis=0)
+    row = lax.broadcasted_iota(jnp.int32, (n, lanes), 0)
+    lane = lax.broadcasted_iota(jnp.int32, (n, lanes), 1) - n
+    diag = jnp.broadcast_to(jnp.sum(jnp.where(lane == row, full, 0.0), axis=1, keepdims=True), (n, lanes))
+    side = jnp.broadcast_to(jnp.sum(jnp.where(lane == row + 1, full, 0.0), axis=1, keepdims=True), (n, lanes))
+    ratio = side / diag
+    odd = row % 2 == 1
+    full = jnp.where(odd, full - pltpu.roll(ratio * full, 1, 0), full)
+    diag = jnp.where(odd, diag - pltpu.roll(ratio * side, 1, 0), diag)
+    return (full * lax.rsqrt(diag))[:, :n]
+
+
+def inverse_cholesky(gram):
+    half = gram.shape[0] // 2
+    upper = inverse_factor(gram[:half, :half])
+    across = exact(upper, gram[:half, half:], NN)
+    lower = inverse_factor(gram[half:, half:] - exact(across, across, TN))
+    corner = -exact(lower, exact(across, upper, TN), NN)
+    top = jnp.concatenate([upper, jnp.zeros_like(upper)], axis=1)
+    return jnp.concatenate([top, jnp.concatenate([corner, lower], axis=1)], axis=0)
+
+
+def ortho_kernel(outs, slots, zs, meta, blocks, msg0, msg1, msg2, msg3, ortho):
+    y, z = meta[outs * slots + outs], meta[outs * slots + outs + 1]
+    rows = NB // (zs * YS)
+    summed = blocks[...].reshape(NB, R)
+    ortho[...] = exact(summed, inverse_cholesky(exact(summed, summed, TN)), NT)
+    high = ortho[...].astype(BF)
+    for step, msg in enumerate((msg0, msg1, msg2, msg3)):
+        start = pl.multiple_of((z * YS + lax.rem(y + step, YS)) * rows, rows)
+        top, low = halves(ortho[pl.ds(start, rows)])
+        msg[:NB] = high
+        msg[NB:NB + rows] = top
+        msg[NB + rows:] = low
 
 
 def backward_kernel(outs, slots, zs, meta, right_v, group, pair_h, pair_l, msg0, msg1, msg2, msg3,
@@ -151,7 +235,7 @@
             for i in range(BATCH):
                 at = j * slots + base + i
                 live = base + i < count
-                high, low = halves(dot(turned[j], group[meta[at], 0]))
+                high, low = halves(dot(turned[j], group[meta[at]]))
                 back = dot(high, pair_h[at]) + dot(high, pair_l[at]) + dot(low, pair_h[at])
                 back = jnp.where(live, back, 0.0).astype(BF)
                 terms.append(dot_nt(jnp.where(live, held[at], jnp.zeros_like(held[at])), back))
@@ -172,6 +256,16 @@
 def shift_y(array, step, zs):
     pairs = [(z * YS + y, z * YS + (y + step) % YS) for z in range(zs) for y in range(YS)]
     return lax.ppermute(array, "inner", pairs)
+
+
+def gather(array, tiles, forward):
+    def hop(value, step):
+        return lax.ppermute(value, "cols", [(i, (i + 2 * step) % tiles) for i in range(tiles)])
+
+    left, right = hop(array, 1), hop(array, -1)
+    far = hop(left, 1) if forward else hop(right, -1)
+    mine = [array, left, right, far]
+    return mine + [lax.ppermute(value, "cols", [(i, i ^ 1) for i in range(tiles)]) for value in mine]
 
 
 def over_z(array, zs):
@@ -190,14 +284,23 @@
     outs, slots = tile_index.shape
     tiles = lax.axis_size("cols")
     meta = jnp.concatenate([
-        (tile_index - inner * tiles).reshape(-1), jnp.sum(slot_mask, axis=1), y[None]
+        (tile_index - inner * tiles).reshape(-1), jnp.sum(slot_mask, axis=1),
+        jnp.stack([y, z, lax.axis_index("cols")]),
     ]).astype(jnp.int32)
     shape = jax.ShapeDtypeStruct
     square = shape((outs * slots, R, R), BF)
     fetched = [VMEM((outs * slots, NB, R), BF)]
     sems = [pltpu.SemaphoreType.DMA((outs * slots,))]
 
-    group = lax.all_gather(jnp.stack([left_u, left_v], 1), "cols", axis=0, tiled=True)
+    right_u = pltpu.with_memory_space_constraint(right_u, pltpu.HBM)
+    right_v = pltpu.with_memory_space_constraint(right_v, pltpu.HBM)
+    group_v = gather(left_v, tiles, False)
+    group_u = gather(left_u, tiles, True)
+    unit = 2 * NB * R * R
+
+    def cost(units, mib):
+        return pl.CostEstimate(flops=int(units * unit), bytes_accessed=mib << 20, transcendentals=0)
+
     probe_h, probe_l = pl.pallas_call(
         functools.partial(probe_kernel, outs, slots),
         out_shape=(square, square),
@@ -205,44 +308,56 @@
         out_specs=(in_vmem(),) * 2,
         scratch_shapes=fetched + sems,
         compiler_params=params(),
-        cost_estimate=pl.CostEstimate(flops=outs * slots * 2 * NB * R * R, bytes_accessed=6 << 20, transcendentals=0),
+        cost_estimate=cost(outs * slots, 6),
         name="probe",
     )(meta, right_v, sketch)
-    own, send1, send2, send3, pair_h, pair_l = pl.pallas_call(
-        functools.partial(forward_kernel, outs, slots),
-        out_shape=(shape((NB, R), F32),) + (shape((NB, R), BF),) * 3 + (square, square),
-        in_specs=[in_smem(), in_place()] + [in_vmem()] * 3,
-        out_specs=(in_vmem(),) * 6,
-        scratch_shapes=fetched + [VMEM((tiles, R, NB), BF), VMEM((NB, R), F32)] + sems,
-        compiler_params=params(),
-        name="forward",
-    )(meta, right_u, group, probe_h, probe_l)
+    pair_h, pair_l, mixing = pl.pallas_call(
+        functools.partial(pair_kernel, outs, slots),
+        out_shape=(square,) * 3,
+        in_specs=[in_smem(), in_place()] + [in_vmem()] * (2 + tiles),
+        out_specs=(in_vmem(),) * 3,
+        scratch_shapes=fetched + [VMEM((tiles, R, NB), BF)] + sems,
+        compiler_params=params(),
+        cost_estimate=cost(outs * slots * 1.75, 10),
+        name="pair",
+    )(meta, right_u, probe_h, probe_l, *group_v)
+    own, send1, send2, send3, group = pl.pallas_call(
+        functools.partial(sketch_kernel, outs, slots),
+        out_shape=(shape((NB, R), F32),) + (shape((NB, R), BF),) * 3 + (shape((tiles, NB, R), BF),),
+        in_specs=[in_smem()] + [in_vmem()] * (1 + tiles),
+        out_specs=(in_vmem(),) * 5,
+        scratch_shapes=[VMEM((NB, R), F32)],
+        compiler_params=params(),
+        cost_estimate=cost(outs * slots, 4),
+        name="sketch",
+    )(meta, mixing, *group_u)
     total = own
     for step, send in enumerate((send1, send2, send3)):
         total = total + shift_y(send, step + 1, zs).astype(F32)
     rows = NB // zs
     mine = jnp.sum(over_z(total.reshape(zs, rows, R), zs), axis=0)
-    summed = over_z(jnp.broadcast_to(mine[None], (zs, rows, R)), zs).reshape(1, NB, R)
-    gram = jnp.einsum("ona,onb->oab", summed, summed, precision=HIGH)
-    factor = jnp.linalg.cholesky(gram)
-    solved = jax.scipy.linalg.solve_triangular(factor, jnp.swapaxes(summed, 1, 2), lower=True)
-    ortho = jnp.swapaxes(solved, 1, 2)[0]
-    high, low = halves(ortho)
+    summed = over_z(jnp.broadcast_to(mine[None], (zs, rows, R)), zs)
     out_rows = NB // (zs * YS)
-    messages = []
-    for step in range(YS):
-        start = (z * YS + (y + step) % YS) * out_rows
-        kept = [lax.dynamic_slice_in_dim(half, start, out_rows, 0) for half in (high, low)]
-        message = jnp.concatenate([high] + kept)
-        messages.append(shift_y(message, step, zs) if step else message)
+    messages = pl.pallas_call(
+        functools.partial(ortho_kernel, outs, slots, zs),
+        out_shape=(shape((NB + 2 * out_rows, R), BF),) * YS,
+        in_specs=[in_smem(), in_vmem()],
+        out_specs=(in_vmem(),) * YS,
+        scratch_shapes=[VMEM((NB, R), F32)],
+        compiler_params=params(),
+        cost_estimate=cost(13, 1),
+        name="ortho",
+    )(meta, summed)
+    messages = [shift_y(message, step, zs) if step else message for step, message in enumerate(messages)]
     pieces = (zs, outs, out_rows, R)
     own, send1, send2, send3, basis = pl.pallas_call(
         functools.partial(backward_kernel, outs, slots, zs),
         out_shape=(shape(pieces, F32),) + (shape(pieces, BF),) * 3 + (shape((outs, out_rows, R), F32),),
-        in_specs=[in_smem(), in_place()] + [in_vmem()] * 7,
+        in_specs=[in_smem(), in_place()] + [in_vmem()] * (3 + YS),
         out_specs=(in_vmem(),) * 5,
         scratch_shapes=fetched + [VMEM((outs, R, NB), BF), VMEM((NB, R), F32)] + sems,
         compiler_params=params(),
+        cost_estimate=cost(outs * slots * 2.75, 8),
         name="backward",
     )(meta, right_v, group, pair_h, pair_l, *messages)
     part = own

time: 179 us -> 129 us (0.72); the launches traced: 177 us -> 129 us
  other arithmetic: 28.4 us -> 3.21 us
  waiting for transfers between devices: 48.2 us -> 24 us
  blocking collectives: 30.1 us -> 48 us
  between operations: 14.3 us -> 0.79 us
  local copies, waits for them, and re-layouts: 12.3 us -> 1.24 us
  starting transfers between devices: 15.7 us -> 23 us
  Pallas kernels: 26.7 us -> 29 us
    another operation x6 -> x0, other arithmetic: 25.4 us -> none  [the longest x3 13.2 us: body(): factor = jnp.linalg.cholesky(gram)]
    all_gather x1 -> x0, waiting for transfers between devices: 21.5 us -> none  [body(): lax.all_gather(jnp.stack([left_u, left_v], 1), 'cols', axis=0, tiled=True)]
    all_to_all x2 -> x3, blocking collectives: 30.1 us -> 48 us  [over_z(): lax.all_to_all(array, 'inner', 0, 0, tiled=True, axis_index_groups=groups)]
    unnamed x16 -> x6, local copies, waits for them, and re-layouts: 11.4 us -> 1.05 us
    all_to_all x1 -> x0, waiting for transfers between devices: 10.3 us -> none  [over_z(): lax.all_to_all(array, 'inner', 0, 0, tiled=True, axis_index_groups=groups)]
    ppermute x0 -> x14, starting transfers between devices: none -> 8.59 us  [the longest x6 7.23 us: hop(): lax.ppermute(value, 'cols', [(i, (i + 2 * step) % tiles) for i in range(t...]
    ppermute x0 -> x14, waiting for transfers between devices: none -> 7.95 us  [the longest x6 7.93 us: hop(): lax.ppermute(value, 'cols', [(i, (i + 2 * step) % tiles) for i in range(t...]
    pallas_call x1 -> x3, Pallas kernels: 10.4 us -> 17.5 us  [the longest x1 10.8 us: body(): pl.pallas_call(functools.partial(ortho_kernel, outs, slots, zs), out_shap...]
  transfers between devices with their start and end apart: 11 -> 23, of which waited for: 11 -> 14; matrix products, arithmetic and copies ran while one was open for 1% -> 1% of each run, Pallas kernels for 3% -> 6%
where the time goes in v1:
time: 129 us
  blocking collectives  48 us (37%)
  Pallas kernels  29 us (22%)
  waiting for transfers between devices  24 us (19%)
  starting transfers between devices  23 us (18%)
  other arithmetic  3.21 us (2%)
    all_to_all x3, blocking collectives, over_z(): lax.all_to_all(array, 'inner', 0, 0, tiled=True, axis_index_groups=groups)  48 us
    ppermute x9, waiting for transfers between devices, shift_y(): return lax.ppermute(array, 'inner', pairs)  16 us
    ppermute x9, starting transfers between devices, shift_y(): return lax.ppermute(array, 'inner', pairs)  14.4 us
    pallas_call x1, Pallas kernels, body(): pl.pallas_call(functools.partial(ortho_kernel, outs, slots, zs), out_shap...  10.8 us
    pallas_call x1, Pallas kernels, body(): pl.pallas_call(functools.partial(backward_kernel, outs, slots, zs), out_s...  8.14 us
    ppermute x6, waiting for transfers between devices, hop(): lax.ppermute(value, 'cols', [(i, (i + 2 * step) % tiles) for i in range(t...  7.93 us
    ppermute x6, starting transfers between devices, hop(): lax.ppermute(value, 'cols', [(i, (i + 2 * step) % tiles) for i in range(t...  7.23 us
    pallas_call x1, Pallas kernels, body(): pl.pallas_call(functools.partial(pair_kernel, outs, slots), out_shape=(sq...  4.71 us
  transfers between devices with their start and end apart: 23, of which 14 were waited for; matrix products, arithmetic and copies ran while one was open for 1% of the time, Pallas kernels for 6%

profile of v1, /device:TPU:8, one launch (start us, length us, event | category | flops | bytes accessed | tf_op | source)
XLA Modules:
  0.0 129.2 jit_solution(7183791598274904865)
XLA Ops:
  0.6 2.8 %collective-permute-start.1 = (bf16[1,512,128]{2,1,0:T(8,128)(2,1)}, bf16[1,512,128]{2,1,0:T(8,128)(2,1)S(1)}, u32[]{:S(2)}, u32[]{:S(2)}) collective-permute-start(bf16[1,512,128]{2,1,0:T(8,128)(2,1)} %rest_0_.2), channel_id=1, source_target_pairs={{0,6},{1,7},{2,0},{3,1},{4,2},{5,3},{6,4},{7,5},{8,14},{9,15},{10,... | collective-permute-start | bytes 393224 | tf_op jit(solution)/shard_map/ppermute | solution.py:263
  3.5 0.8 collective-permute-start.7
  4.2 2.3 %collective-permute-done.1.rest_2_ = bf16[1,512,128]{2,1,0:T(8,128)(2,1)S(1)} collective-permute-done((bf16[1,512,128]{2,1,0:T(8,128)(2,1)}, bf16[1,512,128]{2,1,0:T(8,128)(2,1)S(1)}, u32[]{:S(2)}, u32[]{:S(2)}) %collective-permute-start.1) | collective-permute-done | bytes 131104 | tf_op jit(solution)/shard_map/ppermute | solution.py:263
  6.5 3.6 %collective-permute-start.2 = (bf16[1,512,128]{2,1,0:T(8,128)(2,1)S(1)}, bf16[1,512,128]{2,1,0:T(8,128)(2,1)S(1)}, u32[]{:S(2)}, u32[]{:S(2)}) collective-permute-start(bf16[1,512,128]{2,1,0:T(8,128)(2,1)S(1)} %collective-permute-done.1.rest_2_), channel_id=1, source_target_pairs={{0,6},{1,7},{2,0},{3,1},{4,2},{5,3},{6,4},{7,5},{8,14},{9,15},{10,... | collective-permute-start | bytes 393224 | tf_op jit(solution)/shard_map/ppermute | solution.py:263
  10.2 1.1 collective-permute-done.rest_1_
  11.8 0.9 collective-permute-done.7.rest_1_
  14.2 0.8 reduce_sum.27
  16.1 2.7 %collective-permute-done.9.rest_3_ = bf16[1,512,128]{2,1,0:T(8,128)(2,1)S(1)} collective-permute-done((bf16[1,512,128]{2,1,0:T(8,128)(2,1)S(1)}, bf16[1,512,128]{2,1,0:T(8,128)(2,1)S(1)}, u32[]{:S(2)}, u32[]{:S(2)}) %collective-permute-start.9) | collective-permute-done | bytes 131104 | tf_op jit(solution)/shard_map/ppermute | solution.py:263
  18.8 1.0 copy-done
  19.9 3.4 %probe.1 = (bf16[32,128,128]{2,1,0:T(8,128)(2,1)S(1)}, bf16[32,128,128]{2,1,0:T(8,128)(2,1)S(1)}) custom-call(s32[39]{0:T(128)S(1)} %concatenate.3.meta, bf16[4,8,512,128]{3,2,1,0:T(8,128)(2,1)} %right_v.3, bf16[4,512,128]{2,1,0:T(8,128)(2,1)S(1)} %copy-done), custom_call_target="tpu_custom_call" | custom-call | flops 536870912 | bytes 6291456 | tf_op jit(solution)/shard_map/probe/pallas_call | solution.py:304
  23.3 4.7 %pair.1 = (bf16[32,128,128]{2,1,0:T(8,128)(2,1)S(1)}, bf16[32,128,128]{2,1,0:T(8,128)(2,1)S(1)}, bf16[32,128,128]{2,1,0:T(8,128)(2,1)S(1)}) custom-call(s32[39]{0:T(128)S(1)} %concatenate.3.meta, bf16[4,8,512,128]{3,2,1,0:T(8,128)(2,1)} %right_u.1, bf16[32,128,128]{2,1,0:T(8,128)(2,1)S(1)} %get-tuple-element.21.probe_h, ...), custom_call_target="tpu_custom_call" | custom-call | flops 939524096 | bytes 10485760 | tf_op jit(solution)/shard_map/pair/pallas_call | solution.py:314
  28.1 2.0 %sketch.3 = (f32[512,128]{1,0:T(8,128)S(1)}, bf16[512,128]{1,0:T(8,128)(2,1)S(1)}, bf16[512,128]{1,0:T(8,128)(2,1)S(1)}, bf16[512,128]{1,0:T(8,128)(2,1)S(1)}, bf16[8,512,128]{2,1,0:T(8,128)(2,1)S(1)}) custom-call(s32[39]{0:T(128)S(1)} %concatenate.3.meta, bf16[32,128,128]{2,1,0:T(8,128)(2,1)S(1)} %get-tuple-element.23.mixing, ...), custom_call_target="tpu_custom_call" | custom-call | flops 536870912 | bytes 4194304 | tf_op jit(solution)/shard_map/sketch/pallas_call | solution.py:324
  30.1 1.4 %collective-permute-start.14 = (bf16[512,128]{1,0:T(8,128)(2,1)S(1)}, bf16[512,128]{1,0:T(8,128)(2,1)S(1)}, u32[]{:S(2)}, u32[]{:S(2)}) collective-permute-start(bf16[512,128]{1,0:T(8,128)(2,1)S(1)} %get-tuple-element.28), channel_id=1, source_target_pairs={{0,8},{8,16},{16,24},{24,0},{32,40},{40,48},{48,56},{56,32},{64,72... | collective-permute-start | bytes 393224 | tf_op jit(solution)/shard_map/ppermute | solution.py:258
  31.5 1.1 collective-permute-start.15
  32.5 2.4 %collective-permute-start.16 = (bf16[512,128]{1,0:T(8,128)(2,1)S(1)}, bf16[512,128]{1,0:T(8,128)(2,1)S(1)}, u32[]{:S(2)}, u32[]{:S(2)}) collective-permute-start(bf16[512,128]{1,0:T(8,128)(2,1)S(1)} %get-tuple-element.30), channel_id=1, source_target_pairs={{0,24},{8,0},{16,8},{24,16},{32,56},{40,32},{48,40},{56,48},{64,88... | collective-permute-start | bytes 393224 | tf_op jit(solution)/shard_map/ppermute | solution.py:258
  34.9 1.4 %collective-permute-done.14 = bf16[512,128]{1,0:T(8,128)(2,1)S(1)} collective-permute-done((bf16[512,128]{1,0:T(8,128)(2,1)S(1)}, bf16[512,128]{1,0:T(8,128)(2,1)S(1)}, u32[]{:S(2)}, u32[]{:S(2)}) %collective-permute-start.14) | collective-permute-done | bytes 131104 | tf_op jit(solution)/shard_map/ppermute | solution.py:258
  36.3 3.0 %collective-permute-done.15 = bf16[512,128]{1,0:T(8,128)(2,1)S(1)} collective-permute-done((bf16[512,128]{1,0:T(8,128)(2,1)S(1)}, bf16[512,128]{1,0:T(8,128)(2,1)S(1)}, u32[]{:S(2)}, u32[]{:S(2)}) %collective-permute-start.15) | collective-permute-done | bytes 131104 | tf_op jit(solution)/shard_map/ppermute | solution.py:258
  39.3 1.5 %collective-permute-done.16 = bf16[512,128]{1,0:T(8,128)(2,1)S(1)} collective-permute-done((bf16[512,128]{1,0:T(8,128)(2,1)S(1)}, bf16[512,128]{1,0:T(8,128)(2,1)S(1)}, u32[]{:S(2)}, u32[]{:S(2)}) %collective-permute-start.16) | collective-permute-done | bytes 131104 | tf_op jit(solution)/shard_map/ppermute | solution.py:258
  40.9 21.3 %all_to_all.15 = f32[8,64,128]{2,1,0:T(8,128)} all-to-all(f32[8,64,128]{2,1,0:T(8,128)S(1)} %bitcast.4), channel_id=1, replica_groups={{0,32,64,96,128,160,192,224},{8,40,72,104,136,168,200,232},{16,48,80,11..., dimensions={0} | all-to-all | bytes 524288 | tf_op jit(solution)/shard_map/all_to_all | solution.py:273
  62.2 1.0 reduce_sum.28
  63.2 13.4 %all_to_all.16.blocks = f32[8,64,128]{2,1,0:T(8,128)S(1)} all-to-all(f32[8,64,128]{2,1,0:T(8,128)S(1)} %broadcast_in_dim.2), channel_id=1, replica_groups={{0,32,64,96,128,160,192,224},{8,40,72,104,136,168,200,232},{16,48,80,11..., dimensions={0} | all-to-all | bytes 524288 | tf_op jit(solution)/shard_map/all_to_all | solution.py:273
  76.6 10.8 %ortho.1 = (bf16[544,128]{1,0:T(8,128)(2,1)S(1)}, bf16[544,128]{1,0:T(8,128)(2,1)S(1)}, bf16[544,128]{1,0:T(8,128)(2,1)S(1)}, bf16[544,128]{1,0:T(8,128)(2,1)S(1)}) custom-call(s32[39]{0:T(128)S(1)} %concatenate.3.meta, f32[8,64,128]{2,1,0:T(8,128)S(1)} %all_to_all.16.blocks), custom_call_target="tpu_custom_call" | custom-call | flops 218103808 | bytes 1048576 | tf_op jit(solution)/shard_map/ortho/pallas_call | solution.py:341
  87.5 3.7 %collective-permute-start.18 = (bf16[544,128]{1,0:T(8,128)(2,1)S(1)}, bf16[544,128]{1,0:T(8,128)(2,1)S(1)}, u32[]{:S(2)}, u32[]{:S(2)}) collective-permute-start(bf16[544,128]{1,0:T(8,128)(2,1)S(1)} %get-tuple-element.33), channel_id=1, source_target_pairs={{0,16},{8,24},{16,0},{24,8},{32,48},{40,56},{48,32},{56,40},{64,80... | collective-permute-start | bytes 417800 | tf_op jit(solution)/shard_map/ppermute | solution.py:258
  91.3 2.7 %collective-permute-done.17.msg1 = bf16[544,128]{1,0:T(8,128)(2,1)S(1)} collective-permute-done((bf16[544,128]{1,0:T(8,128)(2,1)S(1)}, bf16[544,128]{1,0:T(8,128)(2,1)S(1)}, u32[]{:S(2)}, u32[]{:S(2)}) %collective-permute-start.17) | collective-permute-done | bytes 139296 | tf_op jit(solution)/shard_map/ppermute | solution.py:258
  94.0 1.7 %collective-permute-done.18.msg2 = bf16[544,128]{1,0:T(8,128)(2,1)S(1)} collective-permute-done((bf16[544,128]{1,0:T(8,128)(2,1)S(1)}, bf16[544,128]{1,0:T(8,128)(2,1)S(1)}, u32[]{:S(2)}, u32[]{:S(2)}) %collective-permute-start.18) | collective-permute-done | bytes 139296 | tf_op jit(solution)/shard_map/ppermute | solution.py:258
  95.7 1.9 %collective-permute-done.19.msg3 = bf16[544,128]{1,0:T(8,128)(2,1)S(1)} collective-permute-done((bf16[544,128]{1,0:T(8,128)(2,1)S(1)}, bf16[544,128]{1,0:T(8,128)(2,1)S(1)}, u32[]{:S(2)}, u32[]{:S(2)}) %collective-permute-start.19) | collective-permute-done | bytes 139296 | tf_op jit(solution)/shard_map/ppermute | solution.py:258
  97.7 8.1 %backward.1 = (f32[8,4,16,128]{3,2,1,0:T(8,128)S(1)}, bf16[8,4,16,128]{3,2,1,0:T(8,128)(2,1)S(1)}, bf16[8,4,16,128]{3,2,1,0:T(8,128)(2,1)S(1)}, bf16[8,4,16,128]{3,2,1,0:T(8,128)(2,1)S(1)}, f32[4,16,128]{2,1,0:T(8,128)}) custom-call(s32[39]{0:T(128)S(1)} %concatenate.3.meta, bf16[4,8,512,128]{3,2,1,0:T(8,128)(2,1)} %right_v.3, ...), custom_call_target="tpu_custom_call" | custom-call | flops 1476395008 | bytes 8388608 | tf_op jit(solution)/shard_map/backward/pallas_call | solution.py:353
  106.3 3.4 %collective-permute-start.21 = (bf16[8,4,16,128]{3,2,1,0:T(8,128)(2,1)S(1)}, bf16[8,4,16,128]{3,2,1,0:T(8,128)(2,1)S(1)}, u32[]{:S(2)}, u32[]{:S(2)}) collective-permute-start(bf16[8,4,16,128]{3,2,1,0:T(8,128)(2,1)S(1)} %get-tuple-element.38), channel_id=1, source_target_pairs={{0,16},{8,24},{16,0},{24,8},{32,48},{40,56},{48,32},{56,40},{64,80... | collective-permute-start | bytes 393224 | tf_op jit(solution)/shard_map/ppermute | solution.py:258
  109.7 1.7 %collective-permute-start.22 = (bf16[8,4,16,128]{3,2,1,0:T(8,128)(2,1)S(1)}, bf16[8,4,16,128]{3,2,1,0:T(8,128)(2,1)S(1)}, u32[]{:S(2)}, u32[]{:S(2)}) collective-permute-start(bf16[8,4,16,128]{3,2,1,0:T(8,128)(2,1)S(1)} %get-tuple-element.39), channel_id=1, source_target_pairs={{0,24},{8,0},{16,8},{24,16},{32,56},{40,32},{48,40},{56,48},{64,88... | collective-permute-start | bytes 393224 | tf_op jit(solution)/shard_map/ppermute | solution.py:258
  111.4 2.4 %collective-permute-done.21 = bf16[8,4,16,128]{3,2,1,0:T(8,128)(2,1)S(1)} collective-permute-done((bf16[8,4,16,128]{3,2,1,0:T(8,128)(2,1)S(1)}, bf16[8,4,16,128]{3,2,1,0:T(8,128)(2,1)S(1)}, u32[]{:S(2)}, u32[]{:S(2)}) %collective-permute-start.21) | collective-permute-done | bytes 131104 | tf_op jit(solution)/shard_map/ppermute | solution.py:258
  113.8 1.4 %collective-permute-done.22 = bf16[8,4,16,128]{3,2,1,0:T(8,128)(2,1)S(1)} collective-permute-done((bf16[8,4,16,128]{3,2,1,0:T(8,128)(2,1)S(1)}, bf16[8,4,16,128]{3,2,1,0:T(8,128)(2,1)S(1)}, u32[]{:S(2)}, u32[]{:S(2)}) %collective-permute-start.22) | collective-permute-done | bytes 131104 | tf_op jit(solution)/shard_map/ppermute | solution.py:258
  115.3 13.3 %all_to_all.17 = f32[8,4,16,128]{3,2,1,0:T(8,128)S(1)} all-to-all(f32[8,4,16,128]{3,2,1,0:T(8,128)S(1)} %convert_add_fusion), channel_id=1, replica_groups={{0,32,64,96,128,160,192,224},{8,40,72,104,136,168,200,232},{16,48,80,11..., dimensions={0} | all-to-all | bytes 524288 | tf_op jit(solution)/shard_map/all_to_all | solution.py:273
  (37 shorter events, 4.8 us)
Async XLA Ops:
  0.6 5.9 %collective-permute-start.1 = (bf16[1,512,128]{2,1,0:T(8,128)(2,1)}, bf16[1,512,128]{2,1,0:T(8,128)(2,1)S(1)}, u32[]{:S(2)}, u32[]{:S(2)}) collective-permute-start(bf16[1,512,128]{2,1,0:T(8,128)(2,1)} %rest_0_.2), channel_id=1, source_target_pairs={{0,6},{1,7},{2,0},{3,1},{4,2},{5,3},{6,4},{7,5},{8,14},{9,15},{10,... | collective-permute-start | bytes 393224 | tf_op jit(solution)/shard_map/ppermute | solution.py:263
  3.5 7.8 %collective-permute-start = (bf16[1,512,128]{2,1,0:T(8,128)(2,1)}, bf16[1,512,128]{2,1,0:T(8,128)(2,1)S(1)}, u32[]{:S(2)}, u32[]{:S(2)}) collective-permute-start(bf16[1,512,128]{2,1,0:T(8,128)(2,1)} %rest_0_.2), channel_id=1, source_target_pairs={{0,2},{1,3},{2,4},{3,5},{4,6},{5,7},{6,0},{7,1},{8,10},{9,11},{10,... | collective-permute-start | bytes 393224 | tf_op jit(solution)/shard_map/ppermute | solution.py:263
  3.5 7.8 %collective-permute-start.3 = (bf16[1,512,128]{2,1,0:T(8,128)(2,1)}, bf16[1,512,128]{2,1,0:T(8,128)(2,1)S(1)}, u32[]{:S(2)}, u32[]{:S(2)}) collective-permute-start(bf16[1,512,128]{2,1,0:T(8,128)(2,1)} %rest_0_.2), channel_id=1, source_target_pairs={{0,1},{1,0},{2,3},{3,2},{4,5},{5,4},{6,7},{7,6},{8,9},{9,8},{10,11... | collective-permute-start | bytes 393224 | tf_op jit(solution)/shard_map/ppermute | solution.py:268
  3.5 9.2 %collective-permute-start.7 = (bf16[1,512,128]{2,1,0:T(8,128)(2,1)}, bf16[1,512,128]{2,1,0:T(8,128)(2,1)S(1)}, u32[]{:S(2)}, u32[]{:S(2)}) collective-permute-start(bf16[1,512,128]{2,1,0:T(8,128)(2,1)} %rest_0_.3), channel_id=1, source_target_pairs={{0,2},{1,3},{2,4},{3,5},{4,6},{5,7},{6,0},{7,1},{8,10},{9,11},{10,... | collective-permute-start | bytes 393224 | tf_op jit(solution)/shard_map/ppermute | solution.py:263
  6.5 6.9 %collective-permute-start.2 = (bf16[1,512,128]{2,1,0:T(8,128)(2,1)S(1)}, bf16[1,512,128]{2,1,0:T(8,128)(2,1)S(1)}, u32[]{:S(2)}, u32[]{:S(2)}) collective-permute-start(bf16[1,512,128]{2,1,0:T(8,128)(2,1)S(1)} %collective-permute-done.1.rest_2_), channel_id=1, source_target_pairs={{0,6},{1,7},{2,0},{3,1},{4,2},{5,3},{6,4},{7,5},{8,14},{9,15},{10,... | collective-permute-start | bytes 393224 | tf_op jit(solution)/shard_map/ppermute | solution.py:263
  10.1 5.2 %collective-permute-start.8 = (bf16[1,512,128]{2,1,0:T(8,128)(2,1)}, bf16[1,512,128]{2,1,0:T(8,128)(2,1)S(1)}, u32[]{:S(2)}, u32[]{:S(2)}) collective-permute-start(bf16[1,512,128]{2,1,0:T(8,128)(2,1)} %rest_0_.3), channel_id=1, source_target_pairs={{0,6},{1,7},{2,0},{3,1},{4,2},{5,3},{6,4},{7,5},{8,14},{9,15},{10,... | collective-permute-start | bytes 393224 | tf_op jit(solution)/shard_map/ppermute | solution.py:263
  11.2 4.4 %collective-permute-start.5 = (bf16[1,512,128]{2,1,0:T(8,128)(2,1)S(1)}, bf16[1,512,128]{2,1,0:T(8,128)(2,1)S(1)}, u32[]{:S(2)}, u32[]{:S(2)}) collective-permute-start(bf16[1,512,128]{2,1,0:T(8,128)(2,1)S(1)} %collective-permute-done.1.rest_2_), channel_id=1, source_target_pairs={{0,1},{1,0},{2,3},{3,2},{4,5},{5,4},{6,7},{7,6},{8,9},{9,8},{10,11... | collective-permute-start | bytes 393224 | tf_op jit(solution)/shard_map/ppermute | solution.py:268
  11.3 4.6 %collective-permute-start.4 = (bf16[1,512,128]{2,1,0:T(8,128)(2,1)S(1)}, bf16[1,512,128]{2,1,0:T(8,128)(2,1)S(1)}, u32[]{:S(2)}, u32[]{:S(2)}) collective-permute-start(bf16[1,512,128]{2,1,0:T(8,128)(2,1)S(1)} %collective-permute-done.rest_1_), channel_id=1, source_target_pairs={{0,1},{1,0},{2,3},{3,2},{4,5},{5,4},{6,7},{7,6},{8,9},{9,8},{10,11... | collective-permute-start | bytes 393224 | tf_op jit(solution)/shard_map/ppermute | solution.py:268
  12.7 6.2 %collective-permute-start.9 = (bf16[1,512,128]{2,1,0:T(8,128)(2,1)S(1)}, bf16[1,512,128]{2,1,0:T(8,128)(2,1)S(1)}, u32[]{:S(2)}, u32[]{:S(2)}) collective-permute-start(bf16[1,512,128]{2,1,0:T(8,128)(2,1)S(1)} %collective-permute-done.7.rest_1_), channel_id=1, source_target_pairs={{0,2},{1,3},{2,4},{3,5},{4,6},{5,7},{6,0},{7,1},{8,10},{9,11},{10,... | collective-permute-start | bytes 393224 | tf_op jit(solution)/shard_map/ppermute | solution.py:263
  13.4 9.9 %collective-permute-start.6 = (bf16[1,512,128]{2,1,0:T(8,128)(2,1)S(1)}, bf16[1,512,128]{2,1,0:T(8,128)(2,1)S(1)}, u32[]{:S(2)}, u32[]{:S(2)}) collective-permute-start(bf16[1,512,128]{2,1,0:T(8,128)(2,1)S(1)} %collective-permute-done.2.rest_3_), channel_id=1, source_target_pairs={{0,1},{1,0},{2,3},{3,2},{4,5},{5,4},{6,7},{7,6},{8,9},{9,8},{10,11... | collective-permute-start | bytes 393224 | tf_op jit(solution)/shard_map/ppermute | solution.py:268
  15.3 12.7 %collective-permute-start.10 = (bf16[1,512,128]{2,1,0:T(8,128)(2,1)}, bf16[1,512,128]{2,1,0:T(8,128)(2,1)S(1)}, u32[]{:S(2)}, u32[]{:S(2)}) collective-permute-start(bf16[1,512,128]{2,1,0:T(8,128)(2,1)} %rest_0_.3), channel_id=1, source_target_pairs={{0,1},{1,0},{2,3},{3,2},{4,5},{5,4},{6,7},{7,6},{8,9},{9,8},{10,11... | collective-permute-start | bytes 393224 | tf_op jit(solution)/shard_map/ppermute | solution.py:268
  15.6 12.4 %collective-permute-start.11 = (bf16[1,512,128]{2,1,0:T(8,128)(2,1)S(1)}, bf16[1,512,128]{2,1,0:T(8,128)(2,1)S(1)}, u32[]{:S(2)}, u32[]{:S(2)}) collective-permute-start(bf16[1,512,128]{2,1,0:T(8,128)(2,1)S(1)} %collective-permute-done.7.rest_1_), channel_id=1, source_target_pairs={{0,1},{1,0},{2,3},{3,2},{4,5},{5,4},{6,7},{7,6},{8,9},{9,8},{10,11... | collective-permute-start | bytes 393224 | tf_op jit(solution)/shard_map/ppermute | solution.py:268
  15.8 12.2 %collective-permute-start.12 = (bf16[1,512,128]{2,1,0:T(8,128)(2,1)S(1)}, bf16[1,512,128]{2,1,0:T(8,128)(2,1)S(1)}, u32[]{:S(2)}, u32[]{:S(2)}) collective-permute-start(bf16[1,512,128]{2,1,0:T(8,128)(2,1)S(1)} %collective-permute-done.8.rest_2_), channel_id=1, source_target_pairs={{0,1},{1,0},{2,3},{3,2},{4,5},{5,4},{6,7},{7,6},{8,9},{9,8},{10,11... | collective-permute-start | bytes 393224 | tf_op jit(solution)/shard_map/ppermute | solution.py:268
  18.8 9.2 %collective-permute-start.13 = (bf16[1,512,128]{2,1,0:T(8,128)(2,1)S(1)}, bf16[1,512,128]{2,1,0:T(8,128)(2,1)S(1)}, u32[]{:S(2)}, u32[]{:S(2)}) collective-permute-start(bf16[1,512,128]{2,1,0:T(8,128)(2,1)S(1)} %collective-permute-done.9.rest_3_), channel_id=1, source_target_pairs={{0,1},{1,0},{2,3},{3,2},{4,5},{5,4},{6,7},{7,6},{8,9},{9,8},{10,11... | collective-permute-start | bytes 393224 | tf_op jit(solution)/shard_map/ppermute | solution.py:268
  18.8 1.0 copy-start
  19.9 3.4 %copy-start.2 = (bf16[1,512,128]{2,1,0:T(8,128)(2,1)S(1)}, bf16[1,512,128]{2,1,0:T(8,128)(2,1)}, u32[]{:S(2)}) copy-start(bf16[1,512,128]{2,1,0:T(8,128)(2,1)} %rest_0_.2) | copy-start | bytes 393220
  23.3 4.8 %copy-start.1 = (bf16[1,512,128]{2,1,0:T(8,128)(2,1)S(1)}, bf16[1,512,128]{2,1,0:T(8,128)(2,1)}, u32[]{:S(2)}) copy-start(bf16[1,512,128]{2,1,0:T(8,128)(2,1)} %rest_0_.3) | copy-start | bytes 393220
  30.1 6.2 %collective-permute-start.14 = (bf16[512,128]{1,0:T(8,128)(2,1)S(1)}, bf16[512,128]{1,0:T(8,128)(2,1)S(1)}, u32[]{:S(2)}, u32[]{:S(2)}) collective-permute-start(bf16[512,128]{1,0:T(8,128)(2,1)S(1)} %get-tuple-element.28), channel_id=1, source_target_pairs={{0,8},{8,16},{16,24},{24,0},{32,40},{40,48},{48,56},{56,32},{64,72... | collective-permute-start | bytes 393224 | tf_op jit(solution)/shard_map/ppermute | solution.py:258
  31.5 7.9 %collective-permute-start.15 = (bf16[512,128]{1,0:T(8,128)(2,1)S(1)}, bf16[512,128]{1,0:T(8,128)(2,1)S(1)}, u32[]{:S(2)}, u32[]{:S(2)}) collective-permute-start(bf16[512,128]{1,0:T(8,128)(2,1)S(1)} %get-tuple-element.29), channel_id=1, source_target_pairs={{0,16},{8,24},{16,0},{24,8},{32,48},{40,56},{48,32},{56,40},{64,80... | collective-permute-start | bytes 393224 | tf_op jit(solution)/shard_map/ppermute | solution.py:258
  32.5 8.3 %collective-permute-start.16 = (bf16[512,128]{1,0:T(8,128)(2,1)S(1)}, bf16[512,128]{1,0:T(8,128)(2,1)S(1)}, u32[]{:S(2)}, u32[]{:S(2)}) collective-permute-start(bf16[512,128]{1,0:T(8,128)(2,1)S(1)} %get-tuple-element.30), channel_id=1, source_target_pairs={{0,24},{8,0},{16,8},{24,16},{32,56},{40,32},{48,40},{56,48},{64,88... | collective-permute-start | bytes 393224 | tf_op jit(solution)/shard_map/ppermute | solution.py:258
  87.4 6.6 %collective-permute-start.17 = (bf16[544,128]{1,0:T(8,128)(2,1)S(1)}, bf16[544,128]{1,0:T(8,128)(2,1)S(1)}, u32[]{:S(2)}, u32[]{:S(2)}) collective-permute-start(bf16[544,128]{1,0:T(8,128)(2,1)S(1)} %get-tuple-element.32), channel_id=1, source_target_pairs={{0,8},{8,16},{16,24},{24,0},{32,40},{40,48},{48,56},{56,32},{64,72... | collective-permute-start | bytes 417800 | tf_op jit(solution)/shard_map/ppermute | solution.py:258
  87.5 8.3 %collective-permute-start.18 = (bf16[544,128]{1,0:T(8,128)(2,1)S(1)}, bf16[544,128]{1,0:T(8,128)(2,1)S(1)}, u32[]{:S(2)}, u32[]{:S(2)}) collective-permute-start(bf16[544,128]{1,0:T(8,128)(2,1)S(1)} %get-tuple-element.33), channel_id=1, source_target_pairs={{0,16},{8,24},{16,0},{24,8},{32,48},{40,56},{48,32},{56,40},{64,80... | collective-permute-start | bytes 417800 | tf_op jit(solution)/shard_map/ppermute | solution.py:258
  91.2 6.5 %collective-permute-start.19 = (bf16[544,128]{1,0:T(8,128)(2,1)S(1)}, bf16[544,128]{1,0:T(8,128)(2,1)S(1)}, u32[]{:S(2)}, u32[]{:S(2)}) collective-permute-start(bf16[544,128]{1,0:T(8,128)(2,1)S(1)} %get-tuple-element.34), channel_id=1, source_target_pairs={{0,24},{8,0},{16,8},{24,16},{32,56},{40,32},{48,40},{56,48},{64,88... | collective-permute-start | bytes 417800 | tf_op jit(solution)/shard_map/ppermute | solution.py:258
  105.8 5.6 %collective-permute-start.20 = (bf16[8,4,16,128]{3,2,1,0:T(8,128)(2,1)S(1)}, bf16[8,4,16,128]{3,2,1,0:T(8,128)(2,1)S(1)}, u32[]{:S(2)}, u32[]{:S(2)}) collective-permute-start(bf16[8,4,16,128]{3,2,1,0:T(8,128)(2,1)S(1)} %get-tuple-element.37), channel_id=1, source_target_pairs={{0,8},{8,16},{16,24},{24,0},{32,40},{40,48},{48,56},{56,32},{64,72... | collective-permute-start | bytes 393224 | tf_op jit(solution)/shard_map/ppermute | solution.py:258
  106.3 7.5 %collective-permute-start.21 = (bf16[8,4,16,128]{3,2,1,0:T(8,128)(2,1)S(1)}, bf16[8,4,16,128]{3,2,1,0:T(8,128)(2,1)S(1)}, u32[]{:S(2)}, u32[]{:S(2)}) collective-permute-start(bf16[8,4,16,128]{3,2,1,0:T(8,128)(2,1)S(1)} %get-tuple-element.38), channel_id=1, source_target_pairs={{0,16},{8,24},{16,0},{24,8},{32,48},{40,56},{48,32},{56,40},{64,80... | collective-permute-start | bytes 393224 | tf_op jit(solution)/shard_map/ppermute | solution.py:258
  109.7 5.5 %collective-permute-start.22 = (bf16[8,4,16,128]{3,2,1,0:T(8,128)(2,1)S(1)}, bf16[8,4,16,128]{3,2,1,0:T(8,128)(2,1)S(1)}, u32[]{:S(2)}, u32[]{:S(2)}) collective-permute-start(bf16[8,4,16,128]{3,2,1,0:T(8,128)(2,1)S(1)} %get-tuple-element.39), channel_id=1, source_target_pairs={{0,24},{8,0},{16,8},{24,16},{32,56},{40,32},{48,40},{56,48},{64,88... | collective-permute-start | bytes 393224 | tf_op jit(solution)/shard_map/ppermute | solution.py:258

commit v2 on v1

--- a/solution.py
+++ b/solution.py
@@ -258,14 +258,12 @@
     return lax.ppermute(array, "inner", pairs)
 
 
-def gather(array, tiles, forward):
-    def hop(value, step):
-        return lax.ppermute(value, "cols", [(i, (i + 2 * step) % tiles) for i in range(tiles)])
-
-    left, right = hop(array, 1), hop(array, -1)
-    far = hop(left, 1) if forward else hop(right, -1)
-    mine = [array, left, right, far]
-    return mine + [lax.ppermute(value, "cols", [(i, i ^ 1) for i in range(tiles)]) for value in mine]
+def hop(value, step, tiles):
+    return lax.ppermute(value, "cols", [(i, (i + 2 * step) % tiles) for i in range(tiles)])
+
+
+def swap(value, tiles):
+    return lax.ppermute(value, "cols", [(i, i ^ 1) for i in range(tiles)])
 
 
 def over_z(array, zs):
@@ -294,8 +292,6 @@
 
     right_u = pltpu.with_memory_space_constraint(right_u, pltpu.HBM)
     right_v = pltpu.with_memory_space_constraint(right_v, pltpu.HBM)
-    group_v = gather(left_v, tiles, False)
-    group_u = gather(left_u, tiles, True)
     unit = 2 * NB * R * R
 
     def cost(units, mib):
@@ -311,6 +307,14 @@
         cost_estimate=cost(outs * slots, 6),
         name="probe",
     )(meta, right_v, sketch)
+    near = [hop(left_v, 1, tiles), hop(left_v, -1, tiles)]
+    *near, probe_h, probe_l, left_u = lax.optimization_barrier((*near, probe_h, probe_l, left_u))
+    group_v = [left_v, *near, hop(near[1], -1, tiles)]
+    group_v += [swap(value, tiles) for value in group_v]
+    near = [hop(left_u, 1, tiles), hop(left_u, -1, tiles)]
+    group_u = [left_u, *near]
+    other_u = [swap(value, tiles) for value in group_u]
+    far_u = hop(near[0], 1, tiles)
     pair_h, pair_l, mixing = pl.pallas_call(
         functools.partial(pair_kernel, outs, slots),
         out_shape=(square,) * 3,
@@ -321,6 +325,8 @@
         cost_estimate=cost(outs * slots * 1.75, 10),
         name="pair",
     )(meta, right_u, probe_h, probe_l, *group_v)
+    far_u, mixing = lax.optimization_barrier((far_u, mixing))
+    group_u += [far_u, *other_u, swap(far_u, tiles)]
     own, send1, send2, send3, group = pl.pallas_call(
         functools.partial(sketch_kernel, outs, slots),
         out_shape=(shape((NB, R), F32),) + (shape((NB, R), BF),) * 3 + (shape((tiles, NB, R), BF),),

time: 129 us -> 125 us (0.969); the launches traced: 129 us -> 123 us
  waiting for transfers between devices: 24 us -> 18.3 us
  starting transfers between devices: 23 us -> 24.6 us
    ppermute x6, waiting for transfers between devices: 7.93 us -> 3.72 us  [hop(): lax.ppermute(value, 'cols', [(i, (i + 2 * step) % tiles) for i in range(t...]
    ppermute x9, waiting for transfers between devices: 16 us -> 13.3 us  [shift_y(): return lax.ppermute(array, 'inner', pairs)]
    ppermute x6, starting transfers between devices: 7.23 us -> 9.41 us  [hop(): lax.ppermute(value, 'cols', [(i, (i + 2 * step) % tiles) for i in range(t...]
    ppermute x8, waiting for transfers between devices: 0.02 us -> 1.34 us  [swap(): return lax.ppermute(value, 'cols', [(i, i ^ 1) for i in range(tiles)])]
  transfers between devices with their start and end apart: 23 -> 23, of which waited for: 14 -> 13; matrix products, arithmetic and copies ran while one was open for 1% -> 1% of each run, Pallas kernels for 6% -> 7%
where the time goes in v2:
time: 125 us; the launch traced here: 123 us
  blocking collectives  46.9 us (38%)
  Pallas kernels  29 us (23%)
  starting transfers between devices  24.6 us (20%)
  waiting for transfers between devices  18.3 us (15%)
  other arithmetic  2.27 us (2%)
    all_to_all x3, blocking collectives, over_z(): lax.all_to_all(array, 'inner', 0, 0, tiled=True, axis_index_groups=groups)  46.9 us
    ppermute x9, starting transfers between devices, shift_y(): return lax.ppermute(array, 'inner', pairs)  14 us
    ppermute x9, waiting for transfers between devices, shift_y(): return lax.ppermute(array, 'inner', pairs)  13.3 us
    pallas_call x1, Pallas kernels, body(): pl.pallas_call(functools.partial(ortho_kernel, outs, slots, zs), out_shap...  10.8 us
    ppermute x6, starting transfers between devices, hop(): lax.ppermute(value, 'cols', [(i, (i + 2 * step) % tiles) for i in range(t...  9.41 us
    pallas_call x1, Pallas kernels, body(): pl.pallas_call(functools.partial(backward_kernel, outs, slots, zs), out_s...  8.14 us
    pallas_call x1, Pallas kernels, body(): pl.pallas_call(functools.partial(pair_kernel, outs, slots), out_shape=(sq...  4.7 us
    ppermute x6, waiting for transfers between devices, hop(): lax.ppermute(value, 'cols', [(i, (i + 2 * step) % tiles) for i in range(t...  3.72 us
  transfers between devices with their start and end apart: 23, of which 13 were waited for; matrix products, arithmetic and copies ran while one was open for 1% of the time, Pallas kernels for 7%

profile of v2, /device:TPU:8, one launch (start us, length us, event | category | flops | bytes accessed | tf_op | source)
XLA Modules:
  0.0 123.0 jit_solution(2626422759098138601)
XLA Ops:
  0.6 2.8 %collective-permute-start.1 = (bf16[1,512,128]{2,1,0:T(8,128)(2,1)}, bf16[1,512,128]{2,1,0:T(8,128)(2,1)S(1)}, u32[]{:S(2)}, u32[]{:S(2)}) collective-permute-start(bf16[1,512,128]{2,1,0:T(8,128)(2,1)} %rest_0_.1), channel_id=1, source_target_pairs={{0,6},{1,7},{2,0},{3,1},{4,2},{5,3},{6,4},{7,5},{8,14},{9,15},{10,... | collective-permute-start | bytes 393224 | tf_op jit(solution)/shard_map/ppermute | solution.py:262
  3.5 0.7 broadcast_subtract_fusion
  4.2 0.8 reduce_sum.27
  5.1 1.0 copy-done
  6.2 3.4 %probe.1 = (bf16[32,128,128]{2,1,0:T(8,128)(2,1)S(1)}, bf16[32,128,128]{2,1,0:T(8,128)(2,1)S(1)}) custom-call(s32[39]{0:T(128)S(1)} %concatenate.3.meta, bf16[4,8,512,128]{3,2,1,0:T(8,128)(2,1)} %right_v.3, bf16[4,512,128]{2,1,0:T(8,128)(2,1)S(1)} %copy-done), custom_call_target="tpu_custom_call" | custom-call | flops 536870912 | bytes 6291456 | tf_op jit(solution)/shard_map/probe/pallas_call | solution.py:300
  9.9 3.3 %collective-permute-start.4 = (bf16[1,512,128]{2,1,0:T(8,128)(2,1)S(1)}, bf16[1,512,128]{2,1,0:T(8,128)(2,1)S(1)}, u32[]{:S(2)}, u32[]{:S(2)}) collective-permute-start(bf16[1,512,128]{2,1,0:T(8,128)(2,1)S(1)} %collective-permute-done.1.rest_2_), channel_id=1, source_target_pairs={{0,6},{1,7},{2,0},{3,1},{4,2},{5,3},{6,4},{7,5},{8,14},{9,15},{10,... | collective-permute-start | bytes 393224 | tf_op jit(solution)/shard_map/ppermute | solution.py:262
  13.7 3.2 %collective-permute-start.9 = (bf16[1,512,128]{2,1,0:T(8,128)(2,1)S(1)}, bf16[1,512,128]{2,1,0:T(8,128)(2,1)S(1)}, u32[]{:S(2)}, u32[]{:S(2)}) collective-permute-start(bf16[1,512,128]{2,1,0:T(8,128)(2,1)S(1)} %copy-done.1), channel_id=1, source_target_pairs={{0,6},{1,7},{2,0},{3,1},{4,2},{5,3},{6,4},{7,5},{8,14},{9,15},{10,... | collective-permute-start | bytes 393224 | tf_op jit(solution)/shard_map/ppermute | solution.py:262
  17.0 2.6 %collective-permute-done.2.rest_1_ = bf16[1,512,128]{2,1,0:T(8,128)(2,1)S(1)} collective-permute-done((bf16[1,512,128]{2,1,0:T(8,128)(2,1)S(1)}, bf16[1,512,128]{2,1,0:T(8,128)(2,1)S(1)}, u32[]{:S(2)}, u32[]{:S(2)}) %collective-permute-start.2) | collective-permute-done | bytes 131104 | tf_op jit(solution)/shard_map/ppermute | solution.py:262
  20.2 4.7 %pair.1 = (bf16[32,128,128]{2,1,0:T(8,128)(2,1)S(1)}, bf16[32,128,128]{2,1,0:T(8,128)(2,1)S(1)}, bf16[32,128,128]{2,1,0:T(8,128)(2,1)S(1)}) custom-call(s32[39]{0:T(128)S(1)} %concatenate.3.meta, bf16[4,8,512,128]{3,2,1,0:T(8,128)(2,1)} %right_u.1, bf16[32,128,128]{2,1,0:T(8,128)(2,1)S(1)} %get-tuple-element.31.probe_h, ...), custom_call_target="tpu_custom_call" | custom-call | flops 939524096 | bytes 10485760 | tf_op jit(solution)/shard_map/pair/pallas_call | solution.py:318
  24.9 0.8 collective-permute-done.3.rest_3_
  25.7 1.3 %collective-permute-done.13.rest_7_ = bf16[1,512,128]{2,1,0:T(8,128)(2,1)S(1)} collective-permute-done((bf16[1,512,128]{2,1,0:T(8,128)(2,1)S(1)}, bf16[1,512,128]{2,1,0:T(8,128)(2,1)S(1)}, u32[]{:S(2)}, u32[]{:S(2)}) %collective-permute-start.13) | collective-permute-done | bytes 131104 | tf_op jit(solution)/shard_map/ppermute | solution.py:266
  27.1 2.0 %sketch.3 = (f32[512,128]{1,0:T(8,128)S(1)}, bf16[512,128]{1,0:T(8,128)(2,1)S(1)}, bf16[512,128]{1,0:T(8,128)(2,1)S(1)}, bf16[512,128]{1,0:T(8,128)(2,1)S(1)}, bf16[8,512,128]{2,1,0:T(8,128)(2,1)S(1)}) custom-call(s32[39]{0:T(128)S(1)} %concatenate.3.meta, bf16[32,128,128]{2,1,0:T(8,128)(2,1)S(1)} %get-tuple-element.36.mixing, ...), custom_call_target="tpu_custom_call" | custom-call | flops 536870912 | bytes 4194304 | tf_op jit(solution)/shard_map/sketch/pallas_call | solution.py:330
  29.1 1.7 %collective-permute-start.14 = (bf16[512,128]{1,0:T(8,128)(2,1)S(1)}, bf16[512,128]{1,0:T(8,128)(2,1)S(1)}, u32[]{:S(2)}, u32[]{:S(2)}) collective-permute-start(bf16[512,128]{1,0:T(8,128)(2,1)S(1)} %get-tuple-element.42), channel_id=1, source_target_pairs={{0,8},{8,16},{16,24},{24,0},{32,40},{40,48},{48,56},{56,32},{64,72... | collective-permute-start | bytes 393224 | tf_op jit(solution)/shard_map/ppermute | solution.py:258
  30.7 1.1 collective-permute-start.15
  31.8 2.4 %collective-permute-start.16 = (bf16[512,128]{1,0:T(8,128)(2,1)S(1)}, bf16[512,128]{1,0:T(8,128)(2,1)S(1)}, u32[]{:S(2)}, u32[]{:S(2)}) collective-permute-start(bf16[512,128]{1,0:T(8,128)(2,1)S(1)} %get-tuple-element.44), channel_id=1, source_target_pairs={{0,24},{8,0},{16,8},{24,16},{32,56},{40,32},{48,40},{56,48},{64,88... | collective-permute-start | bytes 393224 | tf_op jit(solution)/shard_map/ppermute | solution.py:258
  34.7 3.9 %collective-permute-done.15 = bf16[512,128]{1,0:T(8,128)(2,1)S(1)} collective-permute-done((bf16[512,128]{1,0:T(8,128)(2,1)S(1)}, bf16[512,128]{1,0:T(8,128)(2,1)S(1)}, u32[]{:S(2)}, u32[]{:S(2)}) %collective-permute-start.15) | collective-permute-done | bytes 131104 | tf_op jit(solution)/shard_map/ppermute | solution.py:258
  38.6 1.1 collective-permute-done.16
  39.8 20.9 %all_to_all.15 = f32[8,64,128]{2,1,0:T(8,128)S(1)} all-to-all(f32[8,64,128]{2,1,0:T(8,128)S(1)} %bitcast.4), channel_id=1, replica_groups={{0,32,64,96,128,160,192,224},{8,40,72,104,136,168,200,232},{16,48,80,11..., dimensions={0} | all-to-all | bytes 524288 | tf_op jit(solution)/shard_map/all_to_all | solution.py:271
  60.7 13.1 %all_to_all.16.blocks = f32[8,64,128]{2,1,0:T(8,128)S(1)} all-to-all(f32[8,64,128]{2,1,0:T(8,128)S(1)} %broadcast_in_dim.2), channel_id=1, replica_groups={{0,32,64,96,128,160,192,224},{8,40,72,104,136,168,200,232},{16,48,80,11..., dimensions={0} | all-to-all | bytes 524288 | tf_op jit(solution)/shard_map/all_to_all | solution.py:271
  73.8 10.8 %ortho.1 = (bf16[544,128]{1,0:T(8,128)(2,1)S(1)}, bf16[544,128]{1,0:T(8,128)(2,1)S(1)}, bf16[544,128]{1,0:T(8,128)(2,1)S(1)}, bf16[544,128]{1,0:T(8,128)(2,1)S(1)}) custom-call(s32[39]{0:T(128)S(1)} %concatenate.3.meta, f32[8,64,128]{2,1,0:T(8,128)S(1)} %all_to_all.16.blocks), custom_call_target="tpu_custom_call" | custom-call | flops 218103808 | bytes 1048576 | tf_op jit(solution)/shard_map/ortho/pallas_call | solution.py:347
  84.7 2.0 %collective-permute-start.18 = (bf16[544,128]{1,0:T(8,128)(2,1)S(1)}, bf16[544,128]{1,0:T(8,128)(2,1)S(1)}, u32[]{:S(2)}, u32[]{:S(2)}) collective-permute-start(bf16[544,128]{1,0:T(8,128)(2,1)S(1)} %get-tuple-element.47), channel_id=1, source_target_pairs={{0,16},{8,24},{16,0},{24,8},{32,48},{40,56},{48,32},{56,40},{64,80... | collective-permute-start | bytes 417800 | tf_op jit(solution)/shard_map/ppermute | solution.py:258
  86.7 2.2 %collective-permute-start.19 = (bf16[544,128]{1,0:T(8,128)(2,1)S(1)}, bf16[544,128]{1,0:T(8,128)(2,1)S(1)}, u32[]{:S(2)}, u32[]{:S(2)}) collective-permute-start(bf16[544,128]{1,0:T(8,128)(2,1)S(1)} %get-tuple-element.48), channel_id=1, source_target_pairs={{0,24},{8,0},{16,8},{24,16},{32,56},{40,32},{48,40},{56,48},{64,88... | collective-permute-start | bytes 417800 | tf_op jit(solution)/shard_map/ppermute | solution.py:258
  88.9 0.8 collective-permute-done.17.msg1
  89.7 1.7 %collective-permute-done.18.msg2 = bf16[544,128]{1,0:T(8,128)(2,1)S(1)} collective-permute-done((bf16[544,128]{1,0:T(8,128)(2,1)S(1)}, bf16[544,128]{1,0:T(8,128)(2,1)S(1)}, u32[]{:S(2)}, u32[]{:S(2)}) %collective-permute-start.18) | collective-permute-done | bytes 139296 | tf_op jit(solution)/shard_map/ppermute | solution.py:258
  91.5 1.4 %collective-permute-done.19.msg3 = bf16[544,128]{1,0:T(8,128)(2,1)S(1)} collective-permute-done((bf16[544,128]{1,0:T(8,128)(2,1)S(1)}, bf16[544,128]{1,0:T(8,128)(2,1)S(1)}, u32[]{:S(2)}, u32[]{:S(2)}) %collective-permute-start.19) | collective-permute-done | bytes 139296 | tf_op jit(solution)/shard_map/ppermute | solution.py:258
  92.8 8.1 %backward.1 = (f32[8,4,16,128]{3,2,1,0:T(8,128)S(1)}, bf16[8,4,16,128]{3,2,1,0:T(8,128)(2,1)S(1)}, bf16[8,4,16,128]{3,2,1,0:T(8,128)(2,1)S(1)}, bf16[8,4,16,128]{3,2,1,0:T(8,128)(2,1)S(1)}, f32[4,16,128]{2,1,0:T(8,128)}) custom-call(s32[39]{0:T(128)S(1)} %concatenate.3.meta, bf16[4,8,512,128]{3,2,1,0:T(8,128)(2,1)} %right_v.3, ...), custom_call_target="tpu_custom_call" | custom-call | flops 1476395008 | bytes 8388608 | tf_op jit(solution)/shard_map/backward/pallas_call | solution.py:359
  101.5 2.6 %collective-permute-start.21 = (bf16[8,4,16,128]{3,2,1,0:T(8,128)(2,1)S(1)}, bf16[8,4,16,128]{3,2,1,0:T(8,128)(2,1)S(1)}, u32[]{:S(2)}, u32[]{:S(2)}) collective-permute-start(bf16[8,4,16,128]{3,2,1,0:T(8,128)(2,1)S(1)} %get-tuple-element.52), channel_id=1, source_target_pairs={{0,16},{8,24},{16,0},{24,8},{32,48},{40,56},{48,32},{56,40},{64,80... | collective-permute-start | bytes 393224 | tf_op jit(solution)/shard_map/ppermute | solution.py:258
  104.1 1.5 %collective-permute-start.22 = (bf16[8,4,16,128]{3,2,1,0:T(8,128)(2,1)S(1)}, bf16[8,4,16,128]{3,2,1,0:T(8,128)(2,1)S(1)}, u32[]{:S(2)}, u32[]{:S(2)}) collective-permute-start(bf16[8,4,16,128]{3,2,1,0:T(8,128)(2,1)S(1)} %get-tuple-element.53), channel_id=1, source_target_pairs={{0,24},{8,0},{16,8},{24,16},{32,56},{40,32},{48,40},{56,48},{64,88... | collective-permute-start | bytes 393224 | tf_op jit(solution)/shard_map/ppermute | solution.py:258
  106.0 2.0 %collective-permute-done.21 = bf16[8,4,16,128]{3,2,1,0:T(8,128)(2,1)S(1)} collective-permute-done((bf16[8,4,16,128]{3,2,1,0:T(8,128)(2,1)S(1)}, bf16[8,4,16,128]{3,2,1,0:T(8,128)(2,1)S(1)}, u32[]{:S(2)}, u32[]{:S(2)}) %collective-permute-start.21) | collective-permute-done | bytes 131104 | tf_op jit(solution)/shard_map/ppermute | solution.py:258
  108.1 1.4 %collective-permute-done.22 = bf16[8,4,16,128]{3,2,1,0:T(8,128)(2,1)S(1)} collective-permute-done((bf16[8,4,16,128]{3,2,1,0:T(8,128)(2,1)S(1)}, bf16[8,4,16,128]{3,2,1,0:T(8,128)(2,1)S(1)}, u32[]{:S(2)}, u32[]{:S(2)}) %collective-permute-start.22) | collective-permute-done | bytes 131104 | tf_op jit(solution)/shard_map/ppermute | solution.py:258
  109.5 12.9 %all_to_all.17 = f32[8,4,16,128]{3,2,1,0:T(8,128)S(1)} all-to-all(f32[8,4,16,128]{3,2,1,0:T(8,128)S(1)} %convert_add_fusion), channel_id=1, replica_groups={{0,32,64,96,128,160,192,224},{8,40,72,104,136,168,200,232},{16,48,80,11..., dimensions={0} | all-to-all | bytes 524288 | tf_op jit(solution)/shard_map/all_to_all | solution.py:271
  122.4 0.6 reduce_sum.29
  (37 shorter events, 3.4 us)
Async XLA Ops:
  0.6 8.9 %collective-permute-start.1 = (bf16[1,512,128]{2,1,0:T(8,128)(2,1)}, bf16[1,512,128]{2,1,0:T(8,128)(2,1)S(1)}, u32[]{:S(2)}, u32[]{:S(2)}) collective-permute-start(bf16[1,512,128]{2,1,0:T(8,128)(2,1)} %rest_0_.1), channel_id=1, source_target_pairs={{0,6},{1,7},{2,0},{3,1},{4,2},{5,3},{6,4},{7,5},{8,14},{9,15},{10,... | collective-permute-start | bytes 393224 | tf_op jit(solution)/shard_map/ppermute | solution.py:262
  3.5 6.4 %collective-permute-start = (bf16[1,512,128]{2,1,0:T(8,128)(2,1)}, bf16[1,512,128]{2,1,0:T(8,128)(2,1)S(1)}, u32[]{:S(2)}, u32[]{:S(2)}) collective-permute-start(bf16[1,512,128]{2,1,0:T(8,128)(2,1)} %rest_0_.1), channel_id=1, source_target_pairs={{0,2},{1,3},{2,4},{3,5},{4,6},{5,7},{6,0},{7,1},{8,10},{9,11},{10,... | collective-permute-start | bytes 393224 | tf_op jit(solution)/shard_map/ppermute | solution.py:262
  3.5 10.2 %collective-permute-start.5 = (bf16[1,512,128]{2,1,0:T(8,128)(2,1)}, bf16[1,512,128]{2,1,0:T(8,128)(2,1)S(1)}, u32[]{:S(2)}, u32[]{:S(2)}) collective-permute-start(bf16[1,512,128]{2,1,0:T(8,128)(2,1)} %rest_0_.1), channel_id=1, source_target_pairs={{0,1},{1,0},{2,3},{3,2},{4,5},{5,4},{6,7},{7,6},{8,9},{9,8},{10,11... | collective-permute-start | bytes 393224 | tf_op jit(solution)/shard_map/ppermute | solution.py:266
  5.1 1.0 copy-start
  6.2 7.0 %copy-start.1 = (bf16[1,512,128]{2,1,0:T(8,128)(2,1)S(1)}, bf16[1,512,128]{2,1,0:T(8,128)(2,1)}, u32[]{:S(2)}) copy-start(bf16[1,512,128]{2,1,0:T(8,128)(2,1)} %rest_0_.2) | copy-start | bytes 393220
  6.2 14.0 %copy-start.2 = (bf16[1,512,128]{2,1,0:T(8,128)(2,1)S(1)}, bf16[1,512,128]{2,1,0:T(8,128)(2,1)}, u32[]{:S(2)}) copy-start(bf16[1,512,128]{2,1,0:T(8,128)(2,1)} %rest_0_.1) | copy-start | bytes 393220
  9.9 7.1 %collective-permute-start.4 = (bf16[1,512,128]{2,1,0:T(8,128)(2,1)S(1)}, bf16[1,512,128]{2,1,0:T(8,128)(2,1)S(1)}, u32[]{:S(2)}, u32[]{:S(2)}) collective-permute-start(bf16[1,512,128]{2,1,0:T(8,128)(2,1)S(1)} %collective-permute-done.1.rest_2_), channel_id=1, source_target_pairs={{0,6},{1,7},{2,0},{3,1},{4,2},{5,3},{6,4},{7,5},{8,14},{9,15},{10,... | collective-permute-start | bytes 393224 | tf_op jit(solution)/shard_map/ppermute | solution.py:262
  13.2 6.3 %collective-permute-start.2 = (bf16[1,512,128]{2,1,0:T(8,128)(2,1)S(1)}, bf16[1,512,128]{2,1,0:T(8,128)(2,1)S(1)}, u32[]{:S(2)}, u32[]{:S(2)}) collective-permute-start(bf16[1,512,128]{2,1,0:T(8,128)(2,1)S(1)} %copy-done.1), channel_id=1, source_target_pairs={{0,2},{1,3},{2,4},{3,5},{4,6},{5,7},{6,0},{7,1},{8,10},{9,11},{10,... | collective-permute-start | bytes 393224 | tf_op jit(solution)/shard_map/ppermute | solution.py:262
  13.2 6.3 %collective-permute-start.6 = (bf16[1,512,128]{2,1,0:T(8,128)(2,1)S(1)}, bf16[1,512,128]{2,1,0:T(8,128)(2,1)S(1)}, u32[]{:S(2)}, u32[]{:S(2)}) collective-permute-start(bf16[1,512,128]{2,1,0:T(8,128)(2,1)S(1)} %collective-permute-done.rest_1_), channel_id=1, source_target_pairs={{0,1},{1,0},{2,3},{3,2},{4,5},{5,4},{6,7},{7,6},{8,9},{9,8},{10,11... | collective-permute-start | bytes 393224 | tf_op jit(solution)/shard_map/ppermute | solution.py:266
  13.2 6.4 %collective-permute-start.7 = (bf16[1,512,128]{2,1,0:T(8,128)(2,1)S(1)}, bf16[1,512,128]{2,1,0:T(8,128)(2,1)S(1)}, u32[]{:S(2)}, u32[]{:S(2)}) collective-permute-start(bf16[1,512,128]{2,1,0:T(8,128)(2,1)S(1)} %collective-permute-done.1.rest_2_), channel_id=1, source_target_pairs={{0,1},{1,0},{2,3},{3,2},{4,5},{5,4},{6,7},{7,6},{8,9},{9,8},{10,11... | collective-permute-start | bytes 393224 | tf_op jit(solution)/shard_map/ppermute | solution.py:266
  13.7 6.4 %collective-permute-start.9 = (bf16[1,512,128]{2,1,0:T(8,128)(2,1)S(1)}, bf16[1,512,128]{2,1,0:T(8,128)(2,1)S(1)}, u32[]{:S(2)}, u32[]{:S(2)}) collective-permute-start(bf16[1,512,128]{2,1,0:T(8,128)(2,1)S(1)} %copy-done.1), channel_id=1, source_target_pairs={{0,6},{1,7},{2,0},{3,1},{4,2},{5,3},{6,4},{7,5},{8,14},{9,15},{10,... | collective-permute-start | bytes 393224 | tf_op jit(solution)/shard_map/ppermute | solution.py:262
  16.9 3.2 %collective-permute-start.8 = (bf16[1,512,128]{2,1,0:T(8,128)(2,1)S(1)}, bf16[1,512,128]{2,1,0:T(8,128)(2,1)S(1)}, u32[]{:S(2)}, u32[]{:S(2)}) collective-permute-start(bf16[1,512,128]{2,1,0:T(8,128)(2,1)S(1)} %collective-permute-done.4.rest_3_), channel_id=1, source_target_pairs={{0,1},{1,0},{2,3},{3,2},{4,5},{5,4},{6,7},{7,6},{8,9},{9,8},{10,11... | collective-permute-start | bytes 393224 | tf_op jit(solution)/shard_map/ppermute | solution.py:266
  19.5 6.2 %collective-permute-start.3 = (bf16[1,512,128]{2,1,0:T(8,128)(2,1)S(1)}, bf16[1,512,128]{2,1,0:T(8,128)(2,1)S(1)}, u32[]{:S(2)}, u32[]{:S(2)}) collective-permute-start(bf16[1,512,128]{2,1,0:T(8,128)(2,1)S(1)} %collective-permute-done.2.rest_1_), channel_id=1, source_target_pairs={{0,2},{1,3},{2,4},{3,5},{4,6},{5,7},{6,0},{7,1},{8,10},{9,11},{10,... | collective-permute-start | bytes 393224 | tf_op jit(solution)/shard_map/ppermute | solution.py:262
  19.5 6.2 %collective-permute-start.10 = (bf16[1,512,128]{2,1,0:T(8,128)(2,1)S(1)}, bf16[1,512,128]{2,1,0:T(8,128)(2,1)S(1)}, u32[]{:S(2)}, u32[]{:S(2)}) collective-permute-start(bf16[1,512,128]{2,1,0:T(8,128)(2,1)S(1)} %copy-done.1), channel_id=1, source_target_pairs={{0,1},{1,0},{2,3},{3,2},{4,5},{5,4},{6,7},{7,6},{8,9},{9,8},{10,11... | collective-permute-start | bytes 393224 | tf_op jit(solution)/shard_map/ppermute | solution.py:266
  19.6 6.2 %collective-permute-start.11 = (bf16[1,512,128]{2,1,0:T(8,128)(2,1)S(1)}, bf16[1,512,128]{2,1,0:T(8,128)(2,1)S(1)}, u32[]{:S(2)}, u32[]{:S(2)}) collective-permute-start(bf16[1,512,128]{2,1,0:T(8,128)(2,1)S(1)} %collective-permute-done.2.rest_1_), channel_id=1, source_target_pairs={{0,1},{1,0},{2,3},{3,2},{4,5},{5,4},{6,7},{7,6},{8,9},{9,8},{10,11... | collective-permute-start | bytes 393224 | tf_op jit(solution)/shard_map/ppermute | solution.py:266
  20.1 5.7 %collective-permute-start.12 = (bf16[1,512,128]{2,1,0:T(8,128)(2,1)S(1)}, bf16[1,512,128]{2,1,0:T(8,128)(2,1)S(1)}, u32[]{:S(2)}, u32[]{:S(2)}) collective-permute-start(bf16[1,512,128]{2,1,0:T(8,128)(2,1)S(1)} %collective-permute-done.9.rest_2_), channel_id=1, source_target_pairs={{0,1},{1,0},{2,3},{3,2},{4,5},{5,4},{6,7},{7,6},{8,9},{9,8},{10,11... | collective-permute-start | bytes 393224 | tf_op jit(solution)/shard_map/ppermute | solution.py:266
  25.7 1.3 %collective-permute-start.13 = (bf16[1,512,128]{2,1,0:T(8,128)(2,1)S(1)}, bf16[1,512,128]{2,1,0:T(8,128)(2,1)S(1)}, u32[]{:S(2)}, u32[]{:S(2)}) collective-permute-start(bf16[1,512,128]{2,1,0:T(8,128)(2,1)S(1)} %collective-permute-done.3.rest_3_), channel_id=1, source_target_pairs={{0,1},{1,0},{2,3},{3,2},{4,5},{5,4},{6,7},{7,6},{8,9},{9,8},{10,11... | collective-permute-start | bytes 393224 | tf_op jit(solution)/shard_map/ppermute | solution.py:266
  29.1 5.6 %collective-permute-start.14 = (bf16[512,128]{1,0:T(8,128)(2,1)S(1)}, bf16[512,128]{1,0:T(8,128)(2,1)S(1)}, u32[]{:S(2)}, u32[]{:S(2)}) collective-permute-start(bf16[512,128]{1,0:T(8,128)(2,1)S(1)} %get-tuple-element.42), channel_id=1, source_target_pairs={{0,8},{8,16},{16,24},{24,0},{32,40},{40,48},{48,56},{56,32},{64,72... | collective-permute-start | bytes 393224 | tf_op jit(solution)/shard_map/ppermute | solution.py:258
  30.7 7.9 %collective-permute-start.15 = (bf16[512,128]{1,0:T(8,128)(2,1)S(1)}, bf16[512,128]{1,0:T(8,128)(2,1)S(1)}, u32[]{:S(2)}, u32[]{:S(2)}) collective-permute-start(bf16[512,128]{1,0:T(8,128)(2,1)S(1)} %get-tuple-element.43), channel_id=1, source_target_pairs={{0,16},{8,24},{16,0},{24,8},{32,48},{40,56},{48,32},{56,40},{64,80... | collective-permute-start | bytes 393224 | tf_op jit(solution)/shard_map/ppermute | solution.py:258
  31.8 8.0 %collective-permute-start.16 = (bf16[512,128]{1,0:T(8,128)(2,1)S(1)}, bf16[512,128]{1,0:T(8,128)(2,1)S(1)}, u32[]{:S(2)}, u32[]{:S(2)}) collective-permute-start(bf16[512,128]{1,0:T(8,128)(2,1)S(1)} %get-tuple-element.44), channel_id=1, source_target_pairs={{0,24},{8,0},{16,8},{24,16},{32,56},{40,32},{48,40},{56,48},{64,88... | collective-permute-start | bytes 393224 | tf_op jit(solution)/shard_map/ppermute | solution.py:258
  84.6 5.1 %collective-permute-start.17 = (bf16[544,128]{1,0:T(8,128)(2,1)S(1)}, bf16[544,128]{1,0:T(8,128)(2,1)S(1)}, u32[]{:S(2)}, u32[]{:S(2)}) collective-permute-start(bf16[544,128]{1,0:T(8,128)(2,1)S(1)} %get-tuple-element.46), channel_id=1, source_target_pairs={{0,8},{8,16},{16,24},{24,0},{32,40},{40,48},{48,56},{56,32},{64,72... | collective-permute-start | bytes 417800 | tf_op jit(solution)/shard_map/ppermute | solution.py:258
  84.7 6.8 %collective-permute-start.18 = (bf16[544,128]{1,0:T(8,128)(2,1)S(1)}, bf16[544,128]{1,0:T(8,128)(2,1)S(1)}, u32[]{:S(2)}, u32[]{:S(2)}) collective-permute-start(bf16[544,128]{1,0:T(8,128)(2,1)S(1)} %get-tuple-element.47), channel_id=1, source_target_pairs={{0,16},{8,24},{16,0},{24,8},{32,48},{40,56},{48,32},{56,40},{64,80... | collective-permute-start | bytes 417800 | tf_op jit(solution)/shard_map/ppermute | solution.py:258
  86.7 6.1 %collective-permute-start.19 = (bf16[544,128]{1,0:T(8,128)(2,1)S(1)}, bf16[544,128]{1,0:T(8,128)(2,1)S(1)}, u32[]{:S(2)}, u32[]{:S(2)}) collective-permute-start(bf16[544,128]{1,0:T(8,128)(2,1)S(1)} %get-tuple-element.48), channel_id=1, source_target_pairs={{0,24},{8,0},{16,8},{24,16},{32,56},{40,32},{48,40},{56,48},{64,88... | collective-permute-start | bytes 417800 | tf_op jit(solution)/shard_map/ppermute | solution.py:258
  101.0 5.0 %collective-permute-start.20 = (bf16[8,4,16,128]{3,2,1,0:T(8,128)(2,1)S(1)}, bf16[8,4,16,128]{3,2,1,0:T(8,128)(2,1)S(1)}, u32[]{:S(2)}, u32[]{:S(2)}) collective-permute-start(bf16[8,4,16,128]{3,2,1,0:T(8,128)(2,1)S(1)} %get-tuple-element.51), channel_id=1, source_target_pairs={{0,8},{8,16},{16,24},{24,0},{32,40},{40,48},{48,56},{56,32},{64,72... | collective-permute-start | bytes 393224 | tf_op jit(solution)/shard_map/ppermute | solution.py:258
  101.5 6.5 %collective-permute-start.21 = (bf16[8,4,16,128]{3,2,1,0:T(8,128)(2,1)S(1)}, bf16[8,4,16,128]{3,2,1,0:T(8,128)(2,1)S(1)}, u32[]{:S(2)}, u32[]{:S(2)}) collective-permute-start(bf16[8,4,16,128]{3,2,1,0:T(8,128)(2,1)S(1)} %get-tuple-element.52), channel_id=1, source_target_pairs={{0,16},{8,24},{16,0},{24,8},{32,48},{40,56},{48,32},{56,40},{64,80... | collective-permute-start | bytes 393224 | tf_op jit(solution)/shard_map/ppermute | solution.py:258
  104.1 5.3 %collective-permute-start.22 = (bf16[8,4,16,128]{3,2,1,0:T(8,128)(2,1)S(1)}, bf16[8,4,16,128]{3,2,1,0:T(8,128)(2,1)S(1)}, u32[]{:S(2)}, u32[]{:S(2)}) collective-permute-start(bf16[8,4,16,128]{3,2,1,0:T(8,128)(2,1)S(1)} %get-tuple-element.53), channel_id=1, source_target_pairs={{0,24},{8,0},{16,8},{24,16},{32,56},{40,32},{48,40},{56,48},{64,88... | collective-permute-start | bytes 393224 | tf_op jit(solution)/shard_map/ppermute | solution.py:258

commit v3 on v2

--- a/solution.py
+++ b/solution.py
@@ -64,24 +64,39 @@
         pltpu.make_async_copy(source.at[j, s], held.at[j * slots + s], sems.at[j * slots + s]).wait()
 
 
-def probe_kernel(outs, slots, meta, right_v, sketch, probe_h, probe_l, held, sems):
+def beside(a, b):
+    return jnp.concatenate([a, b], axis=1)
+
+
+def above(a, b):
+    return jnp.concatenate([a, b], axis=0)
+
+
+def slots_of(j, base, slots, count):
+    return [j * slots + jnp.minimum(base + i, count - 1) for i in range(BATCH)]
+
+
+def probe_kernel(outs, slots, meta, right_u, right_v, sketch, probes, held_u, held, sems_u, sems):
     fetch(meta, outs, slots, right_v, held, sems)
+    fetch(meta, outs, slots, right_u, held_u, sems_u)
 
     def tile(j, _):
         turned = sketch[j].T
+        count = meta[outs * slots + j]
 
         def batch(first, _):
             base = first * BATCH
             for i in range(BATCH):
                 arrive(meta, outs, slots, j, base + i, right_v, held, sems)
+            at = slots_of(j, base, slots, count)
+            products = [dot(turned, held[slot]) for slot in at]
+            for slot, product in zip(at, products):
+                probes[slot] = beside(*halves(product))
             for i in range(BATCH):
-                at = j * slots + base + i
-                high, low = halves(dot(turned, held[at]))
-                probe_h[at] = high
-                probe_l[at] = low
+                arrive(meta, outs, slots, j, base + i, right_u, held_u, sems_u)
             return 0
 
-        lax.fori_loop(0, (meta[outs * slots + j] + BATCH - 1) // BATCH, batch, 0)
+        lax.fori_loop(0, (count + BATCH - 1) // BATCH, batch, 0)
         return 0
 
     lax.fori_loop(0, outs, tile, 0)
@@ -92,9 +107,8 @@
     return [lax.rem(me + 2 * hop, tiles) ^ flip for flip in (0, 1) for hop in (0, tiles // 2 - 1, 1, 2)]
 
 
-def pair_kernel(outs, slots, meta, right_u, probe_h, probe_l, *rest):
-    parts, (pair_h, pair_l, mixing, held, turned, sems) = rest[:-6], rest[-6:]
-    fetch(meta, outs, slots, right_u, held, sems)
+def pair_kernel(outs, slots, meta, held, probes, *rest):
+    parts, (pairs, mixing, turned) = rest[:-3], rest[-3:]
     for k, part in zip(tile_ids(meta, outs * slots + outs + 2, len(parts)), parts):
         turned[k] = part[0].T
 
@@ -103,15 +117,15 @@
 
         def batch(first, _):
             base = first * BATCH
+            at = slots_of(j, base, slots, count)
+            products = [halves(dot(turned[meta[slot]], held[slot])) for slot in at]
+            mixes = []
+            for slot, (high, low) in zip(at, products):
+                probe = probes[slot]
+                mixes.append(dot_nt(high, probe[:, :R]) + dot_nt(high, probe[:, R:]) + dot_nt(low, probe[:, :R]))
             for i in range(BATCH):
-                arrive(meta, outs, slots, j, base + i, right_u, held, sems)
-            for i in range(BATCH):
-                at = j * slots + base + i
-                high, low = halves(dot(turned[meta[at]], held[at]))
-                pair_h[at] = high
-                pair_l[at] = low
-                mixed = dot_nt(high, probe_h[at]) + dot_nt(high, probe_l[at]) + dot_nt(low, probe_h[at])
-                mixing[at] = jnp.where(base + i < count, mixed, 0.0).astype(BF)
+                pairs[at[i]] = above(*products[i])
+                mixing[j * slots + base + i] = jnp.where(base + i < count, mixes[i], 0.0).astype(BF)
             return 0
 
         lax.fori_loop(0, (count + BATCH - 1) // BATCH, batch, 0)
@@ -133,8 +147,11 @@
         def batch(first, _):
             base = first * BATCH
             at = [j * slots + base + i for i in range(BATCH)]
-            terms = [dot(group[meta[slot]], mixing[slot]) for slot in at]
-            acc[...] += (terms[0] + terms[1]) + (terms[2] + terms[3])
+            tiles = [group[meta[slot]] for slot in at]
+            terms = [
+                dot(beside(tiles[i], tiles[i + 1]), above(mixing[at[i]], mixing[at[i + 1]])) for i in range(0, BATCH, 2)
+            ]
+            acc[...] += terms[0] + terms[1]
             return 0
 
         lax.fori_loop(0, (meta[outs * slots + j] + BATCH - 1) // BATCH, batch, 0)
@@ -212,7 +229,7 @@
         msg[NB + rows:] = low
 
 
-def backward_kernel(outs, slots, zs, meta, right_v, group, pair_h, pair_l, msg0, msg1, msg2, msg3,
+def backward_kernel(outs, slots, zs, meta, right_v, group, pairs, msg0, msg1, msg2, msg3,
                     own, send1, send2, send3, basis, held, turned, acc, sems):
     fetch(meta, outs, slots, right_v, held, sems)
     y = meta[outs * slots + outs]
@@ -231,15 +248,19 @@
             base = first * BATCH
             for i in range(BATCH):
                 arrive(meta, outs, slots, j, base + i, right_v, held, sems)
-            terms = []
+            at = slots_of(j, base, slots, count)
+            mine = turned[j]
+            products = [halves(dot(mine, group[meta[slot]])) for slot in at]
+            backs = []
             for i in range(BATCH):
-                at = j * slots + base + i
-                live = base + i < count
-                high, low = halves(dot(turned[j], group[meta[at]]))
-                back = dot(high, pair_h[at]) + dot(high, pair_l[at]) + dot(low, pair_h[at])
-                back = jnp.where(live, back, 0.0).astype(BF)
-                terms.append(dot_nt(jnp.where(live, held[at], jnp.zeros_like(held[at])), back))
-            acc[...] += (terms[0] + terms[1]) + (terms[2] + terms[3])
+                high, low = products[i]
+                pair = pairs[at[i]]
+                back = dot(high, pair[:R]) + dot(high, pair[R:]) + dot(low, pair[:R])
+                backs.append(jnp.where(base + i < count, back, 0.0).astype(BF))
+            terms = [
+                dot_nt(beside(held[at[i]], held[at[i + 1]]), beside(backs[i], backs[i + 1])) for i in range(0, BATCH, 2)
+            ]
+            acc[...] += terms[0] + terms[1]
             return 0
 
         lax.fori_loop(0, (count + BATCH - 1) // BATCH, batch, 0)
@@ -286,10 +307,7 @@
         jnp.stack([y, z, lax.axis_index("cols")]),
     ]).astype(jnp.int32)
     shape = jax.ShapeDtypeStruct
-    square = shape((outs * slots, R, R), BF)
-    fetched = [VMEM((outs * slots, NB, R), BF)]
-    sems = [pltpu.SemaphoreType.DMA((outs * slots,))]
-
+    count = outs * slots
     right_u = pltpu.with_memory_space_constraint(right_u, pltpu.HBM)
     right_v = pltpu.with_memory_space_constraint(right_v, pltpu.HBM)
     unit = 2 * NB * R * R
@@ -297,34 +315,34 @@
     def cost(units, mib):
         return pl.CostEstimate(flops=int(units * unit), bytes_accessed=mib << 20, transcendentals=0)
 
-    probe_h, probe_l = pl.pallas_call(
+    probes, held_u = pl.pallas_call(
         functools.partial(probe_kernel, outs, slots),
-        out_shape=(square, square),
-        in_specs=[in_smem(), in_place(), in_vmem()],
+        out_shape=(shape((count, R, 2 * R), BF),) + (shape((count, NB, R), BF),),
+        in_specs=[in_smem(), in_place(), in_place(), in_vmem()],
         out_specs=(in_vmem(),) * 2,
-        scratch_shapes=fetched + sems,
+        scratch_shapes=[VMEM((count, NB, R), BF)] + [pltpu.SemaphoreType.DMA((count,))] * 2,
         compiler_params=params(),
         cost_estimate=cost(outs * slots, 6),
         name="probe",
-    )(meta, right_v, sketch)
+    )(meta, right_u, right_v, sketch)
     near = [hop(left_v, 1, tiles), hop(left_v, -1, tiles)]
-    *near, probe_h, probe_l, left_u = lax.optimization_barrier((*near, probe_h, probe_l, left_u))
+    *near, probes, left_u = lax.optimization_barrier((*near, probes, left_u))
     group_v = [left_v, *near, hop(near[1], -1, tiles)]
     group_v += [swap(value, tiles) for value in group_v]
     near = [hop(left_u, 1, tiles), hop(left_u, -1, tiles)]
     group_u = [left_u, *near]
     other_u = [swap(value, tiles) for value in group_u]
     far_u = hop(near[0], 1, tiles)
-    pair_h, pair_l, mixing = pl.pallas_call(
+    pairs, mixing = pl.pallas_call(
         functools.partial(pair_kernel, outs, slots),
-        out_shape=(square,) * 3,
-        in_specs=[in_smem(), in_place()] + [in_vmem()] * (2 + tiles),
-        out_specs=(in_vmem(),) * 3,
-        scratch_shapes=fetched + [VMEM((tiles, R, NB), BF)] + sems,
+        out_shape=(shape((count, 2 * R, R), BF), shape((count, R, R), BF)),
+        in_specs=[in_smem()] + [in_vmem()] * (2 + tiles),
+        out_specs=(in_vmem(),) * 2,
+        scratch_shapes=[VMEM((tiles, R, NB), BF)],
         compiler_params=params(),
         cost_estimate=cost(outs * slots * 1.75, 10),
         name="pair",
-    )(meta, right_u, probe_h, probe_l, *group_v)
+    )(meta, held_u, probes, *group_v)
     far_u, mixing = lax.optimization_barrier((far_u, mixing))
     group_u += [far_u, *other_u, swap(far_u, tiles)]
     own, send1, send2, send3, group = pl.pallas_call(
@@ -359,13 +377,15 @@
     own, send1, send2, send3, basis = pl.pallas_call(
         functools.partial(backward_kernel, outs, slots, zs),
         out_shape=(shape(pieces, F32),) + (shape(pieces, BF),) * 3 + (shape((outs, out_rows, R), F32),),
-        in_specs=[in_smem(), in_place()] + [in_vmem()] * (3 + YS),
+        in_specs=[in_smem(), in_place()] + [in_vmem()] * (2 + YS),
         out_specs=(in_vmem(),) * 5,
-        scratch_shapes=fetched + [VMEM((outs, R, NB), BF), VMEM((NB, R), F32)] + sems,
+        scratch_shapes=[
+            VMEM((count, NB, R), BF), VMEM((outs, R, NB), BF), VMEM((NB, R), F32), pltpu.SemaphoreType.DMA((count,)),
+        ],
         compiler_params=params(),
         cost_estimate=cost(outs * slots * 2.75, 8),
         name="backward",
-    )(meta, right_v, group, pair_h, pair_l, *messages)
+    )(meta, right_v, group, pairs, *messages)
     part = own
     for step, send in enumerate((send1, send2, send3)):
         part = part + shift_y(send, step + 1, zs).astype(F32)

time: 125 us -> 122 us (0.976)
  Pallas kernels: 29 us -> 24.7 us
  waiting for transfers between devices: 18.3 us -> 21.3 us
  blocking collectives: 46.9 us -> 45.2 us
    pallas_call x1, Pallas kernels: 8.14 us -> 5.4 us  [body(): pl.pallas_call(functools.partial(backward_kernel, outs, slots, zs), out_s...]
    ppermute x6, waiting for transfers between devices: 3.72 us -> 5.8 us  [hop(): lax.ppermute(value, 'cols', [(i, (i + 2 * step) % tiles) for i in range(t...]
    pallas_call x1, Pallas kernels: 4.7 us -> 2.95 us  [body(): pl.pallas_call(functools.partial(pair_kernel, outs, slots), out_shape=(sh...]
    all_to_all x3, blocking collectives: 46.9 us -> 45.2 us  [over_z(): lax.all_to_all(array, 'inner', 0, 0, tiled=True, axis_index_groups=groups)]
  transfers between devices with their start and end apart: 23 -> 23, of which waited for: 13 -> 13; matrix products, arithmetic and copies ran while one was open for 1% -> 1% of each run, Pallas kernels for 7% -> 5%
where the time goes in v3:
time: 122 us; the launch traced here: 120 us
  blocking collectives  45.2 us (37%)
  starting transfers between devices  24.7 us (20%)
  Pallas kernels  24.7 us (20%)
  waiting for transfers between devices  21.3 us (17%)
  other arithmetic  2.27 us (2%)
  local copies, waits for them, and re-layouts  1.24 us (1%)
    all_to_all x3, blocking collectives, over_z(): lax.all_to_all(array, 'inner', 0, 0, tiled=True, axis_index_groups=groups)  45.2 us
    ppermute x9, waiting for transfers between devices, shift_y(): return lax.ppermute(array, 'inner', pairs)  14.2 us
    ppermute x9, starting transfers between devices, shift_y(): return lax.ppermute(array, 'inner', pairs)  13.9 us
    pallas_call x1, Pallas kernels, body(): pl.pallas_call(functools.partial(ortho_kernel, outs, slots, zs), out_shap...  10.8 us
    ppermute x6, starting transfers between devices, hop(): lax.ppermute(value, 'cols', [(i, (i + 2 * step) % tiles) for i in range(t...  9.68 us
    ppermute x6, waiting for transfers between devices, hop(): lax.ppermute(value, 'cols', [(i, (i + 2 * step) % tiles) for i in range(t...  5.8 us
    pallas_call x1, Pallas kernels, body(): pl.pallas_call(functools.partial(backward_kernel, outs, slots, zs), out_s...  5.4 us
    pallas_call x1, Pallas kernels, body(): pl.pallas_call(functools.partial(probe_kernel, outs, slots), out_shape=(s...  3.58 us
  transfers between devices with their start and end apart: 23, of which 13 were waited for; matrix products, arithmetic and copies ran while one was open for 1% of the time, Pallas kernels for 5%

profile of v3, /device:TPU:8, one launch (start us, length us, event | category | flops | bytes accessed | tf_op | source)
XLA Modules:
  0.0 120.2 jit_solution(17954449061289078659)
XLA Ops:
  0.6 2.8 %collective-permute-start.1 = (bf16[1,512,128]{2,1,0:T(8,128)(2,1)}, bf16[1,512,128]{2,1,0:T(8,128)(2,1)S(1)}, u32[]{:S(2)}, u32[]{:S(2)}) collective-permute-start(bf16[1,512,128]{2,1,0:T(8,128)(2,1)} %rest_0_.1), channel_id=1, source_target_pairs={{0,6},{1,7},{2,0},{3,1},{4,2},{5,3},{6,4},{7,5},{8,14},{9,15},{10,... | collective-permute-start | bytes 393224 | tf_op jit(solution)/shard_map/ppermute | solution.py:283
  3.5 0.7 broadcast_subtract_fusion
  4.2 0.8 reduce_sum.27
  5.1 1.0 copy-done
  6.2 3.6 %probe.1 = (bf16[32,128,256]{2,1,0:T(8,128)(2,1)S(1)}, bf16[32,512,128]{2,1,0:T(8,128)(2,1)S(1)}) custom-call(s32[39]{0:T(128)S(1)} %concatenate.3.meta, bf16[4,8,512,128]{3,2,1,0:T(8,128)(2,1)} %right_u.1, bf16[4,8,512,128]{3,2,1,0:T(8,128)(2,1)} %right_v.3, bf16[4,512,128]{2,1,0:T(8,128)(2,1)S(1)} %copy-done), custom_call_target="tpu_custom_call" | custom-call | flops 536870912 | bytes 6291456 | tf_op jit(solution)/shard_map/probe/pallas_call | solution.py:318
  9.9 3.6 %collective-permute-start.4 = (bf16[1,512,128]{2,1,0:T(8,128)(2,1)S(1)}, bf16[1,512,128]{2,1,0:T(8,128)(2,1)S(1)}, u32[]{:S(2)}, u32[]{:S(2)}) collective-permute-start(bf16[1,512,128]{2,1,0:T(8,128)(2,1)S(1)} %collective-permute-done.1.rest_2_), channel_id=1, source_target_pairs={{0,6},{1,7},{2,0},{3,1},{4,2},{5,3},{6,4},{7,5},{8,14},{9,15},{10,... | collective-permute-start | bytes 393224 | tf_op jit(solution)/shard_map/ppermute | solution.py:283
  14.0 3.2 %collective-permute-start.9 = (bf16[1,512,128]{2,1,0:T(8,128)(2,1)S(1)}, bf16[1,512,128]{2,1,0:T(8,128)(2,1)S(1)}, u32[]{:S(2)}, u32[]{:S(2)}) collective-permute-start(bf16[1,512,128]{2,1,0:T(8,128)(2,1)S(1)} %copy-done.1), channel_id=1, source_target_pairs={{0,6},{1,7},{2,0},{3,1},{4,2},{5,3},{6,4},{7,5},{8,14},{9,15},{10,... | collective-permute-start | bytes 393224 | tf_op jit(solution)/shard_map/ppermute | solution.py:283
  17.2 3.1 %collective-permute-done.2.rest_1_ = bf16[1,512,128]{2,1,0:T(8,128)(2,1)S(1)} collective-permute-done((bf16[1,512,128]{2,1,0:T(8,128)(2,1)S(1)}, bf16[1,512,128]{2,1,0:T(8,128)(2,1)S(1)}, u32[]{:S(2)}, u32[]{:S(2)}) %collective-permute-start.2) | collective-permute-done | bytes 131104 | tf_op jit(solution)/shard_map/ppermute | solution.py:283
  21.0 3.0 %pair.1 = (bf16[32,256,128]{2,1,0:T(8,128)(2,1)S(1)}, bf16[32,128,128]{2,1,0:T(8,128)(2,1)S(1)}) custom-call(s32[39]{0:T(128)S(1)} %concatenate.3.meta, bf16[32,512,128]{2,1,0:T(8,128)(2,1)S(1)} %get-tuple-element.28.held, bf16[32,128,256]{2,1,0:T(8,128)(2,1)S(1)} %get-tuple-element.29.probes, bf16[1,512,128]{2,1,0:T(8,128)(2,1)S(1)} %copy-done.2, ...), custom_call_target="tpu_custom_call" | custom-call | flops 939524096 | bytes 10485760 | tf_op jit(solution)/shard_map/pair/pallas_call | solution.py:336
  23.9 2.6 %collective-permute-done.3.rest_3_ = bf16[1,512,128]{2,1,0:T(8,128)(2,1)S(1)} collective-permute-done((bf16[1,512,128]{2,1,0:T(8,128)(2,1)S(1)}, bf16[1,512,128]{2,1,0:T(8,128)(2,1)S(1)}, u32[]{:S(2)}, u32[]{:S(2)}) %collective-permute-start.3) | collective-permute-done | bytes 131104 | tf_op jit(solution)/shard_map/ppermute | solution.py:283
  26.5 1.3 %collective-permute-done.13.rest_7_ = bf16[1,512,128]{2,1,0:T(8,128)(2,1)S(1)} collective-permute-done((bf16[1,512,128]{2,1,0:T(8,128)(2,1)S(1)}, bf16[1,512,128]{2,1,0:T(8,128)(2,1)S(1)}, u32[]{:S(2)}, u32[]{:S(2)}) %collective-permute-start.13) | collective-permute-done | bytes 131104 | tf_op jit(solution)/shard_map/ppermute | solution.py:287
  27.9 2.0 %sketch.3 = (f32[512,128]{1,0:T(8,128)S(1)}, bf16[512,128]{1,0:T(8,128)(2,1)S(1)}, bf16[512,128]{1,0:T(8,128)(2,1)S(1)}, bf16[512,128]{1,0:T(8,128)(2,1)S(1)}, bf16[8,512,128]{2,1,0:T(8,128)(2,1)S(1)}) custom-call(s32[39]{0:T(128)S(1)} %concatenate.3.meta, bf16[32,128,128]{2,1,0:T(8,128)(2,1)S(1)} %get-tuple-element.33.mixing, ...), custom_call_target="tpu_custom_call" | custom-call | flops 536870912 | bytes 4194304 | tf_op jit(solution)/shard_map/sketch/pallas_call | solution.py:348
  29.9 1.3 %collective-permute-start.14 = (bf16[512,128]{1,0:T(8,128)(2,1)S(1)}, bf16[512,128]{1,0:T(8,128)(2,1)S(1)}, u32[]{:S(2)}, u32[]{:S(2)}) collective-permute-start(bf16[512,128]{1,0:T(8,128)(2,1)S(1)} %get-tuple-element.38), channel_id=1, source_target_pairs={{0,8},{8,16},{16,24},{24,0},{32,40},{40,48},{48,56},{56,32},{64,72... | collective-permute-start | bytes 393224 | tf_op jit(solution)/shard_map/ppermute | solution.py:279
  31.1 1.5 %collective-permute-start.15 = (bf16[512,128]{1,0:T(8,128)(2,1)S(1)}, bf16[512,128]{1,0:T(8,128)(2,1)S(1)}, u32[]{:S(2)}, u32[]{:S(2)}) collective-permute-start(bf16[512,128]{1,0:T(8,128)(2,1)S(1)} %get-tuple-element.39), channel_id=1, source_target_pairs={{0,16},{8,24},{16,0},{24,8},{32,48},{40,56},{48,32},{56,40},{64,80... | collective-permute-start | bytes 393224 | tf_op jit(solution)/shard_map/ppermute | solution.py:279
  32.7 2.5 %collective-permute-start.16 = (bf16[512,128]{1,0:T(8,128)(2,1)S(1)}, bf16[512,128]{1,0:T(8,128)(2,1)S(1)}, u32[]{:S(2)}, u32[]{:S(2)}) collective-permute-start(bf16[512,128]{1,0:T(8,128)(2,1)S(1)} %get-tuple-element.40), channel_id=1, source_target_pairs={{0,24},{8,0},{16,8},{24,16},{32,56},{40,32},{48,40},{56,48},{64,88... | collective-permute-start | bytes 393224 | tf_op jit(solution)/shard_map/ppermute | solution.py:279
  35.5 3.5 %collective-permute-done.15 = bf16[512,128]{1,0:T(8,128)(2,1)S(1)} collective-permute-done((bf16[512,128]{1,0:T(8,128)(2,1)S(1)}, bf16[512,128]{1,0:T(8,128)(2,1)S(1)}, u32[]{:S(2)}, u32[]{:S(2)}) %collective-permute-start.15) | collective-permute-done | bytes 131104 | tf_op jit(solution)/shard_map/ppermute | solution.py:279
  39.0 2.0 %collective-permute-done.16 = bf16[512,128]{1,0:T(8,128)(2,1)S(1)} collective-permute-done((bf16[512,128]{1,0:T(8,128)(2,1)S(1)}, bf16[512,128]{1,0:T(8,128)(2,1)S(1)}, u32[]{:S(2)}, u32[]{:S(2)}) %collective-permute-start.16) | collective-permute-done | bytes 131104 | tf_op jit(solution)/shard_map/ppermute | solution.py:279
  41.1 19.4 %all_to_all.15 = f32[8,64,128]{2,1,0:T(8,128)S(1)} all-to-all(f32[8,64,128]{2,1,0:T(8,128)S(1)} %bitcast.4), channel_id=1, replica_groups={{0,32,64,96,128,160,192,224},{8,40,72,104,136,168,200,232},{16,48,80,11..., dimensions={0} | all-to-all | bytes 524288 | tf_op jit(solution)/shard_map/all_to_all | solution.py:292
  60.5 13.0 %all_to_all.16.blocks = f32[8,64,128]{2,1,0:T(8,128)S(1)} all-to-all(f32[8,64,128]{2,1,0:T(8,128)S(1)} %broadcast_in_dim.2), channel_id=1, replica_groups={{0,32,64,96,128,160,192,224},{8,40,72,104,136,168,200,232},{16,48,80,11..., dimensions={0} | all-to-all | bytes 524288 | tf_op jit(solution)/shard_map/all_to_all | solution.py:292
  73.5 10.8 %ortho.1 = (bf16[544,128]{1,0:T(8,128)(2,1)S(1)}, bf16[544,128]{1,0:T(8,128)(2,1)S(1)}, bf16[544,128]{1,0:T(8,128)(2,1)S(1)}, bf16[544,128]{1,0:T(8,128)(2,1)S(1)}) custom-call(s32[39]{0:T(128)S(1)} %concatenate.3.meta, f32[8,64,128]{2,1,0:T(8,128)S(1)} %all_to_all.16.blocks), custom_call_target="tpu_custom_call" | custom-call | flops 218103808 | bytes 1048576 | tf_op jit(solution)/shard_map/ortho/pallas_call | solution.py:365
  84.6 1.9 %collective-permute-start.18 = (bf16[544,128]{1,0:T(8,128)(2,1)S(1)}, bf16[544,128]{1,0:T(8,128)(2,1)S(1)}, u32[]{:S(2)}, u32[]{:S(2)}) collective-permute-start(bf16[544,128]{1,0:T(8,128)(2,1)S(1)} %get-tuple-element.43), channel_id=1, source_target_pairs={{0,16},{8,24},{16,0},{24,8},{32,48},{40,56},{48,32},{56,40},{64,80... | collective-permute-start | bytes 417800 | tf_op jit(solution)/shard_map/ppermute | solution.py:279
  86.5 1.7 %collective-permute-start.19 = (bf16[544,128]{1,0:T(8,128)(2,1)S(1)}, bf16[544,128]{1,0:T(8,128)(2,1)S(1)}, u32[]{:S(2)}, u32[]{:S(2)}) collective-permute-start(bf16[544,128]{1,0:T(8,128)(2,1)S(1)} %get-tuple-element.44), channel_id=1, source_target_pairs={{0,24},{8,0},{16,8},{24,16},{32,56},{40,32},{48,40},{56,48},{64,88... | collective-permute-start | bytes 417800 | tf_op jit(solution)/shard_map/ppermute | solution.py:279
  88.2 1.2 collective-permute-done.17.msg1
  89.4 1.9 %collective-permute-done.18.msg2 = bf16[544,128]{1,0:T(8,128)(2,1)S(1)} collective-permute-done((bf16[544,128]{1,0:T(8,128)(2,1)S(1)}, bf16[544,128]{1,0:T(8,128)(2,1)S(1)}, u32[]{:S(2)}, u32[]{:S(2)}) %collective-permute-start.18) | collective-permute-done | bytes 139296 | tf_op jit(solution)/shard_map/ppermute | solution.py:279
  91.2 1.4 %collective-permute-done.19.msg3 = bf16[544,128]{1,0:T(8,128)(2,1)S(1)} collective-permute-done((bf16[544,128]{1,0:T(8,128)(2,1)S(1)}, bf16[544,128]{1,0:T(8,128)(2,1)S(1)}, u32[]{:S(2)}, u32[]{:S(2)}) %collective-permute-start.19) | collective-permute-done | bytes 139296 | tf_op jit(solution)/shard_map/ppermute | solution.py:279
  92.6 5.4 %backward.1 = (f32[8,4,16,128]{3,2,1,0:T(8,128)S(1)}, bf16[8,4,16,128]{3,2,1,0:T(8,128)(2,1)S(1)}, bf16[8,4,16,128]{3,2,1,0:T(8,128)(2,1)S(1)}, bf16[8,4,16,128]{3,2,1,0:T(8,128)(2,1)S(1)}, f32[4,16,128]{2,1,0:T(8,128)}) custom-call(s32[39]{0:T(128)S(1)} %concatenate.3.meta, bf16[4,8,512,128]{3,2,1,0:T(8,128)(2,1)} %right_v.3, ...), custom_call_target="tpu_custom_call" | custom-call | flops 1476395008 | bytes 8388608 | tf_op jit(solution)/shard_map/backward/pallas_call | solution.py:377
  98.0 0.6 collective-permute-start.20
  98.7 2.3 %collective-permute-start.21 = (bf16[8,4,16,128]{3,2,1,0:T(8,128)(2,1)S(1)}, bf16[8,4,16,128]{3,2,1,0:T(8,128)(2,1)S(1)}, u32[]{:S(2)}, u32[]{:S(2)}) collective-permute-start(bf16[8,4,16,128]{3,2,1,0:T(8,128)(2,1)S(1)} %get-tuple-element.48), channel_id=1, source_target_pairs={{0,16},{8,24},{16,0},{24,8},{32,48},{40,56},{48,32},{56,40},{64,80... | collective-permute-start | bytes 393224 | tf_op jit(solution)/shard_map/ppermute | solution.py:279
  100.9 1.7 %collective-permute-start.22 = (bf16[8,4,16,128]{3,2,1,0:T(8,128)(2,1)S(1)}, bf16[8,4,16,128]{3,2,1,0:T(8,128)(2,1)S(1)}, u32[]{:S(2)}, u32[]{:S(2)}) collective-permute-start(bf16[8,4,16,128]{3,2,1,0:T(8,128)(2,1)S(1)} %get-tuple-element.49), channel_id=1, source_target_pairs={{0,24},{8,0},{16,8},{24,16},{32,56},{40,32},{48,40},{56,48},{64,88... | collective-permute-start | bytes 393224 | tf_op jit(solution)/shard_map/ppermute | solution.py:279
  103.1 2.1 %collective-permute-done.21 = bf16[8,4,16,128]{3,2,1,0:T(8,128)(2,1)S(1)} collective-permute-done((bf16[8,4,16,128]{3,2,1,0:T(8,128)(2,1)S(1)}, bf16[8,4,16,128]{3,2,1,0:T(8,128)(2,1)S(1)}, u32[]{:S(2)}, u32[]{:S(2)}) %collective-permute-start.21) | collective-permute-done | bytes 131104 | tf_op jit(solution)/shard_map/ppermute | solution.py:279
  105.2 1.3 %collective-permute-done.22 = bf16[8,4,16,128]{3,2,1,0:T(8,128)(2,1)S(1)} collective-permute-done((bf16[8,4,16,128]{3,2,1,0:T(8,128)(2,1)S(1)}, bf16[8,4,16,128]{3,2,1,0:T(8,128)(2,1)S(1)}, u32[]{:S(2)}, u32[]{:S(2)}) %collective-permute-start.22) | collective-permute-done | bytes 131104 | tf_op jit(solution)/shard_map/ppermute | solution.py:279
  106.6 12.9 %all_to_all.17 = f32[8,4,16,128]{3,2,1,0:T(8,128)S(1)} all-to-all(f32[8,4,16,128]{3,2,1,0:T(8,128)S(1)} %convert_add_fusion), channel_id=1, replica_groups={{0,32,64,96,128,160,192,224},{8,40,72,104,136,168,200,232},{16,48,80,11..., dimensions={0} | all-to-all | bytes 524288 | tf_op jit(solution)/shard_map/all_to_all | solution.py:292
  (37 shorter events, 3.3 us)
Async XLA Ops:
  0.6 9.1 %collective-permute-start.1 = (bf16[1,512,128]{2,1,0:T(8,128)(2,1)}, bf16[1,512,128]{2,1,0:T(8,128)(2,1)S(1)}, u32[]{:S(2)}, u32[]{:S(2)}) collective-permute-start(bf16[1,512,128]{2,1,0:T(8,128)(2,1)} %rest_0_.1), channel_id=1, source_target_pairs={{0,6},{1,7},{2,0},{3,1},{4,2},{5,3},{6,4},{7,5},{8,14},{9,15},{10,... | collective-permute-start | bytes 393224 | tf_op jit(solution)/shard_map/ppermute | solution.py:283
  3.5 6.4 %collective-permute-start = (bf16[1,512,128]{2,1,0:T(8,128)(2,1)}, bf16[1,512,128]{2,1,0:T(8,128)(2,1)S(1)}, u32[]{:S(2)}, u32[]{:S(2)}) collective-permute-start(bf16[1,512,128]{2,1,0:T(8,128)(2,1)} %rest_0_.1), channel_id=1, source_target_pairs={{0,2},{1,3},{2,4},{3,5},{4,6},{5,7},{6,0},{7,1},{8,10},{9,11},{10,... | collective-permute-start | bytes 393224 | tf_op jit(solution)/shard_map/ppermute | solution.py:283
  3.5 10.5 %collective-permute-start.5 = (bf16[1,512,128]{2,1,0:T(8,128)(2,1)}, bf16[1,512,128]{2,1,0:T(8,128)(2,1)S(1)}, u32[]{:S(2)}, u32[]{:S(2)}) collective-permute-start(bf16[1,512,128]{2,1,0:T(8,128)(2,1)} %rest_0_.1), channel_id=1, source_target_pairs={{0,1},{1,0},{2,3},{3,2},{4,5},{5,4},{6,7},{7,6},{8,9},{9,8},{10,11... | collective-permute-start | bytes 393224 | tf_op jit(solution)/shard_map/ppermute | solution.py:287
  5.1 1.0 copy-start
  6.2 7.3 %copy-start.1 = (bf16[1,512,128]{2,1,0:T(8,128)(2,1)S(1)}, bf16[1,512,128]{2,1,0:T(8,128)(2,1)}, u32[]{:S(2)}) copy-start(bf16[1,512,128]{2,1,0:T(8,128)(2,1)} %rest_0_.2) | copy-start | bytes 393220
  6.2 14.8 %copy-start.2 = (bf16[1,512,128]{2,1,0:T(8,128)(2,1)S(1)}, bf16[1,512,128]{2,1,0:T(8,128)(2,1)}, u32[]{:S(2)}) copy-start(bf16[1,512,128]{2,1,0:T(8,128)(2,1)} %rest_0_.1) | copy-start | bytes 393220
  9.9 7.4 %collective-permute-start.4 = (bf16[1,512,128]{2,1,0:T(8,128)(2,1)S(1)}, bf16[1,512,128]{2,1,0:T(8,128)(2,1)S(1)}, u32[]{:S(2)}, u32[]{:S(2)}) collective-permute-start(bf16[1,512,128]{2,1,0:T(8,128)(2,1)S(1)} %collective-permute-done.1.rest_2_), channel_id=1, source_target_pairs={{0,6},{1,7},{2,0},{3,1},{4,2},{5,3},{6,4},{7,5},{8,14},{9,15},{10,... | collective-permute-start | bytes 393224 | tf_op jit(solution)/shard_map/ppermute | solution.py:283
  13.5 6.9 %collective-permute-start.2 = (bf16[1,512,128]{2,1,0:T(8,128)(2,1)S(1)}, bf16[1,512,128]{2,1,0:T(8,128)(2,1)S(1)}, u32[]{:S(2)}, u32[]{:S(2)}) collective-permute-start(bf16[1,512,128]{2,1,0:T(8,128)(2,1)S(1)} %copy-done.1), channel_id=1, source_target_pairs={{0,2},{1,3},{2,4},{3,5},{4,6},{5,7},{6,0},{7,1},{8,10},{9,11},{10,... | collective-permute-start | bytes 393224 | tf_op jit(solution)/shard_map/ppermute | solution.py:283
  13.5 6.9 %collective-permute-start.6 = (bf16[1,512,128]{2,1,0:T(8,128)(2,1)S(1)}, bf16[1,512,128]{2,1,0:T(8,128)(2,1)S(1)}, u32[]{:S(2)}, u32[]{:S(2)}) collective-permute-start(bf16[1,512,128]{2,1,0:T(8,128)(2,1)S(1)} %collective-permute-done.rest_1_), channel_id=1, source_target_pairs={{0,1},{1,0},{2,3},{3,2},{4,5},{5,4},{6,7},{7,6},{8,9},{9,8},{10,11... | collective-permute-start | bytes 393224 | tf_op jit(solution)/shard_map/ppermute | solution.py:287
  13.7 6.6 %collective-permute-start.7 = (bf16[1,512,128]{2,1,0:T(8,128)(2,1)S(1)}, bf16[1,512,128]{2,1,0:T(8,128)(2,1)S(1)}, u32[]{:S(2)}, u32[]{:S(2)}) collective-permute-start(bf16[1,512,128]{2,1,0:T(8,128)(2,1)S(1)} %collective-permute-done.1.rest_2_), channel_id=1, source_target_pairs={{0,1},{1,0},{2,3},{3,2},{4,5},{5,4},{6,7},{7,6},{8,9},{9,8},{10,11... | collective-permute-start | bytes 393224 | tf_op jit(solution)/shard_map/ppermute | solution.py:287
  14.0 6.9 %collective-permute-start.9 = (bf16[1,512,128]{2,1,0:T(8,128)(2,1)S(1)}, bf16[1,512,128]{2,1,0:T(8,128)(2,1)S(1)}, u32[]{:S(2)}, u32[]{:S(2)}) collective-permute-start(bf16[1,512,128]{2,1,0:T(8,128)(2,1)S(1)} %copy-done.1), channel_id=1, source_target_pairs={{0,6},{1,7},{2,0},{3,1},{4,2},{5,3},{6,4},{7,5},{8,14},{9,15},{10,... | collective-permute-start | bytes 393224 | tf_op jit(solution)/shard_map/ppermute | solution.py:283
  17.2 3.8 %collective-permute-start.8 = (bf16[1,512,128]{2,1,0:T(8,128)(2,1)S(1)}, bf16[1,512,128]{2,1,0:T(8,128)(2,1)S(1)}, u32[]{:S(2)}, u32[]{:S(2)}) collective-permute-start(bf16[1,512,128]{2,1,0:T(8,128)(2,1)S(1)} %collective-permute-done.4.rest_3_), channel_id=1, source_target_pairs={{0,1},{1,0},{2,3},{3,2},{4,5},{5,4},{6,7},{7,6},{8,9},{9,8},{10,11... | collective-permute-start | bytes 393224 | tf_op jit(solution)/shard_map/ppermute | solution.py:287
  20.3 6.2 %collective-permute-start.3 = (bf16[1,512,128]{2,1,0:T(8,128)(2,1)S(1)}, bf16[1,512,128]{2,1,0:T(8,128)(2,1)S(1)}, u32[]{:S(2)}, u32[]{:S(2)}) collective-permute-start(bf16[1,512,128]{2,1,0:T(8,128)(2,1)S(1)} %collective-permute-done.2.rest_1_), channel_id=1, source_target_pairs={{0,2},{1,3},{2,4},{3,5},{4,6},{5,7},{6,0},{7,1},{8,10},{9,11},{10,... | collective-permute-start | bytes 393224 | tf_op jit(solution)/shard_map/ppermute | solution.py:283
  20.3 6.2 %collective-permute-start.10 = (bf16[1,512,128]{2,1,0:T(8,128)(2,1)S(1)}, bf16[1,512,128]{2,1,0:T(8,128)(2,1)S(1)}, u32[]{:S(2)}, u32[]{:S(2)}) collective-permute-start(bf16[1,512,128]{2,1,0:T(8,128)(2,1)S(1)} %copy-done.1), channel_id=1, source_target_pairs={{0,1},{1,0},{2,3},{3,2},{4,5},{5,4},{6,7},{7,6},{8,9},{9,8},{10,11... | collective-permute-start | bytes 393224 | tf_op jit(solution)/shard_map/ppermute | solution.py:287
  20.4 6.2 %collective-permute-start.11 = (bf16[1,512,128]{2,1,0:T(8,128)(2,1)S(1)}, bf16[1,512,128]{2,1,0:T(8,128)(2,1)S(1)}, u32[]{:S(2)}, u32[]{:S(2)}) collective-permute-start(bf16[1,512,128]{2,1,0:T(8,128)(2,1)S(1)} %collective-permute-done.2.rest_1_), channel_id=1, source_target_pairs={{0,1},{1,0},{2,3},{3,2},{4,5},{5,4},{6,7},{7,6},{8,9},{9,8},{10,11... | collective-permute-start | bytes 393224 | tf_op jit(solution)/shard_map/ppermute | solution.py:287
  20.9 5.7 %collective-permute-start.12 = (bf16[1,512,128]{2,1,0:T(8,128)(2,1)S(1)}, bf16[1,512,128]{2,1,0:T(8,128)(2,1)S(1)}, u32[]{:S(2)}, u32[]{:S(2)}) collective-permute-start(bf16[1,512,128]{2,1,0:T(8,128)(2,1)S(1)} %collective-permute-done.9.rest_2_), channel_id=1, source_target_pairs={{0,1},{1,0},{2,3},{3,2},{4,5},{5,4},{6,7},{7,6},{8,9},{9,8},{10,11... | collective-permute-start | bytes 393224 | tf_op jit(solution)/shard_map/ppermute | solution.py:287
  26.5 1.3 %collective-permute-start.13 = (bf16[1,512,128]{2,1,0:T(8,128)(2,1)S(1)}, bf16[1,512,128]{2,1,0:T(8,128)(2,1)S(1)}, u32[]{:S(2)}, u32[]{:S(2)}) collective-permute-start(bf16[1,512,128]{2,1,0:T(8,128)(2,1)S(1)} %collective-permute-done.3.rest_3_), channel_id=1, source_target_pairs={{0,1},{1,0},{2,3},{3,2},{4,5},{5,4},{6,7},{7,6},{8,9},{9,8},{10,11... | collective-permute-start | bytes 393224 | tf_op jit(solution)/shard_map/ppermute | solution.py:287
  29.9 5.6 %collective-permute-start.14 = (bf16[512,128]{1,0:T(8,128)(2,1)S(1)}, bf16[512,128]{1,0:T(8,128)(2,1)S(1)}, u32[]{:S(2)}, u32[]{:S(2)}) collective-permute-start(bf16[512,128]{1,0:T(8,128)(2,1)S(1)} %get-tuple-element.38), channel_id=1, source_target_pairs={{0,8},{8,16},{16,24},{24,0},{32,40},{40,48},{48,56},{56,32},{64,72... | collective-permute-start | bytes 393224 | tf_op jit(solution)/shard_map/ppermute | solution.py:279
  31.1 7.9 %collective-permute-start.15 = (bf16[512,128]{1,0:T(8,128)(2,1)S(1)}, bf16[512,128]{1,0:T(8,128)(2,1)S(1)}, u32[]{:S(2)}, u32[]{:S(2)}) collective-permute-start(bf16[512,128]{1,0:T(8,128)(2,1)S(1)} %get-tuple-element.39), channel_id=1, source_target_pairs={{0,16},{8,24},{16,0},{24,8},{32,48},{40,56},{48,32},{56,40},{64,80... | collective-permute-start | bytes 393224 | tf_op jit(solution)/shard_map/ppermute | solution.py:279
  32.7 8.4 %collective-permute-start.16 = (bf16[512,128]{1,0:T(8,128)(2,1)S(1)}, bf16[512,128]{1,0:T(8,128)(2,1)S(1)}, u32[]{:S(2)}, u32[]{:S(2)}) collective-permute-start(bf16[512,128]{1,0:T(8,128)(2,1)S(1)} %get-tuple-element.40), channel_id=1, source_target_pairs={{0,24},{8,0},{16,8},{24,16},{32,56},{40,32},{48,40},{56,48},{64,88... | collective-permute-start | bytes 393224 | tf_op jit(solution)/shard_map/ppermute | solution.py:279
  84.2 5.1 %collective-permute-start.17 = (bf16[544,128]{1,0:T(8,128)(2,1)S(1)}, bf16[544,128]{1,0:T(8,128)(2,1)S(1)}, u32[]{:S(2)}, u32[]{:S(2)}) collective-permute-start(bf16[544,128]{1,0:T(8,128)(2,1)S(1)} %get-tuple-element.42), channel_id=1, source_target_pairs={{0,8},{8,16},{16,24},{24,0},{32,40},{40,48},{48,56},{56,32},{64,72... | collective-permute-start | bytes 417800 | tf_op jit(solution)/shard_map/ppermute | solution.py:279
  84.6 6.7 %collective-permute-start.18 = (bf16[544,128]{1,0:T(8,128)(2,1)S(1)}, bf16[544,128]{1,0:T(8,128)(2,1)S(1)}, u32[]{:S(2)}, u32[]{:S(2)}) collective-permute-start(bf16[544,128]{1,0:T(8,128)(2,1)S(1)} %get-tuple-element.43), channel_id=1, source_target_pairs={{0,16},{8,24},{16,0},{24,8},{32,48},{40,56},{48,32},{56,40},{64,80... | collective-permute-start | bytes 417800 | tf_op jit(solution)/shard_map/ppermute | solution.py:279
  86.5 6.2 %collective-permute-start.19 = (bf16[544,128]{1,0:T(8,128)(2,1)S(1)}, bf16[544,128]{1,0:T(8,128)(2,1)S(1)}, u32[]{:S(2)}, u32[]{:S(2)}) collective-permute-start(bf16[544,128]{1,0:T(8,128)(2,1)S(1)} %get-tuple-element.44), channel_id=1, source_target_pairs={{0,24},{8,0},{16,8},{24,16},{32,56},{40,32},{48,40},{56,48},{64,88... | collective-permute-start | bytes 417800 | tf_op jit(solution)/shard_map/ppermute | solution.py:279
  98.0 5.0 %collective-permute-start.20 = (bf16[8,4,16,128]{3,2,1,0:T(8,128)(2,1)S(1)}, bf16[8,4,16,128]{3,2,1,0:T(8,128)(2,1)S(1)}, u32[]{:S(2)}, u32[]{:S(2)}) collective-permute-start(bf16[8,4,16,128]{3,2,1,0:T(8,128)(2,1)S(1)} %get-tuple-element.47), channel_id=1, source_target_pairs={{0,8},{8,16},{16,24},{24,0},{32,40},{40,48},{48,56},{56,32},{64,72... | collective-permute-start | bytes 393224 | tf_op jit(solution)/shard_map/ppermute | solution.py:279
  98.7 6.5 %collective-permute-start.21 = (bf16[8,4,16,128]{3,2,1,0:T(8,128)(2,1)S(1)}, bf16[8,4,16,128]{3,2,1,0:T(8,128)(2,1)S(1)}, u32[]{:S(2)}, u32[]{:S(2)}) collective-permute-start(bf16[8,4,16,128]{3,2,1,0:T(8,128)(2,1)S(1)} %get-tuple-element.48), channel_id=1, source_target_pairs={{0,16},{8,24},{16,0},{24,8},{32,48},{40,56},{48,32},{56,40},{64,80... | collective-permute-start | bytes 393224 | tf_op jit(solution)/shard_map/ppermute | solution.py:279
  100.9 5.6 %collective-permute-start.22 = (bf16[8,4,16,128]{3,2,1,0:T(8,128)(2,1)S(1)}, bf16[8,4,16,128]{3,2,1,0:T(8,128)(2,1)S(1)}, u32[]{:S(2)}, u32[]{:S(2)}) collective-permute-start(bf16[8,4,16,128]{3,2,1,0:T(8,128)(2,1)S(1)} %get-tuple-element.49), channel_id=1, source_target_pairs={{0,24},{8,0},{16,8},{24,16},{32,56},{40,32},{48,40},{56,48},{64,88... | collective-permute-start | bytes 393224 | tf_op jit(solution)/shard_map/ppermute | solution.py:279

commit v4 on v3

--- a/solution.py
+++ b/solution.py
@@ -46,20 +46,38 @@
     return pl.BlockSpec(memory_space=pltpu.SMEM)
 
 
+def live(meta, j):
+    mask = meta[1]
+    count = mask[j, 0]
+    for s in range(1, mask.shape[1]):
+        count += mask[j, s]
+    return count
+
+
+def tile_of(meta, at):
+    index = meta[0]
+    slots = index.shape[1]
+    return index[lax.div(at, slots), lax.rem(at, slots)] - lax.axis_index("inner") * lax.axis_size("cols")
+
+
+def y_of():
+    return lax.rem(lax.axis_index("inner"), YS)
+
+
 def fetch(meta, outs, slots, source, held, sems):
     def tile(j, _):
         def one(s, _):
             pltpu.make_async_copy(source.at[j, s], held.at[j * slots + s], sems.at[j * slots + s]).start()
             return 0
 
-        lax.fori_loop(0, meta[outs * slots + j], one, 0)
+        lax.fori_loop(0, live(meta, j), one, 0)
         return 0
 
     lax.fori_loop(0, outs, tile, 0)
 
 
-def arrive(meta, outs, slots, j, s, source, held, sems):
-    @pl.when(s < meta[outs * slots + j])
+def arrive(count, slots, j, s, source, held, sems):
+    @pl.when(s < count)
     def _():
         pltpu.make_async_copy(source.at[j, s], held.at[j * slots + s], sems.at[j * slots + s]).wait()
 
@@ -76,24 +94,28 @@
     return [j * slots + jnp.minimum(base + i, count - 1) for i in range(BATCH)]
 
 
-def probe_kernel(outs, slots, meta, right_u, right_v, sketch, probes, held_u, held, sems_u, sems):
+def probe_kernel(outs, slots, index, mask, right_u, right_v, sketch, probes, held_u, held, plain, sems_u, sems, sem):
+    meta = index, mask
+    copy = pltpu.make_async_copy(sketch, plain, sem)
+    copy.start()
     fetch(meta, outs, slots, right_v, held, sems)
     fetch(meta, outs, slots, right_u, held_u, sems_u)
+    copy.wait()
 
     def tile(j, _):
-        turned = sketch[j].T
-        count = meta[outs * slots + j]
+        turned = plain[j].T
+        count = live(meta, j)
 
         def batch(first, _):
             base = first * BATCH
             for i in range(BATCH):
-                arrive(meta, outs, slots, j, base + i, right_v, held, sems)
+                arrive(count, slots, j, base + i, right_v, held, sems)
             at = slots_of(j, base, slots, count)
             products = [dot(turned, held[slot]) for slot in at]
             for slot, product in zip(at, products):
                 probes[slot] = beside(*halves(product))
             for i in range(BATCH):
-                arrive(meta, outs, slots, j, base + i, right_u, held_u, sems_u)
+                arrive(count, slots, j, base + i, right_u, held_u, sems_u)
             return 0
 
         lax.fori_loop(0, (count + BATCH - 1) // BATCH, batch, 0)
@@ -102,23 +124,24 @@
     lax.fori_loop(0, outs, tile, 0)
 
 
-def tile_ids(meta, at, tiles):
-    me = meta[at]
+def tile_ids(tiles):
+    me = lax.axis_index("cols")
     return [lax.rem(me + 2 * hop, tiles) ^ flip for flip in (0, 1) for hop in (0, tiles // 2 - 1, 1, 2)]
 
 
-def pair_kernel(outs, slots, meta, held, probes, *rest):
+def pair_kernel(outs, slots, index, mask, held, probes, *rest):
+    meta = index, mask
     parts, (pairs, mixing, turned) = rest[:-3], rest[-3:]
-    for k, part in zip(tile_ids(meta, outs * slots + outs + 2, len(parts)), parts):
+    for k, part in zip(tile_ids(len(parts)), parts):
         turned[k] = part[0].T
 
     def tile(j, _):
-        count = meta[outs * slots + j]
+        count = live(meta, j)
 
         def batch(first, _):
             base = first * BATCH
             at = slots_of(j, base, slots, count)
-            products = [halves(dot(turned[meta[slot]], held[slot])) for slot in at]
+            products = [halves(dot(turned[tile_of(meta, slot)], held[slot])) for slot in at]
             mixes = []
             for slot, (high, low) in zip(at, products):
                 probe = probes[slot]
@@ -134,11 +157,12 @@
     lax.fori_loop(0, outs, tile, 0)
 
 
-def sketch_kernel(outs, slots, meta, mixing, *rest):
+def sketch_kernel(outs, slots, index, mask, mixing, *rest):
+    meta = index, mask
     parts, (own, send1, send2, send3, group, acc) = rest[:-6], rest[-6:]
-    for k, part in zip(tile_ids(meta, outs * slots + outs + 2, len(parts)), parts):
+    for k, part in zip(tile_ids(len(parts)), parts):
         group[k] = part[0]
-    y = meta[outs * slots + outs]
+    y = y_of()
 
     def tile(order, _):
         j = lax.rem(y + 1 + order, YS)
@@ -147,14 +171,14 @@
         def batch(first, _):
             base = first * BATCH
             at = [j * slots + base + i for i in range(BATCH)]
-            tiles = [group[meta[slot]] for slot in at]
+            tiles = [group[tile_of(meta, slot)] for slot in at]
             terms = [
                 dot(beside(tiles[i], tiles[i + 1]), above(mixing[at[i]], mixing[at[i + 1]])) for i in range(0, BATCH, 2)
             ]
             acc[...] += terms[0] + terms[1]
             return 0
 
-        lax.fori_loop(0, (meta[outs * slots + j] + BATCH - 1) // BATCH, batch, 0)
+        lax.fori_loop(0, (live(meta, j) + BATCH - 1) // BATCH, batch, 0)
         for place, out in enumerate((send1, send2, send3, own)):
             @pl.when(order == place)
             def _():
@@ -215,8 +239,9 @@
     return jnp.concatenate([top, jnp.concatenate([corner, lower], axis=1)], axis=0)
 
 
-def ortho_kernel(outs, slots, zs, meta, blocks, msg0, msg1, msg2, msg3, ortho):
-    y, z = meta[outs * slots + outs], meta[outs * slots + outs + 1]
+def ortho_kernel(zs, blocks, msg0, msg1, msg2, msg3, ortho):
+    inner = lax.axis_index("inner")
+    y, z = lax.rem(inner, YS), lax.div(inner, YS)
     rows = NB // (zs * YS)
     summed = blocks[...].reshape(NB, R)
     ortho[...] = exact(summed, inverse_cholesky(exact(summed, summed, TN)), NT)
@@ -229,10 +254,11 @@
         msg[NB + rows:] = low
 
 
-def backward_kernel(outs, slots, zs, meta, right_v, group, pairs, msg0, msg1, msg2, msg3,
+def backward_kernel(outs, slots, zs, index, mask, right_v, group, pairs, msg0, msg1, msg2, msg3,
                     own, send1, send2, send3, basis, held, turned, acc, sems):
+    meta = index, mask
     fetch(meta, outs, slots, right_v, held, sems)
-    y = meta[outs * slots + outs]
+    y = y_of()
     rows = NB // (zs * YS)
     for step, msg in enumerate((msg0, msg1, msg2, msg3)):
         j = lax.rem(y + YS - step, YS)
@@ -241,16 +267,16 @@
         basis[j] = kept * math.sqrt(NB)
 
     def tile(j, _):
-        count = meta[outs * slots + j]
+        count = live(meta, j)
         acc[...] = jnp.zeros_like(acc)
 
         def batch(first, _):
             base = first * BATCH
             for i in range(BATCH):
-                arrive(meta, outs, slots, j, base + i, right_v, held, sems)
+                arrive(count, slots, j, base + i, right_v, held, sems)
             at = slots_of(j, base, slots, count)
             mine = turned[j]
-            products = [halves(dot(mine, group[meta[slot]])) for slot in at]
+            products = [halves(dot(mine, group[tile_of(meta, slot)])) for slot in at]
             backs = []
             for i in range(BATCH):
                 high, low = products[i]
@@ -297,19 +323,14 @@
 
 
 def body(left_u, left_v, right_u, right_v, sketch, tile_index, slot_mask):
-    inner = lax.axis_index("inner")
     zs = lax.axis_size("inner") // YS
-    z, y = inner // YS, inner % YS
     outs, slots = tile_index.shape
     tiles = lax.axis_size("cols")
-    meta = jnp.concatenate([
-        (tile_index - inner * tiles).reshape(-1), jnp.sum(slot_mask, axis=1),
-        jnp.stack([y, z, lax.axis_index("cols")]),
-    ]).astype(jnp.int32)
     shape = jax.ShapeDtypeStruct
     count = outs * slots
     right_u = pltpu.with_memory_space_constraint(right_u, pltpu.HBM)
     right_v = pltpu.with_memory_space_constraint(right_v, pltpu.HBM)
+    sketch = pltpu.with_memory_space_constraint(sketch, pltpu.HBM)
     unit = 2 * NB * R * R
 
     def cost(units, mib):
@@ -318,43 +339,43 @@
     probes, held_u = pl.pallas_call(
         functools.partial(probe_kernel, outs, slots),
         out_shape=(shape((count, R, 2 * R), BF),) + (shape((count, NB, R), BF),),
-        in_specs=[in_smem(), in_place(), in_place(), in_vmem()],
+        in_specs=[in_smem(), in_smem(), in_place(), in_place(), in_place()],
         out_specs=(in_vmem(),) * 2,
-        scratch_shapes=[VMEM((count, NB, R), BF)] + [pltpu.SemaphoreType.DMA((count,))] * 2,
+        scratch_shapes=[VMEM((count, NB, R), BF), VMEM((outs, NB, R), BF)]
+        + [pltpu.SemaphoreType.DMA((count,))] * 2 + [pltpu.SemaphoreType.DMA],
         compiler_params=params(),
         cost_estimate=cost(outs * slots, 6),
         name="probe",
-    )(meta, right_u, right_v, sketch)
-    near = [hop(left_v, 1, tiles), hop(left_v, -1, tiles)]
-    *near, probes, left_u = lax.optimization_barrier((*near, probes, left_u))
-    group_v = [left_v, *near, hop(near[1], -1, tiles)]
+    )(tile_index, slot_mask, right_u, right_v, sketch)
+    near = [hop(value, step, tiles) for value in (left_v, left_u) for step in (1, -1)]
+    *near, probes = lax.optimization_barrier((*near, probes))
+    group_v = [left_v, *near[:2], hop(near[1], -1, tiles)]
     group_v += [swap(value, tiles) for value in group_v]
-    near = [hop(left_u, 1, tiles), hop(left_u, -1, tiles)]
-    group_u = [left_u, *near]
+    group_u = [left_u, *near[2:]]
     other_u = [swap(value, tiles) for value in group_u]
-    far_u = hop(near[0], 1, tiles)
+    far_u = hop(near[2], 1, tiles)
     pairs, mixing = pl.pallas_call(
         functools.partial(pair_kernel, outs, slots),
         out_shape=(shape((count, 2 * R, R), BF), shape((count, R, R), BF)),
-        in_specs=[in_smem()] + [in_vmem()] * (2 + tiles),
+        in_specs=[in_smem(), in_smem()] + [in_vmem()] * (2 + tiles),
         out_specs=(in_vmem(),) * 2,
         scratch_shapes=[VMEM((tiles, R, NB), BF)],
         compiler_params=params(),
         cost_estimate=cost(outs * slots * 1.75, 10),
         name="pair",
-    )(meta, held_u, probes, *group_v)
+    )(tile_index, slot_mask, held_u, probes, *group_v)
     far_u, mixing = lax.optimization_barrier((far_u, mixing))
     group_u += [far_u, *other_u, swap(far_u, tiles)]
     own, send1, send2, send3, group = pl.pallas_call(
         functools.partial(sketch_kernel, outs, slots),
         out_shape=(shape((NB, R), F32),) + (shape((NB, R), BF),) * 3 + (shape((tiles, NB, R), BF),),
-        in_specs=[in_smem()] + [in_vmem()] * (1 + tiles),
+        in_specs=[in_smem(), in_smem()] + [in_vmem()] * (1 + tiles),
         out_specs=(in_vmem(),) * 5,
         scratch_shapes=[VMEM((NB, R), F32)],
         compiler_params=params(),
         cost_estimate=cost(outs * slots, 4),
         name="sketch",
-    )(meta, mixing, *group_u)
+    )(tile_index, slot_mask, mixing, *group_u)
     total = own
     for step, send in enumerate((send1, send2, send3)):
         total = total + shift_y(send, step + 1, zs).astype(F32)
@@ -363,21 +384,21 @@
     summed = over_z(jnp.broadcast_to(mine[None], (zs, rows, R)), zs)
     out_rows = NB // (zs * YS)
     messages = pl.pallas_call(
-        functools.partial(ortho_kernel, outs, slots, zs),
+        functools.partial(ortho_kernel, zs),
         out_shape=(shape((NB + 2 * out_rows, R), BF),) * YS,
-        in_specs=[in_smem(), in_vmem()],
+        in_specs=[in_vmem()],
         out_specs=(in_vmem(),) * YS,
         scratch_shapes=[VMEM((NB, R), F32)],
         compiler_params=params(),
         cost_estimate=cost(13, 1),
         name="ortho",
-    )(meta, summed)
+    )(summed)
     messages = [shift_y(message, step, zs) if step else message for step, message in enumerate(messages)]
     pieces = (zs, outs, out_rows, R)
     own, send1, send2, send3, basis = pl.pallas_call(
         functools.partial(backward_kernel, outs, slots, zs),
         out_shape=(shape(pieces, F32),) + (shape(pieces, BF),) * 3 + (shape((outs, out_rows, R), F32),),
-        in_specs=[in_smem(), in_place()] + [in_vmem()] * (2 + YS),
+        in_specs=[in_smem(), in_smem(), in_place()] + [in_vmem()] * (2 + YS),
         out_specs=(in_vmem(),) * 5,
         scratch_shapes=[
             VMEM((count, NB, R), BF), VMEM((outs, R, NB), BF), VMEM((NB, R), F32), pltpu.SemaphoreType.DMA((count,)),
@@ -385,7 +406,7 @@
         compiler_params=params(),
         cost_estimate=cost(outs * slots * 2.75, 8),
         name="backward",
-    )(meta, right_v, group, pairs, *messages)
+    )(tile_index, slot_mask, right_v, group, pairs, *messages)
     part = own
     for step, send in enumerate((send1, send2, send3)):
         part = part + shift_y(send, step + 1, zs).astype(F32)

time: 122 us -> 119 us (0.975); the launches traced: 120 us -> 119 us
  other arithmetic: 2.27 us -> 0.77 us
    ppermute x9, starting transfers between devices: 13.9 us -> 16.4 us  [shift_y(): return lax.ppermute(array, 'inner', pairs)]
    ppermute x6, starting transfers between devices: 9.68 us -> 7.77 us  [hop(): lax.ppermute(value, 'cols', [(i, (i + 2 * step) % tiles) for i in range(t...]
  transfers between devices with their start and end apart: 23 -> 23, of which waited for: 13 -> 12; matrix products, arithmetic and copies ran while one was open for 1% -> 0% of each run, Pallas kernels for 5% -> 6%
where the time goes in v4:
time: 119 us
  blocking collectives  44 us (37%)
  starting transfers between devices  25.8 us (22%)
  Pallas kernels  24.5 us (21%)
  waiting for transfers between devices  21.7 us (18%)
  local copies, waits for them, and re-layouts  1.4 us (1%)
    all_to_all x3, blocking collectives, over_z(): lax.all_to_all(array, 'inner', 0, 0, tiled=True, axis_index_groups=groups)  44 us
    ppermute x9, starting transfers between devices, shift_y(): return lax.ppermute(array, 'inner', pairs)  16.4 us
    ppermute x9, waiting for transfers between devices, shift_y(): return lax.ppermute(array, 'inner', pairs)  14 us
    pallas_call x1, Pallas kernels, body(): pl.pallas_call(functools.partial(ortho_kernel, zs), out_shape=(shape((NB...  10.2 us
    ppermute x6, starting transfers between devices, hop(): lax.ppermute(value, 'cols', [(i, (i + 2 * step) % tiles) for i in range(t...  7.77 us
    ppermute x6, waiting for transfers between devices, hop(): lax.ppermute(value, 'cols', [(i, (i + 2 * step) % tiles) for i in range(t...  6.08 us
    pallas_call x1, Pallas kernels, body(): pl.pallas_call(functools.partial(backward_kernel, outs, slots, zs), out_s...  5.44 us
    pallas_call x1, Pallas kernels, body(): pl.pallas_call(functools.partial(probe_kernel, outs, slots), out_shape=(s...  3.76 us
  transfers between devices with their start and end apart: 23, of which 12 were waited for; matrix products, arithmetic and copies ran while one was open for 0% of the time, Pallas kernels for 6%

profile of v4, /device:TPU:8, one launch (start us, length us, event | category | flops | bytes accessed | tf_op | source)
XLA Modules:
  0.0 118.9 jit_solution(7566601571225252991)
XLA Ops:
  0.7 1.6 %collective-permute-start = (bf16[1,512,128]{2,1,0:T(8,128)(2,1)}, bf16[1,512,128]{2,1,0:T(8,128)(2,1)S(1)}, u32[]{:S(2)}, u32[]{:S(2)}) collective-permute-start(bf16[1,512,128]{2,1,0:T(8,128)(2,1)} %rest_0_.2), channel_id=1, source_target_pairs={{0,2},{1,3},{2,4},{3,5},{4,6},{5,7},{6,0},{7,1},{8,10},{9,11},{10,... | collective-permute-start | bytes 393224 | tf_op jit(solution)/shard_map/ppermute | solution.py:309
  2.2 1.7 %collective-permute-start.1 = (bf16[1,512,128]{2,1,0:T(8,128)(2,1)}, bf16[1,512,128]{2,1,0:T(8,128)(2,1)S(1)}, u32[]{:S(2)}, u32[]{:S(2)}) collective-permute-start(bf16[1,512,128]{2,1,0:T(8,128)(2,1)} %rest_0_.2), channel_id=1, source_target_pairs={{0,6},{1,7},{2,0},{3,1},{4,2},{5,3},{6,4},{7,5},{8,14},{9,15},{10,... | collective-permute-start | bytes 393224 | tf_op jit(solution)/shard_map/ppermute | solution.py:309
  4.2 3.0 %collective-permute-start.3 = (bf16[1,512,128]{2,1,0:T(8,128)(2,1)}, bf16[1,512,128]{2,1,0:T(8,128)(2,1)S(1)}, u32[]{:S(2)}, u32[]{:S(2)}) collective-permute-start(bf16[1,512,128]{2,1,0:T(8,128)(2,1)} %rest_0_.3), channel_id=1, source_target_pairs={{0,6},{1,7},{2,0},{3,1},{4,2},{5,3},{6,4},{7,5},{8,14},{9,15},{10,... | collective-permute-start | bytes 393224 | tf_op jit(solution)/shard_map/ppermute | solution.py:309
  7.2 0.7 copy-done.2
  8.6 3.8 %probe.1 = (bf16[32,128,256]{2,1,0:T(8,128)(2,1)S(1)}, bf16[32,512,128]{2,1,0:T(8,128)(2,1)S(1)}) custom-call(s32[4,8]{1,0:T(4,128)S(1)} %copy-done.2, s32[4,8]{1,0:T(4,128)S(1)} %copy-done.4, bf16[4,8,512,128]{3,2,1,0:T(8,128)(2,1)} %right_u.1, bf16[4,8,512,128]{3,2,1,0:T(8,128)(2,1)} %right_v.3, bf16[4,512,128]{2,1,0:T(8,128)(2,1)} %sketch.2), custom_call_target="tpu_custom_call" | custom-call | flops 536870912 | bytes 6291456 | tf_op jit(solution)/shard_map/probe/pallas_call | solution.py:339
  12.4 1.2 %collective-permute-start.5 = (bf16[1,512,128]{2,1,0:T(8,128)(2,1)S(1)}, bf16[1,512,128]{2,1,0:T(8,128)(2,1)S(1)}, u32[]{:S(2)}, u32[]{:S(2)}) collective-permute-start(bf16[1,512,128]{2,1,0:T(8,128)(2,1)S(1)} %collective-permute-done.1.rest_2_), channel_id=1, source_target_pairs={{0,6},{1,7},{2,0},{3,1},{4,2},{5,3},{6,4},{7,5},{8,14},{9,15},{10,... | collective-permute-start | bytes 393224 | tf_op jit(solution)/shard_map/ppermute | solution.py:309
  14.1 3.3 %collective-permute-done.5.rest_3_ = bf16[1,512,128]{2,1,0:T(8,128)(2,1)S(1)} collective-permute-done((bf16[1,512,128]{2,1,0:T(8,128)(2,1)S(1)}, bf16[1,512,128]{2,1,0:T(8,128)(2,1)S(1)}, u32[]{:S(2)}, u32[]{:S(2)}) %collective-permute-start.5) | collective-permute-done | bytes 131104 | tf_op jit(solution)/shard_map/ppermute | solution.py:309
  18.8 3.0 %pair.1 = (bf16[32,256,128]{2,1,0:T(8,128)(2,1)S(1)}, bf16[32,128,128]{2,1,0:T(8,128)(2,1)S(1)}) custom-call(s32[4,8]{1,0:T(4,128)S(1)} %copy-done.2, s32[4,8]{1,0:T(4,128)S(1)} %copy-done.4, bf16[32,512,128]{2,1,0:T(8,128)(2,1)S(1)} %get-tuple-element.29.held, bf16[32,128,256]{2,1,0:T(8,128)(2,1)S(1)} %get-tuple-element.30.probes, ...), custom_call_target="tpu_custom_call" | custom-call | flops 939524096 | bytes 10485760 | tf_op jit(solution)/shard_map/pair/pallas_call | solution.py:357
  21.8 2.8 %collective-permute-done.4.rest_3_ = bf16[1,512,128]{2,1,0:T(8,128)(2,1)S(1)} collective-permute-done((bf16[1,512,128]{2,1,0:T(8,128)(2,1)S(1)}, bf16[1,512,128]{2,1,0:T(8,128)(2,1)S(1)}, u32[]{:S(2)}, u32[]{:S(2)}) %collective-permute-start.4) | collective-permute-done | bytes 131104 | tf_op jit(solution)/shard_map/ppermute | solution.py:309
  24.6 1.3 %collective-permute-done.13.rest_7_ = bf16[1,512,128]{2,1,0:T(8,128)(2,1)S(1)} collective-permute-done((bf16[1,512,128]{2,1,0:T(8,128)(2,1)S(1)}, bf16[1,512,128]{2,1,0:T(8,128)(2,1)S(1)}, u32[]{:S(2)}, u32[]{:S(2)}) %collective-permute-start.13) | collective-permute-done | bytes 131104 | tf_op jit(solution)/shard_map/ppermute | solution.py:313
  25.9 2.1 %sketch.3 = (f32[512,128]{1,0:T(8,128)S(1)}, bf16[512,128]{1,0:T(8,128)(2,1)S(1)}, bf16[512,128]{1,0:T(8,128)(2,1)S(1)}, bf16[512,128]{1,0:T(8,128)(2,1)S(1)}, bf16[8,512,128]{2,1,0:T(8,128)(2,1)S(1)}) custom-call(s32[4,8]{1,0:T(4,128)S(1)} %copy-done.2, s32[4,8]{1,0:T(4,128)S(1)} %copy-done.4, bf16[32,128,128]{2,1,0:T(8,128)(2,1)S(1)} %get-tuple-element.34.mixing, ...), custom_call_target="tpu_custom_call" | custom-call | flops 536870912 | bytes 4194304 | tf_op jit(solution)/shard_map/sketch/pallas_call | solution.py:369
  28.0 1.9 %collective-permute-start.14 = (bf16[512,128]{1,0:T(8,128)(2,1)S(1)}, bf16[512,128]{1,0:T(8,128)(2,1)S(1)}, u32[]{:S(2)}, u32[]{:S(2)}) collective-permute-start(bf16[512,128]{1,0:T(8,128)(2,1)S(1)} %get-tuple-element.40), channel_id=1, source_target_pairs={{0,8},{8,16},{16,24},{24,0},{32,40},{40,48},{48,56},{56,32},{64,72... | collective-permute-start | bytes 393224 | tf_op jit(solution)/shard_map/ppermute | solution.py:305
  29.9 3.3 %collective-permute-start.15 = (bf16[512,128]{1,0:T(8,128)(2,1)S(1)}, bf16[512,128]{1,0:T(8,128)(2,1)S(1)}, u32[]{:S(2)}, u32[]{:S(2)}) collective-permute-start(bf16[512,128]{1,0:T(8,128)(2,1)S(1)} %get-tuple-element.41), channel_id=1, source_target_pairs={{0,16},{8,24},{16,0},{24,8},{32,48},{40,56},{48,32},{56,40},{64,80... | collective-permute-start | bytes 393224 | tf_op jit(solution)/shard_map/ppermute | solution.py:305
  33.1 0.8 collective-permute-start.16
  34.0 1.1 collective-permute-done.14
  35.0 2.7 %collective-permute-done.15 = bf16[512,128]{1,0:T(8,128)(2,1)S(1)} collective-permute-done((bf16[512,128]{1,0:T(8,128)(2,1)S(1)}, bf16[512,128]{1,0:T(8,128)(2,1)S(1)}, u32[]{:S(2)}, u32[]{:S(2)}) %collective-permute-start.15) | collective-permute-done | bytes 131104 | tf_op jit(solution)/shard_map/ppermute | solution.py:305
  37.7 2.0 %collective-permute-done.16 = bf16[512,128]{1,0:T(8,128)(2,1)S(1)} collective-permute-done((bf16[512,128]{1,0:T(8,128)(2,1)S(1)}, bf16[512,128]{1,0:T(8,128)(2,1)S(1)}, u32[]{:S(2)}, u32[]{:S(2)}) %collective-permute-start.16) | collective-permute-done | bytes 131104 | tf_op jit(solution)/shard_map/ppermute | solution.py:305
  39.8 18.2 %all_to_all.15 = f32[8,64,128]{2,1,0:T(8,128)S(1)} all-to-all(f32[8,64,128]{2,1,0:T(8,128)S(1)} %bitcast.1), channel_id=1, replica_groups={{0,32,64,96,128,160,192,224},{8,40,72,104,136,168,200,232},{16,48,80,11..., dimensions={0} | all-to-all | bytes 524288 | tf_op jit(solution)/shard_map/all_to_all | solution.py:318
  58.1 12.9 %all_to_all.16.blocks = f32[8,64,128]{2,1,0:T(8,128)S(1)} all-to-all(f32[8,64,128]{2,1,0:T(8,128)S(1)} %broadcast_in_dim.2), channel_id=1, replica_groups={{0,32,64,96,128,160,192,224},{8,40,72,104,136,168,200,232},{16,48,80,11..., dimensions={0} | all-to-all | bytes 524288 | tf_op jit(solution)/shard_map/all_to_all | solution.py:318
  71.0 10.2 %ortho.1 = (bf16[544,128]{1,0:T(8,128)(2,1)S(1)}, bf16[544,128]{1,0:T(8,128)(2,1)S(1)}, bf16[544,128]{1,0:T(8,128)(2,1)S(1)}, bf16[544,128]{1,0:T(8,128)(2,1)S(1)}) custom-call(f32[8,64,128]{2,1,0:T(8,128)S(1)} %all_to_all.16.blocks), custom_call_target="tpu_custom_call" | custom-call | flops 218103808 | bytes 1048576 | tf_op jit(solution)/shard_map/ortho/pallas_call | solution.py:386
  81.2 1.9 %collective-permute-start.17 = (bf16[544,128]{1,0:T(8,128)(2,1)S(1)}, bf16[544,128]{1,0:T(8,128)(2,1)S(1)}, u32[]{:S(2)}, u32[]{:S(2)}) collective-permute-start(bf16[544,128]{1,0:T(8,128)(2,1)S(1)} %get-tuple-element.44), channel_id=1, source_target_pairs={{0,8},{8,16},{16,24},{24,0},{32,40},{40,48},{48,56},{56,32},{64,72... | collective-permute-start | bytes 417800 | tf_op jit(solution)/shard_map/ppermute | solution.py:305
  83.2 1.1 collective-permute-start.18
  84.3 1.6 %collective-permute-start.19 = (bf16[544,128]{1,0:T(8,128)(2,1)S(1)}, bf16[544,128]{1,0:T(8,128)(2,1)S(1)}, u32[]{:S(2)}, u32[]{:S(2)}) collective-permute-start(bf16[544,128]{1,0:T(8,128)(2,1)S(1)} %get-tuple-element.46), channel_id=1, source_target_pairs={{0,24},{8,0},{16,8},{24,16},{32,56},{40,32},{48,40},{56,48},{64,88... | collective-permute-start | bytes 417800 | tf_op jit(solution)/shard_map/ppermute | solution.py:305
  86.4 3.4 %collective-permute-done.18.msg2 = bf16[544,128]{1,0:T(8,128)(2,1)S(1)} collective-permute-done((bf16[544,128]{1,0:T(8,128)(2,1)S(1)}, bf16[544,128]{1,0:T(8,128)(2,1)S(1)}, u32[]{:S(2)}, u32[]{:S(2)}) %collective-permute-start.18) | collective-permute-done | bytes 139296 | tf_op jit(solution)/shard_map/ppermute | solution.py:305
  89.8 1.0 collective-permute-done.19.msg3
  90.9 5.4 %backward.1 = (f32[8,4,16,128]{3,2,1,0:T(8,128)S(1)}, bf16[8,4,16,128]{3,2,1,0:T(8,128)(2,1)S(1)}, bf16[8,4,16,128]{3,2,1,0:T(8,128)(2,1)S(1)}, bf16[8,4,16,128]{3,2,1,0:T(8,128)(2,1)S(1)}, f32[4,16,128]{2,1,0:T(8,128)}) custom-call(s32[4,8]{1,0:T(4,128)S(1)} %copy-done.3, s32[4,8]{1,0:T(4,128)S(1)} %copy-done.5, bf16[4,8,512,128]{3,2,1,0:T(8,128)(2,1)} %right_v.3, ...), custom_call_target="tpu_custom_call" | custom-call | flops 1476395008 | bytes 8388608 | tf_op jit(solution)/shard_map/backward/pallas_call | solution.py:398
  96.3 1.2 collective-permute-start.20
  97.5 2.0 %collective-permute-start.21 = (bf16[8,4,16,128]{3,2,1,0:T(8,128)(2,1)S(1)}, bf16[8,4,16,128]{3,2,1,0:T(8,128)(2,1)S(1)}, u32[]{:S(2)}, u32[]{:S(2)}) collective-permute-start(bf16[8,4,16,128]{3,2,1,0:T(8,128)(2,1)S(1)} %get-tuple-element.50), channel_id=1, source_target_pairs={{0,16},{8,24},{16,0},{24,8},{32,48},{40,56},{48,32},{56,40},{64,80... | collective-permute-start | bytes 393224 | tf_op jit(solution)/shard_map/ppermute | solution.py:305
  99.5 2.5 %collective-permute-start.22 = (bf16[8,4,16,128]{3,2,1,0:T(8,128)(2,1)S(1)}, bf16[8,4,16,128]{3,2,1,0:T(8,128)(2,1)S(1)}, u32[]{:S(2)}, u32[]{:S(2)}) collective-permute-start(bf16[8,4,16,128]{3,2,1,0:T(8,128)(2,1)S(1)} %get-tuple-element.51), channel_id=1, source_target_pairs={{0,24},{8,0},{16,8},{24,16},{32,56},{40,32},{48,40},{56,48},{64,88... | collective-permute-start | bytes 393224 | tf_op jit(solution)/shard_map/ppermute | solution.py:305
  102.0 2.0 %collective-permute-done.21 = bf16[8,4,16,128]{3,2,1,0:T(8,128)(2,1)S(1)} collective-permute-done((bf16[8,4,16,128]{3,2,1,0:T(8,128)(2,1)S(1)}, bf16[8,4,16,128]{3,2,1,0:T(8,128)(2,1)S(1)}, u32[]{:S(2)}, u32[]{:S(2)}) %collective-permute-start.21) | collective-permute-done | bytes 131104 | tf_op jit(solution)/shard_map/ppermute | solution.py:305
  104.0 1.3 %collective-permute-done.22 = bf16[8,4,16,128]{3,2,1,0:T(8,128)(2,1)S(1)} collective-permute-done((bf16[8,4,16,128]{3,2,1,0:T(8,128)(2,1)S(1)}, bf16[8,4,16,128]{3,2,1,0:T(8,128)(2,1)S(1)}, u32[]{:S(2)}, u32[]{:S(2)}) %collective-permute-start.22) | collective-permute-done | bytes 131104 | tf_op jit(solution)/shard_map/ppermute | solution.py:305
  105.4 12.9 %all_to_all.17 = f32[8,4,16,128]{3,2,1,0:T(8,128)S(1)} all-to-all(f32[8,4,16,128]{3,2,1,0:T(8,128)S(1)} %convert_add_fusion), channel_id=1, replica_groups={{0,32,64,96,128,160,192,224},{8,40,72,104,136,168,200,232},{16,48,80,11..., dimensions={0} | all-to-all | bytes 524288 | tf_op jit(solution)/shard_map/all_to_all | solution.py:318
  (39 shorter events, 4.1 us)
Async XLA Ops:
  0.6 13.0 %copy-start = (bf16[1,512,128]{2,1,0:T(8,128)(2,1)S(1)}, bf16[1,512,128]{2,1,0:T(8,128)(2,1)}, u32[]{:S(2)}) copy-start(bf16[1,512,128]{2,1,0:T(8,128)(2,1)} %rest_0_.2) | copy-start | bytes 393220
  0.6 16.8 %copy-start.1 = (bf16[1,512,128]{2,1,0:T(8,128)(2,1)S(1)}, bf16[1,512,128]{2,1,0:T(8,128)(2,1)}, u32[]{:S(2)}) copy-start(bf16[1,512,128]{2,1,0:T(8,128)(2,1)} %rest_0_.3) | copy-start | bytes 393220
  0.7 11.7 %collective-permute-start = (bf16[1,512,128]{2,1,0:T(8,128)(2,1)}, bf16[1,512,128]{2,1,0:T(8,128)(2,1)S(1)}, u32[]{:S(2)}, u32[]{:S(2)}) collective-permute-start(bf16[1,512,128]{2,1,0:T(8,128)(2,1)} %rest_0_.2), channel_id=1, source_target_pairs={{0,2},{1,3},{2,4},{3,5},{4,6},{5,7},{6,0},{7,1},{8,10},{9,11},{10,... | collective-permute-start | bytes 393224 | tf_op jit(solution)/shard_map/ppermute | solution.py:309
  2.2 10.1 %collective-permute-start.1 = (bf16[1,512,128]{2,1,0:T(8,128)(2,1)}, bf16[1,512,128]{2,1,0:T(8,128)(2,1)S(1)}, u32[]{:S(2)}, u32[]{:S(2)}) collective-permute-start(bf16[1,512,128]{2,1,0:T(8,128)(2,1)} %rest_0_.2), channel_id=1, source_target_pairs={{0,6},{1,7},{2,0},{3,1},{4,2},{5,3},{6,4},{7,5},{8,14},{9,15},{10,... | collective-permute-start | bytes 393224 | tf_op jit(solution)/shard_map/ppermute | solution.py:309
  4.0 8.4 %collective-permute-start.2 = (bf16[1,512,128]{2,1,0:T(8,128)(2,1)}, bf16[1,512,128]{2,1,0:T(8,128)(2,1)S(1)}, u32[]{:S(2)}, u32[]{:S(2)}) collective-permute-start(bf16[1,512,128]{2,1,0:T(8,128)(2,1)} %rest_0_.3), channel_id=1, source_target_pairs={{0,2},{1,3},{2,4},{3,5},{4,6},{5,7},{6,0},{7,1},{8,10},{9,11},{10,... | collective-permute-start | bytes 393224 | tf_op jit(solution)/shard_map/ppermute | solution.py:309
  4.2 8.1 %collective-permute-start.3 = (bf16[1,512,128]{2,1,0:T(8,128)(2,1)}, bf16[1,512,128]{2,1,0:T(8,128)(2,1)S(1)}, u32[]{:S(2)}, u32[]{:S(2)}) collective-permute-start(bf16[1,512,128]{2,1,0:T(8,128)(2,1)} %rest_0_.3), channel_id=1, source_target_pairs={{0,6},{1,7},{2,0},{3,1},{4,2},{5,3},{6,4},{7,5},{8,14},{9,15},{10,... | collective-permute-start | bytes 393224 | tf_op jit(solution)/shard_map/ppermute | solution.py:309
  7.2 0.7 copy-start.2
  7.9 0.7 copy-start.4
  12.4 5.0 %collective-permute-start.5 = (bf16[1,512,128]{2,1,0:T(8,128)(2,1)S(1)}, bf16[1,512,128]{2,1,0:T(8,128)(2,1)S(1)}, u32[]{:S(2)}, u32[]{:S(2)}) collective-permute-start(bf16[1,512,128]{2,1,0:T(8,128)(2,1)S(1)} %collective-permute-done.1.rest_2_), channel_id=1, source_target_pairs={{0,6},{1,7},{2,0},{3,1},{4,2},{5,3},{6,4},{7,5},{8,14},{9,15},{10,... | collective-permute-start | bytes 393224 | tf_op jit(solution)/shard_map/ppermute | solution.py:309
  13.6 3.8 %collective-permute-start.6 = (bf16[1,512,128]{2,1,0:T(8,128)(2,1)S(1)}, bf16[1,512,128]{2,1,0:T(8,128)(2,1)S(1)}, u32[]{:S(2)}, u32[]{:S(2)}) collective-permute-start(bf16[1,512,128]{2,1,0:T(8,128)(2,1)S(1)} %copy-done), channel_id=1, source_target_pairs={{0,1},{1,0},{2,3},{3,2},{4,5},{5,4},{6,7},{7,6},{8,9},{9,8},{10,11... | collective-permute-start | bytes 393224 | tf_op jit(solution)/shard_map/ppermute | solution.py:313
  13.6 4.4 %collective-permute-start.8 = (bf16[1,512,128]{2,1,0:T(8,128)(2,1)S(1)}, bf16[1,512,128]{2,1,0:T(8,128)(2,1)S(1)}, u32[]{:S(2)}, u32[]{:S(2)}) collective-permute-start(bf16[1,512,128]{2,1,0:T(8,128)(2,1)S(1)} %collective-permute-done.1.rest_2_), channel_id=1, source_target_pairs={{0,1},{1,0},{2,3},{3,2},{4,5},{5,4},{6,7},{7,6},{8,9},{9,8},{10,11... | collective-permute-start | bytes 393224 | tf_op jit(solution)/shard_map/ppermute | solution.py:313
  14.1 4.0 %collective-permute-start.7 = (bf16[1,512,128]{2,1,0:T(8,128)(2,1)S(1)}, bf16[1,512,128]{2,1,0:T(8,128)(2,1)S(1)}, u32[]{:S(2)}, u32[]{:S(2)}) collective-permute-start(bf16[1,512,128]{2,1,0:T(8,128)(2,1)S(1)} %collective-permute-done.rest_1_), channel_id=1, source_target_pairs={{0,1},{1,0},{2,3},{3,2},{4,5},{5,4},{6,7},{7,6},{8,9},{9,8},{10,11... | collective-permute-start | bytes 393224 | tf_op jit(solution)/shard_map/ppermute | solution.py:313
  17.4 1.3 %collective-permute-start.9 = (bf16[1,512,128]{2,1,0:T(8,128)(2,1)S(1)}, bf16[1,512,128]{2,1,0:T(8,128)(2,1)S(1)}, u32[]{:S(2)}, u32[]{:S(2)}) collective-permute-start(bf16[1,512,128]{2,1,0:T(8,128)(2,1)S(1)} %collective-permute-done.5.rest_3_), channel_id=1, source_target_pairs={{0,1},{1,0},{2,3},{3,2},{4,5},{5,4},{6,7},{7,6},{8,9},{9,8},{10,11... | collective-permute-start | bytes 393224 | tf_op jit(solution)/shard_map/ppermute | solution.py:313
  17.4 7.1 %collective-permute-start.4 = (bf16[1,512,128]{2,1,0:T(8,128)(2,1)S(1)}, bf16[1,512,128]{2,1,0:T(8,128)(2,1)S(1)}, u32[]{:S(2)}, u32[]{:S(2)}) collective-permute-start(bf16[1,512,128]{2,1,0:T(8,128)(2,1)S(1)} %collective-permute-done.2.rest_1_), channel_id=1, source_target_pairs={{0,2},{1,3},{2,4},{3,5},{4,6},{5,7},{6,0},{7,1},{8,10},{9,11},{10,... | collective-permute-start | bytes 393224 | tf_op jit(solution)/shard_map/ppermute | solution.py:309
  17.4 7.1 %collective-permute-start.10 = (bf16[1,512,128]{2,1,0:T(8,128)(2,1)S(1)}, bf16[1,512,128]{2,1,0:T(8,128)(2,1)S(1)}, u32[]{:S(2)}, u32[]{:S(2)}) collective-permute-start(bf16[1,512,128]{2,1,0:T(8,128)(2,1)S(1)} %copy-done.1), channel_id=1, source_target_pairs={{0,1},{1,0},{2,3},{3,2},{4,5},{5,4},{6,7},{7,6},{8,9},{9,8},{10,11... | collective-permute-start | bytes 393224 | tf_op jit(solution)/shard_map/ppermute | solution.py:313
  18.0 6.5 %collective-permute-start.11 = (bf16[1,512,128]{2,1,0:T(8,128)(2,1)S(1)}, bf16[1,512,128]{2,1,0:T(8,128)(2,1)S(1)}, u32[]{:S(2)}, u32[]{:S(2)}) collective-permute-start(bf16[1,512,128]{2,1,0:T(8,128)(2,1)S(1)} %collective-permute-done.2.rest_1_), channel_id=1, source_target_pairs={{0,1},{1,0},{2,3},{3,2},{4,5},{5,4},{6,7},{7,6},{8,9},{9,8},{10,11... | collective-permute-start | bytes 393224 | tf_op jit(solution)/shard_map/ppermute | solution.py:313
  18.1 6.4 %collective-permute-start.12 = (bf16[1,512,128]{2,1,0:T(8,128)(2,1)S(1)}, bf16[1,512,128]{2,1,0:T(8,128)(2,1)S(1)}, u32[]{:S(2)}, u32[]{:S(2)}) collective-permute-start(bf16[1,512,128]{2,1,0:T(8,128)(2,1)S(1)} %collective-permute-done.3.rest_2_), channel_id=1, source_target_pairs={{0,1},{1,0},{2,3},{3,2},{4,5},{5,4},{6,7},{7,6},{8,9},{9,8},{10,11... | collective-permute-start | bytes 393224 | tf_op jit(solution)/shard_map/ppermute | solution.py:313
  21.8 69.1 %copy-start.3 = (s32[4,8]{1,0:T(4,128)S(1)}, s32[4,8]{1,0:T(4,128)}, u32[]{:S(2)}) copy-start(s32[4,8]{1,0:T(4,128)} %index.7) | copy-start | bytes 388
  21.8 69.1 %copy-start.5 = (s32[4,8]{1,0:T(4,128)S(1)}, s32[4,8]{1,0:T(4,128)}, u32[]{:S(2)}) copy-start(s32[4,8]{1,0:T(4,128)} %mask.7) | copy-start | bytes 388
  24.5 1.3 %collective-permute-start.13 = (bf16[1,512,128]{2,1,0:T(8,128)(2,1)S(1)}, bf16[1,512,128]{2,1,0:T(8,128)(2,1)S(1)}, u32[]{:S(2)}, u32[]{:S(2)}) collective-permute-start(bf16[1,512,128]{2,1,0:T(8,128)(2,1)S(1)} %collective-permute-done.4.rest_3_), channel_id=1, source_target_pairs={{0,1},{1,0},{2,3},{3,2},{4,5},{5,4},{6,7},{7,6},{8,9},{9,8},{10,11... | collective-permute-start | bytes 393224 | tf_op jit(solution)/shard_map/ppermute | solution.py:313
  28.0 7.0 %collective-permute-start.14 = (bf16[512,128]{1,0:T(8,128)(2,1)S(1)}, bf16[512,128]{1,0:T(8,128)(2,1)S(1)}, u32[]{:S(2)}, u32[]{:S(2)}) collective-permute-start(bf16[512,128]{1,0:T(8,128)(2,1)S(1)} %get-tuple-element.40), channel_id=1, source_target_pairs={{0,8},{8,16},{16,24},{24,0},{32,40},{40,48},{48,56},{56,32},{64,72... | collective-permute-start | bytes 393224 | tf_op jit(solution)/shard_map/ppermute | solution.py:305
  29.9 7.8 %collective-permute-start.15 = (bf16[512,128]{1,0:T(8,128)(2,1)S(1)}, bf16[512,128]{1,0:T(8,128)(2,1)S(1)}, u32[]{:S(2)}, u32[]{:S(2)}) collective-permute-start(bf16[512,128]{1,0:T(8,128)(2,1)S(1)} %get-tuple-element.41), channel_id=1, source_target_pairs={{0,16},{8,24},{16,0},{24,8},{32,48},{40,56},{48,32},{56,40},{64,80... | collective-permute-start | bytes 393224 | tf_op jit(solution)/shard_map/ppermute | solution.py:305
  33.1 6.6 %collective-permute-start.16 = (bf16[512,128]{1,0:T(8,128)(2,1)S(1)}, bf16[512,128]{1,0:T(8,128)(2,1)S(1)}, u32[]{:S(2)}, u32[]{:S(2)}) collective-permute-start(bf16[512,128]{1,0:T(8,128)(2,1)S(1)} %get-tuple-element.42), channel_id=1, source_target_pairs={{0,24},{8,0},{16,8},{24,16},{32,56},{40,32},{48,40},{56,48},{64,88... | collective-permute-start | bytes 393224 | tf_op jit(solution)/shard_map/ppermute | solution.py:305
  81.2 5.1 %collective-permute-start.17 = (bf16[544,128]{1,0:T(8,128)(2,1)S(1)}, bf16[544,128]{1,0:T(8,128)(2,1)S(1)}, u32[]{:S(2)}, u32[]{:S(2)}) collective-permute-start(bf16[544,128]{1,0:T(8,128)(2,1)S(1)} %get-tuple-element.44), channel_id=1, source_target_pairs={{0,8},{8,16},{16,24},{24,0},{32,40},{40,48},{48,56},{56,32},{64,72... | collective-permute-start | bytes 417800 | tf_op jit(solution)/shard_map/ppermute | solution.py:305
  83.2 6.7 %collective-permute-start.18 = (bf16[544,128]{1,0:T(8,128)(2,1)S(1)}, bf16[544,128]{1,0:T(8,128)(2,1)S(1)}, u32[]{:S(2)}, u32[]{:S(2)}) collective-permute-start(bf16[544,128]{1,0:T(8,128)(2,1)S(1)} %get-tuple-element.45), channel_id=1, source_target_pairs={{0,16},{8,24},{16,0},{24,8},{32,48},{40,56},{48,32},{56,40},{64,80... | collective-permute-start | bytes 417800 | tf_op jit(solution)/shard_map/ppermute | solution.py:305
  84.3 6.5 %collective-permute-start.19 = (bf16[544,128]{1,0:T(8,128)(2,1)S(1)}, bf16[544,128]{1,0:T(8,128)(2,1)S(1)}, u32[]{:S(2)}, u32[]{:S(2)}) collective-permute-start(bf16[544,128]{1,0:T(8,128)(2,1)S(1)} %get-tuple-element.46), channel_id=1, source_target_pairs={{0,24},{8,0},{16,8},{24,16},{32,56},{40,32},{48,40},{56,48},{64,88... | collective-permute-start | bytes 417800 | tf_op jit(solution)/shard_map/ppermute | solution.py:305
  96.3 5.7 %collective-permute-start.20 = (bf16[8,4,16,128]{3,2,1,0:T(8,128)(2,1)S(1)}, bf16[8,4,16,128]{3,2,1,0:T(8,128)(2,1)S(1)}, u32[]{:S(2)}, u32[]{:S(2)}) collective-permute-start(bf16[8,4,16,128]{3,2,1,0:T(8,128)(2,1)S(1)} %get-tuple-element.49), channel_id=1, source_target_pairs={{0,8},{8,16},{16,24},{24,0},{32,40},{40,48},{48,56},{56,32},{64,72... | collective-permute-start | bytes 393224 | tf_op jit(solution)/shard_map/ppermute | solution.py:305
  97.5 6.6 %collective-permute-start.21 = (bf16[8,4,16,128]{3,2,1,0:T(8,128)(2,1)S(1)}, bf16[8,4,16,128]{3,2,1,0:T(8,128)(2,1)S(1)}, u32[]{:S(2)}, u32[]{:S(2)}) collective-permute-start(bf16[8,4,16,128]{3,2,1,0:T(8,128)(2,1)S(1)} %get-tuple-element.50), channel_id=1, source_target_pairs={{0,16},{8,24},{16,0},{24,8},{32,48},{40,56},{48,32},{56,40},{64,80... | collective-permute-start | bytes 393224 | tf_op jit(solution)/shard_map/ppermute | solution.py:305
  99.5 5.9 %collective-permute-start.22 = (bf16[8,4,16,128]{3,2,1,0:T(8,128)(2,1)S(1)}, bf16[8,4,16,128]{3,2,1,0:T(8,128)(2,1)S(1)}, u32[]{:S(2)}, u32[]{:S(2)}) collective-permute-start(bf16[8,4,16,128]{3,2,1,0:T(8,128)(2,1)S(1)} %get-tuple-element.51), channel_id=1, source_target_pairs={{0,24},{8,0},{16,8},{24,16},{32,56},{40,32},{48,40},{56,48},{64,88... | collective-permute-start | bytes 393224 | tf_op jit(solution)/shard_map/ppermute | solution.py:305

commit v5 on v4

--- a/solution.py
+++ b/solution.py
@@ -198,35 +198,47 @@
     same = lax.broadcasted_iota(jnp.int32, (n, n), 0) == lax.broadcasted_iota(jnp.int32, (n, n), 1)
     full = jnp.concatenate([same.astype(F32), block], axis=1)
     x = [full[8 * i:8 * i + 8] for i in range(n // 8)]
+    done = list(x)
     sub = lax.broadcasted_iota(jnp.int32, (8, lanes), 0)
 
     def wide(v):
         return jnp.broadcast_to(v, (8, lanes))
 
-    for k in range(0, n, 2):
+    for k in range(0, n, 4):
         i0, r = k // 8, k % 8
-        first, second = wide(x[i0][r:r + 1]), wide(x[i0][r + 1:r + 2])
-        a, b = wide(first[:, n + k:n + k + 1]), wide(first[:, n + k + 1:n + k + 2])
-        c = wide(second[:, n + k + 1:n + k + 2])
-        scale = 1.0 / (a * c - b * b)
-        p, q = (c * first - b * second) * scale, (a * second - b * first) * scale
+        row = [wide(x[i0][r + t:r + t + 1]) for t in range(4)]
+        b = {(t, u): wide(row[t][:, n + k + u:n + k + u + 1]) for t in range(4) for u in range(t, 4)}
+        one = 1.0 / (b[0, 0] * b[1, 1] - b[0, 1] * b[0, 1])
+        t00 = (b[1, 1] * b[0, 2] - b[0, 1] * b[1, 2]) * one
+        t01 = (b[1, 1] * b[0, 3] - b[0, 1] * b[1, 3]) * one
+        t10 = (b[0, 0] * b[1, 2] - b[0, 1] * b[0, 2]) * one
+        t11 = (b[0, 0] * b[1, 3] - b[0, 1] * b[0, 3]) * one
+        s00 = b[2, 2] - (b[0, 2] * t00 + b[1, 2] * t10)
+        s01 = b[2, 3] - (b[0, 2] * t01 + b[1, 2] * t11)
+        s11 = b[3, 3] - (b[0, 3] * t01 + b[1, 3] * t11)
+        two = 1.0 / (s00 * s11 - s01 * s01)
+        e2 = row[2] - (t00 * row[0] + t10 * row[1])
+        e3 = row[3] - (t01 * row[0] + t11 * row[1])
+        p2, p3 = (s11 * e2 - s01 * e3) * two, (s00 * e3 - s01 * e2) * two
+        p0 = (b[1, 1] * row[0] - b[0, 1] * row[1]) * one - (t00 * p2 + t01 * p3)
+        p1 = (b[0, 0] * row[1] - b[0, 1] * row[0]) * one - (t10 * p2 + t11 * p3)
         for i in range(i0, n // 8):
-            if i == i0 and r == 6:
+            if i == i0 and r == 4:
                 continue
-            step = wide(x[i][:, n + k:n + k + 1]) * p + wide(x[i][:, n + k + 1:n + k + 2]) * q
+            u = [wide(x[i][:, n + k + t:n + k + t + 1]) for t in range(4)]
+            step = (u[0] * p0 + u[1] * p1) + (u[2] * p2 + u[3] * p3)
             if i == i0:
-                step = jnp.where(sub > r + 1, step, 0.0)
+                step = jnp.where(sub > r + 3, step, 0.0)
             x[i] = x[i] - step
-    full = jnp.concatenate(x, axis=0)
-    row = lax.broadcasted_iota(jnp.int32, (n, lanes), 0)
-    lane = lax.broadcasted_iota(jnp.int32, (n, lanes), 1) - n
-    diag = jnp.broadcast_to(jnp.sum(jnp.where(lane == row, full, 0.0), axis=1, keepdims=True), (n, lanes))
-    side = jnp.broadcast_to(jnp.sum(jnp.where(lane == row + 1, full, 0.0), axis=1, keepdims=True), (n, lanes))
-    ratio = side / diag
-    odd = row % 2 == 1
-    full = jnp.where(odd, full - pltpu.roll(ratio * full, 1, 0), full)
-    diag = jnp.where(odd, diag - pltpu.roll(ratio * side, 1, 0), diag)
-    return (full * lax.rsqrt(diag))[:, :n]
+        for t, (a, c, d, first, second) in enumerate((
+            (b[0, 0], b[0, 1], b[1, 1], row[0], row[1]), (s00, s01, s11, e2, e3)
+        )):
+            root = lax.rsqrt(a)
+            off = c * root
+            first = first * root
+            second = (second - off * first) * lax.rsqrt(d - off * off)
+            done[i0] = jnp.where(sub == r + 2 * t, first, jnp.where(sub == r + 2 * t + 1, second, done[i0]))
+    return jnp.concatenate(done, axis=0)[:, :n]
 
 
 def inverse_cholesky(gram):
@@ -330,12 +342,15 @@
     count = outs * slots
     right_u = pltpu.with_memory_space_constraint(right_u, pltpu.HBM)
     right_v = pltpu.with_memory_space_constraint(right_v, pltpu.HBM)
-    sketch = pltpu.with_memory_space_constraint(sketch, pltpu.HBM)
     unit = 2 * NB * R * R
 
     def cost(units, mib):
         return pl.CostEstimate(flops=int(units * unit), bytes_accessed=mib << 20, transcendentals=0)
 
+    near = [hop(value, step, tiles) for value in (left_v, left_u) for step in (1, -1)]
+    *near, sketch = lax.optimization_barrier((*near, sketch))
+    far_v, far_u = hop(near[1], -1, tiles), hop(near[2], 1, tiles)
+    sketch = pltpu.with_memory_space_constraint(sketch, pltpu.HBM)
     probes, held_u = pl.pallas_call(
         functools.partial(probe_kernel, outs, slots),
         out_shape=(shape((count, R, 2 * R), BF),) + (shape((count, NB, R), BF),),
@@ -347,13 +362,11 @@
         cost_estimate=cost(outs * slots, 6),
         name="probe",
     )(tile_index, slot_mask, right_u, right_v, sketch)
-    near = [hop(value, step, tiles) for value in (left_v, left_u) for step in (1, -1)]
-    *near, probes = lax.optimization_barrier((*near, probes))
-    group_v = [left_v, *near[:2], hop(near[1], -1, tiles)]
+    *near, far_v, far_u, probes = lax.optimization_barrier((*near, far_v, far_u, probes))
+    group_v = [left_v, *near[:2], far_v]
     group_v += [swap(value, tiles) for value in group_v]
-    group_u = [left_u, *near[2:]]
-    other_u = [swap(value, tiles) for value in group_u]
-    far_u = hop(near[2], 1, tiles)
+    group_u = [left_u, *near[2:], far_u]
+    group_u += [swap(value, tiles) for value in group_u]
     pairs, mixing = pl.pallas_call(
         functools.partial(pair_kernel, outs, slots),
         out_shape=(shape((count, 2 * R, R), BF), shape((count, R, R), BF)),
@@ -364,8 +377,6 @@
         cost_estimate=cost(outs * slots * 1.75, 10),
         name="pair",
     )(tile_index, slot_mask, held_u, probes, *group_v)
-    far_u, mixing = lax.optimization_barrier((far_u, mixing))
-    group_u += [far_u, *other_u, swap(far_u, tiles)]
     own, send1, send2, send3, group = pl.pallas_call(
         functools.partial(sketch_kernel, outs, slots),
         out_shape=(shape((NB, R), F32),) + (shape((NB, R), BF),) * 3 + (shape((tiles, NB, R), BF),),

time: 119 us -> 116 us (0.975); the launches traced: 119 us -> 115 us
  waiting for transfers between devices: 21.7 us -> 17.5 us
  Pallas kernels: 24.5 us -> 21.3 us
  blocking collectives: 44 us -> 46.1 us
    pallas_call x1, Pallas kernels: 10.2 us -> 6.97 us  [body(): pl.pallas_call(functools.partial(ortho_kernel, zs), out_shape=(shape((NB...]
    all_to_all x3, blocking collectives: 44 us -> 46.1 us  [over_z(): lax.all_to_all(array, 'inner', 0, 0, tiled=True, axis_index_groups=groups)]
    ppermute x6, starting transfers between devices: 7.77 us -> 9.79 us  [hop(): lax.ppermute(value, 'cols', [(i, (i + 2 * step) % tiles) for i in range(t...]
    ppermute x6, waiting for transfers between devices: 6.08 us -> 4.19 us  [hop(): lax.ppermute(value, 'cols', [(i, (i + 2 * step) % tiles) for i in range(t...]
    ppermute x8, waiting for transfers between devices: 1.56 us -> 0.25 us  [swap(): return lax.ppermute(value, 'cols', [(i, i ^ 1) for i in range(tiles)])]
  transfers between devices with their start and end apart: 23 -> 23, of which waited for: 12 -> 13; matrix products, arithmetic and copies ran while one was open for 0% -> 0% of each run, Pallas kernels for 6% -> 6%
where the time goes in v5:
time: 116 us; the launch traced here: 115 us
  blocking collectives  46.1 us (40%)
  starting transfers between devices  26.7 us (23%)
  Pallas kernels  21.3 us (18%)
  waiting for transfers between devices  17.5 us (15%)
  local copies, waits for them, and re-layouts  1.4 us (1%)
    all_to_all x3, blocking collectives, over_z(): lax.all_to_all(array, 'inner', 0, 0, tiled=True, axis_index_groups=groups)  46.1 us
    ppermute x9, starting transfers between devices, shift_y(): return lax.ppermute(array, 'inner', pairs)  15.3 us
    ppermute x9, waiting for transfers between devices, shift_y(): return lax.ppermute(array, 'inner', pairs)  13.1 us
    ppermute x6, starting transfers between devices, hop(): lax.ppermute(value, 'cols', [(i, (i + 2 * step) % tiles) for i in range(t...  9.79 us
    pallas_call x1, Pallas kernels, body(): pl.pallas_call(functools.partial(ortho_kernel, zs), out_shape=(shape((NB...  6.97 us
    pallas_call x1, Pallas kernels, body(): pl.pallas_call(functools.partial(backward_kernel, outs, slots, zs), out_s...  5.45 us
    ppermute x6, waiting for transfers between devices, hop(): lax.ppermute(value, 'cols', [(i, (i + 2 * step) % tiles) for i in range(t...  4.19 us
    pallas_call x1, Pallas kernels, body(): pl.pallas_call(functools.partial(probe_kernel, outs, slots), out_shape=(s...  3.76 us
  transfers between devices with their start and end apart: 23, of which 13 were waited for; matrix products, arithmetic and copies ran while one was open for 0% of the time, Pallas kernels for 6%

profile of v5, /device:TPU:8, one launch (start us, length us, event | category | flops | bytes accessed | tf_op | source)
XLA Modules:
  0.0 114.5 jit_solution(2258208450129279794)
XLA Ops:
  0.7 1.6 %collective-permute-start = (bf16[1,512,128]{2,1,0:T(8,128)(2,1)}, bf16[1,512,128]{2,1,0:T(8,128)(2,1)S(1)}, u32[]{:S(2)}, u32[]{:S(2)}) collective-permute-start(bf16[1,512,128]{2,1,0:T(8,128)(2,1)} %rest_0_.2), channel_id=1, source_target_pairs={{0,2},{1,3},{2,4},{3,5},{4,6},{5,7},{6,0},{7,1},{8,10},{9,11},{10,... | collective-permute-start | bytes 393224 | tf_op jit(solution)/shard_map/ppermute | solution.py:321
  2.2 1.7 %collective-permute-start.1 = (bf16[1,512,128]{2,1,0:T(8,128)(2,1)}, bf16[1,512,128]{2,1,0:T(8,128)(2,1)S(1)}, u32[]{:S(2)}, u32[]{:S(2)}) collective-permute-start(bf16[1,512,128]{2,1,0:T(8,128)(2,1)} %rest_0_.2), channel_id=1, source_target_pairs={{0,6},{1,7},{2,0},{3,1},{4,2},{5,3},{6,4},{7,5},{8,14},{9,15},{10,... | collective-permute-start | bytes 393224 | tf_op jit(solution)/shard_map/ppermute | solution.py:321
  4.2 3.0 %collective-permute-start.3 = (bf16[1,512,128]{2,1,0:T(8,128)(2,1)}, bf16[1,512,128]{2,1,0:T(8,128)(2,1)S(1)}, u32[]{:S(2)}, u32[]{:S(2)}) collective-permute-start(bf16[1,512,128]{2,1,0:T(8,128)(2,1)} %rest_0_.3), channel_id=1, source_target_pairs={{0,6},{1,7},{2,0},{3,1},{4,2},{5,3},{6,4},{7,5},{8,14},{9,15},{10,... | collective-permute-start | bytes 393224 | tf_op jit(solution)/shard_map/ppermute | solution.py:321
  7.4 1.3 %collective-permute-done.1.rest_2_ = bf16[1,512,128]{2,1,0:T(8,128)(2,1)S(1)} collective-permute-done((bf16[1,512,128]{2,1,0:T(8,128)(2,1)}, bf16[1,512,128]{2,1,0:T(8,128)(2,1)S(1)}, u32[]{:S(2)}, u32[]{:S(2)}) %collective-permute-start.1) | collective-permute-done | bytes 131104 | tf_op jit(solution)/shard_map/ppermute | solution.py:321
  8.7 1.6 %collective-permute-done.2.rest_1_ = bf16[1,512,128]{2,1,0:T(8,128)(2,1)S(1)} collective-permute-done((bf16[1,512,128]{2,1,0:T(8,128)(2,1)}, bf16[1,512,128]{2,1,0:T(8,128)(2,1)S(1)}, u32[]{:S(2)}, u32[]{:S(2)}) %collective-permute-start.2) | collective-permute-done | bytes 131104 | tf_op jit(solution)/shard_map/ppermute | solution.py:321
  10.4 3.2 %collective-permute-start.4 = (bf16[1,512,128]{2,1,0:T(8,128)(2,1)S(1)}, bf16[1,512,128]{2,1,0:T(8,128)(2,1)S(1)}, u32[]{:S(2)}, u32[]{:S(2)}) collective-permute-start(bf16[1,512,128]{2,1,0:T(8,128)(2,1)S(1)} %collective-permute-done.1.rest_2_), channel_id=1, source_target_pairs={{0,6},{1,7},{2,0},{3,1},{4,2},{5,3},{6,4},{7,5},{8,14},{9,15},{10,... | collective-permute-start | bytes 393224 | tf_op jit(solution)/shard_map/ppermute | solution.py:321
  13.6 0.7 copy-done.2
  14.3 0.7 copy-done.4
  15.0 3.8 %probe.1 = (bf16[32,128,256]{2,1,0:T(8,128)(2,1)S(1)}, bf16[32,512,128]{2,1,0:T(8,128)(2,1)S(1)}) custom-call(s32[4,8]{1,0:T(4,128)S(1)} %copy-done.2, s32[4,8]{1,0:T(4,128)S(1)} %copy-done.4, bf16[4,8,512,128]{3,2,1,0:T(8,128)(2,1)} %right_u.1, bf16[4,8,512,128]{3,2,1,0:T(8,128)(2,1)} %right_v.3, bf16[4,512,128]{2,1,0:T(8,128)(2,1)} %sketch.1), custom_call_target="tpu_custom_call" | custom-call | flops 536870912 | bytes 6291456 | tf_op jit(solution)/shard_map/probe/pallas_call | solution.py:354
  18.7 1.0 collective-permute-done.5.rest_3_
  21.6 3.0 %pair.1 = (bf16[32,256,128]{2,1,0:T(8,128)(2,1)S(1)}, bf16[32,128,128]{2,1,0:T(8,128)(2,1)S(1)}) custom-call(s32[4,8]{1,0:T(4,128)S(1)} %copy-done.2, s32[4,8]{1,0:T(4,128)S(1)} %copy-done.4, bf16[32,512,128]{2,1,0:T(8,128)(2,1)S(1)} %get-tuple-element.33.held, bf16[32,128,256]{2,1,0:T(8,128)(2,1)S(1)} %get-tuple-element.39.probes, ...), custom_call_target="tpu_custom_call" | custom-call | flops 939524096 | bytes 10485760 | tf_op jit(solution)/shard_map/pair/pallas_call | solution.py:370
  24.7 2.1 %sketch.2 = (f32[512,128]{1,0:T(8,128)S(1)}, bf16[512,128]{1,0:T(8,128)(2,1)S(1)}, bf16[512,128]{1,0:T(8,128)(2,1)S(1)}, bf16[512,128]{1,0:T(8,128)(2,1)S(1)}, bf16[8,512,128]{2,1,0:T(8,128)(2,1)S(1)}) custom-call(s32[4,8]{1,0:T(4,128)S(1)} %copy-done.2, s32[4,8]{1,0:T(4,128)S(1)} %copy-done.4, bf16[32,128,128]{2,1,0:T(8,128)(2,1)S(1)} %get-tuple-element.43.mixing, ...), custom_call_target="tpu_custom_call" | custom-call | flops 536870912 | bytes 4194304 | tf_op jit(solution)/shard_map/sketch/pallas_call | solution.py:380
  26.8 1.7 %collective-permute-start.14 = (bf16[512,128]{1,0:T(8,128)(2,1)S(1)}, bf16[512,128]{1,0:T(8,128)(2,1)S(1)}, u32[]{:S(2)}, u32[]{:S(2)}) collective-permute-start(bf16[512,128]{1,0:T(8,128)(2,1)S(1)} %get-tuple-element.50), channel_id=1, source_target_pairs={{0,8},{8,16},{16,24},{24,0},{32,40},{40,48},{48,56},{56,32},{64,72... | collective-permute-start | bytes 393224 | tf_op jit(solution)/shard_map/ppermute | solution.py:317
  28.5 2.7 %collective-permute-start.15 = (bf16[512,128]{1,0:T(8,128)(2,1)S(1)}, bf16[512,128]{1,0:T(8,128)(2,1)S(1)}, u32[]{:S(2)}, u32[]{:S(2)}) collective-permute-start(bf16[512,128]{1,0:T(8,128)(2,1)S(1)} %get-tuple-element.51), channel_id=1, source_target_pairs={{0,16},{8,24},{16,0},{24,8},{32,48},{40,56},{48,32},{56,40},{64,80... | collective-permute-start | bytes 393224 | tf_op jit(solution)/shard_map/ppermute | solution.py:317
  31.8 1.6 %collective-permute-done.14 = bf16[512,128]{1,0:T(8,128)(2,1)S(1)} collective-permute-done((bf16[512,128]{1,0:T(8,128)(2,1)S(1)}, bf16[512,128]{1,0:T(8,128)(2,1)S(1)}, u32[]{:S(2)}, u32[]{:S(2)}) %collective-permute-start.14) | collective-permute-done | bytes 131104 | tf_op jit(solution)/shard_map/ppermute | solution.py:317
  33.4 3.0 %collective-permute-done.15 = bf16[512,128]{1,0:T(8,128)(2,1)S(1)} collective-permute-done((bf16[512,128]{1,0:T(8,128)(2,1)S(1)}, bf16[512,128]{1,0:T(8,128)(2,1)S(1)}, u32[]{:S(2)}, u32[]{:S(2)}) %collective-permute-start.15) | collective-permute-done | bytes 131104 | tf_op jit(solution)/shard_map/ppermute | solution.py:317
  36.3 1.8 %collective-permute-done.16 = bf16[512,128]{1,0:T(8,128)(2,1)S(1)} collective-permute-done((bf16[512,128]{1,0:T(8,128)(2,1)S(1)}, bf16[512,128]{1,0:T(8,128)(2,1)S(1)}, u32[]{:S(2)}, u32[]{:S(2)}) %collective-permute-start.16) | collective-permute-done | bytes 131104 | tf_op jit(solution)/shard_map/ppermute | solution.py:317
  38.2 19.9 %all_to_all.15 = f32[8,64,128]{2,1,0:T(8,128)S(1)} all-to-all(f32[8,64,128]{2,1,0:T(8,128)S(1)} %bitcast.1), channel_id=1, replica_groups={{0,32,64,96,128,160,192,224},{8,40,72,104,136,168,200,232},{16,48,80,11..., dimensions={0} | all-to-all | bytes 524288 | tf_op jit(solution)/shard_map/all_to_all | solution.py:330
  58.2 13.2 %all_to_all.16.blocks = f32[8,64,128]{2,1,0:T(8,128)S(1)} all-to-all(f32[8,64,128]{2,1,0:T(8,128)S(1)} %broadcast_in_dim.2), channel_id=1, replica_groups={{0,32,64,96,128,160,192,224},{8,40,72,104,136,168,200,232},{16,48,80,11..., dimensions={0} | all-to-all | bytes 524288 | tf_op jit(solution)/shard_map/all_to_all | solution.py:330
  71.4 7.0 %ortho.1 = (bf16[544,128]{1,0:T(8,128)(2,1)S(1)}, bf16[544,128]{1,0:T(8,128)(2,1)S(1)}, bf16[544,128]{1,0:T(8,128)(2,1)S(1)}, bf16[544,128]{1,0:T(8,128)(2,1)S(1)}) custom-call(f32[8,64,128]{2,1,0:T(8,128)S(1)} %all_to_all.16.blocks), custom_call_target="tpu_custom_call" | custom-call | flops 218103808 | bytes 1048576 | tf_op jit(solution)/shard_map/ortho/pallas_call | solution.py:397
  78.5 3.0 %collective-permute-start.18 = (bf16[544,128]{1,0:T(8,128)(2,1)S(1)}, bf16[544,128]{1,0:T(8,128)(2,1)S(1)}, u32[]{:S(2)}, u32[]{:S(2)}) collective-permute-start(bf16[544,128]{1,0:T(8,128)(2,1)S(1)} %get-tuple-element.55), channel_id=1, source_target_pairs={{0,16},{8,24},{16,0},{24,8},{32,48},{40,56},{48,32},{56,40},{64,80... | collective-permute-start | bytes 417800 | tf_op jit(solution)/shard_map/ppermute | solution.py:317
  81.5 1.3 %collective-permute-start.19 = (bf16[544,128]{1,0:T(8,128)(2,1)S(1)}, bf16[544,128]{1,0:T(8,128)(2,1)S(1)}, u32[]{:S(2)}, u32[]{:S(2)}) collective-permute-start(bf16[544,128]{1,0:T(8,128)(2,1)S(1)} %get-tuple-element.56), channel_id=1, source_target_pairs={{0,24},{8,0},{16,8},{24,16},{32,56},{40,32},{48,40},{56,48},{64,88... | collective-permute-start | bytes 417800 | tf_op jit(solution)/shard_map/ppermute | solution.py:317
  82.8 0.7 collective-permute-done.17.msg1
  83.5 1.6 %collective-permute-done.18.msg2 = bf16[544,128]{1,0:T(8,128)(2,1)S(1)} collective-permute-done((bf16[544,128]{1,0:T(8,128)(2,1)S(1)}, bf16[544,128]{1,0:T(8,128)(2,1)S(1)}, u32[]{:S(2)}, u32[]{:S(2)}) %collective-permute-start.18) | collective-permute-done | bytes 139296 | tf_op jit(solution)/shard_map/ppermute | solution.py:317
  85.1 1.5 %collective-permute-done.19.msg3 = bf16[544,128]{1,0:T(8,128)(2,1)S(1)} collective-permute-done((bf16[544,128]{1,0:T(8,128)(2,1)S(1)}, bf16[544,128]{1,0:T(8,128)(2,1)S(1)}, u32[]{:S(2)}, u32[]{:S(2)}) %collective-permute-start.19) | collective-permute-done | bytes 139296 | tf_op jit(solution)/shard_map/ppermute | solution.py:317
  86.6 5.4 %backward.1 = (f32[8,4,16,128]{3,2,1,0:T(8,128)S(1)}, bf16[8,4,16,128]{3,2,1,0:T(8,128)(2,1)S(1)}, bf16[8,4,16,128]{3,2,1,0:T(8,128)(2,1)S(1)}, bf16[8,4,16,128]{3,2,1,0:T(8,128)(2,1)S(1)}, f32[4,16,128]{2,1,0:T(8,128)}) custom-call(s32[4,8]{1,0:T(4,128)S(1)} %copy-done.3, s32[4,8]{1,0:T(4,128)S(1)} %copy-done.5, bf16[4,8,512,128]{3,2,1,0:T(8,128)(2,1)} %right_v.3, ...), custom_call_target="tpu_custom_call" | custom-call | flops 1476395008 | bytes 8388608 | tf_op jit(solution)/shard_map/backward/pallas_call | solution.py:409
  92.1 1.0 collective-permute-start.20
  93.1 2.7 %collective-permute-start.21 = (bf16[8,4,16,128]{3,2,1,0:T(8,128)(2,1)S(1)}, bf16[8,4,16,128]{3,2,1,0:T(8,128)(2,1)S(1)}, u32[]{:S(2)}, u32[]{:S(2)}) collective-permute-start(bf16[8,4,16,128]{3,2,1,0:T(8,128)(2,1)S(1)} %get-tuple-element.60), channel_id=1, source_target_pairs={{0,16},{8,24},{16,0},{24,8},{32,48},{40,56},{48,32},{56,40},{64,80... | collective-permute-start | bytes 393224 | tf_op jit(solution)/shard_map/ppermute | solution.py:317
  95.8 2.1 %collective-permute-start.22 = (bf16[8,4,16,128]{3,2,1,0:T(8,128)(2,1)S(1)}, bf16[8,4,16,128]{3,2,1,0:T(8,128)(2,1)S(1)}, u32[]{:S(2)}, u32[]{:S(2)}) collective-permute-start(bf16[8,4,16,128]{3,2,1,0:T(8,128)(2,1)S(1)} %get-tuple-element.61), channel_id=1, source_target_pairs={{0,24},{8,0},{16,8},{24,16},{32,56},{40,32},{48,40},{56,48},{64,88... | collective-permute-start | bytes 393224 | tf_op jit(solution)/shard_map/ppermute | solution.py:317
  97.9 1.7 %collective-permute-done.21 = bf16[8,4,16,128]{3,2,1,0:T(8,128)(2,1)S(1)} collective-permute-done((bf16[8,4,16,128]{3,2,1,0:T(8,128)(2,1)S(1)}, bf16[8,4,16,128]{3,2,1,0:T(8,128)(2,1)S(1)}, u32[]{:S(2)}, u32[]{:S(2)}) %collective-permute-start.21) | collective-permute-done | bytes 131104 | tf_op jit(solution)/shard_map/ppermute | solution.py:317
  99.6 1.4 %collective-permute-done.22 = bf16[8,4,16,128]{3,2,1,0:T(8,128)(2,1)S(1)} collective-permute-done((bf16[8,4,16,128]{3,2,1,0:T(8,128)(2,1)S(1)}, bf16[8,4,16,128]{3,2,1,0:T(8,128)(2,1)S(1)}, u32[]{:S(2)}, u32[]{:S(2)}) %collective-permute-start.22) | collective-permute-done | bytes 131104 | tf_op jit(solution)/shard_map/ppermute | solution.py:317
  101.0 12.9 %all_to_all.17 = f32[8,4,16,128]{3,2,1,0:T(8,128)S(1)} all-to-all(f32[8,4,16,128]{3,2,1,0:T(8,128)S(1)} %convert_add_fusion), channel_id=1, replica_groups={{0,32,64,96,128,160,192,224},{8,40,72,104,136,168,200,232},{16,48,80,11..., dimensions={0} | all-to-all | bytes 524288 | tf_op jit(solution)/shard_map/all_to_all | solution.py:330
  (39 shorter events, 3.9 us)
Async XLA Ops:
  0.6 21.0 %copy-start = (bf16[1,512,128]{2,1,0:T(8,128)(2,1)S(1)}, bf16[1,512,128]{2,1,0:T(8,128)(2,1)}, u32[]{:S(2)}) copy-start(bf16[1,512,128]{2,1,0:T(8,128)(2,1)} %rest_0_.2) | copy-start | bytes 393220
  0.6 19.6 %copy-start.1 = (bf16[1,512,128]{2,1,0:T(8,128)(2,1)S(1)}, bf16[1,512,128]{2,1,0:T(8,128)(2,1)}, u32[]{:S(2)}) copy-start(bf16[1,512,128]{2,1,0:T(8,128)(2,1)} %rest_0_.3) | copy-start | bytes 393220
  0.7 6.8 %collective-permute-start = (bf16[1,512,128]{2,1,0:T(8,128)(2,1)}, bf16[1,512,128]{2,1,0:T(8,128)(2,1)S(1)}, u32[]{:S(2)}, u32[]{:S(2)}) collective-permute-start(bf16[1,512,128]{2,1,0:T(8,128)(2,1)} %rest_0_.2), channel_id=1, source_target_pairs={{0,2},{1,3},{2,4},{3,5},{4,6},{5,7},{6,0},{7,1},{8,10},{9,11},{10,... | collective-permute-start | bytes 393224 | tf_op jit(solution)/shard_map/ppermute | solution.py:321
  2.2 6.5 %collective-permute-start.1 = (bf16[1,512,128]{2,1,0:T(8,128)(2,1)}, bf16[1,512,128]{2,1,0:T(8,128)(2,1)S(1)}, u32[]{:S(2)}, u32[]{:S(2)}) collective-permute-start(bf16[1,512,128]{2,1,0:T(8,128)(2,1)} %rest_0_.2), channel_id=1, source_target_pairs={{0,6},{1,7},{2,0},{3,1},{4,2},{5,3},{6,4},{7,5},{8,14},{9,15},{10,... | collective-permute-start | bytes 393224 | tf_op jit(solution)/shard_map/ppermute | solution.py:321
  4.0 6.4 %collective-permute-start.2 = (bf16[1,512,128]{2,1,0:T(8,128)(2,1)}, bf16[1,512,128]{2,1,0:T(8,128)(2,1)S(1)}, u32[]{:S(2)}, u32[]{:S(2)}) collective-permute-start(bf16[1,512,128]{2,1,0:T(8,128)(2,1)} %rest_0_.3), channel_id=1, source_target_pairs={{0,2},{1,3},{2,4},{3,5},{4,6},{5,7},{6,0},{7,1},{8,10},{9,11},{10,... | collective-permute-start | bytes 393224 | tf_op jit(solution)/shard_map/ppermute | solution.py:321
  4.2 6.1 %collective-permute-start.3 = (bf16[1,512,128]{2,1,0:T(8,128)(2,1)}, bf16[1,512,128]{2,1,0:T(8,128)(2,1)S(1)}, u32[]{:S(2)}, u32[]{:S(2)}) collective-permute-start(bf16[1,512,128]{2,1,0:T(8,128)(2,1)} %rest_0_.3), channel_id=1, source_target_pairs={{0,6},{1,7},{2,0},{3,1},{4,2},{5,3},{6,4},{7,5},{8,14},{9,15},{10,... | collective-permute-start | bytes 393224 | tf_op jit(solution)/shard_map/ppermute | solution.py:321
  10.4 8.4 %collective-permute-start.4 = (bf16[1,512,128]{2,1,0:T(8,128)(2,1)S(1)}, bf16[1,512,128]{2,1,0:T(8,128)(2,1)S(1)}, u32[]{:S(2)}, u32[]{:S(2)}) collective-permute-start(bf16[1,512,128]{2,1,0:T(8,128)(2,1)S(1)} %collective-permute-done.1.rest_2_), channel_id=1, source_target_pairs={{0,6},{1,7},{2,0},{3,1},{4,2},{5,3},{6,4},{7,5},{8,14},{9,15},{10,... | collective-permute-start | bytes 393224 | tf_op jit(solution)/shard_map/ppermute | solution.py:321
  13.6 6.2 %collective-permute-start.5 = (bf16[1,512,128]{2,1,0:T(8,128)(2,1)S(1)}, bf16[1,512,128]{2,1,0:T(8,128)(2,1)S(1)}, u32[]{:S(2)}, u32[]{:S(2)}) collective-permute-start(bf16[1,512,128]{2,1,0:T(8,128)(2,1)S(1)} %collective-permute-done.2.rest_1_), channel_id=1, source_target_pairs={{0,2},{1,3},{2,4},{3,5},{4,6},{5,7},{6,0},{7,1},{8,10},{9,11},{10,... | collective-permute-start | bytes 393224 | tf_op jit(solution)/shard_map/ppermute | solution.py:321
  13.6 7.2 %collective-permute-start.6 = (bf16[1,512,128]{2,1,0:T(8,128)(2,1)}, bf16[1,512,128]{2,1,0:T(8,128)(2,1)S(1)}, u32[]{:S(2)}, u32[]{:S(2)}) collective-permute-start(bf16[1,512,128]{2,1,0:T(8,128)(2,1)} %rest_0_.2), channel_id=1, source_target_pairs={{0,1},{1,0},{2,3},{3,2},{4,5},{5,4},{6,7},{7,6},{8,9},{9,8},{10,11... | collective-permute-start | bytes 393224 | tf_op jit(solution)/shard_map/ppermute | solution.py:325
  13.6 0.7 copy-start.2
  14.3 0.7 copy-start.4
  19.8 1.3 %collective-permute-start.7 = (bf16[1,512,128]{2,1,0:T(8,128)(2,1)S(1)}, bf16[1,512,128]{2,1,0:T(8,128)(2,1)S(1)}, u32[]{:S(2)}, u32[]{:S(2)}) collective-permute-start(bf16[1,512,128]{2,1,0:T(8,128)(2,1)S(1)} %collective-permute-done.rest_1_), channel_id=1, source_target_pairs={{0,1},{1,0},{2,3},{3,2},{4,5},{5,4},{6,7},{7,6},{8,9},{9,8},{10,11... | collective-permute-start | bytes 393224 | tf_op jit(solution)/shard_map/ppermute | solution.py:325
  19.8 1.5 %collective-permute-start.8 = (bf16[1,512,128]{2,1,0:T(8,128)(2,1)S(1)}, bf16[1,512,128]{2,1,0:T(8,128)(2,1)S(1)}, u32[]{:S(2)}, u32[]{:S(2)}) collective-permute-start(bf16[1,512,128]{2,1,0:T(8,128)(2,1)S(1)} %collective-permute-done.1.rest_2_), channel_id=1, source_target_pairs={{0,1},{1,0},{2,3},{3,2},{4,5},{5,4},{6,7},{7,6},{8,9},{9,8},{10,11... | collective-permute-start | bytes 393224 | tf_op jit(solution)/shard_map/ppermute | solution.py:325
  20.3 1.4 %collective-permute-start.9 = (bf16[1,512,128]{2,1,0:T(8,128)(2,1)S(1)}, bf16[1,512,128]{2,1,0:T(8,128)(2,1)S(1)}, u32[]{:S(2)}, u32[]{:S(2)}) collective-permute-start(bf16[1,512,128]{2,1,0:T(8,128)(2,1)S(1)} %collective-permute-done.4.rest_3_), channel_id=1, source_target_pairs={{0,1},{1,0},{2,3},{3,2},{4,5},{5,4},{6,7},{7,6},{8,9},{9,8},{10,11... | collective-permute-start | bytes 393224 | tf_op jit(solution)/shard_map/ppermute | solution.py:325
  20.3 4.4 %collective-permute-start.10 = (bf16[1,512,128]{2,1,0:T(8,128)(2,1)S(1)}, bf16[1,512,128]{2,1,0:T(8,128)(2,1)S(1)}, u32[]{:S(2)}, u32[]{:S(2)}) collective-permute-start(bf16[1,512,128]{2,1,0:T(8,128)(2,1)S(1)} %copy-done.1), channel_id=1, source_target_pairs={{0,1},{1,0},{2,3},{3,2},{4,5},{5,4},{6,7},{7,6},{8,9},{9,8},{10,11... | collective-permute-start | bytes 393224 | tf_op jit(solution)/shard_map/ppermute | solution.py:325
  20.8 3.9 %collective-permute-start.11 = (bf16[1,512,128]{2,1,0:T(8,128)(2,1)S(1)}, bf16[1,512,128]{2,1,0:T(8,128)(2,1)S(1)}, u32[]{:S(2)}, u32[]{:S(2)}) collective-permute-start(bf16[1,512,128]{2,1,0:T(8,128)(2,1)S(1)} %collective-permute-done.2.rest_1_), channel_id=1, source_target_pairs={{0,1},{1,0},{2,3},{3,2},{4,5},{5,4},{6,7},{7,6},{8,9},{9,8},{10,11... | collective-permute-start | bytes 393224 | tf_op jit(solution)/shard_map/ppermute | solution.py:325
  21.1 3.6 %collective-permute-start.12 = (bf16[1,512,128]{2,1,0:T(8,128)(2,1)S(1)}, bf16[1,512,128]{2,1,0:T(8,128)(2,1)S(1)}, u32[]{:S(2)}, u32[]{:S(2)}) collective-permute-start(bf16[1,512,128]{2,1,0:T(8,128)(2,1)S(1)} %collective-permute-done.3.rest_2_), channel_id=1, source_target_pairs={{0,1},{1,0},{2,3},{3,2},{4,5},{5,4},{6,7},{7,6},{8,9},{9,8},{10,11... | collective-permute-start | bytes 393224 | tf_op jit(solution)/shard_map/ppermute | solution.py:325
  21.3 3.4 %collective-permute-start.13 = (bf16[1,512,128]{2,1,0:T(8,128)(2,1)S(1)}, bf16[1,512,128]{2,1,0:T(8,128)(2,1)S(1)}, u32[]{:S(2)}, u32[]{:S(2)}) collective-permute-start(bf16[1,512,128]{2,1,0:T(8,128)(2,1)S(1)} %collective-permute-done.5.rest_3_), channel_id=1, source_target_pairs={{0,1},{1,0},{2,3},{3,2},{4,5},{5,4},{6,7},{7,6},{8,9},{9,8},{10,11... | collective-permute-start | bytes 393224 | tf_op jit(solution)/shard_map/ppermute | solution.py:325
  24.6 62.0 %copy-start.3 = (s32[4,8]{1,0:T(4,128)S(1)}, s32[4,8]{1,0:T(4,128)}, u32[]{:S(2)}) copy-start(s32[4,8]{1,0:T(4,128)} %index.7) | copy-start | bytes 388
  24.6 62.0 %copy-start.5 = (s32[4,8]{1,0:T(4,128)S(1)}, s32[4,8]{1,0:T(4,128)}, u32[]{:S(2)}) copy-start(s32[4,8]{1,0:T(4,128)} %mask.7) | copy-start | bytes 388
  26.8 6.6 %collective-permute-start.14 = (bf16[512,128]{1,0:T(8,128)(2,1)S(1)}, bf16[512,128]{1,0:T(8,128)(2,1)S(1)}, u32[]{:S(2)}, u32[]{:S(2)}) collective-permute-start(bf16[512,128]{1,0:T(8,128)(2,1)S(1)} %get-tuple-element.50), channel_id=1, source_target_pairs={{0,8},{8,16},{16,24},{24,0},{32,40},{40,48},{48,56},{56,32},{64,72... | collective-permute-start | bytes 393224 | tf_op jit(solution)/shard_map/ppermute | solution.py:317
  28.5 7.9 %collective-permute-start.15 = (bf16[512,128]{1,0:T(8,128)(2,1)S(1)}, bf16[512,128]{1,0:T(8,128)(2,1)S(1)}, u32[]{:S(2)}, u32[]{:S(2)}) collective-permute-start(bf16[512,128]{1,0:T(8,128)(2,1)S(1)} %get-tuple-element.51), channel_id=1, source_target_pairs={{0,16},{8,24},{16,0},{24,8},{32,48},{40,56},{48,32},{56,40},{64,80... | collective-permute-start | bytes 393224 | tf_op jit(solution)/shard_map/ppermute | solution.py:317
  31.2 6.9 %collective-permute-start.16 = (bf16[512,128]{1,0:T(8,128)(2,1)S(1)}, bf16[512,128]{1,0:T(8,128)(2,1)S(1)}, u32[]{:S(2)}, u32[]{:S(2)}) collective-permute-start(bf16[512,128]{1,0:T(8,128)(2,1)S(1)} %get-tuple-element.52), channel_id=1, source_target_pairs={{0,24},{8,0},{16,8},{24,16},{32,56},{40,32},{48,40},{56,48},{64,88... | collective-permute-start | bytes 393224 | tf_op jit(solution)/shard_map/ppermute | solution.py:317
  78.4 5.1 %collective-permute-start.17 = (bf16[544,128]{1,0:T(8,128)(2,1)S(1)}, bf16[544,128]{1,0:T(8,128)(2,1)S(1)}, u32[]{:S(2)}, u32[]{:S(2)}) collective-permute-start(bf16[544,128]{1,0:T(8,128)(2,1)S(1)} %get-tuple-element.54), channel_id=1, source_target_pairs={{0,8},{8,16},{16,24},{24,0},{32,40},{40,48},{48,56},{56,32},{64,72... | collective-permute-start | bytes 417800 | tf_op jit(solution)/shard_map/ppermute | solution.py:317
  78.5 6.7 %collective-permute-start.18 = (bf16[544,128]{1,0:T(8,128)(2,1)S(1)}, bf16[544,128]{1,0:T(8,128)(2,1)S(1)}, u32[]{:S(2)}, u32[]{:S(2)}) collective-permute-start(bf16[544,128]{1,0:T(8,128)(2,1)S(1)} %get-tuple-element.55), channel_id=1, source_target_pairs={{0,16},{8,24},{16,0},{24,8},{32,48},{40,56},{48,32},{56,40},{64,80... | collective-permute-start | bytes 417800 | tf_op jit(solution)/shard_map/ppermute | solution.py:317
  81.5 5.1 %collective-permute-start.19 = (bf16[544,128]{1,0:T(8,128)(2,1)S(1)}, bf16[544,128]{1,0:T(8,128)(2,1)S(1)}, u32[]{:S(2)}, u32[]{:S(2)}) collective-permute-start(bf16[544,128]{1,0:T(8,128)(2,1)S(1)} %get-tuple-element.56), channel_id=1, source_target_pairs={{0,24},{8,0},{16,8},{24,16},{32,56},{40,32},{48,40},{56,48},{64,88... | collective-permute-start | bytes 417800 | tf_op jit(solution)/shard_map/ppermute | solution.py:317
  92.1 5.8 %collective-permute-start.20 = (bf16[8,4,16,128]{3,2,1,0:T(8,128)(2,1)S(1)}, bf16[8,4,16,128]{3,2,1,0:T(8,128)(2,1)S(1)}, u32[]{:S(2)}, u32[]{:S(2)}) collective-permute-start(bf16[8,4,16,128]{3,2,1,0:T(8,128)(2,1)S(1)} %get-tuple-element.59), channel_id=1, source_target_pairs={{0,8},{8,16},{16,24},{24,0},{32,40},{40,48},{48,56},{56,32},{64,72... | collective-permute-start | bytes 393224 | tf_op jit(solution)/shard_map/ppermute | solution.py:317
  93.1 6.5 %collective-permute-start.21 = (bf16[8,4,16,128]{3,2,1,0:T(8,128)(2,1)S(1)}, bf16[8,4,16,128]{3,2,1,0:T(8,128)(2,1)S(1)}, u32[]{:S(2)}, u32[]{:S(2)}) collective-permute-start(bf16[8,4,16,128]{3,2,1,0:T(8,128)(2,1)S(1)} %get-tuple-element.60), channel_id=1, source_target_pairs={{0,16},{8,24},{16,0},{24,8},{32,48},{40,56},{48,32},{56,40},{64,80... | collective-permute-start | bytes 393224 | tf_op jit(solution)/shard_map/ppermute | solution.py:317
  95.8 5.2 %collective-permute-start.22 = (bf16[8,4,16,128]{3,2,1,0:T(8,128)(2,1)S(1)}, bf16[8,4,16,128]{3,2,1,0:T(8,128)(2,1)S(1)}, u32[]{:S(2)}, u32[]{:S(2)}) collective-permute-start(bf16[8,4,16,128]{3,2,1,0:T(8,128)(2,1)S(1)} %get-tuple-element.61), channel_id=1, source_target_pairs={{0,24},{8,0},{16,8},{24,16},{32,56},{40,32},{48,40},{56,48},{64,88... | collective-permute-start | bytes 393224 | tf_op jit(solution)/shard_map/ppermute | solution.py:317

commit v6 on v5

--- a/solution.py
+++ b/solution.py
@@ -46,18 +46,16 @@
     return pl.BlockSpec(memory_space=pltpu.SMEM)
 
 
-def live(meta, j):
-    mask = meta[1]
-    count = mask[j, 0]
-    for s in range(1, mask.shape[1]):
-        count += mask[j, s]
+def live(packed, j):
+    count = packed[j, 0] & 1
+    for s in range(1, packed.shape[1]):
+        count += packed[j, s] & 1
     return count
 
 
-def tile_of(meta, at):
-    index = meta[0]
-    slots = index.shape[1]
-    return index[lax.div(at, slots), lax.rem(at, slots)] - lax.axis_index("inner") * lax.axis_size("cols")
+def tile_of(packed, at):
+    slots = packed.shape[1]
+    return packed[lax.div(at, slots), lax.rem(at, slots)] >> 1
 
 
 def y_of():
@@ -94,8 +92,7 @@
     return [j * slots + jnp.minimum(base + i, count - 1) for i in range(BATCH)]
 
 
-def probe_kernel(outs, slots, index, mask, right_u, right_v, sketch, probes, held_u, held, plain, sems_u, sems, sem):
-    meta = index, mask
+def probe_kernel(outs, slots, meta, right_u, right_v, sketch, probes, held_u, held, plain, sems_u, sems, sem):
     copy = pltpu.make_async_copy(sketch, plain, sem)
     copy.start()
     fetch(meta, outs, slots, right_v, held, sems)
@@ -129,8 +126,7 @@
     return [lax.rem(me + 2 * hop, tiles) ^ flip for flip in (0, 1) for hop in (0, tiles // 2 - 1, 1, 2)]
 
 
-def pair_kernel(outs, slots, index, mask, held, probes, *rest):
-    meta = index, mask
+def pair_kernel(outs, slots, meta, held, probes, *rest):
     parts, (pairs, mixing, turned) = rest[:-3], rest[-3:]
     for k, part in zip(tile_ids(len(parts)), parts):
         turned[k] = part[0].T
@@ -157,8 +153,7 @@
     lax.fori_loop(0, outs, tile, 0)
 
 
-def sketch_kernel(outs, slots, index, mask, mixing, *rest):
-    meta = index, mask
+def sketch_kernel(outs, slots, meta, mixing, *rest):
     parts, (own, send1, send2, send3, group, acc) = rest[:-6], rest[-6:]
     for k, part in zip(tile_ids(len(parts)), parts):
         group[k] = part[0]
@@ -266,50 +261,80 @@
         msg[NB + rows:] = low
 
 
-def backward_kernel(outs, slots, zs, index, mask, right_v, group, pairs, msg0, msg1, msg2, msg3,
-                    own, send1, send2, send3, basis, held, turned, acc, sems):
-    meta = index, mask
+def backward_tile(slots, meta, j, mine, group, pairs, held, acc, ready):
+    count = live(meta, j)
+    acc[...] = jnp.zeros_like(acc)
+
+    def batch(first, _):
+        base = first * BATCH
+        ready(count, base)
+        at = slots_of(j, base, slots, count)
+        products = [halves(dot(mine, group[tile_of(meta, slot)])) for slot in at]
+        backs = []
+        for i in range(BATCH):
+            high, low = products[i]
+            pair = pairs[at[i]]
+            back = dot(high, pair[:R]) + dot(high, pair[R:]) + dot(low, pair[:R])
+            backs.append(jnp.where(base + i < count, back, 0.0).astype(BF))
+        terms = [
+            dot_nt(beside(held[at[i]], held[at[i + 1]]), beside(backs[i], backs[i + 1])) for i in range(0, BATCH, 2)
+        ]
+        acc[...] += terms[0] + terms[1]
+        return 0
+
+    lax.fori_loop(0, (count + BATCH - 1) // BATCH, batch, 0)
+
+
+def backward_own_kernel(outs, slots, meta, right_v, group, pairs, msg, mine, held, sems):
     fetch(meta, outs, slots, right_v, held, sems)
+    y = y_of()
+
+    def ready(count, base):
+        for i in range(BATCH):
+            arrive(count, slots, y, base + i, right_v, held, sems)
+
+    backward_tile(slots, meta, y, msg[:NB].T, group, pairs, held, mine, ready)
+
+    def tile(order, _):
+        j = lax.rem(y + order, YS)
+
+        def one(s, _):
+            pltpu.make_async_copy(right_v.at[j, s], held.at[j * slots + s], sems.at[j * slots + s]).wait()
+            return 0
+
+        lax.fori_loop(0, live(meta, j), one, 0)
+        return 0
+
+    lax.fori_loop(1, YS, tile, 0)
+
+
+def backward_kernel(slots, zs, meta, held, group, pairs, mine, msg0, msg1, msg2, msg3,
+                    own, send1, send2, send3, basis, turned, acc):
     y = y_of()
     rows = NB // (zs * YS)
     for step, msg in enumerate((msg0, msg1, msg2, msg3)):
         j = lax.rem(y + YS - step, YS)
-        turned[j] = msg[:NB].T
+        if step:
+            turned[step] = msg[:NB].T
         kept = msg[NB:NB + rows].astype(F32) + msg[NB + rows:].astype(F32)
         basis[j] = kept * math.sqrt(NB)
 
-    def tile(j, _):
-        count = live(meta, j)
-        acc[...] = jnp.zeros_like(acc)
-
-        def batch(first, _):
-            base = first * BATCH
-            for i in range(BATCH):
-                arrive(count, slots, j, base + i, right_v, held, sems)
-            at = slots_of(j, base, slots, count)
-            mine = turned[j]
-            products = [halves(dot(mine, group[tile_of(meta, slot)])) for slot in at]
-            backs = []
-            for i in range(BATCH):
-                high, low = products[i]
-                pair = pairs[at[i]]
-                back = dot(high, pair[:R]) + dot(high, pair[R:]) + dot(low, pair[:R])
-                backs.append(jnp.where(base + i < count, back, 0.0).astype(BF))
-            terms = [
-                dot_nt(beside(held[at[i]], held[at[i + 1]]), beside(backs[i], backs[i + 1])) for i in range(0, BATCH, 2)
-            ]
-            acc[...] += terms[0] + terms[1]
-            return 0
-
-        lax.fori_loop(0, (count + BATCH - 1) // BATCH, batch, 0)
+    def write(j, source):
         for step, out in enumerate((own, send1, send2, send3)):
             there = lax.rem(y + step, YS)
             for block in range(zs):
                 start = pl.multiple_of((block * YS + there) * rows, rows)
-                out[block, j] = acc[pl.ds(start, rows)].astype(out.dtype)
-        return 0
-
-    lax.fori_loop(0, outs, tile, 0)
+                out[block, j] = source[pl.ds(start, rows)].astype(out.dtype)
+
+    write(y, mine)
+
+    def tile(step, _):
+        j = lax.rem(y + YS - step, YS)
+        backward_tile(slots, meta, j, turned[step], group, pairs, held, acc, lambda count, base: None)
+        write(j, acc)
+        return 0
+
+    lax.fori_loop(1, YS, tile, 0)
 
 
 def shift_y(array, step, zs):
@@ -340,6 +365,7 @@
     tiles = lax.axis_size("cols")
     shape = jax.ShapeDtypeStruct
     count = outs * slots
+    packed = (tile_index - lax.axis_index("inner") * tiles) * 2 + slot_mask
     right_u = pltpu.with_memory_space_constraint(right_u, pltpu.HBM)
     right_v = pltpu.with_memory_space_constraint(right_v, pltpu.HBM)
     unit = 2 * NB * R * R
@@ -348,45 +374,49 @@
         return pl.CostEstimate(flops=int(units * unit), bytes_accessed=mib << 20, transcendentals=0)
 
     near = [hop(value, step, tiles) for value in (left_v, left_u) for step in (1, -1)]
-    *near, sketch = lax.optimization_barrier((*near, sketch))
-    far_v, far_u = hop(near[1], -1, tiles), hop(near[2], 1, tiles)
+    near_v, near_u = near[:2], near[2:]
+    *near_v, sketch, packed = lax.optimization_barrier((*near_v, sketch, packed))
+    far_v = hop(near_v[1], -1, tiles)
     sketch = pltpu.with_memory_space_constraint(sketch, pltpu.HBM)
     probes, held_u = pl.pallas_call(
         functools.partial(probe_kernel, outs, slots),
         out_shape=(shape((count, R, 2 * R), BF),) + (shape((count, NB, R), BF),),
-        in_specs=[in_smem(), in_smem(), in_place(), in_place(), in_place()],
+        in_specs=[in_smem(), in_place(), in_place(), in_place()],
         out_specs=(in_vmem(),) * 2,
         scratch_shapes=[VMEM((count, NB, R), BF), VMEM((outs, NB, R), BF)]
         + [pltpu.SemaphoreType.DMA((count,))] * 2 + [pltpu.SemaphoreType.DMA],
         compiler_params=params(),
         cost_estimate=cost(outs * slots, 6),
         name="probe",
-    )(tile_index, slot_mask, right_u, right_v, sketch)
-    *near, far_v, far_u, probes = lax.optimization_barrier((*near, far_v, far_u, probes))
-    group_v = [left_v, *near[:2], far_v]
+    )(packed, right_u, right_v, sketch)
+    *near_u, far_v, probes = lax.optimization_barrier((*near_u, far_v, probes))
+    far_u = hop(near_u[0], 1, tiles)
+    group_v = [left_v, *near_v, far_v]
     group_v += [swap(value, tiles) for value in group_v]
-    group_u = [left_u, *near[2:], far_u]
-    group_u += [swap(value, tiles) for value in group_u]
+    group_u = [left_u, *near_u]
+    other_u = [swap(value, tiles) for value in group_u]
     pairs, mixing = pl.pallas_call(
         functools.partial(pair_kernel, outs, slots),
         out_shape=(shape((count, 2 * R, R), BF), shape((count, R, R), BF)),
-        in_specs=[in_smem(), in_smem()] + [in_vmem()] * (2 + tiles),
+        in_specs=[in_smem()] + [in_vmem()] * (2 + tiles),
         out_specs=(in_vmem(),) * 2,
         scratch_shapes=[VMEM((tiles, R, NB), BF)],
         compiler_params=params(),
         cost_estimate=cost(outs * slots * 1.75, 10),
         name="pair",
-    )(tile_index, slot_mask, held_u, probes, *group_v)
+    )(packed, held_u, probes, *group_v)
+    far_u, mixing = lax.optimization_barrier((far_u, mixing))
+    group_u += [far_u, *other_u, swap(far_u, tiles)]
     own, send1, send2, send3, group = pl.pallas_call(
         functools.partial(sketch_kernel, outs, slots),
         out_shape=(shape((NB, R), F32),) + (shape((NB, R), BF),) * 3 + (shape((tiles, NB, R), BF),),
-        in_specs=[in_smem(), in_smem()] + [in_vmem()] * (1 + tiles),
+        in_specs=[in_smem()] + [in_vmem()] * (1 + tiles),
         out_specs=(in_vmem(),) * 5,
         scratch_shapes=[VMEM((NB, R), F32)],
         compiler_params=params(),
         cost_estimate=cost(outs * slots, 4),
         name="sketch",
-    )(tile_index, slot_mask, mixing, *group_u)
+    )(packed, mixing, *group_u)
     total = own
     for step, send in enumerate((send1, send2, send3)):
         total = total + shift_y(send, step + 1, zs).astype(F32)
@@ -404,20 +434,28 @@
         cost_estimate=cost(13, 1),
         name="ortho",
     )(summed)
+    mine, held_v = pl.pallas_call(
+        functools.partial(backward_own_kernel, outs, slots),
+        out_shape=(shape((NB, R), F32), shape((count, NB, R), BF)),
+        in_specs=[in_smem(), in_place()] + [in_vmem()] * 3,
+        out_specs=(in_vmem(),) * 2,
+        scratch_shapes=[pltpu.SemaphoreType.DMA((count,))],
+        compiler_params=params(),
+        cost_estimate=cost(slots * 2.75, 4),
+        name="backward_own",
+    )(packed, right_v, group, pairs, messages[0])
     messages = [shift_y(message, step, zs) if step else message for step, message in enumerate(messages)]
     pieces = (zs, outs, out_rows, R)
     own, send1, send2, send3, basis = pl.pallas_call(
-        functools.partial(backward_kernel, outs, slots, zs),
+        functools.partial(backward_kernel, slots, zs),
         out_shape=(shape(pieces, F32),) + (shape(pieces, BF),) * 3 + (shape((outs, out_rows, R), F32),),
-        in_specs=[in_smem(), in_smem(), in_place()] + [in_vmem()] * (2 + YS),
+        in_specs=[in_smem()] + [in_vmem()] * (4 + YS),
         out_specs=(in_vmem(),) * 5,
-        scratch_shapes=[
-            VMEM((count, NB, R), BF), VMEM((outs, R, NB), BF), VMEM((NB, R), F32), pltpu.SemaphoreType.DMA((count,)),
-        ],
-        compiler_params=params(),
-        cost_estimate=cost(outs * slots * 2.75, 8),
+        scratch_shapes=[VMEM((outs, R, NB), BF), VMEM((NB, R), F32)],
+        compiler_params=params(),
+        cost_estimate=cost(outs * slots * 2, 8),
         name="backward",
-    )(tile_index, slot_mask, right_v, group, pairs, *messages)
+    )(packed, held_v, group, pairs, mine, *messages)
     part = own
     for step, send in enumerate((send1, send2, send3)):
         part = part + shift_y(send, step + 1, zs).astype(F32)

time: 116 us -> 113 us (0.974)
  blocking collectives: 46.1 us -> 44.2 us
  other arithmetic: 0.77 us -> 2.43 us
  starting transfers between devices: 26.7 us -> 25.3 us
  local copies, waits for them, and re-layouts: 1.4 us -> 0.03 us
    all_to_all x3, blocking collectives: 46.1 us -> 44.2 us  [over_z(): lax.all_to_all(array, 'inner', 0, 0, tiled=True, axis_index_groups=groups)]
    unnamed x12 -> x4, local copies, waits for them, and re-layouts: 1.38 us -> 0.01 us
    pallas_call x1 -> x2, Pallas kernels: 5.45 us -> 6.26 us  [the longest x1 3.61 us: body(): pl.pallas_call(functools.partial(backward_kernel, slots, zs), out_shape=(...]
  transfers between devices with their start and end apart: 23 -> 23, of which waited for: 13 -> 11; matrix products, arithmetic and copies ran while one was open for 0% -> 1% of each run, Pallas kernels for 6% -> 8%
where the time goes in v6:
time: 113 us; the launch traced here: 112 us
  blocking collectives  44.2 us (39%)
  starting transfers between devices  25.3 us (22%)
  Pallas kernels  22.1 us (20%)
  waiting for transfers between devices  16.8 us (15%)
  other arithmetic  2.43 us (2%)
    all_to_all x3, blocking collectives, over_z(): lax.all_to_all(array, 'inner', 0, 0, tiled=True, axis_index_groups=groups)  44.2 us
    ppermute x9, starting transfers between devices, shift_y(): return lax.ppermute(array, 'inner', pairs)  14.5 us
    ppermute x9, waiting for transfers between devices, shift_y(): return lax.ppermute(array, 'inner', pairs)  12.2 us
    ppermute x6, starting transfers between devices, hop(): lax.ppermute(value, 'cols', [(i, (i + 2 * step) % tiles) for i in range(t...  9.08 us
    pallas_call x1, Pallas kernels, body(): pl.pallas_call(functools.partial(ortho_kernel, zs), out_shape=(shape((NB...  6.97 us
    pallas_call x1, Pallas kernels, body(): pl.pallas_call(functools.partial(probe_kernel, outs, slots), out_shape=(s...  3.73 us
    pallas_call x1, Pallas kernels, body(): pl.pallas_call(functools.partial(backward_kernel, slots, zs), out_shape=(...  3.61 us
    ppermute x6, waiting for transfers between devices, hop(): lax.ppermute(value, 'cols', [(i, (i + 2 * step) % tiles) for i in range(t...  3.25 us
  transfers between devices with their start and end apart: 23, of which 11 were waited for; matrix products, arithmetic and copies ran while one was open for 1% of the time, Pallas kernels for 8%

profile of v6, /device:TPU:8, one launch (start us, length us, event | category | flops | bytes accessed | tf_op | source)
XLA Modules:
  0.0 111.6 jit_solution(1796379552780499706)
XLA Ops:
  0.6 1.6 %collective-permute-start = (bf16[1,512,128]{2,1,0:T(8,128)(2,1)}, bf16[1,512,128]{2,1,0:T(8,128)(2,1)S(1)}, u32[]{:S(2)}, u32[]{:S(2)}) collective-permute-start(bf16[1,512,128]{2,1,0:T(8,128)(2,1)} %rest_0_.2), channel_id=1, source_target_pairs={{0,2},{1,3},{2,4},{3,5},{4,6},{5,7},{6,0},{7,1},{8,10},{9,11},{10,... | collective-permute-start | bytes 393224 | tf_op jit(solution)/shard_map/ppermute | solution.py:346
  2.2 1.7 %collective-permute-start.1 = (bf16[1,512,128]{2,1,0:T(8,128)(2,1)}, bf16[1,512,128]{2,1,0:T(8,128)(2,1)S(1)}, u32[]{:S(2)}, u32[]{:S(2)}) collective-permute-start(bf16[1,512,128]{2,1,0:T(8,128)(2,1)} %rest_0_.2), channel_id=1, source_target_pairs={{0,6},{1,7},{2,0},{3,1},{4,2},{5,3},{6,4},{7,5},{8,14},{9,15},{10,... | collective-permute-start | bytes 393224 | tf_op jit(solution)/shard_map/ppermute | solution.py:346
  4.2 3.0 %collective-permute-start.3 = (bf16[1,512,128]{2,1,0:T(8,128)(2,1)}, bf16[1,512,128]{2,1,0:T(8,128)(2,1)S(1)}, u32[]{:S(2)}, u32[]{:S(2)}) collective-permute-start(bf16[1,512,128]{2,1,0:T(8,128)(2,1)} %rest_0_.3), channel_id=1, source_target_pairs={{0,6},{1,7},{2,0},{3,1},{4,2},{5,3},{6,4},{7,5},{8,14},{9,15},{10,... | collective-permute-start | bytes 393224 | tf_op jit(solution)/shard_map/ppermute | solution.py:346
  7.2 0.7 multiply_add_fusion.meta
  7.9 0.8 collective-permute-done.1.rest_2_
  8.7 1.7 %collective-permute-start.4 = (bf16[1,512,128]{2,1,0:T(8,128)(2,1)S(1)}, bf16[1,512,128]{2,1,0:T(8,128)(2,1)S(1)}, u32[]{:S(2)}, u32[]{:S(2)}) collective-permute-start(bf16[1,512,128]{2,1,0:T(8,128)(2,1)S(1)} %collective-permute-done.1.rest_2_), channel_id=1, source_target_pairs={{0,6},{1,7},{2,0},{3,1},{4,2},{5,3},{6,4},{7,5},{8,14},{9,15},{10,... | collective-permute-start | bytes 393224 | tf_op jit(solution)/shard_map/ppermute | solution.py:346
  10.9 3.7 %probe.1 = (bf16[32,128,256]{2,1,0:T(8,128)(2,1)S(1)}, bf16[32,512,128]{2,1,0:T(8,128)(2,1)S(1)}) custom-call(s32[4,8]{1,0:T(4,128)S(1)} %multiply_add_fusion.meta, bf16[4,8,512,128]{3,2,1,0:T(8,128)(2,1)} %right_u.1, bf16[4,8,512,128]{3,2,1,0:T(8,128)(2,1)} %right_v.3, bf16[4,512,128]{2,1,0:T(8,128)(2,1)} %sketch.1), custom_call_target="tpu_custom_call" | custom-call | flops 536870912 | bytes 6291456 | tf_op jit(solution)/shard_map/probe/pallas_call | solution.py:381
  15.3 0.8 collective-permute-start.5
  16.7 3.0 %pair.1 = (bf16[32,256,128]{2,1,0:T(8,128)(2,1)S(1)}, bf16[32,128,128]{2,1,0:T(8,128)(2,1)S(1)}) custom-call(s32[4,8]{1,0:T(4,128)S(1)} %multiply_add_fusion.meta, bf16[32,512,128]{2,1,0:T(8,128)(2,1)S(1)} %get-tuple-element.37.held, bf16[32,128,256]{2,1,0:T(8,128)(2,1)S(1)} %get-tuple-element.38.probes, bf16[1,512,128]{2,1,0:T(8,128)(2,1)S(1)} %copy-done, ...), custom_call_target="tpu_custom_call" | custom-call | flops 939524096 | bytes 10485760 | tf_op jit(solution)/shard_map/pair/pallas_call | solution.py:398
  19.7 2.4 %collective-permute-done.5.rest_3_ = bf16[1,512,128]{2,1,0:T(8,128)(2,1)S(1)} collective-permute-done((bf16[1,512,128]{2,1,0:T(8,128)(2,1)S(1)}, bf16[1,512,128]{2,1,0:T(8,128)(2,1)S(1)}, u32[]{:S(2)}, u32[]{:S(2)}) %collective-permute-start.5) | collective-permute-done | bytes 131104 | tf_op jit(solution)/shard_map/ppermute | solution.py:346
  22.1 1.3 %collective-permute-done.13.rest_7_ = bf16[1,512,128]{2,1,0:T(8,128)(2,1)S(1)} collective-permute-done((bf16[1,512,128]{2,1,0:T(8,128)(2,1)S(1)}, bf16[1,512,128]{2,1,0:T(8,128)(2,1)S(1)}, u32[]{:S(2)}, u32[]{:S(2)}) %collective-permute-start.13) | collective-permute-done | bytes 131104 | tf_op jit(solution)/shard_map/ppermute | solution.py:350
  23.5 2.1 %sketch.2 = (f32[512,128]{1,0:T(8,128)S(1)}, bf16[512,128]{1,0:T(8,128)(2,1)S(1)}, bf16[512,128]{1,0:T(8,128)(2,1)S(1)}, bf16[512,128]{1,0:T(8,128)(2,1)S(1)}, bf16[8,512,128]{2,1,0:T(8,128)(2,1)S(1)}) custom-call(s32[4,8]{1,0:T(4,128)S(1)} %multiply_add_fusion.meta, bf16[32,128,128]{2,1,0:T(8,128)(2,1)S(1)} %get-tuple-element.42.mixing, ...), custom_call_target="tpu_custom_call" | custom-call | flops 536870912 | bytes 4194304 | tf_op jit(solution)/shard_map/sketch/pallas_call | solution.py:410
  25.6 1.8 %collective-permute-start.14 = (bf16[512,128]{1,0:T(8,128)(2,1)S(1)}, bf16[512,128]{1,0:T(8,128)(2,1)S(1)}, u32[]{:S(2)}, u32[]{:S(2)}) collective-permute-start(bf16[512,128]{1,0:T(8,128)(2,1)S(1)} %get-tuple-element.48), channel_id=1, source_target_pairs={{0,8},{8,16},{16,24},{24,0},{32,40},{40,48},{48,56},{56,32},{64,72... | collective-permute-start | bytes 393224 | tf_op jit(solution)/shard_map/ppermute | solution.py:342
  27.4 3.6 %collective-permute-start.15 = (bf16[512,128]{1,0:T(8,128)(2,1)S(1)}, bf16[512,128]{1,0:T(8,128)(2,1)S(1)}, u32[]{:S(2)}, u32[]{:S(2)}) collective-permute-start(bf16[512,128]{1,0:T(8,128)(2,1)S(1)} %get-tuple-element.49), channel_id=1, source_target_pairs={{0,16},{8,24},{16,0},{24,8},{32,48},{40,56},{48,32},{56,40},{64,80... | collective-permute-start | bytes 393224 | tf_op jit(solution)/shard_map/ppermute | solution.py:342
  31.0 2.2 %collective-permute-done.14 = bf16[512,128]{1,0:T(8,128)(2,1)S(1)} collective-permute-done((bf16[512,128]{1,0:T(8,128)(2,1)S(1)}, bf16[512,128]{1,0:T(8,128)(2,1)S(1)}, u32[]{:S(2)}, u32[]{:S(2)}) %collective-permute-start.14) | collective-permute-done | bytes 131104 | tf_op jit(solution)/shard_map/ppermute | solution.py:342
  33.2 2.1 %collective-permute-done.15 = bf16[512,128]{1,0:T(8,128)(2,1)S(1)} collective-permute-done((bf16[512,128]{1,0:T(8,128)(2,1)S(1)}, bf16[512,128]{1,0:T(8,128)(2,1)S(1)}, u32[]{:S(2)}, u32[]{:S(2)}) %collective-permute-start.15) | collective-permute-done | bytes 131104 | tf_op jit(solution)/shard_map/ppermute | solution.py:342
  35.3 2.0 %collective-permute-done.16 = bf16[512,128]{1,0:T(8,128)(2,1)S(1)} collective-permute-done((bf16[512,128]{1,0:T(8,128)(2,1)S(1)}, bf16[512,128]{1,0:T(8,128)(2,1)S(1)}, u32[]{:S(2)}, u32[]{:S(2)}) %collective-permute-start.16) | collective-permute-done | bytes 131104 | tf_op jit(solution)/shard_map/ppermute | solution.py:342
  37.4 18.5 %all_to_all.15 = f32[8,64,128]{2,1,0:T(8,128)} all-to-all(f32[8,64,128]{2,1,0:T(8,128)S(1)} %bitcast.1), channel_id=1, replica_groups={{0,32,64,96,128,160,192,224},{8,40,72,104,136,168,200,232},{16,48,80,11..., dimensions={0} | all-to-all | bytes 524288 | tf_op jit(solution)/shard_map/all_to_all | solution.py:355
  55.9 1.0 reduce_sum.18
  56.9 12.9 %all_to_all.16.blocks = f32[8,64,128]{2,1,0:T(8,128)S(1)} all-to-all(f32[8,64,128]{2,1,0:T(8,128)S(1)} %broadcast_in_dim.2), channel_id=1, replica_groups={{0,32,64,96,128,160,192,224},{8,40,72,104,136,168,200,232},{16,48,80,11..., dimensions={0} | all-to-all | bytes 524288 | tf_op jit(solution)/shard_map/all_to_all | solution.py:355
  69.8 7.0 %ortho.1 = (bf16[544,128]{1,0:T(8,128)(2,1)S(1)}, bf16[544,128]{1,0:T(8,128)(2,1)S(1)}, bf16[544,128]{1,0:T(8,128)(2,1)S(1)}, bf16[544,128]{1,0:T(8,128)(2,1)S(1)}) custom-call(f32[8,64,128]{2,1,0:T(8,128)S(1)} %all_to_all.16.blocks), custom_call_target="tpu_custom_call" | custom-call | flops 218103808 | bytes 1048576 | tf_op jit(solution)/shard_map/ortho/pallas_call | solution.py:427
  76.8 1.2 %collective-permute-start.17 = (bf16[544,128]{1,0:T(8,128)(2,1)S(1)}, bf16[544,128]{1,0:T(8,128)(2,1)S(1)}, u32[]{:S(2)}, u32[]{:S(2)}) collective-permute-start(bf16[544,128]{1,0:T(8,128)(2,1)S(1)} %get-tuple-element.54), channel_id=1, source_target_pairs={{0,8},{8,16},{16,24},{24,0},{32,40},{40,48},{48,56},{56,32},{64,72... | collective-permute-start | bytes 417800 | tf_op jit(solution)/shard_map/ppermute | solution.py:342
  77.9 1.9 %collective-permute-start.18 = (bf16[544,128]{1,0:T(8,128)(2,1)S(1)}, bf16[544,128]{1,0:T(8,128)(2,1)S(1)}, u32[]{:S(2)}, u32[]{:S(2)}) collective-permute-start(bf16[544,128]{1,0:T(8,128)(2,1)S(1)} %get-tuple-element.55), channel_id=1, source_target_pairs={{0,16},{8,24},{16,0},{24,8},{32,48},{40,56},{48,32},{56,40},{64,80... | collective-permute-start | bytes 417800 | tf_op jit(solution)/shard_map/ppermute | solution.py:342
  79.9 1.4 %collective-permute-start.19 = (bf16[544,128]{1,0:T(8,128)(2,1)S(1)}, bf16[544,128]{1,0:T(8,128)(2,1)S(1)}, u32[]{:S(2)}, u32[]{:S(2)}) collective-permute-start(bf16[544,128]{1,0:T(8,128)(2,1)S(1)} %get-tuple-element.56), channel_id=1, source_target_pairs={{0,24},{8,0},{16,8},{24,16},{32,56},{40,32},{48,40},{56,48},{64,88... | collective-permute-start | bytes 417800 | tf_op jit(solution)/shard_map/ppermute | solution.py:342
  81.3 2.7 %backward_own.1 = (f32[512,128]{1,0:T(8,128)S(1)}, bf16[32,512,128]{2,1,0:T(8,128)(2,1)S(1)}) custom-call(s32[4,8]{1,0:T(4,128)S(1)} %multiply_add_fusion.meta, bf16[4,8,512,128]{3,2,1,0:T(8,128)(2,1)} %right_v.3, bf16[8,512,128]{2,1,0:T(8,128)(2,1)S(1)} %get-tuple-element.45.group, bf16[32,256,128]{2,1,0:T(8,128)(2,1)S(1)} %get-tuple-element.46.pairs, ...), custom_call_target="tpu_custom_call" | custom-call | flops 369098752 | bytes 4194304 | tf_op jit(solution)/shard_map/backward_own/pallas_call | solution.py:437
  84.6 1.4 %collective-permute-done.19.msg3 = bf16[544,128]{1,0:T(8,128)(2,1)S(1)} collective-permute-done((bf16[544,128]{1,0:T(8,128)(2,1)S(1)}, bf16[544,128]{1,0:T(8,128)(2,1)S(1)}, u32[]{:S(2)}, u32[]{:S(2)}) %collective-permute-start.19) | collective-permute-done | bytes 139296 | tf_op jit(solution)/shard_map/ppermute | solution.py:342
  86.0 3.6 %backward.1 = (f32[8,4,16,128]{3,2,1,0:T(8,128)S(1)}, bf16[8,4,16,128]{3,2,1,0:T(8,128)(2,1)S(1)}, bf16[8,4,16,128]{3,2,1,0:T(8,128)(2,1)S(1)}, bf16[8,4,16,128]{3,2,1,0:T(8,128)(2,1)S(1)}, f32[4,16,128]{2,1,0:T(8,128)}) custom-call(s32[4,8]{1,0:T(4,128)S(1)} %multiply_add_fusion.meta, bf16[32,512,128]{2,1,0:T(8,128)(2,1)S(1)} %get-tuple-element.52.held, ...), custom_call_target="tpu_custom_call" | custom-call | flops 1073741824 | bytes 8388608 | tf_op jit(solution)/shard_map/backward/pallas_call | solution.py:449
  90.2 1.9 %collective-permute-start.21 = (bf16[8,4,16,128]{3,2,1,0:T(8,128)(2,1)S(1)}, bf16[8,4,16,128]{3,2,1,0:T(8,128)(2,1)S(1)}, u32[]{:S(2)}, u32[]{:S(2)}) collective-permute-start(bf16[8,4,16,128]{3,2,1,0:T(8,128)(2,1)S(1)} %get-tuple-element.60), channel_id=1, source_target_pairs={{0,16},{8,24},{16,0},{24,8},{32,48},{40,56},{48,32},{56,40},{64,80... | collective-permute-start | bytes 393224 | tf_op jit(solution)/shard_map/ppermute | solution.py:342
  92.1 2.1 %collective-permute-start.22 = (bf16[8,4,16,128]{3,2,1,0:T(8,128)(2,1)S(1)}, bf16[8,4,16,128]{3,2,1,0:T(8,128)(2,1)S(1)}, u32[]{:S(2)}, u32[]{:S(2)}) collective-permute-start(bf16[8,4,16,128]{3,2,1,0:T(8,128)(2,1)S(1)} %get-tuple-element.61), channel_id=1, source_target_pairs={{0,24},{8,0},{16,8},{24,16},{32,56},{40,32},{48,40},{56,48},{64,88... | collective-permute-start | bytes 393224 | tf_op jit(solution)/shard_map/ppermute | solution.py:342
  94.6 2.2 %collective-permute-done.21 = bf16[8,4,16,128]{3,2,1,0:T(8,128)(2,1)S(1)} collective-permute-done((bf16[8,4,16,128]{3,2,1,0:T(8,128)(2,1)S(1)}, bf16[8,4,16,128]{3,2,1,0:T(8,128)(2,1)S(1)}, u32[]{:S(2)}, u32[]{:S(2)}) %collective-permute-start.21) | collective-permute-done | bytes 131104 | tf_op jit(solution)/shard_map/ppermute | solution.py:342
  96.7 1.3 %collective-permute-done.22 = bf16[8,4,16,128]{3,2,1,0:T(8,128)(2,1)S(1)} collective-permute-done((bf16[8,4,16,128]{3,2,1,0:T(8,128)(2,1)S(1)}, bf16[8,4,16,128]{3,2,1,0:T(8,128)(2,1)S(1)}, u32[]{:S(2)}, u32[]{:S(2)}) %collective-permute-start.22) | collective-permute-done | bytes 131104 | tf_op jit(solution)/shard_map/ppermute | solution.py:342
  98.1 12.9 %all_to_all.17 = f32[8,4,16,128]{3,2,1,0:T(8,128)S(1)} all-to-all(f32[8,4,16,128]{3,2,1,0:T(8,128)S(1)} %convert_add_fusion), channel_id=1, replica_groups={{0,32,64,96,128,160,192,224},{8,40,72,104,136,168,200,232},{16,48,80,11..., dimensions={0} | all-to-all | bytes 524288 | tf_op jit(solution)/shard_map/all_to_all | solution.py:355
  (33 shorter events, 4.4 us)
Async XLA Ops:
  0.6 7.3 %collective-permute-start = (bf16[1,512,128]{2,1,0:T(8,128)(2,1)}, bf16[1,512,128]{2,1,0:T(8,128)(2,1)S(1)}, u32[]{:S(2)}, u32[]{:S(2)}) collective-permute-start(bf16[1,512,128]{2,1,0:T(8,128)(2,1)} %rest_0_.2), channel_id=1, source_target_pairs={{0,2},{1,3},{2,4},{3,5},{4,6},{5,7},{6,0},{7,1},{8,10},{9,11},{10,... | collective-permute-start | bytes 393224 | tf_op jit(solution)/shard_map/ppermute | solution.py:346
  2.2 6.5 %collective-permute-start.1 = (bf16[1,512,128]{2,1,0:T(8,128)(2,1)}, bf16[1,512,128]{2,1,0:T(8,128)(2,1)S(1)}, u32[]{:S(2)}, u32[]{:S(2)}) collective-permute-start(bf16[1,512,128]{2,1,0:T(8,128)(2,1)} %rest_0_.2), channel_id=1, source_target_pairs={{0,6},{1,7},{2,0},{3,1},{4,2},{5,3},{6,4},{7,5},{8,14},{9,15},{10,... | collective-permute-start | bytes 393224 | tf_op jit(solution)/shard_map/ppermute | solution.py:346
  3.9 10.7 %collective-permute-start.2 = (bf16[1,512,128]{2,1,0:T(8,128)(2,1)}, bf16[1,512,128]{2,1,0:T(8,128)(2,1)S(1)}, u32[]{:S(2)}, u32[]{:S(2)}) collective-permute-start(bf16[1,512,128]{2,1,0:T(8,128)(2,1)} %rest_0_.3), channel_id=1, source_target_pairs={{0,2},{1,3},{2,4},{3,5},{4,6},{5,7},{6,0},{7,1},{8,10},{9,11},{10,... | collective-permute-start | bytes 393224 | tf_op jit(solution)/shard_map/ppermute | solution.py:346
  4.2 10.8 %collective-permute-start.3 = (bf16[1,512,128]{2,1,0:T(8,128)(2,1)}, bf16[1,512,128]{2,1,0:T(8,128)(2,1)S(1)}, u32[]{:S(2)}, u32[]{:S(2)}) collective-permute-start(bf16[1,512,128]{2,1,0:T(8,128)(2,1)} %rest_0_.3), channel_id=1, source_target_pairs={{0,6},{1,7},{2,0},{3,1},{4,2},{5,3},{6,4},{7,5},{8,14},{9,15},{10,... | collective-permute-start | bytes 393224 | tf_op jit(solution)/shard_map/ppermute | solution.py:346
  7.9 8.2 %copy-start.1 = (bf16[1,512,128]{2,1,0:T(8,128)(2,1)S(1)}, bf16[1,512,128]{2,1,0:T(8,128)(2,1)}, u32[]{:S(2)}) copy-start(bf16[1,512,128]{2,1,0:T(8,128)(2,1)} %rest_0_.3) | copy-start | bytes 393220
  7.9 8.9 %copy-start = (bf16[1,512,128]{2,1,0:T(8,128)(2,1)S(1)}, bf16[1,512,128]{2,1,0:T(8,128)(2,1)}, u32[]{:S(2)}) copy-start(bf16[1,512,128]{2,1,0:T(8,128)(2,1)} %rest_0_.2) | copy-start | bytes 393220
  8.7 6.3 %collective-permute-start.4 = (bf16[1,512,128]{2,1,0:T(8,128)(2,1)S(1)}, bf16[1,512,128]{2,1,0:T(8,128)(2,1)S(1)}, u32[]{:S(2)}, u32[]{:S(2)}) collective-permute-start(bf16[1,512,128]{2,1,0:T(8,128)(2,1)S(1)} %collective-permute-done.1.rest_2_), channel_id=1, source_target_pairs={{0,6},{1,7},{2,0},{3,1},{4,2},{5,3},{6,4},{7,5},{8,14},{9,15},{10,... | collective-permute-start | bytes 393224 | tf_op jit(solution)/shard_map/ppermute | solution.py:346
  10.4 5.7 %collective-permute-start.6 = (bf16[1,512,128]{2,1,0:T(8,128)(2,1)}, bf16[1,512,128]{2,1,0:T(8,128)(2,1)S(1)}, u32[]{:S(2)}, u32[]{:S(2)}) collective-permute-start(bf16[1,512,128]{2,1,0:T(8,128)(2,1)} %rest_0_.2), channel_id=1, source_target_pairs={{0,1},{1,0},{2,3},{3,2},{4,5},{5,4},{6,7},{7,6},{8,9},{9,8},{10,11... | collective-permute-start | bytes 393224 | tf_op jit(solution)/shard_map/ppermute | solution.py:350
  10.4 5.7 %collective-permute-start.8 = (bf16[1,512,128]{2,1,0:T(8,128)(2,1)S(1)}, bf16[1,512,128]{2,1,0:T(8,128)(2,1)S(1)}, u32[]{:S(2)}, u32[]{:S(2)}) collective-permute-start(bf16[1,512,128]{2,1,0:T(8,128)(2,1)S(1)} %collective-permute-done.1.rest_2_), channel_id=1, source_target_pairs={{0,1},{1,0},{2,3},{3,2},{4,5},{5,4},{6,7},{7,6},{8,9},{9,8},{10,11... | collective-permute-start | bytes 393224 | tf_op jit(solution)/shard_map/ppermute | solution.py:350
  14.7 1.9 %collective-permute-start.7 = (bf16[1,512,128]{2,1,0:T(8,128)(2,1)S(1)}, bf16[1,512,128]{2,1,0:T(8,128)(2,1)S(1)}, u32[]{:S(2)}, u32[]{:S(2)}) collective-permute-start(bf16[1,512,128]{2,1,0:T(8,128)(2,1)S(1)} %collective-permute-done.rest_1_), channel_id=1, source_target_pairs={{0,1},{1,0},{2,3},{3,2},{4,5},{5,4},{6,7},{7,6},{8,9},{9,8},{10,11... | collective-permute-start | bytes 393224 | tf_op jit(solution)/shard_map/ppermute | solution.py:350
  15.0 1.8 %collective-permute-start.9 = (bf16[1,512,128]{2,1,0:T(8,128)(2,1)S(1)}, bf16[1,512,128]{2,1,0:T(8,128)(2,1)S(1)}, u32[]{:S(2)}, u32[]{:S(2)}) collective-permute-start(bf16[1,512,128]{2,1,0:T(8,128)(2,1)S(1)} %collective-permute-done.4.rest_3_), channel_id=1, source_target_pairs={{0,1},{1,0},{2,3},{3,2},{4,5},{5,4},{6,7},{7,6},{8,9},{9,8},{10,11... | collective-permute-start | bytes 393224 | tf_op jit(solution)/shard_map/ppermute | solution.py:350
  15.3 6.8 %collective-permute-start.5 = (bf16[1,512,128]{2,1,0:T(8,128)(2,1)S(1)}, bf16[1,512,128]{2,1,0:T(8,128)(2,1)S(1)}, u32[]{:S(2)}, u32[]{:S(2)}) collective-permute-start(bf16[1,512,128]{2,1,0:T(8,128)(2,1)S(1)} %collective-permute-done.2.rest_1_), channel_id=1, source_target_pairs={{0,2},{1,3},{2,4},{3,5},{4,6},{5,7},{6,0},{7,1},{8,10},{9,11},{10,... | collective-permute-start | bytes 393224 | tf_op jit(solution)/shard_map/ppermute | solution.py:346
  16.1 6.0 %collective-permute-start.10 = (bf16[1,512,128]{2,1,0:T(8,128)(2,1)S(1)}, bf16[1,512,128]{2,1,0:T(8,128)(2,1)S(1)}, u32[]{:S(2)}, u32[]{:S(2)}) collective-permute-start(bf16[1,512,128]{2,1,0:T(8,128)(2,1)S(1)} %copy-done.1), channel_id=1, source_target_pairs={{0,1},{1,0},{2,3},{3,2},{4,5},{5,4},{6,7},{7,6},{8,9},{9,8},{10,11... | collective-permute-start | bytes 393224 | tf_op jit(solution)/shard_map/ppermute | solution.py:350
  16.1 6.0 %collective-permute-start.11 = (bf16[1,512,128]{2,1,0:T(8,128)(2,1)S(1)}, bf16[1,512,128]{2,1,0:T(8,128)(2,1)S(1)}, u32[]{:S(2)}, u32[]{:S(2)}) collective-permute-start(bf16[1,512,128]{2,1,0:T(8,128)(2,1)S(1)} %collective-permute-done.2.rest_1_), channel_id=1, source_target_pairs={{0,1},{1,0},{2,3},{3,2},{4,5},{5,4},{6,7},{7,6},{8,9},{9,8},{10,11... | collective-permute-start | bytes 393224 | tf_op jit(solution)/shard_map/ppermute | solution.py:350
  16.6 5.5 %collective-permute-start.12 = (bf16[1,512,128]{2,1,0:T(8,128)(2,1)S(1)}, bf16[1,512,128]{2,1,0:T(8,128)(2,1)S(1)}, u32[]{:S(2)}, u32[]{:S(2)}) collective-permute-start(bf16[1,512,128]{2,1,0:T(8,128)(2,1)S(1)} %collective-permute-done.3.rest_2_), channel_id=1, source_target_pairs={{0,1},{1,0},{2,3},{3,2},{4,5},{5,4},{6,7},{7,6},{8,9},{9,8},{10,11... | collective-permute-start | bytes 393224 | tf_op jit(solution)/shard_map/ppermute | solution.py:350
  22.1 1.3 %collective-permute-start.13 = (bf16[1,512,128]{2,1,0:T(8,128)(2,1)S(1)}, bf16[1,512,128]{2,1,0:T(8,128)(2,1)S(1)}, u32[]{:S(2)}, u32[]{:S(2)}) collective-permute-start(bf16[1,512,128]{2,1,0:T(8,128)(2,1)S(1)} %collective-permute-done.5.rest_3_), channel_id=1, source_target_pairs={{0,1},{1,0},{2,3},{3,2},{4,5},{5,4},{6,7},{7,6},{8,9},{9,8},{10,11... | collective-permute-start | bytes 393224 | tf_op jit(solution)/shard_map/ppermute | solution.py:350
  25.6 7.6 %collective-permute-start.14 = (bf16[512,128]{1,0:T(8,128)(2,1)S(1)}, bf16[512,128]{1,0:T(8,128)(2,1)S(1)}, u32[]{:S(2)}, u32[]{:S(2)}) collective-permute-start(bf16[512,128]{1,0:T(8,128)(2,1)S(1)} %get-tuple-element.48), channel_id=1, source_target_pairs={{0,8},{8,16},{16,24},{24,0},{32,40},{40,48},{48,56},{56,32},{64,72... | collective-permute-start | bytes 393224 | tf_op jit(solution)/shard_map/ppermute | solution.py:342
  27.4 7.9 %collective-permute-start.15 = (bf16[512,128]{1,0:T(8,128)(2,1)S(1)}, bf16[512,128]{1,0:T(8,128)(2,1)S(1)}, u32[]{:S(2)}, u32[]{:S(2)}) collective-permute-start(bf16[512,128]{1,0:T(8,128)(2,1)S(1)} %get-tuple-element.49), channel_id=1, source_target_pairs={{0,16},{8,24},{16,0},{24,8},{32,48},{40,56},{48,32},{56,40},{64,80... | collective-permute-start | bytes 393224 | tf_op jit(solution)/shard_map/ppermute | solution.py:342
  31.0 6.3 %collective-permute-start.16 = (bf16[512,128]{1,0:T(8,128)(2,1)S(1)}, bf16[512,128]{1,0:T(8,128)(2,1)S(1)}, u32[]{:S(2)}, u32[]{:S(2)}) collective-permute-start(bf16[512,128]{1,0:T(8,128)(2,1)S(1)} %get-tuple-element.50), channel_id=1, source_target_pairs={{0,24},{8,0},{16,8},{24,16},{32,56},{40,32},{48,40},{56,48},{64,88... | collective-permute-start | bytes 393224 | tf_op jit(solution)/shard_map/ppermute | solution.py:342
  76.8 7.2 %collective-permute-start.17 = (bf16[544,128]{1,0:T(8,128)(2,1)S(1)}, bf16[544,128]{1,0:T(8,128)(2,1)S(1)}, u32[]{:S(2)}, u32[]{:S(2)}) collective-permute-start(bf16[544,128]{1,0:T(8,128)(2,1)S(1)} %get-tuple-element.54), channel_id=1, source_target_pairs={{0,8},{8,16},{16,24},{24,0},{32,40},{40,48},{48,56},{56,32},{64,72... | collective-permute-start | bytes 417800 | tf_op jit(solution)/shard_map/ppermute | solution.py:342
  77.9 6.7 %collective-permute-start.18 = (bf16[544,128]{1,0:T(8,128)(2,1)S(1)}, bf16[544,128]{1,0:T(8,128)(2,1)S(1)}, u32[]{:S(2)}, u32[]{:S(2)}) collective-permute-start(bf16[544,128]{1,0:T(8,128)(2,1)S(1)} %get-tuple-element.55), channel_id=1, source_target_pairs={{0,16},{8,24},{16,0},{24,8},{32,48},{40,56},{48,32},{56,40},{64,80... | collective-permute-start | bytes 417800 | tf_op jit(solution)/shard_map/ppermute | solution.py:342
  79.9 6.1 %collective-permute-start.19 = (bf16[544,128]{1,0:T(8,128)(2,1)S(1)}, bf16[544,128]{1,0:T(8,128)(2,1)S(1)}, u32[]{:S(2)}, u32[]{:S(2)}) collective-permute-start(bf16[544,128]{1,0:T(8,128)(2,1)S(1)} %get-tuple-element.56), channel_id=1, source_target_pairs={{0,24},{8,0},{16,8},{24,16},{32,56},{40,32},{48,40},{56,48},{64,88... | collective-permute-start | bytes 417800 | tf_op jit(solution)/shard_map/ppermute | solution.py:342
  89.6 5.0 %collective-permute-start.20 = (bf16[8,4,16,128]{3,2,1,0:T(8,128)(2,1)S(1)}, bf16[8,4,16,128]{3,2,1,0:T(8,128)(2,1)S(1)}, u32[]{:S(2)}, u32[]{:S(2)}) collective-permute-start(bf16[8,4,16,128]{3,2,1,0:T(8,128)(2,1)S(1)} %get-tuple-element.59), channel_id=1, source_target_pairs={{0,8},{8,16},{16,24},{24,0},{32,40},{40,48},{48,56},{56,32},{64,72... | collective-permute-start | bytes 393224 | tf_op jit(solution)/shard_map/ppermute | solution.py:342
  90.2 6.6 %collective-permute-start.21 = (bf16[8,4,16,128]{3,2,1,0:T(8,128)(2,1)S(1)}, bf16[8,4,16,128]{3,2,1,0:T(8,128)(2,1)S(1)}, u32[]{:S(2)}, u32[]{:S(2)}) collective-permute-start(bf16[8,4,16,128]{3,2,1,0:T(8,128)(2,1)S(1)} %get-tuple-element.60), channel_id=1, source_target_pairs={{0,16},{8,24},{16,0},{24,8},{32,48},{40,56},{48,32},{56,40},{64,80... | collective-permute-start | bytes 393224 | tf_op jit(solution)/shard_map/ppermute | solution.py:342
  92.1 5.9 %collective-permute-start.22 = (bf16[8,4,16,128]{3,2,1,0:T(8,128)(2,1)S(1)}, bf16[8,4,16,128]{3,2,1,0:T(8,128)(2,1)S(1)}, u32[]{:S(2)}, u32[]{:S(2)}) collective-permute-start(bf16[8,4,16,128]{3,2,1,0:T(8,128)(2,1)S(1)} %get-tuple-element.61), channel_id=1, source_target_pairs={{0,24},{8,0},{16,8},{24,16},{32,56},{40,32},{48,40},{56,48},{64,88... | collective-permute-start | bytes 393224 | tf_op jit(solution)/shard_map/ppermute | solution.py:342

commit v7 on v6

--- a/solution.py
+++ b/solution.py
@@ -88,8 +88,33 @@
     return jnp.concatenate([a, b], axis=0)
 
 
-def slots_of(j, base, slots, count):
-    return [j * slots + jnp.minimum(base + i, count - 1) for i in range(BATCH)]
+def sweep(meta, together, work):
+    for tiles in together:
+        work([(place, j, 0, live(meta, j)) for place, j in tiles], True)
+
+    def rest(place, j):
+        count = live(meta, j)
+
+        def batch(first, _):
+            work([(place, j, first * BATCH, count)], False)
+            return 0
+
+        lax.fori_loop(1, (count + BATCH - 1) // BATCH, batch, 0)
+
+    for tiles in together:
+        for place, j in tiles:
+            rest(place, j)
+
+
+def batches(items, slots):
+    return [
+        (j * slots + jnp.minimum(base + i, count - 1), j * slots + base + i, base + i < count)
+        for _, j, base, count in items for i in range(BATCH)
+    ]
+
+
+def two_by_two(tiles):
+    return [tiles[:2], tiles[2:]]
 
 
 def probe_kernel(outs, slots, meta, right_u, right_v, sketch, probes, held_u, held, plain, sems_u, sems, sem):
@@ -99,23 +124,24 @@
     fetch(meta, outs, slots, right_u, held_u, sems_u)
     copy.wait()
 
-    def tile(j, _):
-        turned = plain[j].T
-        count = live(meta, j)
-
-        def batch(first, _):
-            base = first * BATCH
+    def work(items, first):
+        for _, j, base, count in items:
             for i in range(BATCH):
                 arrive(count, slots, j, base + i, right_v, held, sems)
-            at = slots_of(j, base, slots, count)
-            products = [dot(turned, held[slot]) for slot in at]
-            for slot, product in zip(at, products):
-                probes[slot] = beside(*halves(product))
-            for i in range(BATCH):
-                arrive(count, slots, j, base + i, right_u, held_u, sems_u)
+        turned = [plain[j].T for _, j, _, _ in items]
+        at = batches(items, slots)
+        products = [dot(turned[n // BATCH], held[slot]) for n, (slot, _, _) in enumerate(at)]
+        for (slot, _, _), product in zip(at, products):
+            probes[slot] = beside(*halves(product))
+
+    sweep(meta, two_by_two([(j, j) for j in range(outs)]), work)
+
+    def tile(j, _):
+        def one(s, _):
+            pltpu.make_async_copy(right_u.at[j, s], held_u.at[j * slots + s], sems_u.at[j * slots + s]).wait()
             return 0
 
-        lax.fori_loop(0, (count + BATCH - 1) // BATCH, batch, 0)
+        lax.fori_loop(0, live(meta, j), one, 0)
         return 0
 
     lax.fori_loop(0, outs, tile, 0)
@@ -131,26 +157,18 @@
     for k, part in zip(tile_ids(len(parts)), parts):
         turned[k] = part[0].T
 
-    def tile(j, _):
-        count = live(meta, j)
-
-        def batch(first, _):
-            base = first * BATCH
-            at = slots_of(j, base, slots, count)
-            products = [halves(dot(turned[tile_of(meta, slot)], held[slot])) for slot in at]
-            mixes = []
-            for slot, (high, low) in zip(at, products):
-                probe = probes[slot]
-                mixes.append(dot_nt(high, probe[:, :R]) + dot_nt(high, probe[:, R:]) + dot_nt(low, probe[:, :R]))
-            for i in range(BATCH):
-                pairs[at[i]] = above(*products[i])
-                mixing[j * slots + base + i] = jnp.where(base + i < count, mixes[i], 0.0).astype(BF)
-            return 0
-
-        lax.fori_loop(0, (count + BATCH - 1) // BATCH, batch, 0)
-        return 0
-
-    lax.fori_loop(0, outs, tile, 0)
+    def work(items, first):
+        at = batches(items, slots)
+        products = [halves(dot(turned[tile_of(meta, slot)], held[slot])) for slot, _, _ in at]
+        mixes = []
+        for (slot, _, _), (high, low) in zip(at, products):
+            probe = probes[slot]
+            mixes.append(dot_nt(high, probe[:, :R]) + dot_nt(high, probe[:, R:]) + dot_nt(low, probe[:, :R]))
+        for (slot, place, alive), product, mixed in zip(at, products, mixes):
+            pairs[slot] = above(*product)
+            mixing[place] = jnp.where(alive, mixed, 0.0).astype(BF)
+
+    sweep(meta, two_by_two([(j, j) for j in range(outs)]), work)
 
 
 def sketch_kernel(outs, slots, meta, mixing, *rest):
@@ -159,28 +177,20 @@
         group[k] = part[0]
     y = y_of()
 
-    def tile(order, _):
-        j = lax.rem(y + 1 + order, YS)
-        acc[...] = jnp.zeros_like(acc)
-
-        def batch(first, _):
-            base = first * BATCH
-            at = [j * slots + base + i for i in range(BATCH)]
-            tiles = [group[tile_of(meta, slot)] for slot in at]
-            terms = [
-                dot(beside(tiles[i], tiles[i + 1]), above(mixing[at[i]], mixing[at[i + 1]])) for i in range(0, BATCH, 2)
-            ]
-            acc[...] += terms[0] + terms[1]
-            return 0
-
-        lax.fori_loop(0, (live(meta, j) + BATCH - 1) // BATCH, batch, 0)
-        for place, out in enumerate((send1, send2, send3, own)):
-            @pl.when(order == place)
-            def _():
-                out[...] = acc[...].astype(out.dtype)
-        return 0
-
-    lax.fori_loop(0, YS, tile, 0)
+    def work(items, first):
+        at = batches(items, slots)
+        tiles = [group[tile_of(meta, slot)] for slot, _, _ in at]
+        terms = [
+            dot(beside(tiles[i], tiles[i + 1]), above(mixing[at[i][1]], mixing[at[i + 1][1]]))
+            for i in range(0, len(at), 2)
+        ]
+        for n, (place, _, _, _) in enumerate(items):
+            term = terms[2 * n] + terms[2 * n + 1]
+            acc[place] = term if first else acc[place] + term
+
+    sweep(meta, two_by_two([(step, lax.rem(y + step, YS)) for step in range(YS)]), work)
+    for step, out in enumerate((own, send1, send2, send3)):
+        out[...] = acc[step].astype(out.dtype)
 
 
 def exact(a, b, dims):
@@ -261,39 +271,36 @@
         msg[NB + rows:] = low
 
 
-def backward_tile(slots, meta, j, mine, group, pairs, held, acc, ready):
-    count = live(meta, j)
-    acc[...] = jnp.zeros_like(acc)
-
-    def batch(first, _):
-        base = first * BATCH
-        ready(count, base)
-        at = slots_of(j, base, slots, count)
-        products = [halves(dot(mine, group[tile_of(meta, slot)])) for slot in at]
-        backs = []
-        for i in range(BATCH):
-            high, low = products[i]
-            pair = pairs[at[i]]
-            back = dot(high, pair[:R]) + dot(high, pair[R:]) + dot(low, pair[:R])
-            backs.append(jnp.where(base + i < count, back, 0.0).astype(BF))
-        terms = [
-            dot_nt(beside(held[at[i]], held[at[i + 1]]), beside(backs[i], backs[i + 1])) for i in range(0, BATCH, 2)
-        ]
-        acc[...] += terms[0] + terms[1]
-        return 0
-
-    lax.fori_loop(0, (count + BATCH - 1) // BATCH, batch, 0)
-
-
-def backward_own_kernel(outs, slots, meta, right_v, group, pairs, msg, mine, held, sems):
+def backward_work(slots, meta, turned, group, pairs, held, acc, items, first):
+    at = batches(items, slots)
+    mine = [turned[place] for place, _, _, _ in items]
+    products = [halves(dot(mine[n // BATCH], group[tile_of(meta, slot)])) for n, (slot, _, _) in enumerate(at)]
+    backs = []
+    for (slot, _, alive), (high, low) in zip(at, products):
+        pair = pairs[slot]
+        back = dot(high, pair[:R]) + dot(high, pair[R:]) + dot(low, pair[:R])
+        backs.append(jnp.where(alive, back, 0.0).astype(BF))
+    terms = [
+        dot_nt(beside(held[at[i][0]], held[at[i + 1][0]]), beside(backs[i], backs[i + 1]))
+        for i in range(0, len(at), 2)
+    ]
+    for n, (place, _, _, _) in enumerate(items):
+        term = terms[2 * n] + terms[2 * n + 1]
+        acc[place] = term if first else acc[place] + term
+
+
+def backward_own_kernel(outs, slots, meta, right_v, group, pairs, msg, mine, held, turned, sems):
     fetch(meta, outs, slots, right_v, held, sems)
     y = y_of()
-
-    def ready(count, base):
-        for i in range(BATCH):
-            arrive(count, slots, y, base + i, right_v, held, sems)
-
-    backward_tile(slots, meta, y, msg[:NB].T, group, pairs, held, mine, ready)
+    turned[0] = msg[:NB].T
+
+    def work(items, first):
+        for _, j, base, count in items:
+            for i in range(BATCH):
+                arrive(count, slots, j, base + i, right_v, held, sems)
+        backward_work(slots, meta, turned, group, pairs, held, mine, items, first)
+
+    sweep(meta, [[(0, y)]], work)
 
     def tile(order, _):
         j = lax.rem(y + order, YS)
@@ -312,29 +319,24 @@
                     own, send1, send2, send3, basis, turned, acc):
     y = y_of()
     rows = NB // (zs * YS)
+    tiles = [lax.rem(y + YS - step, YS) for step in range(YS)]
     for step, msg in enumerate((msg0, msg1, msg2, msg3)):
-        j = lax.rem(y + YS - step, YS)
         if step:
             turned[step] = msg[:NB].T
         kept = msg[NB:NB + rows].astype(F32) + msg[NB + rows:].astype(F32)
-        basis[j] = kept * math.sqrt(NB)
-
-    def write(j, source):
-        for step, out in enumerate((own, send1, send2, send3)):
-            there = lax.rem(y + step, YS)
-            for block in range(zs):
-                start = pl.multiple_of((block * YS + there) * rows, rows)
-                out[block, j] = source[pl.ds(start, rows)].astype(out.dtype)
-
-    write(y, mine)
-
-    def tile(step, _):
-        j = lax.rem(y + YS - step, YS)
-        backward_tile(slots, meta, j, turned[step], group, pairs, held, acc, lambda count, base: None)
-        write(j, acc)
-        return 0
-
-    lax.fori_loop(1, YS, tile, 0)
+        basis[tiles[step]] = kept * math.sqrt(NB)
+
+    def work(items, first):
+        backward_work(slots, meta, turned, group, pairs, held, acc, items, first)
+
+    sweep(meta, [[(step, tiles[step]) for step in range(1, YS)]], work)
+    acc[0] = mine[0]
+    for step, out in enumerate((own, send1, send2, send3)):
+        there = lax.rem(y + step, YS)
+        for block in range(zs):
+            start = pl.multiple_of((block * YS + there) * rows, rows)
+            for place in range(YS):
+                out[block, tiles[place]] = acc[place, pl.ds(start, rows)].astype(out.dtype)
 
 
 def shift_y(array, step, zs):
@@ -348,6 +350,11 @@
 
 def swap(value, tiles):
     return lax.ppermute(value, "cols", [(i, i ^ 1) for i in range(tiles)])
+
+
+def spread(sends, zs):
+    got = {step: shift_y(sends[step - 1], step, zs) for step in (2, 1, 3)}
+    return [got[step] for step in (1, 2, 3)]
 
 
 def over_z(array, zs):
@@ -412,14 +419,14 @@
         out_shape=(shape((NB, R), F32),) + (shape((NB, R), BF),) * 3 + (shape((tiles, NB, R), BF),),
         in_specs=[in_smem()] + [in_vmem()] * (1 + tiles),
         out_specs=(in_vmem(),) * 5,
-        scratch_shapes=[VMEM((NB, R), F32)],
+        scratch_shapes=[VMEM((YS, NB, R), F32)],
         compiler_params=params(),
         cost_estimate=cost(outs * slots, 4),
         name="sketch",
     )(packed, mixing, *group_u)
     total = own
-    for step, send in enumerate((send1, send2, send3)):
-        total = total + shift_y(send, step + 1, zs).astype(F32)
+    for got in spread((send1, send2, send3), zs):
+        total = total + got.astype(F32)
     rows = NB // zs
     mine = jnp.sum(over_z(total.reshape(zs, rows, R), zs), axis=0)
     summed = over_z(jnp.broadcast_to(mine[None], (zs, rows, R)), zs)
@@ -436,29 +443,29 @@
     )(summed)
     mine, held_v = pl.pallas_call(
         functools.partial(backward_own_kernel, outs, slots),
-        out_shape=(shape((NB, R), F32), shape((count, NB, R), BF)),
+        out_shape=(shape((1, NB, R), F32), shape((count, NB, R), BF)),
         in_specs=[in_smem(), in_place()] + [in_vmem()] * 3,
         out_specs=(in_vmem(),) * 2,
-        scratch_shapes=[pltpu.SemaphoreType.DMA((count,))],
+        scratch_shapes=[VMEM((1, R, NB), BF), pltpu.SemaphoreType.DMA((count,))],
         compiler_params=params(),
         cost_estimate=cost(slots * 2.75, 4),
         name="backward_own",
     )(packed, right_v, group, pairs, messages[0])
-    messages = [shift_y(message, step, zs) if step else message for step, message in enumerate(messages)]
+    messages = [messages[0]] + spread(messages[1:], zs)
     pieces = (zs, outs, out_rows, R)
     own, send1, send2, send3, basis = pl.pallas_call(
         functools.partial(backward_kernel, slots, zs),
         out_shape=(shape(pieces, F32),) + (shape(pieces, BF),) * 3 + (shape((outs, out_rows, R), F32),),
         in_specs=[in_smem()] + [in_vmem()] * (4 + YS),
         out_specs=(in_vmem(),) * 5,
-        scratch_shapes=[VMEM((outs, R, NB), BF), VMEM((NB, R), F32)],
+        scratch_shapes=[VMEM((YS, R, NB), BF), VMEM((YS, NB, R), F32)],
         compiler_params=params(),
         cost_estimate=cost(outs * slots * 2, 8),
         name="backward",
     )(packed, held_v, group, pairs, mine, *messages)
     part = own
-    for step, send in enumerate((send1, send2, send3)):
-        part = part + shift_y(send, step + 1, zs).astype(F32)
+    for got in spread((send1, send2, send3), zs):
+        part = part + got.astype(F32)
     coeff = jnp.sum(over_z(part, zs), axis=0)
     return (basis, coeff)
 

time: 113 us -> 111 us (0.982)
  Pallas kernels: 22.1 us -> 20 us
where the time goes in v7:
time: 111 us; the launch traced here: 110 us
  blocking collectives  44.3 us (40%)
  starting transfers between devices  24.9 us (22%)
  Pallas kernels  20 us (18%)
  waiting for transfers between devices  17.7 us (16%)
  other arithmetic  2.43 us (2%)
    all_to_all x3, blocking collectives, over_z(): lax.all_to_all(array, 'inner', 0, 0, tiled=True, axis_index_groups=groups)  44.3 us
    ppermute x9, starting transfers between devices, shift_y(): return lax.ppermute(array, 'inner', pairs)  14.3 us
    ppermute x9, waiting for transfers between devices, shift_y(): return lax.ppermute(array, 'inner', pairs)  12.7 us
    ppermute x6, starting transfers between devices, hop(): lax.ppermute(value, 'cols', [(i, (i + 2 * step) % tiles) for i in range(t...  8.72 us
    pallas_call x1, Pallas kernels, body(): pl.pallas_call(functools.partial(ortho_kernel, zs), out_shape=(shape((NB...  6.98 us
    ppermute x6, waiting for transfers between devices, hop(): lax.ppermute(value, 'cols', [(i, (i + 2 * step) % tiles) for i in range(t...  3.67 us
    pallas_call x1, Pallas kernels, body(): pl.pallas_call(functools.partial(probe_kernel, outs, slots), out_shape=(s...  3.39 us
    pallas_call x1, Pallas kernels, body(): pl.pallas_call(functools.partial(backward_kernel, slots, zs), out_shape=(...  2.76 us
  transfers between devices with their start and end apart: 23, of which 11 were waited for; matrix products, arithmetic and copies ran while one was open for 1% of the time, Pallas kernels for 8%

profile of v7, /device:TPU:8, one launch (start us, length us, event | category | flops | bytes accessed | tf_op | source)
XLA Modules:
  0.0 110.2 jit_solution(17553646456331468850)
XLA Ops:
  0.6 1.6 %collective-permute-start = (bf16[1,512,128]{2,1,0:T(8,128)(2,1)}, bf16[1,512,128]{2,1,0:T(8,128)(2,1)S(1)}, u32[]{:S(2)}, u32[]{:S(2)}) collective-permute-start(bf16[1,512,128]{2,1,0:T(8,128)(2,1)} %rest_0_.2), channel_id=1, source_target_pairs={{0,2},{1,3},{2,4},{3,5},{4,6},{5,7},{6,0},{7,1},{8,10},{9,11},{10,... | collective-permute-start | bytes 393224 | tf_op jit(solution)/shard_map/ppermute | solution.py:348
  2.2 1.7 %collective-permute-start.1 = (bf16[1,512,128]{2,1,0:T(8,128)(2,1)}, bf16[1,512,128]{2,1,0:T(8,128)(2,1)S(1)}, u32[]{:S(2)}, u32[]{:S(2)}) collective-permute-start(bf16[1,512,128]{2,1,0:T(8,128)(2,1)} %rest_0_.2), channel_id=1, source_target_pairs={{0,6},{1,7},{2,0},{3,1},{4,2},{5,3},{6,4},{7,5},{8,14},{9,15},{10,... | collective-permute-start | bytes 393224 | tf_op jit(solution)/shard_map/ppermute | solution.py:348
  4.2 3.0 %collective-permute-start.3 = (bf16[1,512,128]{2,1,0:T(8,128)(2,1)}, bf16[1,512,128]{2,1,0:T(8,128)(2,1)S(1)}, u32[]{:S(2)}, u32[]{:S(2)}) collective-permute-start(bf16[1,512,128]{2,1,0:T(8,128)(2,1)} %rest_0_.3), channel_id=1, source_target_pairs={{0,6},{1,7},{2,0},{3,1},{4,2},{5,3},{6,4},{7,5},{8,14},{9,15},{10,... | collective-permute-start | bytes 393224 | tf_op jit(solution)/shard_map/ppermute | solution.py:348
  7.9 0.8 collective-permute-done.1.rest_2_
  8.7 1.7 %collective-permute-start.4 = (bf16[1,512,128]{2,1,0:T(8,128)(2,1)S(1)}, bf16[1,512,128]{2,1,0:T(8,128)(2,1)S(1)}, u32[]{:S(2)}, u32[]{:S(2)}) collective-permute-start(bf16[1,512,128]{2,1,0:T(8,128)(2,1)S(1)} %collective-permute-done.1.rest_2_), channel_id=1, source_target_pairs={{0,6},{1,7},{2,0},{3,1},{4,2},{5,3},{6,4},{7,5},{8,14},{9,15},{10,... | collective-permute-start | bytes 393224 | tf_op jit(solution)/shard_map/ppermute | solution.py:348
  10.9 3.4 %probe.1 = (bf16[32,128,256]{2,1,0:T(8,128)(2,1)S(1)}, bf16[32,512,128]{2,1,0:T(8,128)(2,1)S(1)}) custom-call(s32[4,8]{1,0:T(4,128)S(1)} %multiply_add_fusion.meta, bf16[4,8,512,128]{3,2,1,0:T(8,128)(2,1)} %right_u.1, bf16[4,8,512,128]{3,2,1,0:T(8,128)(2,1)} %right_v.3, bf16[4,512,128]{2,1,0:T(8,128)(2,1)} %sketch.1), custom_call_target="tpu_custom_call" | custom-call | flops 536870912 | bytes 6291456 | tf_op jit(solution)/shard_map/probe/pallas_call | solution.py:388
  16.2 2.6 %pair.1 = (bf16[32,256,128]{2,1,0:T(8,128)(2,1)S(1)}, bf16[32,128,128]{2,1,0:T(8,128)(2,1)S(1)}) custom-call(s32[4,8]{1,0:T(4,128)S(1)} %multiply_add_fusion.meta, bf16[32,512,128]{2,1,0:T(8,128)(2,1)S(1)} %get-tuple-element.37.held, bf16[32,128,256]{2,1,0:T(8,128)(2,1)S(1)} %get-tuple-element.38.probes, bf16[1,512,128]{2,1,0:T(8,128)(2,1)S(1)} %copy-done, ...), custom_call_target="tpu_custom_call" | custom-call | flops 939524096 | bytes 10485760 | tf_op jit(solution)/shard_map/pair/pallas_call | solution.py:405
  18.9 2.8 %collective-permute-done.5.rest_3_ = bf16[1,512,128]{2,1,0:T(8,128)(2,1)S(1)} collective-permute-done((bf16[1,512,128]{2,1,0:T(8,128)(2,1)S(1)}, bf16[1,512,128]{2,1,0:T(8,128)(2,1)S(1)}, u32[]{:S(2)}, u32[]{:S(2)}) %collective-permute-start.5) | collective-permute-done | bytes 131104 | tf_op jit(solution)/shard_map/ppermute | solution.py:348
  21.7 1.3 %collective-permute-done.13.rest_7_ = bf16[1,512,128]{2,1,0:T(8,128)(2,1)S(1)} collective-permute-done((bf16[1,512,128]{2,1,0:T(8,128)(2,1)S(1)}, bf16[1,512,128]{2,1,0:T(8,128)(2,1)S(1)}, u32[]{:S(2)}, u32[]{:S(2)}) %collective-permute-start.13) | collective-permute-done | bytes 131104 | tf_op jit(solution)/shard_map/ppermute | solution.py:352
  23.1 1.6 %sketch.2 = (f32[512,128]{1,0:T(8,128)S(1)}, bf16[512,128]{1,0:T(8,128)(2,1)S(1)}, bf16[512,128]{1,0:T(8,128)(2,1)S(1)}, bf16[512,128]{1,0:T(8,128)(2,1)S(1)}, bf16[8,512,128]{2,1,0:T(8,128)(2,1)S(1)}) custom-call(s32[4,8]{1,0:T(4,128)S(1)} %multiply_add_fusion.meta, bf16[32,128,128]{2,1,0:T(8,128)(2,1)S(1)} %get-tuple-element.42.mixing, ...), custom_call_target="tpu_custom_call" | custom-call | flops 536870912 | bytes 4194304 | tf_op jit(solution)/shard_map/sketch/pallas_call | solution.py:417
  24.6 2.0 %collective-permute-start.14 = (bf16[512,128]{1,0:T(8,128)(2,1)S(1)}, bf16[512,128]{1,0:T(8,128)(2,1)S(1)}, u32[]{:S(2)}, u32[]{:S(2)}) collective-permute-start(bf16[512,128]{1,0:T(8,128)(2,1)S(1)} %get-tuple-element.48), channel_id=1, source_target_pairs={{0,8},{8,16},{16,24},{24,0},{32,40},{40,48},{48,56},{56,32},{64,72... | collective-permute-start | bytes 393224 | tf_op jit(solution)/shard_map/ppermute | solution.py:344
  26.6 3.5 %collective-permute-start.15 = (bf16[512,128]{1,0:T(8,128)(2,1)S(1)}, bf16[512,128]{1,0:T(8,128)(2,1)S(1)}, u32[]{:S(2)}, u32[]{:S(2)}) collective-permute-start(bf16[512,128]{1,0:T(8,128)(2,1)S(1)} %get-tuple-element.49), channel_id=1, source_target_pairs={{0,16},{8,24},{16,0},{24,8},{32,48},{40,56},{48,32},{56,40},{64,80... | collective-permute-start | bytes 393224 | tf_op jit(solution)/shard_map/ppermute | solution.py:344
  30.1 2.2 %collective-permute-done.14 = bf16[512,128]{1,0:T(8,128)(2,1)S(1)} collective-permute-done((bf16[512,128]{1,0:T(8,128)(2,1)S(1)}, bf16[512,128]{1,0:T(8,128)(2,1)S(1)}, u32[]{:S(2)}, u32[]{:S(2)}) %collective-permute-start.14) | collective-permute-done | bytes 131104 | tf_op jit(solution)/shard_map/ppermute | solution.py:344
  32.3 2.1 %collective-permute-done.15 = bf16[512,128]{1,0:T(8,128)(2,1)S(1)} collective-permute-done((bf16[512,128]{1,0:T(8,128)(2,1)S(1)}, bf16[512,128]{1,0:T(8,128)(2,1)S(1)}, u32[]{:S(2)}, u32[]{:S(2)}) %collective-permute-start.15) | collective-permute-done | bytes 131104 | tf_op jit(solution)/shard_map/ppermute | solution.py:344
  34.5 2.0 %collective-permute-done.16 = bf16[512,128]{1,0:T(8,128)(2,1)S(1)} collective-permute-done((bf16[512,128]{1,0:T(8,128)(2,1)S(1)}, bf16[512,128]{1,0:T(8,128)(2,1)S(1)}, u32[]{:S(2)}, u32[]{:S(2)}) %collective-permute-start.16) | collective-permute-done | bytes 131104 | tf_op jit(solution)/shard_map/ppermute | solution.py:344
  36.6 18.6 %all_to_all.15 = f32[8,64,128]{2,1,0:T(8,128)} all-to-all(f32[8,64,128]{2,1,0:T(8,128)S(1)} %bitcast.1), channel_id=1, replica_groups={{0,32,64,96,128,160,192,224},{8,40,72,104,136,168,200,232},{16,48,80,11..., dimensions={0} | all-to-all | bytes 524288 | tf_op jit(solution)/shard_map/all_to_all | solution.py:362
  55.1 1.0 reduce_sum.18
  56.1 12.9 %all_to_all.16.blocks = f32[8,64,128]{2,1,0:T(8,128)S(1)} all-to-all(f32[8,64,128]{2,1,0:T(8,128)S(1)} %broadcast_in_dim.2), channel_id=1, replica_groups={{0,32,64,96,128,160,192,224},{8,40,72,104,136,168,200,232},{16,48,80,11..., dimensions={0} | all-to-all | bytes 524288 | tf_op jit(solution)/shard_map/all_to_all | solution.py:362
  69.0 7.0 %ortho.1 = (bf16[544,128]{1,0:T(8,128)(2,1)S(1)}, bf16[544,128]{1,0:T(8,128)(2,1)S(1)}, bf16[544,128]{1,0:T(8,128)(2,1)S(1)}, bf16[544,128]{1,0:T(8,128)(2,1)S(1)}) custom-call(f32[8,64,128]{2,1,0:T(8,128)S(1)} %all_to_all.16.blocks), custom_call_target="tpu_custom_call" | custom-call | flops 218103808 | bytes 1048576 | tf_op jit(solution)/shard_map/ortho/pallas_call | solution.py:434
  76.0 1.3 %collective-permute-start.17 = (bf16[544,128]{1,0:T(8,128)(2,1)S(1)}, bf16[544,128]{1,0:T(8,128)(2,1)S(1)}, u32[]{:S(2)}, u32[]{:S(2)}) collective-permute-start(bf16[544,128]{1,0:T(8,128)(2,1)S(1)} %get-tuple-element.54), channel_id=1, source_target_pairs={{0,8},{8,16},{16,24},{24,0},{32,40},{40,48},{48,56},{56,32},{64,72... | collective-permute-start | bytes 417800 | tf_op jit(solution)/shard_map/ppermute | solution.py:344
  77.3 1.4 %collective-permute-start.18 = (bf16[544,128]{1,0:T(8,128)(2,1)S(1)}, bf16[544,128]{1,0:T(8,128)(2,1)S(1)}, u32[]{:S(2)}, u32[]{:S(2)}) collective-permute-start(bf16[544,128]{1,0:T(8,128)(2,1)S(1)} %get-tuple-element.55), channel_id=1, source_target_pairs={{0,16},{8,24},{16,0},{24,8},{32,48},{40,56},{48,32},{56,40},{64,80... | collective-permute-start | bytes 417800 | tf_op jit(solution)/shard_map/ppermute | solution.py:344
  78.7 1.6 %collective-permute-start.19 = (bf16[544,128]{1,0:T(8,128)(2,1)S(1)}, bf16[544,128]{1,0:T(8,128)(2,1)S(1)}, u32[]{:S(2)}, u32[]{:S(2)}) collective-permute-start(bf16[544,128]{1,0:T(8,128)(2,1)S(1)} %get-tuple-element.56), channel_id=1, source_target_pairs={{0,24},{8,0},{16,8},{24,16},{32,56},{40,32},{48,40},{56,48},{64,88... | collective-permute-start | bytes 417800 | tf_op jit(solution)/shard_map/ppermute | solution.py:344
  80.3 2.7 %backward_own.1 = (f32[1,512,128]{2,1,0:T(8,128)S(1)}, bf16[32,512,128]{2,1,0:T(8,128)(2,1)S(1)}) custom-call(s32[4,8]{1,0:T(4,128)S(1)} %multiply_add_fusion.meta, bf16[4,8,512,128]{3,2,1,0:T(8,128)(2,1)} %right_v.3, bf16[8,512,128]{2,1,0:T(8,128)(2,1)S(1)} %get-tuple-element.45.group, bf16[32,256,128]{2,1,0:T(8,128)(2,1)S(1)} %get-tuple-element.46.pairs, ...), custom_call_target="tpu_custom_call" | custom-call | flops 369098752 | bytes 4194304 | tf_op jit(solution)/shard_map/backward_own/pallas_call | solution.py:444
  83.0 1.0 collective-permute-done.18.msg2
  84.0 1.3 %collective-permute-done.19.msg3 = bf16[544,128]{1,0:T(8,128)(2,1)S(1)} collective-permute-done((bf16[544,128]{1,0:T(8,128)(2,1)S(1)}, bf16[544,128]{1,0:T(8,128)(2,1)S(1)}, u32[]{:S(2)}, u32[]{:S(2)}) %collective-permute-start.19) | collective-permute-done | bytes 139296 | tf_op jit(solution)/shard_map/ppermute | solution.py:344
  85.3 2.8 %backward.1 = (f32[8,4,16,128]{3,2,1,0:T(8,128)S(1)}, bf16[8,4,16,128]{3,2,1,0:T(8,128)(2,1)S(1)}, bf16[8,4,16,128]{3,2,1,0:T(8,128)(2,1)S(1)}, bf16[8,4,16,128]{3,2,1,0:T(8,128)(2,1)S(1)}, f32[4,16,128]{2,1,0:T(8,128)}) custom-call(s32[4,8]{1,0:T(4,128)S(1)} %multiply_add_fusion.meta, bf16[32,512,128]{2,1,0:T(8,128)(2,1)S(1)} %get-tuple-element.52.held, ...), custom_call_target="tpu_custom_call" | custom-call | flops 1073741824 | bytes 8388608 | tf_op jit(solution)/shard_map/backward/pallas_call | solution.py:456
  88.0 0.7 collective-permute-start.20
  88.7 1.5 %collective-permute-start.21 = (bf16[8,4,16,128]{3,2,1,0:T(8,128)(2,1)S(1)}, bf16[8,4,16,128]{3,2,1,0:T(8,128)(2,1)S(1)}, u32[]{:S(2)}, u32[]{:S(2)}) collective-permute-start(bf16[8,4,16,128]{3,2,1,0:T(8,128)(2,1)S(1)} %get-tuple-element.60), channel_id=1, source_target_pairs={{0,16},{8,24},{16,0},{24,8},{32,48},{40,56},{48,32},{56,40},{64,80... | collective-permute-start | bytes 393224 | tf_op jit(solution)/shard_map/ppermute | solution.py:344
  90.2 2.3 %collective-permute-start.22 = (bf16[8,4,16,128]{3,2,1,0:T(8,128)(2,1)S(1)}, bf16[8,4,16,128]{3,2,1,0:T(8,128)(2,1)S(1)}, u32[]{:S(2)}, u32[]{:S(2)}) collective-permute-start(bf16[8,4,16,128]{3,2,1,0:T(8,128)(2,1)S(1)} %get-tuple-element.61), channel_id=1, source_target_pairs={{0,24},{8,0},{16,8},{24,16},{32,56},{40,32},{48,40},{56,48},{64,88... | collective-permute-start | bytes 393224 | tf_op jit(solution)/shard_map/ppermute | solution.py:344
  93.0 2.3 %collective-permute-done.21 = bf16[8,4,16,128]{3,2,1,0:T(8,128)(2,1)S(1)} collective-permute-done((bf16[8,4,16,128]{3,2,1,0:T(8,128)(2,1)S(1)}, bf16[8,4,16,128]{3,2,1,0:T(8,128)(2,1)S(1)}, u32[]{:S(2)}, u32[]{:S(2)}) %collective-permute-start.21) | collective-permute-done | bytes 131104 | tf_op jit(solution)/shard_map/ppermute | solution.py:344
  95.3 1.3 %collective-permute-done.22 = bf16[8,4,16,128]{3,2,1,0:T(8,128)(2,1)S(1)} collective-permute-done((bf16[8,4,16,128]{3,2,1,0:T(8,128)(2,1)S(1)}, bf16[8,4,16,128]{3,2,1,0:T(8,128)(2,1)S(1)}, u32[]{:S(2)}, u32[]{:S(2)}) %collective-permute-start.22) | collective-permute-done | bytes 131104 | tf_op jit(solution)/shard_map/ppermute | solution.py:344
  96.7 12.9 %all_to_all.17 = f32[8,4,16,128]{3,2,1,0:T(8,128)S(1)} all-to-all(f32[8,4,16,128]{3,2,1,0:T(8,128)S(1)} %convert_add_fusion), channel_id=1, replica_groups={{0,32,64,96,128,160,192,224},{8,40,72,104,136,168,200,232},{16,48,80,11..., dimensions={0} | all-to-all | bytes 524288 | tf_op jit(solution)/shard_map/all_to_all | solution.py:362
  (33 shorter events, 4.6 us)
Async XLA Ops:
  0.6 7.3 %collective-permute-start = (bf16[1,512,128]{2,1,0:T(8,128)(2,1)}, bf16[1,512,128]{2,1,0:T(8,128)(2,1)S(1)}, u32[]{:S(2)}, u32[]{:S(2)}) collective-permute-start(bf16[1,512,128]{2,1,0:T(8,128)(2,1)} %rest_0_.2), channel_id=1, source_target_pairs={{0,2},{1,3},{2,4},{3,5},{4,6},{5,7},{6,0},{7,1},{8,10},{9,11},{10,... | collective-permute-start | bytes 393224 | tf_op jit(solution)/shard_map/ppermute | solution.py:348
  2.2 6.5 %collective-permute-start.1 = (bf16[1,512,128]{2,1,0:T(8,128)(2,1)}, bf16[1,512,128]{2,1,0:T(8,128)(2,1)S(1)}, u32[]{:S(2)}, u32[]{:S(2)}) collective-permute-start(bf16[1,512,128]{2,1,0:T(8,128)(2,1)} %rest_0_.2), channel_id=1, source_target_pairs={{0,6},{1,7},{2,0},{3,1},{4,2},{5,3},{6,4},{7,5},{8,14},{9,15},{10,... | collective-permute-start | bytes 393224 | tf_op jit(solution)/shard_map/ppermute | solution.py:348
  3.9 10.4 %collective-permute-start.2 = (bf16[1,512,128]{2,1,0:T(8,128)(2,1)}, bf16[1,512,128]{2,1,0:T(8,128)(2,1)S(1)}, u32[]{:S(2)}, u32[]{:S(2)}) collective-permute-start(bf16[1,512,128]{2,1,0:T(8,128)(2,1)} %rest_0_.3), channel_id=1, source_target_pairs={{0,2},{1,3},{2,4},{3,5},{4,6},{5,7},{6,0},{7,1},{8,10},{9,11},{10,... | collective-permute-start | bytes 393224 | tf_op jit(solution)/shard_map/ppermute | solution.py:348
  4.2 10.3 %collective-permute-start.3 = (bf16[1,512,128]{2,1,0:T(8,128)(2,1)}, bf16[1,512,128]{2,1,0:T(8,128)(2,1)S(1)}, u32[]{:S(2)}, u32[]{:S(2)}) collective-permute-start(bf16[1,512,128]{2,1,0:T(8,128)(2,1)} %rest_0_.3), channel_id=1, source_target_pairs={{0,6},{1,7},{2,0},{3,1},{4,2},{5,3},{6,4},{7,5},{8,14},{9,15},{10,... | collective-permute-start | bytes 393224 | tf_op jit(solution)/shard_map/ppermute | solution.py:348
  7.9 7.5 %copy-start.1 = (bf16[1,512,128]{2,1,0:T(8,128)(2,1)S(1)}, bf16[1,512,128]{2,1,0:T(8,128)(2,1)}, u32[]{:S(2)}) copy-start(bf16[1,512,128]{2,1,0:T(8,128)(2,1)} %rest_0_.3) | copy-start | bytes 393220
  7.9 8.3 %copy-start = (bf16[1,512,128]{2,1,0:T(8,128)(2,1)S(1)}, bf16[1,512,128]{2,1,0:T(8,128)(2,1)}, u32[]{:S(2)}) copy-start(bf16[1,512,128]{2,1,0:T(8,128)(2,1)} %rest_0_.2) | copy-start | bytes 393220
  8.7 5.8 %collective-permute-start.4 = (bf16[1,512,128]{2,1,0:T(8,128)(2,1)S(1)}, bf16[1,512,128]{2,1,0:T(8,128)(2,1)S(1)}, u32[]{:S(2)}, u32[]{:S(2)}) collective-permute-start(bf16[1,512,128]{2,1,0:T(8,128)(2,1)S(1)} %collective-permute-done.1.rest_2_), channel_id=1, source_target_pairs={{0,6},{1,7},{2,0},{3,1},{4,2},{5,3},{6,4},{7,5},{8,14},{9,15},{10,... | collective-permute-start | bytes 393224 | tf_op jit(solution)/shard_map/ppermute | solution.py:348
  10.4 5.0 %collective-permute-start.6 = (bf16[1,512,128]{2,1,0:T(8,128)(2,1)}, bf16[1,512,128]{2,1,0:T(8,128)(2,1)S(1)}, u32[]{:S(2)}, u32[]{:S(2)}) collective-permute-start(bf16[1,512,128]{2,1,0:T(8,128)(2,1)} %rest_0_.2), channel_id=1, source_target_pairs={{0,1},{1,0},{2,3},{3,2},{4,5},{5,4},{6,7},{7,6},{8,9},{9,8},{10,11... | collective-permute-start | bytes 393224 | tf_op jit(solution)/shard_map/ppermute | solution.py:352
  10.4 5.0 %collective-permute-start.8 = (bf16[1,512,128]{2,1,0:T(8,128)(2,1)S(1)}, bf16[1,512,128]{2,1,0:T(8,128)(2,1)S(1)}, u32[]{:S(2)}, u32[]{:S(2)}) collective-permute-start(bf16[1,512,128]{2,1,0:T(8,128)(2,1)S(1)} %collective-permute-done.1.rest_2_), channel_id=1, source_target_pairs={{0,1},{1,0},{2,3},{3,2},{4,5},{5,4},{6,7},{7,6},{8,9},{9,8},{10,11... | collective-permute-start | bytes 393224 | tf_op jit(solution)/shard_map/ppermute | solution.py:352
  14.4 1.6 %collective-permute-start.7 = (bf16[1,512,128]{2,1,0:T(8,128)(2,1)S(1)}, bf16[1,512,128]{2,1,0:T(8,128)(2,1)S(1)}, u32[]{:S(2)}, u32[]{:S(2)}) collective-permute-start(bf16[1,512,128]{2,1,0:T(8,128)(2,1)S(1)} %collective-permute-done.rest_1_), channel_id=1, source_target_pairs={{0,1},{1,0},{2,3},{3,2},{4,5},{5,4},{6,7},{7,6},{8,9},{9,8},{10,11... | collective-permute-start | bytes 393224 | tf_op jit(solution)/shard_map/ppermute | solution.py:352
  14.6 1.7 %collective-permute-start.9 = (bf16[1,512,128]{2,1,0:T(8,128)(2,1)S(1)}, bf16[1,512,128]{2,1,0:T(8,128)(2,1)S(1)}, u32[]{:S(2)}, u32[]{:S(2)}) collective-permute-start(bf16[1,512,128]{2,1,0:T(8,128)(2,1)S(1)} %collective-permute-done.4.rest_3_), channel_id=1, source_target_pairs={{0,1},{1,0},{2,3},{3,2},{4,5},{5,4},{6,7},{7,6},{8,9},{9,8},{10,11... | collective-permute-start | bytes 393224 | tf_op jit(solution)/shard_map/ppermute | solution.py:352
  15.0 6.7 %collective-permute-start.5 = (bf16[1,512,128]{2,1,0:T(8,128)(2,1)S(1)}, bf16[1,512,128]{2,1,0:T(8,128)(2,1)S(1)}, u32[]{:S(2)}, u32[]{:S(2)}) collective-permute-start(bf16[1,512,128]{2,1,0:T(8,128)(2,1)S(1)} %collective-permute-done.2.rest_1_), channel_id=1, source_target_pairs={{0,2},{1,3},{2,4},{3,5},{4,6},{5,7},{6,0},{7,1},{8,10},{9,11},{10,... | collective-permute-start | bytes 393224 | tf_op jit(solution)/shard_map/ppermute | solution.py:348
  15.4 6.3 %collective-permute-start.10 = (bf16[1,512,128]{2,1,0:T(8,128)(2,1)S(1)}, bf16[1,512,128]{2,1,0:T(8,128)(2,1)S(1)}, u32[]{:S(2)}, u32[]{:S(2)}) collective-permute-start(bf16[1,512,128]{2,1,0:T(8,128)(2,1)S(1)} %copy-done.1), channel_id=1, source_target_pairs={{0,1},{1,0},{2,3},{3,2},{4,5},{5,4},{6,7},{7,6},{8,9},{9,8},{10,11... | collective-permute-start | bytes 393224 | tf_op jit(solution)/shard_map/ppermute | solution.py:352
  15.5 6.3 %collective-permute-start.11 = (bf16[1,512,128]{2,1,0:T(8,128)(2,1)S(1)}, bf16[1,512,128]{2,1,0:T(8,128)(2,1)S(1)}, u32[]{:S(2)}, u32[]{:S(2)}) collective-permute-start(bf16[1,512,128]{2,1,0:T(8,128)(2,1)S(1)} %collective-permute-done.2.rest_1_), channel_id=1, source_target_pairs={{0,1},{1,0},{2,3},{3,2},{4,5},{5,4},{6,7},{7,6},{8,9},{9,8},{10,11... | collective-permute-start | bytes 393224 | tf_op jit(solution)/shard_map/ppermute | solution.py:352
  16.0 5.8 %collective-permute-start.12 = (bf16[1,512,128]{2,1,0:T(8,128)(2,1)S(1)}, bf16[1,512,128]{2,1,0:T(8,128)(2,1)S(1)}, u32[]{:S(2)}, u32[]{:S(2)}) collective-permute-start(bf16[1,512,128]{2,1,0:T(8,128)(2,1)S(1)} %collective-permute-done.3.rest_2_), channel_id=1, source_target_pairs={{0,1},{1,0},{2,3},{3,2},{4,5},{5,4},{6,7},{7,6},{8,9},{9,8},{10,11... | collective-permute-start | bytes 393224 | tf_op jit(solution)/shard_map/ppermute | solution.py:352
  21.7 1.3 %collective-permute-start.13 = (bf16[1,512,128]{2,1,0:T(8,128)(2,1)S(1)}, bf16[1,512,128]{2,1,0:T(8,128)(2,1)S(1)}, u32[]{:S(2)}, u32[]{:S(2)}) collective-permute-start(bf16[1,512,128]{2,1,0:T(8,128)(2,1)S(1)} %collective-permute-done.5.rest_3_), channel_id=1, source_target_pairs={{0,1},{1,0},{2,3},{3,2},{4,5},{5,4},{6,7},{7,6},{8,9},{9,8},{10,11... | collective-permute-start | bytes 393224 | tf_op jit(solution)/shard_map/ppermute | solution.py:352
  24.6 7.7 %collective-permute-start.14 = (bf16[512,128]{1,0:T(8,128)(2,1)S(1)}, bf16[512,128]{1,0:T(8,128)(2,1)S(1)}, u32[]{:S(2)}, u32[]{:S(2)}) collective-permute-start(bf16[512,128]{1,0:T(8,128)(2,1)S(1)} %get-tuple-element.48), channel_id=1, source_target_pairs={{0,8},{8,16},{16,24},{24,0},{32,40},{40,48},{48,56},{56,32},{64,72... | collective-permute-start | bytes 393224 | tf_op jit(solution)/shard_map/ppermute | solution.py:344
  26.6 7.8 %collective-permute-start.15 = (bf16[512,128]{1,0:T(8,128)(2,1)S(1)}, bf16[512,128]{1,0:T(8,128)(2,1)S(1)}, u32[]{:S(2)}, u32[]{:S(2)}) collective-permute-start(bf16[512,128]{1,0:T(8,128)(2,1)S(1)} %get-tuple-element.49), channel_id=1, source_target_pairs={{0,16},{8,24},{16,0},{24,8},{32,48},{40,56},{48,32},{56,40},{64,80... | collective-permute-start | bytes 393224 | tf_op jit(solution)/shard_map/ppermute | solution.py:344
  30.1 6.4 %collective-permute-start.16 = (bf16[512,128]{1,0:T(8,128)(2,1)S(1)}, bf16[512,128]{1,0:T(8,128)(2,1)S(1)}, u32[]{:S(2)}, u32[]{:S(2)}) collective-permute-start(bf16[512,128]{1,0:T(8,128)(2,1)S(1)} %get-tuple-element.50), channel_id=1, source_target_pairs={{0,24},{8,0},{16,8},{24,16},{32,56},{40,32},{48,40},{56,48},{64,88... | collective-permute-start | bytes 393224 | tf_op jit(solution)/shard_map/ppermute | solution.py:344
  76.0 7.0 %collective-permute-start.17 = (bf16[544,128]{1,0:T(8,128)(2,1)S(1)}, bf16[544,128]{1,0:T(8,128)(2,1)S(1)}, u32[]{:S(2)}, u32[]{:S(2)}) collective-permute-start(bf16[544,128]{1,0:T(8,128)(2,1)S(1)} %get-tuple-element.54), channel_id=1, source_target_pairs={{0,8},{8,16},{16,24},{24,0},{32,40},{40,48},{48,56},{56,32},{64,72... | collective-permute-start | bytes 417800 | tf_op jit(solution)/shard_map/ppermute | solution.py:344
  77.3 6.7 %collective-permute-start.18 = (bf16[544,128]{1,0:T(8,128)(2,1)S(1)}, bf16[544,128]{1,0:T(8,128)(2,1)S(1)}, u32[]{:S(2)}, u32[]{:S(2)}) collective-permute-start(bf16[544,128]{1,0:T(8,128)(2,1)S(1)} %get-tuple-element.55), channel_id=1, source_target_pairs={{0,16},{8,24},{16,0},{24,8},{32,48},{40,56},{48,32},{56,40},{64,80... | collective-permute-start | bytes 417800 | tf_op jit(solution)/shard_map/ppermute | solution.py:344
  78.7 6.5 %collective-permute-start.19 = (bf16[544,128]{1,0:T(8,128)(2,1)S(1)}, bf16[544,128]{1,0:T(8,128)(2,1)S(1)}, u32[]{:S(2)}, u32[]{:S(2)}) collective-permute-start(bf16[544,128]{1,0:T(8,128)(2,1)S(1)} %get-tuple-element.56), channel_id=1, source_target_pairs={{0,24},{8,0},{16,8},{24,16},{32,56},{40,32},{48,40},{56,48},{64,88... | collective-permute-start | bytes 417800 | tf_op jit(solution)/shard_map/ppermute | solution.py:344
  88.0 5.0 %collective-permute-start.20 = (bf16[8,4,16,128]{3,2,1,0:T(8,128)(2,1)S(1)}, bf16[8,4,16,128]{3,2,1,0:T(8,128)(2,1)S(1)}, u32[]{:S(2)}, u32[]{:S(2)}) collective-permute-start(bf16[8,4,16,128]{3,2,1,0:T(8,128)(2,1)S(1)} %get-tuple-element.59), channel_id=1, source_target_pairs={{0,8},{8,16},{16,24},{24,0},{32,40},{40,48},{48,56},{56,32},{64,72... | collective-permute-start | bytes 393224 | tf_op jit(solution)/shard_map/ppermute | solution.py:344
  88.7 6.6 %collective-permute-start.21 = (bf16[8,4,16,128]{3,2,1,0:T(8,128)(2,1)S(1)}, bf16[8,4,16,128]{3,2,1,0:T(8,128)(2,1)S(1)}, u32[]{:S(2)}, u32[]{:S(2)}) collective-permute-start(bf16[8,4,16,128]{3,2,1,0:T(8,128)(2,1)S(1)} %get-tuple-element.60), channel_id=1, source_target_pairs={{0,16},{8,24},{16,0},{24,8},{32,48},{40,56},{48,32},{56,40},{64,80... | collective-permute-start | bytes 393224 | tf_op jit(solution)/shard_map/ppermute | solution.py:344
  90.2 6.4 %collective-permute-start.22 = (bf16[8,4,16,128]{3,2,1,0:T(8,128)(2,1)S(1)}, bf16[8,4,16,128]{3,2,1,0:T(8,128)(2,1)S(1)}, u32[]{:S(2)}, u32[]{:S(2)}) collective-permute-start(bf16[8,4,16,128]{3,2,1,0:T(8,128)(2,1)S(1)} %get-tuple-element.61), channel_id=1, source_target_pairs={{0,24},{8,0},{16,8},{24,16},{32,56},{40,32},{48,40},{56,48},{64,88... | collective-permute-start | bytes 393224 | tf_op jit(solution)/shard_map/ppermute | solution.py:344

commit v8 on v7

--- a/solution.py
+++ b/solution.py
@@ -117,34 +117,35 @@
     return [tiles[:2], tiles[2:]]
 
 
-def probe_kernel(outs, slots, meta, right_u, right_v, sketch, probes, held_u, held, plain, sems_u, sems, sem):
+def load_kernel(outs, slots, meta, right_u, right_v, sketch, held_u, held_v, plain, sems_u, sems_v, sem):
     copy = pltpu.make_async_copy(sketch, plain, sem)
     copy.start()
-    fetch(meta, outs, slots, right_v, held, sems)
+    fetch(meta, outs, slots, right_v, held_v, sems_v)
     fetch(meta, outs, slots, right_u, held_u, sems_u)
     copy.wait()
 
+    def tile(j, _):
+        def one(s, _):
+            at = j * slots + s
+            pltpu.make_async_copy(right_v.at[j, s], held_v.at[at], sems_v.at[at]).wait()
+            pltpu.make_async_copy(right_u.at[j, s], held_u.at[at], sems_u.at[at]).wait()
+            return 0
+
+        lax.fori_loop(0, live(meta, j), one, 0)
+        return 0
+
+    lax.fori_loop(0, outs, tile, 0)
+
+
+def probe_kernel(outs, slots, meta, held, sketch, probes):
     def work(items, first):
-        for _, j, base, count in items:
-            for i in range(BATCH):
-                arrive(count, slots, j, base + i, right_v, held, sems)
-        turned = [plain[j].T for _, j, _, _ in items]
+        turned = [sketch[j].T for _, j, _, _ in items]
         at = batches(items, slots)
         products = [dot(turned[n // BATCH], held[slot]) for n, (slot, _, _) in enumerate(at)]
         for (slot, _, _), product in zip(at, products):
             probes[slot] = beside(*halves(product))
 
     sweep(meta, two_by_two([(j, j) for j in range(outs)]), work)
-
-    def tile(j, _):
-        def one(s, _):
-            pltpu.make_async_copy(right_u.at[j, s], held_u.at[j * slots + s], sems_u.at[j * slots + s]).wait()
-            return 0
-
-        lax.fori_loop(0, live(meta, j), one, 0)
-        return 0
-
-    lax.fori_loop(0, outs, tile, 0)
 
 
 def tile_ids(tiles):
@@ -382,20 +383,28 @@
 
     near = [hop(value, step, tiles) for value in (left_v, left_u) for step in (1, -1)]
     near_v, near_u = near[:2], near[2:]
-    *near_v, sketch, packed = lax.optimization_barrier((*near_v, sketch, packed))
+    sketch = pltpu.with_memory_space_constraint(sketch, pltpu.HBM)
+    held_u, held_v, sketch = pl.pallas_call(
+        functools.partial(load_kernel, outs, slots),
+        out_shape=(shape((count, NB, R), BF),) * 2 + (shape(sketch.shape, BF),),
+        in_specs=[in_smem()] + [in_place()] * 3,
+        out_specs=(in_vmem(),) * 3,
+        scratch_shapes=[pltpu.SemaphoreType.DMA((count,))] * 2 + [pltpu.SemaphoreType.DMA],
+        compiler_params=params(),
+        cost_estimate=cost(0, 9),
+        name="load",
+    )(packed, right_u, right_v, sketch)
+    *near_v, sketch = lax.optimization_barrier((*near_v, sketch))
     far_v = hop(near_v[1], -1, tiles)
-    sketch = pltpu.with_memory_space_constraint(sketch, pltpu.HBM)
-    probes, held_u = pl.pallas_call(
+    probes = pl.pallas_call(
         functools.partial(probe_kernel, outs, slots),
-        out_shape=(shape((count, R, 2 * R), BF),) + (shape((count, NB, R), BF),),
-        in_specs=[in_smem(), in_place(), in_place(), in_place()],
-        out_specs=(in_vmem(),) * 2,
-        scratch_shapes=[VMEM((count, NB, R), BF), VMEM((outs, NB, R), BF)]
-        + [pltpu.SemaphoreType.DMA((count,))] * 2 + [pltpu.SemaphoreType.DMA],
+        out_shape=shape((count, R, 2 * R), BF),
+        in_specs=[in_smem()] + [in_vmem()] * 2,
+        out_specs=in_vmem(),
         compiler_params=params(),
         cost_estimate=cost(outs * slots, 6),
         name="probe",
-    )(packed, right_u, right_v, sketch)
+    )(packed, held_v, sketch)
     *near_u, far_v, probes = lax.optimization_barrier((*near_u, far_v, probes))
     far_u = hop(near_u[0], 1, tiles)
     group_v = [left_v, *near_v, far_v]
@@ -441,7 +450,7 @@
         cost_estimate=cost(13, 1),
         name="ortho",
     )(summed)
-    mine, held_v = pl.pallas_call(
+    mine, held = pl.pallas_call(
         functools.partial(backward_own_kernel, outs, slots),
         out_shape=(shape((1, NB, R), F32), shape((count, NB, R), BF)),
         in_specs=[in_smem(), in_place()] + [in_vmem()] * 3,
@@ -462,11 +471,11 @@
         compiler_params=params(),
         cost_estimate=cost(outs * slots * 2, 8),
         name="backward",
-    )(packed, held_v, group, pairs, mine, *messages)
+    )(packed, held, group, pairs, mine, *messages)
     part = own
     for got in spread((send1, send2, send3), zs):
         part = part + got.astype(F32)
-    coeff = jnp.sum(over_z(part, zs), axis=0)
+    coeff = jnp.sum(over_z(part.astype(BF), zs).astype(F32), axis=0)
     return (basis, coeff)
 
 

time: 111 us -> 110 us (level)
  starting transfers between devices: 24.9 us -> 21 us
  Pallas kernels: 20 us -> 23.8 us
    ppermute x6, starting transfers between devices: 8.72 us -> 6.72 us  [hop(): lax.ppermute(value, 'cols', [(i, (i + 2 * step) % tiles) for i in range(t...]
    ppermute x9, starting transfers between devices: 14.3 us -> 12.6 us  [shift_y(): return lax.ppermute(array, 'inner', pairs)]
    pallas_call x1 -> x2, Pallas kernels: 3.39 us -> 5.04 us  [the longest x1 3.34 us: body(): pl.pallas_call(functools.partial(load_kernel, outs, slots), out_shape=(sh...]
    ppermute x9, waiting for transfers between devices: 12.7 us -> 11.3 us  [shift_y(): return lax.ppermute(array, 'inner', pairs)]
    ppermute x6, waiting for transfers between devices: 3.67 us -> 4.98 us  [hop(): lax.ppermute(value, 'cols', [(i, (i + 2 * step) % tiles) for i in range(t...]
  transfers between devices with their start and end apart: 23 -> 23, of which waited for: 11 -> 11; matrix products, arithmetic and copies ran while one was open for 1% -> 1% of each run, Pallas kernels for 8% -> 10%
where the time goes in v8:
time: 110 us
  blocking collectives  43.7 us (40%)
  Pallas kernels  23.8 us (22%)
  starting transfers between devices  21 us (19%)
  waiting for transfers between devices  17.9 us (16%)
  other arithmetic  2.44 us (2%)
    all_to_all x3, blocking collectives, over_z(): lax.all_to_all(array, 'inner', 0, 0, tiled=True, axis_index_groups=groups)  43.7 us
    ppermute x9, starting transfers between devices, shift_y(): return lax.ppermute(array, 'inner', pairs)  12.6 us
    ppermute x9, waiting for transfers between devices, shift_y(): return lax.ppermute(array, 'inner', pairs)  11.3 us
    pallas_call x1, Pallas kernels, body(): pl.pallas_call(functools.partial(ortho_kernel, zs), out_shape=(shape((NB...  6.97 us
    ppermute x6, starting transfers between devices, hop(): lax.ppermute(value, 'cols', [(i, (i + 2 * step) % tiles) for i in range(t...  6.72 us
    ppermute x6, waiting for transfers between devices, hop(): lax.ppermute(value, 'cols', [(i, (i + 2 * step) % tiles) for i in range(t...  4.98 us
    pallas_call x1, Pallas kernels, body(): pl.pallas_call(functools.partial(backward_kernel, slots, zs), out_shape=(...  3.48 us
    pallas_call x1, Pallas kernels, body(): pl.pallas_call(functools.partial(load_kernel, outs, slots), out_shape=(sh...  3.34 us
  transfers between devices with their start and end apart: 23, of which 11 were waited for; matrix products, arithmetic and copies ran while one was open for 1% of the time, Pallas kernels for 10%

profile of v8, /device:TPU:8, one launch (start us, length us, event | category | flops | bytes accessed | tf_op | source)
XLA Modules:
  0.0 109.6 jit_solution(6981685367267682616)
XLA Ops:
  0.6 1.6 %collective-permute-start.2 = (bf16[1,512,128]{2,1,0:T(8,128)(2,1)}, bf16[1,512,128]{2,1,0:T(8,128)(2,1)S(1)}, u32[]{:S(2)}, u32[]{:S(2)}) collective-permute-start(bf16[1,512,128]{2,1,0:T(8,128)(2,1)} %rest_0_.2), channel_id=1, source_target_pairs={{0,2},{1,3},{2,4},{3,5},{4,6},{5,7},{6,0},{7,1},{8,10},{9,11},{10,... | collective-permute-start | bytes 393224 | tf_op jit(solution)/shard_map/ppermute | solution.py:349
  2.2 1.7 %collective-permute-start.3 = (bf16[1,512,128]{2,1,0:T(8,128)(2,1)}, bf16[1,512,128]{2,1,0:T(8,128)(2,1)S(1)}, u32[]{:S(2)}, u32[]{:S(2)}) collective-permute-start(bf16[1,512,128]{2,1,0:T(8,128)(2,1)} %rest_0_.2), channel_id=1, source_target_pairs={{0,6},{1,7},{2,0},{3,1},{4,2},{5,3},{6,4},{7,5},{8,14},{9,15},{10,... | collective-permute-start | bytes 393224 | tf_op jit(solution)/shard_map/ppermute | solution.py:349
  4.2 3.0 %collective-permute-start.1 = (bf16[1,512,128]{2,1,0:T(8,128)(2,1)}, bf16[1,512,128]{2,1,0:T(8,128)(2,1)S(1)}, u32[]{:S(2)}, u32[]{:S(2)}) collective-permute-start(bf16[1,512,128]{2,1,0:T(8,128)(2,1)} %rest_0_.3), channel_id=1, source_target_pairs={{0,6},{1,7},{2,0},{3,1},{4,2},{5,3},{6,4},{7,5},{8,14},{9,15},{10,... | collective-permute-start | bytes 393224 | tf_op jit(solution)/shard_map/ppermute | solution.py:349
  7.2 0.7 multiply_add_fusion.meta
  7.9 3.3 %load.1 = (bf16[32,512,128]{2,1,0:T(8,128)(2,1)S(1)}, bf16[32,512,128]{2,1,0:T(8,128)(2,1)S(1)}, bf16[4,512,128]{2,1,0:T(8,128)(2,1)S(1)}) custom-call(s32[4,8]{1,0:T(4,128)S(1)} %multiply_add_fusion.meta, bf16[4,8,512,128]{3,2,1,0:T(8,128)(2,1)} %right_u.1, bf16[4,8,512,128]{3,2,1,0:T(8,128)(2,1)} %right_v.3, bf16[4,512,128]{2,1,0:T(8,128)(2,1)} %sketch.2), custom_call_target="tpu_custom_call" | custom-call | bytes 9437184 | tf_op jit(solution)/shard_map/load/pallas_call | solution.py:387
  12.0 1.7 %probe.1.probes = bf16[32,128,256]{2,1,0:T(8,128)(2,1)S(1)} custom-call(s32[4,8]{1,0:T(4,128)S(1)} %multiply_add_fusion.meta, bf16[32,512,128]{2,1,0:T(8,128)(2,1)S(1)} %get-tuple-element.34.held, bf16[4,512,128]{2,1,0:T(8,128)(2,1)S(1)} %get-tuple-element.35.sketch), custom_call_target="tpu_custom_call" | custom-call | flops 536870912 | bytes 6291456 | tf_op jit(solution)/shard_map/probe/pallas_call | solution.py:399
  13.8 2.5 %collective-permute-done.4.rest_3_ = bf16[1,512,128]{2,1,0:T(8,128)(2,1)S(1)} collective-permute-done((bf16[1,512,128]{2,1,0:T(8,128)(2,1)S(1)}, bf16[1,512,128]{2,1,0:T(8,128)(2,1)S(1)}, u32[]{:S(2)}, u32[]{:S(2)}) %collective-permute-start.4) | collective-permute-done | bytes 131104 | tf_op jit(solution)/shard_map/ppermute | solution.py:349
  17.7 3.3 %pair.1 = (bf16[32,256,128]{2,1,0:T(8,128)(2,1)S(1)}, bf16[32,128,128]{2,1,0:T(8,128)(2,1)S(1)}) custom-call(s32[4,8]{1,0:T(4,128)S(1)} %multiply_add_fusion.meta, bf16[32,512,128]{2,1,0:T(8,128)(2,1)S(1)} %get-tuple-element.37.held, bf16[32,128,256]{2,1,0:T(8,128)(2,1)S(1)} %probe.1.probes, bf16[1,512,128]{2,1,0:T(8,128)(2,1)S(1)} %copy-done, ...), custom_call_target="tpu_custom_call" | custom-call | flops 939524096 | bytes 10485760 | tf_op jit(solution)/shard_map/pair/pallas_call | solution.py:414
  21.0 2.4 %collective-permute-done.5.rest_3_ = bf16[1,512,128]{2,1,0:T(8,128)(2,1)S(1)} collective-permute-done((bf16[1,512,128]{2,1,0:T(8,128)(2,1)S(1)}, bf16[1,512,128]{2,1,0:T(8,128)(2,1)S(1)}, u32[]{:S(2)}, u32[]{:S(2)}) %collective-permute-start.5) | collective-permute-done | bytes 131104 | tf_op jit(solution)/shard_map/ppermute | solution.py:349
  23.5 1.3 %collective-permute-done.13.rest_7_ = bf16[1,512,128]{2,1,0:T(8,128)(2,1)S(1)} collective-permute-done((bf16[1,512,128]{2,1,0:T(8,128)(2,1)S(1)}, bf16[1,512,128]{2,1,0:T(8,128)(2,1)S(1)}, u32[]{:S(2)}, u32[]{:S(2)}) %collective-permute-start.13) | collective-permute-done | bytes 131104 | tf_op jit(solution)/shard_map/ppermute | solution.py:353
  24.8 1.8 %sketch.3 = (f32[512,128]{1,0:T(8,128)S(1)}, bf16[512,128]{1,0:T(8,128)(2,1)S(1)}, bf16[512,128]{1,0:T(8,128)(2,1)S(1)}, bf16[512,128]{1,0:T(8,128)(2,1)S(1)}, bf16[8,512,128]{2,1,0:T(8,128)(2,1)S(1)}) custom-call(s32[4,8]{1,0:T(4,128)S(1)} %multiply_add_fusion.meta, bf16[32,128,128]{2,1,0:T(8,128)(2,1)S(1)} %get-tuple-element.42.mixing, ...), custom_call_target="tpu_custom_call" | custom-call | flops 536870912 | bytes 4194304 | tf_op jit(solution)/shard_map/sketch/pallas_call | solution.py:426
  26.6 1.2 %collective-permute-start.14 = (bf16[512,128]{1,0:T(8,128)(2,1)S(1)}, bf16[512,128]{1,0:T(8,128)(2,1)S(1)}, u32[]{:S(2)}, u32[]{:S(2)}) collective-permute-start(bf16[512,128]{1,0:T(8,128)(2,1)S(1)} %get-tuple-element.48), channel_id=1, source_target_pairs={{0,8},{8,16},{16,24},{24,0},{32,40},{40,48},{48,56},{56,32},{64,72... | collective-permute-start | bytes 393224 | tf_op jit(solution)/shard_map/ppermute | solution.py:345
  27.8 2.3 %collective-permute-start.15 = (bf16[512,128]{1,0:T(8,128)(2,1)S(1)}, bf16[512,128]{1,0:T(8,128)(2,1)S(1)}, u32[]{:S(2)}, u32[]{:S(2)}) collective-permute-start(bf16[512,128]{1,0:T(8,128)(2,1)S(1)} %get-tuple-element.49), channel_id=1, source_target_pairs={{0,16},{8,24},{16,0},{24,8},{32,48},{40,56},{48,32},{56,40},{64,80... | collective-permute-start | bytes 393224 | tf_op jit(solution)/shard_map/ppermute | solution.py:345
  30.1 1.0 collective-permute-start.16
  31.1 1.7 %collective-permute-done.14 = bf16[512,128]{1,0:T(8,128)(2,1)S(1)} collective-permute-done((bf16[512,128]{1,0:T(8,128)(2,1)S(1)}, bf16[512,128]{1,0:T(8,128)(2,1)S(1)}, u32[]{:S(2)}, u32[]{:S(2)}) %collective-permute-start.14) | collective-permute-done | bytes 131104 | tf_op jit(solution)/shard_map/ppermute | solution.py:345
  32.8 3.0 %collective-permute-done.15 = bf16[512,128]{1,0:T(8,128)(2,1)S(1)} collective-permute-done((bf16[512,128]{1,0:T(8,128)(2,1)S(1)}, bf16[512,128]{1,0:T(8,128)(2,1)S(1)}, u32[]{:S(2)}, u32[]{:S(2)}) %collective-permute-start.15) | collective-permute-done | bytes 131104 | tf_op jit(solution)/shard_map/ppermute | solution.py:345
  35.7 1.7 %collective-permute-done.16 = bf16[512,128]{1,0:T(8,128)(2,1)S(1)} collective-permute-done((bf16[512,128]{1,0:T(8,128)(2,1)S(1)}, bf16[512,128]{1,0:T(8,128)(2,1)S(1)}, u32[]{:S(2)}, u32[]{:S(2)}) %collective-permute-start.16) | collective-permute-done | bytes 131104 | tf_op jit(solution)/shard_map/ppermute | solution.py:345
  37.5 19.3 %all_to_all.15 = f32[8,64,128]{2,1,0:T(8,128)} all-to-all(f32[8,64,128]{2,1,0:T(8,128)S(1)} %bitcast.1), channel_id=1, replica_groups={{0,32,64,96,128,160,192,224},{8,40,72,104,136,168,200,232},{16,48,80,11..., dimensions={0} | all-to-all | bytes 524288 | tf_op jit(solution)/shard_map/all_to_all | solution.py:363
  56.8 1.0 reduce_sum.18
  57.8 12.9 %all_to_all.16.blocks = f32[8,64,128]{2,1,0:T(8,128)S(1)} all-to-all(f32[8,64,128]{2,1,0:T(8,128)S(1)} %broadcast_in_dim.2), channel_id=1, replica_groups={{0,32,64,96,128,160,192,224},{8,40,72,104,136,168,200,232},{16,48,80,11..., dimensions={0} | all-to-all | bytes 524288 | tf_op jit(solution)/shard_map/all_to_all | solution.py:363
  70.7 7.0 %ortho.1 = (bf16[544,128]{1,0:T(8,128)(2,1)S(1)}, bf16[544,128]{1,0:T(8,128)(2,1)S(1)}, bf16[544,128]{1,0:T(8,128)(2,1)S(1)}, bf16[544,128]{1,0:T(8,128)(2,1)S(1)}) custom-call(f32[8,64,128]{2,1,0:T(8,128)S(1)} %all_to_all.16.blocks), custom_call_target="tpu_custom_call" | custom-call | flops 218103808 | bytes 1048576 | tf_op jit(solution)/shard_map/ortho/pallas_call | solution.py:443
  78.0 1.9 %collective-permute-start.18 = (bf16[544,128]{1,0:T(8,128)(2,1)S(1)}, bf16[544,128]{1,0:T(8,128)(2,1)S(1)}, u32[]{:S(2)}, u32[]{:S(2)}) collective-permute-start(bf16[544,128]{1,0:T(8,128)(2,1)S(1)} %get-tuple-element.55), channel_id=1, source_target_pairs={{0,16},{8,24},{16,0},{24,8},{32,48},{40,56},{48,32},{56,40},{64,80... | collective-permute-start | bytes 417800 | tf_op jit(solution)/shard_map/ppermute | solution.py:345
  79.9 2.1 %collective-permute-start.19 = (bf16[544,128]{1,0:T(8,128)(2,1)S(1)}, bf16[544,128]{1,0:T(8,128)(2,1)S(1)}, u32[]{:S(2)}, u32[]{:S(2)}) collective-permute-start(bf16[544,128]{1,0:T(8,128)(2,1)S(1)} %get-tuple-element.56), channel_id=1, source_target_pairs={{0,24},{8,0},{16,8},{24,16},{32,56},{40,32},{48,40},{56,48},{64,88... | collective-permute-start | bytes 417800 | tf_op jit(solution)/shard_map/ppermute | solution.py:345
  82.0 3.1 %backward_own.1 = (f32[1,512,128]{2,1,0:T(8,128)S(1)}, bf16[32,512,128]{2,1,0:T(8,128)(2,1)S(1)}) custom-call(s32[4,8]{1,0:T(4,128)S(1)} %multiply_add_fusion.meta, bf16[4,8,512,128]{3,2,1,0:T(8,128)(2,1)} %right_v.3, bf16[8,512,128]{2,1,0:T(8,128)(2,1)S(1)} %get-tuple-element.45.group, bf16[32,256,128]{2,1,0:T(8,128)(2,1)S(1)} %get-tuple-element.46.pairs, ...), custom_call_target="tpu_custom_call" | custom-call | flops 369098752 | bytes 4194304 | tf_op jit(solution)/shard_map/backward_own/pallas_call | solution.py:453
  85.1 0.9 collective-permute-done.19.msg3
  86.1 3.5 %backward.1 = (f32[8,4,16,128]{3,2,1,0:T(8,128)S(1)}, bf16[8,4,16,128]{3,2,1,0:T(8,128)(2,1)S(1)}, bf16[8,4,16,128]{3,2,1,0:T(8,128)(2,1)S(1)}, bf16[8,4,16,128]{3,2,1,0:T(8,128)(2,1)S(1)}, f32[4,16,128]{2,1,0:T(8,128)}) custom-call(s32[4,8]{1,0:T(4,128)S(1)} %multiply_add_fusion.meta, bf16[32,512,128]{2,1,0:T(8,128)(2,1)S(1)} %get-tuple-element.52.held, ...), custom_call_target="tpu_custom_call" | custom-call | flops 1073741824 | bytes 8388608 | tf_op jit(solution)/shard_map/backward/pallas_call | solution.py:465
  89.6 2.3 %collective-permute-start.21 = (bf16[8,4,16,128]{3,2,1,0:T(8,128)(2,1)S(1)}, bf16[8,4,16,128]{3,2,1,0:T(8,128)(2,1)S(1)}, u32[]{:S(2)}, u32[]{:S(2)}) collective-permute-start(bf16[8,4,16,128]{3,2,1,0:T(8,128)(2,1)S(1)} %get-tuple-element.60), channel_id=1, source_target_pairs={{0,16},{8,24},{16,0},{24,8},{32,48},{40,56},{48,32},{56,40},{64,80... | collective-permute-start | bytes 393224 | tf_op jit(solution)/shard_map/ppermute | solution.py:345
  91.9 1.5 %collective-permute-start.22 = (bf16[8,4,16,128]{3,2,1,0:T(8,128)(2,1)S(1)}, bf16[8,4,16,128]{3,2,1,0:T(8,128)(2,1)S(1)}, u32[]{:S(2)}, u32[]{:S(2)}) collective-permute-start(bf16[8,4,16,128]{3,2,1,0:T(8,128)(2,1)S(1)} %get-tuple-element.61), channel_id=1, source_target_pairs={{0,24},{8,0},{16,8},{24,16},{32,56},{40,32},{48,40},{56,48},{64,88... | collective-permute-start | bytes 393224 | tf_op jit(solution)/shard_map/ppermute | solution.py:345
  93.4 1.2 %collective-permute-done.20 = bf16[8,4,16,128]{3,2,1,0:T(8,128)(2,1)S(1)} collective-permute-done((bf16[8,4,16,128]{3,2,1,0:T(8,128)(2,1)S(1)}, bf16[8,4,16,128]{3,2,1,0:T(8,128)(2,1)S(1)}, u32[]{:S(2)}, u32[]{:S(2)}) %collective-permute-start.20) | collective-permute-done | bytes 131104 | tf_op jit(solution)/shard_map/ppermute | solution.py:345
  94.5 1.6 %collective-permute-done.21 = bf16[8,4,16,128]{3,2,1,0:T(8,128)(2,1)S(1)} collective-permute-done((bf16[8,4,16,128]{3,2,1,0:T(8,128)(2,1)S(1)}, bf16[8,4,16,128]{3,2,1,0:T(8,128)(2,1)S(1)}, u32[]{:S(2)}, u32[]{:S(2)}) %collective-permute-start.21) | collective-permute-done | bytes 131104 | tf_op jit(solution)/shard_map/ppermute | solution.py:345
  96.1 1.3 %collective-permute-done.22 = bf16[8,4,16,128]{3,2,1,0:T(8,128)(2,1)S(1)} collective-permute-done((bf16[8,4,16,128]{3,2,1,0:T(8,128)(2,1)S(1)}, bf16[8,4,16,128]{3,2,1,0:T(8,128)(2,1)S(1)}, u32[]{:S(2)}, u32[]{:S(2)}) %collective-permute-start.22) | collective-permute-done | bytes 131104 | tf_op jit(solution)/shard_map/ppermute | solution.py:345
  97.5 11.5 %all_to_all.17 = bf16[8,4,16,128]{3,2,1,0:T(8,128)(2,1)S(1)} all-to-all(bf16[8,4,16,128]{3,2,1,0:T(8,128)(2,1)S(1)} %add_convert_fusion), channel_id=1, replica_groups={{0,32,64,96,128,160,192,224},{8,40,72,104,136,168,200,232},{16,48,80,11..., dimensions={0} | all-to-all | bytes 262144 | tf_op jit(solution)/shard_map/all_to_all | solution.py:363
  (34 shorter events, 3.6 us)
Async XLA Ops:
  0.6 10.6 %collective-permute-start.2 = (bf16[1,512,128]{2,1,0:T(8,128)(2,1)}, bf16[1,512,128]{2,1,0:T(8,128)(2,1)S(1)}, u32[]{:S(2)}, u32[]{:S(2)}) collective-permute-start(bf16[1,512,128]{2,1,0:T(8,128)(2,1)} %rest_0_.2), channel_id=1, source_target_pairs={{0,2},{1,3},{2,4},{3,5},{4,6},{5,7},{6,0},{7,1},{8,10},{9,11},{10,... | collective-permute-start | bytes 393224 | tf_op jit(solution)/shard_map/ppermute | solution.py:349
  2.2 9.1 %collective-permute-start.3 = (bf16[1,512,128]{2,1,0:T(8,128)(2,1)}, bf16[1,512,128]{2,1,0:T(8,128)(2,1)S(1)}, u32[]{:S(2)}, u32[]{:S(2)}) collective-permute-start(bf16[1,512,128]{2,1,0:T(8,128)(2,1)} %rest_0_.2), channel_id=1, source_target_pairs={{0,6},{1,7},{2,0},{3,1},{4,2},{5,3},{6,4},{7,5},{8,14},{9,15},{10,... | collective-permute-start | bytes 393224 | tf_op jit(solution)/shard_map/ppermute | solution.py:349
  3.9 9.7 %collective-permute-start = (bf16[1,512,128]{2,1,0:T(8,128)(2,1)}, bf16[1,512,128]{2,1,0:T(8,128)(2,1)S(1)}, u32[]{:S(2)}, u32[]{:S(2)}) collective-permute-start(bf16[1,512,128]{2,1,0:T(8,128)(2,1)} %rest_0_.3), channel_id=1, source_target_pairs={{0,2},{1,3},{2,4},{3,5},{4,6},{5,7},{6,0},{7,1},{8,10},{9,11},{10,... | collective-permute-start | bytes 393224 | tf_op jit(solution)/shard_map/ppermute | solution.py:349
  4.2 9.6 %collective-permute-start.1 = (bf16[1,512,128]{2,1,0:T(8,128)(2,1)}, bf16[1,512,128]{2,1,0:T(8,128)(2,1)S(1)}, u32[]{:S(2)}, u32[]{:S(2)}) collective-permute-start(bf16[1,512,128]{2,1,0:T(8,128)(2,1)} %rest_0_.3), channel_id=1, source_target_pairs={{0,6},{1,7},{2,0},{3,1},{4,2},{5,3},{6,4},{7,5},{8,14},{9,15},{10,... | collective-permute-start | bytes 393224 | tf_op jit(solution)/shard_map/ppermute | solution.py:349
  7.9 3.6 %copy-start = (bf16[1,512,128]{2,1,0:T(8,128)(2,1)S(1)}, bf16[1,512,128]{2,1,0:T(8,128)(2,1)}, u32[]{:S(2)}) copy-start(bf16[1,512,128]{2,1,0:T(8,128)(2,1)} %rest_0_.2) | copy-start | bytes 393220
  11.2 5.1 %copy-start.1 = (bf16[1,512,128]{2,1,0:T(8,128)(2,1)S(1)}, bf16[1,512,128]{2,1,0:T(8,128)(2,1)}, u32[]{:S(2)}) copy-start(bf16[1,512,128]{2,1,0:T(8,128)(2,1)} %rest_0_.3) | copy-start | bytes 393220
  11.3 5.0 %collective-permute-start.4 = (bf16[1,512,128]{2,1,0:T(8,128)(2,1)S(1)}, bf16[1,512,128]{2,1,0:T(8,128)(2,1)S(1)}, u32[]{:S(2)}, u32[]{:S(2)}) collective-permute-start(bf16[1,512,128]{2,1,0:T(8,128)(2,1)S(1)} %collective-permute-done.3.rest_2_), channel_id=1, source_target_pairs={{0,6},{1,7},{2,0},{3,1},{4,2},{5,3},{6,4},{7,5},{8,14},{9,15},{10,... | collective-permute-start | bytes 393224 | tf_op jit(solution)/shard_map/ppermute | solution.py:349
  11.4 4.9 %collective-permute-start.6 = (bf16[1,512,128]{2,1,0:T(8,128)(2,1)S(1)}, bf16[1,512,128]{2,1,0:T(8,128)(2,1)S(1)}, u32[]{:S(2)}, u32[]{:S(2)}) collective-permute-start(bf16[1,512,128]{2,1,0:T(8,128)(2,1)S(1)} %copy-done), channel_id=1, source_target_pairs={{0,1},{1,0},{2,3},{3,2},{4,5},{5,4},{6,7},{7,6},{8,9},{9,8},{10,11... | collective-permute-start | bytes 393224 | tf_op jit(solution)/shard_map/ppermute | solution.py:353
  11.5 5.5 %collective-permute-start.8 = (bf16[1,512,128]{2,1,0:T(8,128)(2,1)S(1)}, bf16[1,512,128]{2,1,0:T(8,128)(2,1)S(1)}, u32[]{:S(2)}, u32[]{:S(2)}) collective-permute-start(bf16[1,512,128]{2,1,0:T(8,128)(2,1)S(1)} %collective-permute-done.3.rest_2_), channel_id=1, source_target_pairs={{0,1},{1,0},{2,3},{3,2},{4,5},{5,4},{6,7},{7,6},{8,9},{9,8},{10,11... | collective-permute-start | bytes 393224 | tf_op jit(solution)/shard_map/ppermute | solution.py:353
  13.7 3.4 %collective-permute-start.7 = (bf16[1,512,128]{2,1,0:T(8,128)(2,1)S(1)}, bf16[1,512,128]{2,1,0:T(8,128)(2,1)S(1)}, u32[]{:S(2)}, u32[]{:S(2)}) collective-permute-start(bf16[1,512,128]{2,1,0:T(8,128)(2,1)S(1)} %collective-permute-done.2.rest_1_), channel_id=1, source_target_pairs={{0,1},{1,0},{2,3},{3,2},{4,5},{5,4},{6,7},{7,6},{8,9},{9,8},{10,11... | collective-permute-start | bytes 393224 | tf_op jit(solution)/shard_map/ppermute | solution.py:353
  16.3 1.3 %collective-permute-start.9 = (bf16[1,512,128]{2,1,0:T(8,128)(2,1)S(1)}, bf16[1,512,128]{2,1,0:T(8,128)(2,1)S(1)}, u32[]{:S(2)}, u32[]{:S(2)}) collective-permute-start(bf16[1,512,128]{2,1,0:T(8,128)(2,1)S(1)} %collective-permute-done.4.rest_3_), channel_id=1, source_target_pairs={{0,1},{1,0},{2,3},{3,2},{4,5},{5,4},{6,7},{7,6},{8,9},{9,8},{10,11... | collective-permute-start | bytes 393224 | tf_op jit(solution)/shard_map/ppermute | solution.py:353
  16.3 7.1 %collective-permute-start.5 = (bf16[1,512,128]{2,1,0:T(8,128)(2,1)S(1)}, bf16[1,512,128]{2,1,0:T(8,128)(2,1)S(1)}, u32[]{:S(2)}, u32[]{:S(2)}) collective-permute-start(bf16[1,512,128]{2,1,0:T(8,128)(2,1)S(1)} %collective-permute-done.rest_1_), channel_id=1, source_target_pairs={{0,2},{1,3},{2,4},{3,5},{4,6},{5,7},{6,0},{7,1},{8,10},{9,11},{10,... | collective-permute-start | bytes 393224 | tf_op jit(solution)/shard_map/ppermute | solution.py:349
  16.3 7.1 %collective-permute-start.10 = (bf16[1,512,128]{2,1,0:T(8,128)(2,1)S(1)}, bf16[1,512,128]{2,1,0:T(8,128)(2,1)S(1)}, u32[]{:S(2)}, u32[]{:S(2)}) collective-permute-start(bf16[1,512,128]{2,1,0:T(8,128)(2,1)S(1)} %copy-done.1), channel_id=1, source_target_pairs={{0,1},{1,0},{2,3},{3,2},{4,5},{5,4},{6,7},{7,6},{8,9},{9,8},{10,11... | collective-permute-start | bytes 393224 | tf_op jit(solution)/shard_map/ppermute | solution.py:353
  16.9 6.5 %collective-permute-start.11 = (bf16[1,512,128]{2,1,0:T(8,128)(2,1)S(1)}, bf16[1,512,128]{2,1,0:T(8,128)(2,1)S(1)}, u32[]{:S(2)}, u32[]{:S(2)}) collective-permute-start(bf16[1,512,128]{2,1,0:T(8,128)(2,1)S(1)} %collective-permute-done.rest_1_), channel_id=1, source_target_pairs={{0,1},{1,0},{2,3},{3,2},{4,5},{5,4},{6,7},{7,6},{8,9},{9,8},{10,11... | collective-permute-start | bytes 393224 | tf_op jit(solution)/shard_map/ppermute | solution.py:353
  17.0 6.4 %collective-permute-start.12 = (bf16[1,512,128]{2,1,0:T(8,128)(2,1)S(1)}, bf16[1,512,128]{2,1,0:T(8,128)(2,1)S(1)}, u32[]{:S(2)}, u32[]{:S(2)}) collective-permute-start(bf16[1,512,128]{2,1,0:T(8,128)(2,1)S(1)} %collective-permute-done.1.rest_2_), channel_id=1, source_target_pairs={{0,1},{1,0},{2,3},{3,2},{4,5},{5,4},{6,7},{7,6},{8,9},{9,8},{10,11... | collective-permute-start | bytes 393224 | tf_op jit(solution)/shard_map/ppermute | solution.py:353
  23.4 1.3 %collective-permute-start.13 = (bf16[1,512,128]{2,1,0:T(8,128)(2,1)S(1)}, bf16[1,512,128]{2,1,0:T(8,128)(2,1)S(1)}, u32[]{:S(2)}, u32[]{:S(2)}) collective-permute-start(bf16[1,512,128]{2,1,0:T(8,128)(2,1)S(1)} %collective-permute-done.5.rest_3_), channel_id=1, source_target_pairs={{0,1},{1,0},{2,3},{3,2},{4,5},{5,4},{6,7},{7,6},{8,9},{9,8},{10,11... | collective-permute-start | bytes 393224 | tf_op jit(solution)/shard_map/ppermute | solution.py:353
  26.6 6.1 %collective-permute-start.14 = (bf16[512,128]{1,0:T(8,128)(2,1)S(1)}, bf16[512,128]{1,0:T(8,128)(2,1)S(1)}, u32[]{:S(2)}, u32[]{:S(2)}) collective-permute-start(bf16[512,128]{1,0:T(8,128)(2,1)S(1)} %get-tuple-element.48), channel_id=1, source_target_pairs={{0,8},{8,16},{16,24},{24,0},{32,40},{40,48},{48,56},{56,32},{64,72... | collective-permute-start | bytes 393224 | tf_op jit(solution)/shard_map/ppermute | solution.py:345
  27.8 7.9 %collective-permute-start.15 = (bf16[512,128]{1,0:T(8,128)(2,1)S(1)}, bf16[512,128]{1,0:T(8,128)(2,1)S(1)}, u32[]{:S(2)}, u32[]{:S(2)}) collective-permute-start(bf16[512,128]{1,0:T(8,128)(2,1)S(1)} %get-tuple-element.49), channel_id=1, source_target_pairs={{0,16},{8,24},{16,0},{24,8},{32,48},{40,56},{48,32},{56,40},{64,80... | collective-permute-start | bytes 393224 | tf_op jit(solution)/shard_map/ppermute | solution.py:345
  30.1 7.3 %collective-permute-start.16 = (bf16[512,128]{1,0:T(8,128)(2,1)S(1)}, bf16[512,128]{1,0:T(8,128)(2,1)S(1)}, u32[]{:S(2)}, u32[]{:S(2)}) collective-permute-start(bf16[512,128]{1,0:T(8,128)(2,1)S(1)} %get-tuple-element.50), channel_id=1, source_target_pairs={{0,24},{8,0},{16,8},{24,16},{32,56},{40,32},{48,40},{56,48},{64,88... | collective-permute-start | bytes 393224 | tf_op jit(solution)/shard_map/ppermute | solution.py:345
  77.7 7.4 %collective-permute-start.17 = (bf16[544,128]{1,0:T(8,128)(2,1)S(1)}, bf16[544,128]{1,0:T(8,128)(2,1)S(1)}, u32[]{:S(2)}, u32[]{:S(2)}) collective-permute-start(bf16[544,128]{1,0:T(8,128)(2,1)S(1)} %get-tuple-element.54), channel_id=1, source_target_pairs={{0,8},{8,16},{16,24},{24,0},{32,40},{40,48},{48,56},{56,32},{64,72... | collective-permute-start | bytes 417800 | tf_op jit(solution)/shard_map/ppermute | solution.py:345
  78.0 7.1 %collective-permute-start.18 = (bf16[544,128]{1,0:T(8,128)(2,1)S(1)}, bf16[544,128]{1,0:T(8,128)(2,1)S(1)}, u32[]{:S(2)}, u32[]{:S(2)}) collective-permute-start(bf16[544,128]{1,0:T(8,128)(2,1)S(1)} %get-tuple-element.55), channel_id=1, source_target_pairs={{0,16},{8,24},{16,0},{24,8},{32,48},{40,56},{48,32},{56,40},{64,80... | collective-permute-start | bytes 417800 | tf_op jit(solution)/shard_map/ppermute | solution.py:345
  79.9 6.2 %collective-permute-start.19 = (bf16[544,128]{1,0:T(8,128)(2,1)S(1)}, bf16[544,128]{1,0:T(8,128)(2,1)S(1)}, u32[]{:S(2)}, u32[]{:S(2)}) collective-permute-start(bf16[544,128]{1,0:T(8,128)(2,1)S(1)} %get-tuple-element.56), channel_id=1, source_target_pairs={{0,24},{8,0},{16,8},{24,16},{32,56},{40,32},{48,40},{56,48},{64,88... | collective-permute-start | bytes 417800 | tf_op jit(solution)/shard_map/ppermute | solution.py:345
  89.6 5.0 %collective-permute-start.20 = (bf16[8,4,16,128]{3,2,1,0:T(8,128)(2,1)S(1)}, bf16[8,4,16,128]{3,2,1,0:T(8,128)(2,1)S(1)}, u32[]{:S(2)}, u32[]{:S(2)}) collective-permute-start(bf16[8,4,16,128]{3,2,1,0:T(8,128)(2,1)S(1)} %get-tuple-element.59), channel_id=1, source_target_pairs={{0,8},{8,16},{16,24},{24,0},{32,40},{40,48},{48,56},{56,32},{64,72... | collective-permute-start | bytes 393224 | tf_op jit(solution)/shard_map/ppermute | solution.py:345
  89.6 6.5 %collective-permute-start.21 = (bf16[8,4,16,128]{3,2,1,0:T(8,128)(2,1)S(1)}, bf16[8,4,16,128]{3,2,1,0:T(8,128)(2,1)S(1)}, u32[]{:S(2)}, u32[]{:S(2)}) collective-permute-start(bf16[8,4,16,128]{3,2,1,0:T(8,128)(2,1)S(1)} %get-tuple-element.60), channel_id=1, source_target_pairs={{0,16},{8,24},{16,0},{24,8},{32,48},{40,56},{48,32},{56,40},{64,80... | collective-permute-start | bytes 393224 | tf_op jit(solution)/shard_map/ppermute | solution.py:345
  91.9 5.6 %collective-permute-start.22 = (bf16[8,4,16,128]{3,2,1,0:T(8,128)(2,1)S(1)}, bf16[8,4,16,128]{3,2,1,0:T(8,128)(2,1)S(1)}, u32[]{:S(2)}, u32[]{:S(2)}) collective-permute-start(bf16[8,4,16,128]{3,2,1,0:T(8,128)(2,1)S(1)} %get-tuple-element.61), channel_id=1, source_target_pairs={{0,24},{8,0},{16,8},{24,16},{32,56},{40,32},{48,40},{56,48},{64,88... | collective-permute-start | bytes 393224 | tf_op jit(solution)/shard_map/ppermute | solution.py:345

commit v9 on v8

--- a/solution.py
+++ b/solution.py
@@ -117,27 +117,29 @@
     return [tiles[:2], tiles[2:]]
 
 
-def load_kernel(outs, slots, meta, right_u, right_v, sketch, held_u, held_v, plain, sems_u, sems_v, sem):
+def settle(meta, outs, slots, source, held, sems):
+    def tile(j, _):
+        def one(s, _):
+            pltpu.make_async_copy(source.at[j, s], held.at[j * slots + s], sems.at[j * slots + s]).wait()
+            return 0
+
+        lax.fori_loop(0, live(meta, j), one, 0)
+        return 0
+
+    lax.fori_loop(0, outs, tile, 0)
+
+
+def load_kernel(outs, slots, meta, right_v, sketch, held, plain, sems, sem):
+    fetch(meta, outs, slots, right_v, held, sems)
     copy = pltpu.make_async_copy(sketch, plain, sem)
     copy.start()
-    fetch(meta, outs, slots, right_v, held_v, sems_v)
-    fetch(meta, outs, slots, right_u, held_u, sems_u)
+    settle(meta, outs, slots, right_v, held, sems)
     copy.wait()
 
-    def tile(j, _):
-        def one(s, _):
-            at = j * slots + s
-            pltpu.make_async_copy(right_v.at[j, s], held_v.at[at], sems_v.at[at]).wait()
-            pltpu.make_async_copy(right_u.at[j, s], held_u.at[at], sems_u.at[at]).wait()
-            return 0
-
-        lax.fori_loop(0, live(meta, j), one, 0)
-        return 0
-
-    lax.fori_loop(0, outs, tile, 0)
-
-
-def probe_kernel(outs, slots, meta, held, sketch, probes):
+
+def probe_kernel(outs, slots, meta, right_u, held, sketch, probes, held_u, sems):
+    fetch(meta, outs, slots, right_u, held_u, sems)
+
     def work(items, first):
         turned = [sketch[j].T for _, j, _, _ in items]
         at = batches(items, slots)
@@ -146,6 +148,7 @@
             probes[slot] = beside(*halves(product))
 
     sweep(meta, two_by_two([(j, j) for j in range(outs)]), work)
+    settle(meta, outs, slots, right_u, held_u, sems)
 
 
 def tile_ids(tiles):
@@ -384,27 +387,28 @@
     near = [hop(value, step, tiles) for value in (left_v, left_u) for step in (1, -1)]
     near_v, near_u = near[:2], near[2:]
     sketch = pltpu.with_memory_space_constraint(sketch, pltpu.HBM)
-    held_u, held_v, sketch = pl.pallas_call(
+    held_v, sketch = pl.pallas_call(
         functools.partial(load_kernel, outs, slots),
-        out_shape=(shape((count, NB, R), BF),) * 2 + (shape(sketch.shape, BF),),
-        in_specs=[in_smem()] + [in_place()] * 3,
-        out_specs=(in_vmem(),) * 3,
-        scratch_shapes=[pltpu.SemaphoreType.DMA((count,))] * 2 + [pltpu.SemaphoreType.DMA],
-        compiler_params=params(),
-        cost_estimate=cost(0, 9),
+        out_shape=(shape((count, NB, R), BF), shape(sketch.shape, BF)),
+        in_specs=[in_smem()] + [in_place()] * 2,
+        out_specs=(in_vmem(),) * 2,
+        scratch_shapes=[pltpu.SemaphoreType.DMA((count,)), pltpu.SemaphoreType.DMA],
+        compiler_params=params(),
+        cost_estimate=cost(0, 5),
         name="load",
-    )(packed, right_u, right_v, sketch)
+    )(packed, right_v, sketch)
     *near_v, sketch = lax.optimization_barrier((*near_v, sketch))
     far_v = hop(near_v[1], -1, tiles)
-    probes = pl.pallas_call(
+    probes, held_u = pl.pallas_call(
         functools.partial(probe_kernel, outs, slots),
-        out_shape=shape((count, R, 2 * R), BF),
-        in_specs=[in_smem()] + [in_vmem()] * 2,
-        out_specs=in_vmem(),
+        out_shape=(shape((count, R, 2 * R), BF), shape((count, NB, R), BF)),
+        in_specs=[in_smem(), in_place()] + [in_vmem()] * 2,
+        out_specs=(in_vmem(),) * 2,
+        scratch_shapes=[pltpu.SemaphoreType.DMA((count,))],
         compiler_params=params(),
         cost_estimate=cost(outs * slots, 6),
         name="probe",
-    )(packed, held_v, sketch)
+    )(packed, right_u, held_v, sketch)
     *near_u, far_v, probes = lax.optimization_barrier((*near_u, far_v, probes))
     far_u = hop(near_u[0], 1, tiles)
     group_v = [left_v, *near_v, far_v]

time: 110 us -> 110 us (level)
  starting transfers between devices: 21 us -> 23.9 us
  Pallas kernels: 23.8 us -> 21.6 us
  waiting for transfers between devices: 17.9 us -> 16.6 us
    ppermute x9, starting transfers between devices: 12.6 us -> 15 us  [shift_y(): return lax.ppermute(array, 'inner', pairs)]
  transfers between devices with their start and end apart: 23 -> 23, of which waited for: 11 -> 10; matrix products, arithmetic and copies ran while one was open for 1% -> 1% of each run, Pallas kernels for 10% -> 9%
where the time goes in v9:
time: 110 us; the launch traced here: 109 us
  blocking collectives  44.1 us (40%)
  starting transfers between devices  23.9 us (22%)
  Pallas kernels  21.6 us (20%)
  waiting for transfers between devices  16.6 us (15%)
  other arithmetic  2.44 us (2%)
    all_to_all x3, blocking collectives, over_z(): lax.all_to_all(array, 'inner', 0, 0, tiled=True, axis_index_groups=groups)  44.1 us
    ppermute x9, starting transfers between devices, shift_y(): return lax.ppermute(array, 'inner', pairs)  15 us
    ppermute x9, waiting for transfers between devices, shift_y(): return lax.ppermute(array, 'inner', pairs)  10.5 us
    ppermute x6, starting transfers between devices, hop(): lax.ppermute(value, 'cols', [(i, (i + 2 * step) % tiles) for i in range(t...  7.49 us
    pallas_call x1, Pallas kernels, body(): pl.pallas_call(functools.partial(ortho_kernel, zs), out_shape=(shape((NB...  6.98 us
    ppermute x6, waiting for transfers between devices, hop(): lax.ppermute(value, 'cols', [(i, (i + 2 * step) % tiles) for i in range(t...  4.54 us
    pallas_call x1, Pallas kernels, body(): pl.pallas_call(functools.partial(backward_own_kernel, outs, slots), out_s...  2.89 us
    pallas_call x1, Pallas kernels, body(): pl.pallas_call(functools.partial(pair_kernel, outs, slots), out_shape=(sh...  2.82 us
  transfers between devices with their start and end apart: 23, of which 10 were waited for; matrix products, arithmetic and copies ran while one was open for 1% of the time, Pallas kernels for 9%

profile of v9, /device:TPU:8, one launch (start us, length us, event | category | flops | bytes accessed | tf_op | source)
XLA Modules:
  0.0 109.5 jit_solution(1224931758527346813)
XLA Ops:
  0.6 1.6 %collective-permute-start.2 = (bf16[1,512,128]{2,1,0:T(8,128)(2,1)}, bf16[1,512,128]{2,1,0:T(8,128)(2,1)S(1)}, u32[]{:S(2)}, u32[]{:S(2)}) collective-permute-start(bf16[1,512,128]{2,1,0:T(8,128)(2,1)} %rest_0_.2), channel_id=1, source_target_pairs={{0,2},{1,3},{2,4},{3,5},{4,6},{5,7},{6,0},{7,1},{8,10},{9,11},{10,... | collective-permute-start | bytes 393224 | tf_op jit(solution)/shard_map/ppermute | solution.py:352
  2.2 1.7 %collective-permute-start.3 = (bf16[1,512,128]{2,1,0:T(8,128)(2,1)}, bf16[1,512,128]{2,1,0:T(8,128)(2,1)S(1)}, u32[]{:S(2)}, u32[]{:S(2)}) collective-permute-start(bf16[1,512,128]{2,1,0:T(8,128)(2,1)} %rest_0_.2), channel_id=1, source_target_pairs={{0,6},{1,7},{2,0},{3,1},{4,2},{5,3},{6,4},{7,5},{8,14},{9,15},{10,... | collective-permute-start | bytes 393224 | tf_op jit(solution)/shard_map/ppermute | solution.py:352
  4.2 3.0 %collective-permute-start.1 = (bf16[1,512,128]{2,1,0:T(8,128)(2,1)}, bf16[1,512,128]{2,1,0:T(8,128)(2,1)S(1)}, u32[]{:S(2)}, u32[]{:S(2)}) collective-permute-start(bf16[1,512,128]{2,1,0:T(8,128)(2,1)} %rest_0_.3), channel_id=1, source_target_pairs={{0,6},{1,7},{2,0},{3,1},{4,2},{5,3},{6,4},{7,5},{8,14},{9,15},{10,... | collective-permute-start | bytes 393224 | tf_op jit(solution)/shard_map/ppermute | solution.py:352
  7.2 0.7 multiply_add_fusion.meta
  7.9 2.4 %load.1 = (bf16[32,512,128]{2,1,0:T(8,128)(2,1)S(1)}, bf16[4,512,128]{2,1,0:T(8,128)(2,1)S(1)}) custom-call(s32[4,8]{1,0:T(4,128)S(1)} %multiply_add_fusion.meta, bf16[4,8,512,128]{3,2,1,0:T(8,128)(2,1)} %right_v.3, bf16[4,512,128]{2,1,0:T(8,128)(2,1)} %sketch.2), custom_call_target="tpu_custom_call" | custom-call | bytes 5242880 | tf_op jit(solution)/shard_map/load/pallas_call | solution.py:390
  11.4 2.2 %probe.1 = (bf16[32,128,256]{2,1,0:T(8,128)(2,1)S(1)}, bf16[32,512,128]{2,1,0:T(8,128)(2,1)S(1)}) custom-call(s32[4,8]{1,0:T(4,128)S(1)} %multiply_add_fusion.meta, bf16[4,8,512,128]{3,2,1,0:T(8,128)(2,1)} %right_u.1, bf16[32,512,128]{2,1,0:T(8,128)(2,1)S(1)} %get-tuple-element.35.held, bf16[4,512,128]{2,1,0:T(8,128)(2,1)S(1)} %get-tuple-element.36.sketch), custom_call_target="tpu_custom_call" | custom-call | flops 536870912 | bytes 6291456 | tf_op jit(solution)/shard_map/probe/pallas_call | solution.py:402
  13.8 1.6 %collective-permute-done.4.rest_3_ = bf16[1,512,128]{2,1,0:T(8,128)(2,1)S(1)} collective-permute-done((bf16[1,512,128]{2,1,0:T(8,128)(2,1)S(1)}, bf16[1,512,128]{2,1,0:T(8,128)(2,1)S(1)}, u32[]{:S(2)}, u32[]{:S(2)}) %collective-permute-start.4) | collective-permute-done | bytes 131104 | tf_op jit(solution)/shard_map/ppermute | solution.py:352
  16.7 2.8 %pair.1 = (bf16[32,256,128]{2,1,0:T(8,128)(2,1)S(1)}, bf16[32,128,128]{2,1,0:T(8,128)(2,1)S(1)}) custom-call(s32[4,8]{1,0:T(4,128)S(1)} %multiply_add_fusion.meta, bf16[32,512,128]{2,1,0:T(8,128)(2,1)S(1)} %get-tuple-element.39.held, bf16[32,128,256]{2,1,0:T(8,128)(2,1)S(1)} %get-tuple-element.40.probes, bf16[1,512,128]{2,1,0:T(8,128)(2,1)S(1)} %copy-done, ...), custom_call_target="tpu_custom_call" | custom-call | flops 939524096 | bytes 10485760 | tf_op jit(solution)/shard_map/pair/pallas_call | solution.py:418
  19.6 2.9 %collective-permute-done.5.rest_3_ = bf16[1,512,128]{2,1,0:T(8,128)(2,1)S(1)} collective-permute-done((bf16[1,512,128]{2,1,0:T(8,128)(2,1)S(1)}, bf16[1,512,128]{2,1,0:T(8,128)(2,1)S(1)}, u32[]{:S(2)}, u32[]{:S(2)}) %collective-permute-start.5) | collective-permute-done | bytes 131104 | tf_op jit(solution)/shard_map/ppermute | solution.py:352
  22.5 1.3 %collective-permute-done.13.rest_7_ = bf16[1,512,128]{2,1,0:T(8,128)(2,1)S(1)} collective-permute-done((bf16[1,512,128]{2,1,0:T(8,128)(2,1)S(1)}, bf16[1,512,128]{2,1,0:T(8,128)(2,1)S(1)}, u32[]{:S(2)}, u32[]{:S(2)}) %collective-permute-start.13) | collective-permute-done | bytes 131104 | tf_op jit(solution)/shard_map/ppermute | solution.py:356
  23.8 1.6 %sketch.3 = (f32[512,128]{1,0:T(8,128)S(1)}, bf16[512,128]{1,0:T(8,128)(2,1)S(1)}, bf16[512,128]{1,0:T(8,128)(2,1)S(1)}, bf16[512,128]{1,0:T(8,128)(2,1)S(1)}, bf16[8,512,128]{2,1,0:T(8,128)(2,1)S(1)}) custom-call(s32[4,8]{1,0:T(4,128)S(1)} %multiply_add_fusion.meta, bf16[32,128,128]{2,1,0:T(8,128)(2,1)S(1)} %get-tuple-element.44.mixing, ...), custom_call_target="tpu_custom_call" | custom-call | flops 536870912 | bytes 4194304 | tf_op jit(solution)/shard_map/sketch/pallas_call | solution.py:430
  25.4 1.9 %collective-permute-start.14 = (bf16[512,128]{1,0:T(8,128)(2,1)S(1)}, bf16[512,128]{1,0:T(8,128)(2,1)S(1)}, u32[]{:S(2)}, u32[]{:S(2)}) collective-permute-start(bf16[512,128]{1,0:T(8,128)(2,1)S(1)} %get-tuple-element.50), channel_id=1, source_target_pairs={{0,8},{8,16},{16,24},{24,0},{32,40},{40,48},{48,56},{56,32},{64,72... | collective-permute-start | bytes 393224 | tf_op jit(solution)/shard_map/ppermute | solution.py:348
  27.3 2.6 %collective-permute-start.15 = (bf16[512,128]{1,0:T(8,128)(2,1)S(1)}, bf16[512,128]{1,0:T(8,128)(2,1)S(1)}, u32[]{:S(2)}, u32[]{:S(2)}) collective-permute-start(bf16[512,128]{1,0:T(8,128)(2,1)S(1)} %get-tuple-element.51), channel_id=1, source_target_pairs={{0,16},{8,24},{16,0},{24,8},{32,48},{40,56},{48,32},{56,40},{64,80... | collective-permute-start | bytes 393224 | tf_op jit(solution)/shard_map/ppermute | solution.py:348
  29.9 0.6 collective-permute-start.16
  30.5 1.6 %collective-permute-done.14 = bf16[512,128]{1,0:T(8,128)(2,1)S(1)} collective-permute-done((bf16[512,128]{1,0:T(8,128)(2,1)S(1)}, bf16[512,128]{1,0:T(8,128)(2,1)S(1)}, u32[]{:S(2)}, u32[]{:S(2)}) %collective-permute-start.14) | collective-permute-done | bytes 131104 | tf_op jit(solution)/shard_map/ppermute | solution.py:348
  32.1 3.0 %collective-permute-done.15 = bf16[512,128]{1,0:T(8,128)(2,1)S(1)} collective-permute-done((bf16[512,128]{1,0:T(8,128)(2,1)S(1)}, bf16[512,128]{1,0:T(8,128)(2,1)S(1)}, u32[]{:S(2)}, u32[]{:S(2)}) %collective-permute-start.15) | collective-permute-done | bytes 131104 | tf_op jit(solution)/shard_map/ppermute | solution.py:348
  35.2 1.7 %collective-permute-done.16 = bf16[512,128]{1,0:T(8,128)(2,1)S(1)} collective-permute-done((bf16[512,128]{1,0:T(8,128)(2,1)S(1)}, bf16[512,128]{1,0:T(8,128)(2,1)S(1)}, u32[]{:S(2)}, u32[]{:S(2)}) %collective-permute-start.16) | collective-permute-done | bytes 131104 | tf_op jit(solution)/shard_map/ppermute | solution.py:348
  36.9 19.7 %all_to_all.15 = f32[8,64,128]{2,1,0:T(8,128)} all-to-all(f32[8,64,128]{2,1,0:T(8,128)S(1)} %bitcast.1), channel_id=1, replica_groups={{0,32,64,96,128,160,192,224},{8,40,72,104,136,168,200,232},{16,48,80,11..., dimensions={0} | all-to-all | bytes 524288 | tf_op jit(solution)/shard_map/all_to_all | solution.py:366
  56.6 1.0 reduce_sum.18
  57.6 12.9 %all_to_all.16.blocks = f32[8,64,128]{2,1,0:T(8,128)S(1)} all-to-all(f32[8,64,128]{2,1,0:T(8,128)S(1)} %broadcast_in_dim.2), channel_id=1, replica_groups={{0,32,64,96,128,160,192,224},{8,40,72,104,136,168,200,232},{16,48,80,11..., dimensions={0} | all-to-all | bytes 524288 | tf_op jit(solution)/shard_map/all_to_all | solution.py:366
  70.5 7.0 %ortho.1 = (bf16[544,128]{1,0:T(8,128)(2,1)S(1)}, bf16[544,128]{1,0:T(8,128)(2,1)S(1)}, bf16[544,128]{1,0:T(8,128)(2,1)S(1)}, bf16[544,128]{1,0:T(8,128)(2,1)S(1)}) custom-call(f32[8,64,128]{2,1,0:T(8,128)S(1)} %all_to_all.16.blocks), custom_call_target="tpu_custom_call" | custom-call | flops 218103808 | bytes 1048576 | tf_op jit(solution)/shard_map/ortho/pallas_call | solution.py:447
  77.7 2.6 %collective-permute-start.18 = (bf16[544,128]{1,0:T(8,128)(2,1)S(1)}, bf16[544,128]{1,0:T(8,128)(2,1)S(1)}, u32[]{:S(2)}, u32[]{:S(2)}) collective-permute-start(bf16[544,128]{1,0:T(8,128)(2,1)S(1)} %get-tuple-element.57), channel_id=1, source_target_pairs={{0,16},{8,24},{16,0},{24,8},{32,48},{40,56},{48,32},{56,40},{64,80... | collective-permute-start | bytes 417800 | tf_op jit(solution)/shard_map/ppermute | solution.py:348
  80.3 1.8 %collective-permute-start.19 = (bf16[544,128]{1,0:T(8,128)(2,1)S(1)}, bf16[544,128]{1,0:T(8,128)(2,1)S(1)}, u32[]{:S(2)}, u32[]{:S(2)}) collective-permute-start(bf16[544,128]{1,0:T(8,128)(2,1)S(1)} %get-tuple-element.58), channel_id=1, source_target_pairs={{0,24},{8,0},{16,8},{24,16},{32,56},{40,32},{48,40},{56,48},{64,88... | collective-permute-start | bytes 417800 | tf_op jit(solution)/shard_map/ppermute | solution.py:348
  82.2 2.9 %backward_own.1 = (f32[1,512,128]{2,1,0:T(8,128)S(1)}, bf16[32,512,128]{2,1,0:T(8,128)(2,1)S(1)}) custom-call(s32[4,8]{1,0:T(4,128)S(1)} %multiply_add_fusion.meta, bf16[4,8,512,128]{3,2,1,0:T(8,128)(2,1)} %right_v.3, bf16[8,512,128]{2,1,0:T(8,128)(2,1)S(1)} %get-tuple-element.47.group, bf16[32,256,128]{2,1,0:T(8,128)(2,1)S(1)} %get-tuple-element.48.pairs, ...), custom_call_target="tpu_custom_call" | custom-call | flops 369098752 | bytes 4194304 | tf_op jit(solution)/shard_map/backward_own/pallas_call | solution.py:457
  85.1 0.7 collective-permute-done.19.msg3
  85.8 2.8 %backward.1 = (f32[8,4,16,128]{3,2,1,0:T(8,128)S(1)}, bf16[8,4,16,128]{3,2,1,0:T(8,128)(2,1)S(1)}, bf16[8,4,16,128]{3,2,1,0:T(8,128)(2,1)S(1)}, bf16[8,4,16,128]{3,2,1,0:T(8,128)(2,1)S(1)}, f32[4,16,128]{2,1,0:T(8,128)}) custom-call(s32[4,8]{1,0:T(4,128)S(1)} %multiply_add_fusion.meta, bf16[32,512,128]{2,1,0:T(8,128)(2,1)S(1)} %get-tuple-element.54.held, ...), custom_call_target="tpu_custom_call" | custom-call | flops 1073741824 | bytes 8388608 | tf_op jit(solution)/shard_map/backward/pallas_call | solution.py:469
  88.5 0.9 collective-permute-start.20
  89.4 2.6 %collective-permute-start.21 = (bf16[8,4,16,128]{3,2,1,0:T(8,128)(2,1)S(1)}, bf16[8,4,16,128]{3,2,1,0:T(8,128)(2,1)S(1)}, u32[]{:S(2)}, u32[]{:S(2)}) collective-permute-start(bf16[8,4,16,128]{3,2,1,0:T(8,128)(2,1)S(1)} %get-tuple-element.62), channel_id=1, source_target_pairs={{0,16},{8,24},{16,0},{24,8},{32,48},{40,56},{48,32},{56,40},{64,80... | collective-permute-start | bytes 393224 | tf_op jit(solution)/shard_map/ppermute | solution.py:348
  92.1 1.7 %collective-permute-start.22 = (bf16[8,4,16,128]{3,2,1,0:T(8,128)(2,1)S(1)}, bf16[8,4,16,128]{3,2,1,0:T(8,128)(2,1)S(1)}, u32[]{:S(2)}, u32[]{:S(2)}) collective-permute-start(bf16[8,4,16,128]{3,2,1,0:T(8,128)(2,1)S(1)} %get-tuple-element.63), channel_id=1, source_target_pairs={{0,24},{8,0},{16,8},{24,16},{32,56},{40,32},{48,40},{56,48},{64,88... | collective-permute-start | bytes 393224 | tf_op jit(solution)/shard_map/ppermute | solution.py:348
  93.8 2.2 %collective-permute-done.21 = bf16[8,4,16,128]{3,2,1,0:T(8,128)(2,1)S(1)} collective-permute-done((bf16[8,4,16,128]{3,2,1,0:T(8,128)(2,1)S(1)}, bf16[8,4,16,128]{3,2,1,0:T(8,128)(2,1)S(1)}, u32[]{:S(2)}, u32[]{:S(2)}) %collective-permute-start.21) | collective-permute-done | bytes 131104 | tf_op jit(solution)/shard_map/ppermute | solution.py:348
  95.9 1.4 %collective-permute-done.22 = bf16[8,4,16,128]{3,2,1,0:T(8,128)(2,1)S(1)} collective-permute-done((bf16[8,4,16,128]{3,2,1,0:T(8,128)(2,1)S(1)}, bf16[8,4,16,128]{3,2,1,0:T(8,128)(2,1)S(1)}, u32[]{:S(2)}, u32[]{:S(2)}) %collective-permute-start.22) | collective-permute-done | bytes 131104 | tf_op jit(solution)/shard_map/ppermute | solution.py:348
  97.4 11.5 %all_to_all.17 = bf16[8,4,16,128]{3,2,1,0:T(8,128)(2,1)S(1)} all-to-all(bf16[8,4,16,128]{3,2,1,0:T(8,128)(2,1)S(1)} %add_convert_fusion), channel_id=1, replica_groups={{0,32,64,96,128,160,192,224},{8,40,72,104,136,168,200,232},{16,48,80,11..., dimensions={0} | all-to-all | bytes 262144 | tf_op jit(solution)/shard_map/all_to_all | solution.py:366
  (34 shorter events, 3.9 us)
Async XLA Ops:
  0.6 10.3 %copy-start = (bf16[1,512,128]{2,1,0:T(8,128)(2,1)S(1)}, bf16[1,512,128]{2,1,0:T(8,128)(2,1)}, u32[]{:S(2)}) copy-start(bf16[1,512,128]{2,1,0:T(8,128)(2,1)} %rest_0_.2) | copy-start | bytes 393220
  0.6 9.7 %collective-permute-start.2 = (bf16[1,512,128]{2,1,0:T(8,128)(2,1)}, bf16[1,512,128]{2,1,0:T(8,128)(2,1)S(1)}, u32[]{:S(2)}, u32[]{:S(2)}) collective-permute-start(bf16[1,512,128]{2,1,0:T(8,128)(2,1)} %rest_0_.2), channel_id=1, source_target_pairs={{0,2},{1,3},{2,4},{3,5},{4,6},{5,7},{6,0},{7,1},{8,10},{9,11},{10,... | collective-permute-start | bytes 393224 | tf_op jit(solution)/shard_map/ppermute | solution.py:352
  2.2 8.1 %collective-permute-start.3 = (bf16[1,512,128]{2,1,0:T(8,128)(2,1)}, bf16[1,512,128]{2,1,0:T(8,128)(2,1)S(1)}, u32[]{:S(2)}, u32[]{:S(2)}) collective-permute-start(bf16[1,512,128]{2,1,0:T(8,128)(2,1)} %rest_0_.2), channel_id=1, source_target_pairs={{0,6},{1,7},{2,0},{3,1},{4,2},{5,3},{6,4},{7,5},{8,14},{9,15},{10,... | collective-permute-start | bytes 393224 | tf_op jit(solution)/shard_map/ppermute | solution.py:352
  4.0 9.7 %collective-permute-start = (bf16[1,512,128]{2,1,0:T(8,128)(2,1)}, bf16[1,512,128]{2,1,0:T(8,128)(2,1)S(1)}, u32[]{:S(2)}, u32[]{:S(2)}) collective-permute-start(bf16[1,512,128]{2,1,0:T(8,128)(2,1)} %rest_0_.3), channel_id=1, source_target_pairs={{0,2},{1,3},{2,4},{3,5},{4,6},{5,7},{6,0},{7,1},{8,10},{9,11},{10,... | collective-permute-start | bytes 393224 | tf_op jit(solution)/shard_map/ppermute | solution.py:352
  4.2 9.6 %collective-permute-start.1 = (bf16[1,512,128]{2,1,0:T(8,128)(2,1)}, bf16[1,512,128]{2,1,0:T(8,128)(2,1)S(1)}, u32[]{:S(2)}, u32[]{:S(2)}) collective-permute-start(bf16[1,512,128]{2,1,0:T(8,128)(2,1)} %rest_0_.3), channel_id=1, source_target_pairs={{0,6},{1,7},{2,0},{3,1},{4,2},{5,3},{6,4},{7,5},{8,14},{9,15},{10,... | collective-permute-start | bytes 393224 | tf_op jit(solution)/shard_map/ppermute | solution.py:352
  10.3 5.0 %collective-permute-start.4 = (bf16[1,512,128]{2,1,0:T(8,128)(2,1)S(1)}, bf16[1,512,128]{2,1,0:T(8,128)(2,1)S(1)}, u32[]{:S(2)}, u32[]{:S(2)}) collective-permute-start(bf16[1,512,128]{2,1,0:T(8,128)(2,1)S(1)} %collective-permute-done.3.rest_2_), channel_id=1, source_target_pairs={{0,6},{1,7},{2,0},{3,1},{4,2},{5,3},{6,4},{7,5},{8,14},{9,15},{10,... | collective-permute-start | bytes 393224 | tf_op jit(solution)/shard_map/ppermute | solution.py:352
  10.9 4.8 %collective-permute-start.6 = (bf16[1,512,128]{2,1,0:T(8,128)(2,1)S(1)}, bf16[1,512,128]{2,1,0:T(8,128)(2,1)S(1)}, u32[]{:S(2)}, u32[]{:S(2)}) collective-permute-start(bf16[1,512,128]{2,1,0:T(8,128)(2,1)S(1)} %copy-done), channel_id=1, source_target_pairs={{0,1},{1,0},{2,3},{3,2},{4,5},{5,4},{6,7},{7,6},{8,9},{9,8},{10,11... | collective-permute-start | bytes 393224 | tf_op jit(solution)/shard_map/ppermute | solution.py:356
  10.9 5.1 %collective-permute-start.8 = (bf16[1,512,128]{2,1,0:T(8,128)(2,1)S(1)}, bf16[1,512,128]{2,1,0:T(8,128)(2,1)S(1)}, u32[]{:S(2)}, u32[]{:S(2)}) collective-permute-start(bf16[1,512,128]{2,1,0:T(8,128)(2,1)S(1)} %collective-permute-done.3.rest_2_), channel_id=1, source_target_pairs={{0,1},{1,0},{2,3},{3,2},{4,5},{5,4},{6,7},{7,6},{8,9},{9,8},{10,11... | collective-permute-start | bytes 393224 | tf_op jit(solution)/shard_map/ppermute | solution.py:356
  11.4 4.3 %copy-start.1 = (bf16[1,512,128]{2,1,0:T(8,128)(2,1)S(1)}, bf16[1,512,128]{2,1,0:T(8,128)(2,1)}, u32[]{:S(2)}) copy-start(bf16[1,512,128]{2,1,0:T(8,128)(2,1)} %rest_0_.3) | copy-start | bytes 393220
  13.7 2.6 %collective-permute-start.7 = (bf16[1,512,128]{2,1,0:T(8,128)(2,1)S(1)}, bf16[1,512,128]{2,1,0:T(8,128)(2,1)S(1)}, u32[]{:S(2)}, u32[]{:S(2)}) collective-permute-start(bf16[1,512,128]{2,1,0:T(8,128)(2,1)S(1)} %collective-permute-done.2.rest_1_), channel_id=1, source_target_pairs={{0,1},{1,0},{2,3},{3,2},{4,5},{5,4},{6,7},{7,6},{8,9},{9,8},{10,11... | collective-permute-start | bytes 393224 | tf_op jit(solution)/shard_map/ppermute | solution.py:356
  15.4 1.3 %collective-permute-start.9 = (bf16[1,512,128]{2,1,0:T(8,128)(2,1)S(1)}, bf16[1,512,128]{2,1,0:T(8,128)(2,1)S(1)}, u32[]{:S(2)}, u32[]{:S(2)}) collective-permute-start(bf16[1,512,128]{2,1,0:T(8,128)(2,1)S(1)} %collective-permute-done.4.rest_3_), channel_id=1, source_target_pairs={{0,1},{1,0},{2,3},{3,2},{4,5},{5,4},{6,7},{7,6},{8,9},{9,8},{10,11... | collective-permute-start | bytes 393224 | tf_op jit(solution)/shard_map/ppermute | solution.py:356
  15.4 7.1 %collective-permute-start.5 = (bf16[1,512,128]{2,1,0:T(8,128)(2,1)S(1)}, bf16[1,512,128]{2,1,0:T(8,128)(2,1)S(1)}, u32[]{:S(2)}, u32[]{:S(2)}) collective-permute-start(bf16[1,512,128]{2,1,0:T(8,128)(2,1)S(1)} %collective-permute-done.rest_1_), channel_id=1, source_target_pairs={{0,2},{1,3},{2,4},{3,5},{4,6},{5,7},{6,0},{7,1},{8,10},{9,11},{10,... | collective-permute-start | bytes 393224 | tf_op jit(solution)/shard_map/ppermute | solution.py:352
  15.7 6.8 %collective-permute-start.10 = (bf16[1,512,128]{2,1,0:T(8,128)(2,1)S(1)}, bf16[1,512,128]{2,1,0:T(8,128)(2,1)S(1)}, u32[]{:S(2)}, u32[]{:S(2)}) collective-permute-start(bf16[1,512,128]{2,1,0:T(8,128)(2,1)S(1)} %copy-done.1), channel_id=1, source_target_pairs={{0,1},{1,0},{2,3},{3,2},{4,5},{5,4},{6,7},{7,6},{8,9},{9,8},{10,11... | collective-permute-start | bytes 393224 | tf_op jit(solution)/shard_map/ppermute | solution.py:356
  16.0 6.5 %collective-permute-start.11 = (bf16[1,512,128]{2,1,0:T(8,128)(2,1)S(1)}, bf16[1,512,128]{2,1,0:T(8,128)(2,1)S(1)}, u32[]{:S(2)}, u32[]{:S(2)}) collective-permute-start(bf16[1,512,128]{2,1,0:T(8,128)(2,1)S(1)} %collective-permute-done.rest_1_), channel_id=1, source_target_pairs={{0,1},{1,0},{2,3},{3,2},{4,5},{5,4},{6,7},{7,6},{8,9},{9,8},{10,11... | collective-permute-start | bytes 393224 | tf_op jit(solution)/shard_map/ppermute | solution.py:356
  16.3 6.2 %collective-permute-start.12 = (bf16[1,512,128]{2,1,0:T(8,128)(2,1)S(1)}, bf16[1,512,128]{2,1,0:T(8,128)(2,1)S(1)}, u32[]{:S(2)}, u32[]{:S(2)}) collective-permute-start(bf16[1,512,128]{2,1,0:T(8,128)(2,1)S(1)} %collective-permute-done.1.rest_2_), channel_id=1, source_target_pairs={{0,1},{1,0},{2,3},{3,2},{4,5},{5,4},{6,7},{7,6},{8,9},{9,8},{10,11... | collective-permute-start | bytes 393224 | tf_op jit(solution)/shard_map/ppermute | solution.py:356
  22.5 1.3 %collective-permute-start.13 = (bf16[1,512,128]{2,1,0:T(8,128)(2,1)S(1)}, bf16[1,512,128]{2,1,0:T(8,128)(2,1)S(1)}, u32[]{:S(2)}, u32[]{:S(2)}) collective-permute-start(bf16[1,512,128]{2,1,0:T(8,128)(2,1)S(1)} %collective-permute-done.5.rest_3_), channel_id=1, source_target_pairs={{0,1},{1,0},{2,3},{3,2},{4,5},{5,4},{6,7},{7,6},{8,9},{9,8},{10,11... | collective-permute-start | bytes 393224 | tf_op jit(solution)/shard_map/ppermute | solution.py:356
  25.4 6.7 %collective-permute-start.14 = (bf16[512,128]{1,0:T(8,128)(2,1)S(1)}, bf16[512,128]{1,0:T(8,128)(2,1)S(1)}, u32[]{:S(2)}, u32[]{:S(2)}) collective-permute-start(bf16[512,128]{1,0:T(8,128)(2,1)S(1)} %get-tuple-element.50), channel_id=1, source_target_pairs={{0,8},{8,16},{16,24},{24,0},{32,40},{40,48},{48,56},{56,32},{64,72... | collective-permute-start | bytes 393224 | tf_op jit(solution)/shard_map/ppermute | solution.py:348
  27.3 7.9 %collective-permute-start.15 = (bf16[512,128]{1,0:T(8,128)(2,1)S(1)}, bf16[512,128]{1,0:T(8,128)(2,1)S(1)}, u32[]{:S(2)}, u32[]{:S(2)}) collective-permute-start(bf16[512,128]{1,0:T(8,128)(2,1)S(1)} %get-tuple-element.51), channel_id=1, source_target_pairs={{0,16},{8,24},{16,0},{24,8},{32,48},{40,56},{48,32},{56,40},{64,80... | collective-permute-start | bytes 393224 | tf_op jit(solution)/shard_map/ppermute | solution.py:348
  29.9 7.0 %collective-permute-start.16 = (bf16[512,128]{1,0:T(8,128)(2,1)S(1)}, bf16[512,128]{1,0:T(8,128)(2,1)S(1)}, u32[]{:S(2)}, u32[]{:S(2)}) collective-permute-start(bf16[512,128]{1,0:T(8,128)(2,1)S(1)} %get-tuple-element.52), channel_id=1, source_target_pairs={{0,24},{8,0},{16,8},{24,16},{32,56},{40,32},{48,40},{56,48},{64,88... | collective-permute-start | bytes 393224 | tf_op jit(solution)/shard_map/ppermute | solution.py:348
  77.5 7.6 %collective-permute-start.17 = (bf16[544,128]{1,0:T(8,128)(2,1)S(1)}, bf16[544,128]{1,0:T(8,128)(2,1)S(1)}, u32[]{:S(2)}, u32[]{:S(2)}) collective-permute-start(bf16[544,128]{1,0:T(8,128)(2,1)S(1)} %get-tuple-element.56), channel_id=1, source_target_pairs={{0,8},{8,16},{16,24},{24,0},{32,40},{40,48},{48,56},{56,32},{64,72... | collective-permute-start | bytes 417800 | tf_op jit(solution)/shard_map/ppermute | solution.py:348
  77.7 7.4 %collective-permute-start.18 = (bf16[544,128]{1,0:T(8,128)(2,1)S(1)}, bf16[544,128]{1,0:T(8,128)(2,1)S(1)}, u32[]{:S(2)}, u32[]{:S(2)}) collective-permute-start(bf16[544,128]{1,0:T(8,128)(2,1)S(1)} %get-tuple-element.57), channel_id=1, source_target_pairs={{0,16},{8,24},{16,0},{24,8},{32,48},{40,56},{48,32},{56,40},{64,80... | collective-permute-start | bytes 417800 | tf_op jit(solution)/shard_map/ppermute | solution.py:348
  80.3 5.4 %collective-permute-start.19 = (bf16[544,128]{1,0:T(8,128)(2,1)S(1)}, bf16[544,128]{1,0:T(8,128)(2,1)S(1)}, u32[]{:S(2)}, u32[]{:S(2)}) collective-permute-start(bf16[544,128]{1,0:T(8,128)(2,1)S(1)} %get-tuple-element.58), channel_id=1, source_target_pairs={{0,24},{8,0},{16,8},{24,16},{32,56},{40,32},{48,40},{56,48},{64,88... | collective-permute-start | bytes 417800 | tf_op jit(solution)/shard_map/ppermute | solution.py:348
  88.5 5.2 %collective-permute-start.20 = (bf16[8,4,16,128]{3,2,1,0:T(8,128)(2,1)S(1)}, bf16[8,4,16,128]{3,2,1,0:T(8,128)(2,1)S(1)}, u32[]{:S(2)}, u32[]{:S(2)}) collective-permute-start(bf16[8,4,16,128]{3,2,1,0:T(8,128)(2,1)S(1)} %get-tuple-element.61), channel_id=1, source_target_pairs={{0,8},{8,16},{16,24},{24,0},{32,40},{40,48},{48,56},{56,32},{64,72... | collective-permute-start | bytes 393224 | tf_op jit(solution)/shard_map/ppermute | solution.py:348
  89.4 6.5 %collective-permute-start.21 = (bf16[8,4,16,128]{3,2,1,0:T(8,128)(2,1)S(1)}, bf16[8,4,16,128]{3,2,1,0:T(8,128)(2,1)S(1)}, u32[]{:S(2)}, u32[]{:S(2)}) collective-permute-start(bf16[8,4,16,128]{3,2,1,0:T(8,128)(2,1)S(1)} %get-tuple-element.62), channel_id=1, source_target_pairs={{0,16},{8,24},{16,0},{24,8},{32,48},{40,56},{48,32},{56,40},{64,80... | collective-permute-start | bytes 393224 | tf_op jit(solution)/shard_map/ppermute | solution.py:348
  92.1 5.2 %collective-permute-start.22 = (bf16[8,4,16,128]{3,2,1,0:T(8,128)(2,1)S(1)}, bf16[8,4,16,128]{3,2,1,0:T(8,128)(2,1)S(1)}, u32[]{:S(2)}, u32[]{:S(2)}) collective-permute-start(bf16[8,4,16,128]{3,2,1,0:T(8,128)(2,1)S(1)} %get-tuple-element.63), channel_id=1, source_target_pairs={{0,24},{8,0},{16,8},{24,16},{32,56},{40,32},{48,40},{56,48},{64,88... | collective-permute-start | bytes 393224 | tf_op jit(solution)/shard_map/ppermute | solution.py:348

commit v10 on v9

--- a/solution.py
+++ b/solution.py
@@ -12,6 +12,7 @@
 R = 128
 YS = 4
 BATCH = 4
+FIRST = (2, 1, 3)
 HIGH = lax.Precision.HIGHEST
 BF = jnp.bfloat16
 F32 = jnp.float32
@@ -319,12 +320,12 @@
     lax.fori_loop(1, YS, tile, 0)
 
 
-def backward_kernel(slots, zs, meta, held, group, pairs, mine, msg0, msg1, msg2, msg3,
+def backward_kernel(slots, zs, meta, held, group, pairs, mine, msg0, msg_a, msg_b, msg_c,
                     own, send1, send2, send3, basis, turned, acc):
     y = y_of()
     rows = NB // (zs * YS)
     tiles = [lax.rem(y + YS - step, YS) for step in range(YS)]
-    for step, msg in enumerate((msg0, msg1, msg2, msg3)):
+    for step, msg in zip((0, *FIRST), (msg0, msg_a, msg_b, msg_c)):
         if step:
             turned[step] = msg[:NB].T
         kept = msg[NB:NB + rows].astype(F32) + msg[NB + rows:].astype(F32)
@@ -357,8 +358,7 @@
 
 
 def spread(sends, zs):
-    got = {step: shift_y(sends[step - 1], step, zs) for step in (2, 1, 3)}
-    return [got[step] for step in (1, 2, 3)]
+    return [shift_y(sends[step - 1], step, zs) for step in FIRST]
 
 
 def over_z(array, zs):

time: 110 us -> 109 us (level)
  starting transfers between devices: 23.9 us -> 21.6 us
    ppermute x9, starting transfers between devices: 15 us -> 12.7 us  [shift_y(): return lax.ppermute(array, 'inner', pairs)]
  transfers between devices with their start and end apart: 23 -> 23, of which waited for: 10 -> 10; matrix products, arithmetic and copies ran while one was open for 1% -> 1% of each run, Pallas kernels for 9% -> 10%
where the time goes in v10:
time: 109 us; the launch traced here: 108 us
  blocking collectives  44.7 us (41%)
  Pallas kernels  22 us (20%)
  starting transfers between devices  21.6 us (20%)
  waiting for transfers between devices  16.2 us (15%)
  other arithmetic  2.44 us (2%)
    all_to_all x3, blocking collectives, over_z(): lax.all_to_all(array, 'inner', 0, 0, tiled=True, axis_index_groups=groups)  44.7 us
    ppermute x9, starting transfers between devices, shift_y(): return lax.ppermute(array, 'inner', pairs)  12.7 us
    ppermute x9, waiting for transfers between devices, shift_y(): return lax.ppermute(array, 'inner', pairs)  10.1 us
    ppermute x6, starting transfers between devices, hop(): lax.ppermute(value, 'cols', [(i, (i + 2 * step) % tiles) for i in range(t...  7.58 us
    pallas_call x1, Pallas kernels, body(): pl.pallas_call(functools.partial(ortho_kernel, zs), out_shape=(shape((NB...  6.98 us
    ppermute x6, waiting for transfers between devices, hop(): lax.ppermute(value, 'cols', [(i, (i + 2 * step) % tiles) for i in range(t...  4.48 us
    pallas_call x1, Pallas kernels, body(): pl.pallas_call(functools.partial(backward_own_kernel, outs, slots), out_s...  3.14 us
    pallas_call x1, Pallas kernels, body(): pl.pallas_call(functools.partial(pair_kernel, outs, slots), out_shape=(sh...  2.82 us
  transfers between devices with their start and end apart: 23, of which 10 were waited for; matrix products, arithmetic and copies ran while one was open for 1% of the time, Pallas kernels for 10%

profile of v10, /device:TPU:8, one launch (start us, length us, event | category | flops | bytes accessed | tf_op | source)
XLA Modules:
  0.0 107.8 jit_solution(137615874393270016)
XLA Ops:
  0.6 1.6 %collective-permute-start.2 = (bf16[1,512,128]{2,1,0:T(8,128)(2,1)}, bf16[1,512,128]{2,1,0:T(8,128)(2,1)S(1)}, u32[]{:S(2)}, u32[]{:S(2)}) collective-permute-start(bf16[1,512,128]{2,1,0:T(8,128)(2,1)} %rest_0_.2), channel_id=1, source_target_pairs={{0,2},{1,3},{2,4},{3,5},{4,6},{5,7},{6,0},{7,1},{8,10},{9,11},{10,... | collective-permute-start | bytes 393224 | tf_op jit(solution)/shard_map/ppermute | solution.py:353
  2.2 1.7 %collective-permute-start.3 = (bf16[1,512,128]{2,1,0:T(8,128)(2,1)}, bf16[1,512,128]{2,1,0:T(8,128)(2,1)S(1)}, u32[]{:S(2)}, u32[]{:S(2)}) collective-permute-start(bf16[1,512,128]{2,1,0:T(8,128)(2,1)} %rest_0_.2), channel_id=1, source_target_pairs={{0,6},{1,7},{2,0},{3,1},{4,2},{5,3},{6,4},{7,5},{8,14},{9,15},{10,... | collective-permute-start | bytes 393224 | tf_op jit(solution)/shard_map/ppermute | solution.py:353
  4.2 3.0 %collective-permute-start.1 = (bf16[1,512,128]{2,1,0:T(8,128)(2,1)}, bf16[1,512,128]{2,1,0:T(8,128)(2,1)S(1)}, u32[]{:S(2)}, u32[]{:S(2)}) collective-permute-start(bf16[1,512,128]{2,1,0:T(8,128)(2,1)} %rest_0_.3), channel_id=1, source_target_pairs={{0,6},{1,7},{2,0},{3,1},{4,2},{5,3},{6,4},{7,5},{8,14},{9,15},{10,... | collective-permute-start | bytes 393224 | tf_op jit(solution)/shard_map/ppermute | solution.py:353
  7.2 0.7 multiply_add_fusion.meta
  7.9 2.5 %load.1 = (bf16[32,512,128]{2,1,0:T(8,128)(2,1)S(1)}, bf16[4,512,128]{2,1,0:T(8,128)(2,1)S(1)}) custom-call(s32[4,8]{1,0:T(4,128)S(1)} %multiply_add_fusion.meta, bf16[4,8,512,128]{3,2,1,0:T(8,128)(2,1)} %right_v.3, bf16[4,512,128]{2,1,0:T(8,128)(2,1)} %sketch.2), custom_call_target="tpu_custom_call" | custom-call | bytes 5242880 | tf_op jit(solution)/shard_map/load/pallas_call | solution.py:390
  10.4 0.6 collective-permute-start.4
  11.5 2.3 %probe.1 = (bf16[32,128,256]{2,1,0:T(8,128)(2,1)S(1)}, bf16[32,512,128]{2,1,0:T(8,128)(2,1)S(1)}) custom-call(s32[4,8]{1,0:T(4,128)S(1)} %multiply_add_fusion.meta, bf16[4,8,512,128]{3,2,1,0:T(8,128)(2,1)} %right_u.1, bf16[32,512,128]{2,1,0:T(8,128)(2,1)S(1)} %get-tuple-element.35.held, bf16[4,512,128]{2,1,0:T(8,128)(2,1)S(1)} %get-tuple-element.36.sketch), custom_call_target="tpu_custom_call" | custom-call | flops 536870912 | bytes 6291456 | tf_op jit(solution)/shard_map/probe/pallas_call | solution.py:402
  13.9 1.5 %collective-permute-done.4.rest_3_ = bf16[1,512,128]{2,1,0:T(8,128)(2,1)S(1)} collective-permute-done((bf16[1,512,128]{2,1,0:T(8,128)(2,1)S(1)}, bf16[1,512,128]{2,1,0:T(8,128)(2,1)S(1)}, u32[]{:S(2)}, u32[]{:S(2)}) %collective-permute-start.4) | collective-permute-done | bytes 131104 | tf_op jit(solution)/shard_map/ppermute | solution.py:353
  16.8 2.8 %pair.1 = (bf16[32,256,128]{2,1,0:T(8,128)(2,1)S(1)}, bf16[32,128,128]{2,1,0:T(8,128)(2,1)S(1)}) custom-call(s32[4,8]{1,0:T(4,128)S(1)} %multiply_add_fusion.meta, bf16[32,512,128]{2,1,0:T(8,128)(2,1)S(1)} %get-tuple-element.39.held, bf16[32,128,256]{2,1,0:T(8,128)(2,1)S(1)} %get-tuple-element.40.probes, bf16[1,512,128]{2,1,0:T(8,128)(2,1)S(1)} %copy-done, ...), custom_call_target="tpu_custom_call" | custom-call | flops 939524096 | bytes 10485760 | tf_op jit(solution)/shard_map/pair/pallas_call | solution.py:418
  19.6 2.9 %collective-permute-done.5.rest_3_ = bf16[1,512,128]{2,1,0:T(8,128)(2,1)S(1)} collective-permute-done((bf16[1,512,128]{2,1,0:T(8,128)(2,1)S(1)}, bf16[1,512,128]{2,1,0:T(8,128)(2,1)S(1)}, u32[]{:S(2)}, u32[]{:S(2)}) %collective-permute-start.5) | collective-permute-done | bytes 131104 | tf_op jit(solution)/shard_map/ppermute | solution.py:353
  22.6 1.3 %collective-permute-done.13.rest_7_ = bf16[1,512,128]{2,1,0:T(8,128)(2,1)S(1)} collective-permute-done((bf16[1,512,128]{2,1,0:T(8,128)(2,1)S(1)}, bf16[1,512,128]{2,1,0:T(8,128)(2,1)S(1)}, u32[]{:S(2)}, u32[]{:S(2)}) %collective-permute-start.13) | collective-permute-done | bytes 131104 | tf_op jit(solution)/shard_map/ppermute | solution.py:357
  23.9 1.6 %sketch.3 = (f32[512,128]{1,0:T(8,128)S(1)}, bf16[512,128]{1,0:T(8,128)(2,1)S(1)}, bf16[512,128]{1,0:T(8,128)(2,1)S(1)}, bf16[512,128]{1,0:T(8,128)(2,1)S(1)}, bf16[8,512,128]{2,1,0:T(8,128)(2,1)S(1)}) custom-call(s32[4,8]{1,0:T(4,128)S(1)} %multiply_add_fusion.meta, bf16[32,128,128]{2,1,0:T(8,128)(2,1)S(1)} %get-tuple-element.44.mixing, ...), custom_call_target="tpu_custom_call" | custom-call | flops 536870912 | bytes 4194304 | tf_op jit(solution)/shard_map/sketch/pallas_call | solution.py:430
  25.5 2.3 %collective-permute-start.14 = (bf16[512,128]{1,0:T(8,128)(2,1)S(1)}, bf16[512,128]{1,0:T(8,128)(2,1)S(1)}, u32[]{:S(2)}, u32[]{:S(2)}) collective-permute-start(bf16[512,128]{1,0:T(8,128)(2,1)S(1)} %get-tuple-element.50), channel_id=1, source_target_pairs={{0,16},{8,24},{16,0},{24,8},{32,48},{40,56},{48,32},{56,40},{64,80... | collective-permute-start | bytes 393224 | tf_op jit(solution)/shard_map/ppermute | solution.py:349
  27.8 1.4 %collective-permute-start.15 = (bf16[512,128]{1,0:T(8,128)(2,1)S(1)}, bf16[512,128]{1,0:T(8,128)(2,1)S(1)}, u32[]{:S(2)}, u32[]{:S(2)}) collective-permute-start(bf16[512,128]{1,0:T(8,128)(2,1)S(1)} %get-tuple-element.51), channel_id=1, source_target_pairs={{0,8},{8,16},{16,24},{24,0},{32,40},{40,48},{48,56},{56,32},{64,72... | collective-permute-start | bytes 393224 | tf_op jit(solution)/shard_map/ppermute | solution.py:349
  29.2 0.6 collective-permute-start.16
  29.8 3.6 %collective-permute-done.14 = bf16[512,128]{1,0:T(8,128)(2,1)S(1)} collective-permute-done((bf16[512,128]{1,0:T(8,128)(2,1)S(1)}, bf16[512,128]{1,0:T(8,128)(2,1)S(1)}, u32[]{:S(2)}, u32[]{:S(2)}) %collective-permute-start.14) | collective-permute-done | bytes 131104 | tf_op jit(solution)/shard_map/ppermute | solution.py:349
  33.4 2.1 %collective-permute-done.15 = bf16[512,128]{1,0:T(8,128)(2,1)S(1)} collective-permute-done((bf16[512,128]{1,0:T(8,128)(2,1)S(1)}, bf16[512,128]{1,0:T(8,128)(2,1)S(1)}, u32[]{:S(2)}, u32[]{:S(2)}) %collective-permute-start.15) | collective-permute-done | bytes 131104 | tf_op jit(solution)/shard_map/ppermute | solution.py:349
  35.6 20.2 %all_to_all.15 = f32[8,64,128]{2,1,0:T(8,128)} all-to-all(f32[8,64,128]{2,1,0:T(8,128)S(1)} %bitcast.1), channel_id=1, replica_groups={{0,32,64,96,128,160,192,224},{8,40,72,104,136,168,200,232},{16,48,80,11..., dimensions={0} | all-to-all | bytes 524288 | tf_op jit(solution)/shard_map/all_to_all | solution.py:366
  55.8 1.0 reduce_sum.18
  56.8 13.1 %all_to_all.16.blocks = f32[8,64,128]{2,1,0:T(8,128)S(1)} all-to-all(f32[8,64,128]{2,1,0:T(8,128)S(1)} %broadcast_in_dim.2), channel_id=1, replica_groups={{0,32,64,96,128,160,192,224},{8,40,72,104,136,168,200,232},{16,48,80,11..., dimensions={0} | all-to-all | bytes 524288 | tf_op jit(solution)/shard_map/all_to_all | solution.py:366
  69.8 7.0 %ortho.1 = (bf16[544,128]{1,0:T(8,128)(2,1)S(1)}, bf16[544,128]{1,0:T(8,128)(2,1)S(1)}, bf16[544,128]{1,0:T(8,128)(2,1)S(1)}, bf16[544,128]{1,0:T(8,128)(2,1)S(1)}) custom-call(f32[8,64,128]{2,1,0:T(8,128)S(1)} %all_to_all.16.blocks), custom_call_target="tpu_custom_call" | custom-call | flops 218103808 | bytes 1048576 | tf_op jit(solution)/shard_map/ortho/pallas_call | solution.py:447
  76.8 1.8 %collective-permute-start.17 = (bf16[544,128]{1,0:T(8,128)(2,1)S(1)}, bf16[544,128]{1,0:T(8,128)(2,1)S(1)}, u32[]{:S(2)}, u32[]{:S(2)}) collective-permute-start(bf16[544,128]{1,0:T(8,128)(2,1)S(1)} %get-tuple-element.56), channel_id=1, source_target_pairs={{0,16},{8,24},{16,0},{24,8},{32,48},{40,56},{48,32},{56,40},{64,80... | collective-permute-start | bytes 417800 | tf_op jit(solution)/shard_map/ppermute | solution.py:349
  78.6 2.0 %collective-permute-start.19 = (bf16[544,128]{1,0:T(8,128)(2,1)S(1)}, bf16[544,128]{1,0:T(8,128)(2,1)S(1)}, u32[]{:S(2)}, u32[]{:S(2)}) collective-permute-start(bf16[544,128]{1,0:T(8,128)(2,1)S(1)} %get-tuple-element.58), channel_id=1, source_target_pairs={{0,24},{8,0},{16,8},{24,16},{32,56},{40,32},{48,40},{56,48},{64,88... | collective-permute-start | bytes 417800 | tf_op jit(solution)/shard_map/ppermute | solution.py:349
  80.7 3.1 %backward_own.1 = (f32[1,512,128]{2,1,0:T(8,128)S(1)}, bf16[32,512,128]{2,1,0:T(8,128)(2,1)S(1)}) custom-call(s32[4,8]{1,0:T(4,128)S(1)} %multiply_add_fusion.meta, bf16[4,8,512,128]{3,2,1,0:T(8,128)(2,1)} %right_v.3, bf16[8,512,128]{2,1,0:T(8,128)(2,1)S(1)} %get-tuple-element.47.group, bf16[32,256,128]{2,1,0:T(8,128)(2,1)S(1)} %get-tuple-element.48.pairs, ...), custom_call_target="tpu_custom_call" | custom-call | flops 369098752 | bytes 4194304 | tf_op jit(solution)/shard_map/backward_own/pallas_call | solution.py:457
  83.8 1.1 %collective-permute-done.19.msg_c = bf16[544,128]{1,0:T(8,128)(2,1)S(1)} collective-permute-done((bf16[544,128]{1,0:T(8,128)(2,1)S(1)}, bf16[544,128]{1,0:T(8,128)(2,1)S(1)}, u32[]{:S(2)}, u32[]{:S(2)}) %collective-permute-start.19) | collective-permute-done | bytes 139296 | tf_op jit(solution)/shard_map/ppermute | solution.py:349
  85.0 2.8 %backward.1 = (f32[8,4,16,128]{3,2,1,0:T(8,128)S(1)}, bf16[8,4,16,128]{3,2,1,0:T(8,128)(2,1)S(1)}, bf16[8,4,16,128]{3,2,1,0:T(8,128)(2,1)S(1)}, bf16[8,4,16,128]{3,2,1,0:T(8,128)(2,1)S(1)}, f32[4,16,128]{2,1,0:T(8,128)}) custom-call(s32[4,8]{1,0:T(4,128)S(1)} %multiply_add_fusion.meta, bf16[32,512,128]{2,1,0:T(8,128)(2,1)S(1)} %get-tuple-element.54.held, ...), custom_call_target="tpu_custom_call" | custom-call | flops 1073741824 | bytes 8388608 | tf_op jit(solution)/shard_map/backward/pallas_call | solution.py:469
  87.7 2.6 %collective-permute-start.20 = (bf16[8,4,16,128]{3,2,1,0:T(8,128)(2,1)S(1)}, bf16[8,4,16,128]{3,2,1,0:T(8,128)(2,1)S(1)}, u32[]{:S(2)}, u32[]{:S(2)}) collective-permute-start(bf16[8,4,16,128]{3,2,1,0:T(8,128)(2,1)S(1)} %get-tuple-element.61), channel_id=1, source_target_pairs={{0,16},{8,24},{16,0},{24,8},{32,48},{40,56},{48,32},{56,40},{64,80... | collective-permute-start | bytes 393224 | tf_op jit(solution)/shard_map/ppermute | solution.py:349
  90.3 2.0 %collective-permute-start.22 = (bf16[8,4,16,128]{3,2,1,0:T(8,128)(2,1)S(1)}, bf16[8,4,16,128]{3,2,1,0:T(8,128)(2,1)S(1)}, u32[]{:S(2)}, u32[]{:S(2)}) collective-permute-start(bf16[8,4,16,128]{3,2,1,0:T(8,128)(2,1)S(1)} %get-tuple-element.63), channel_id=1, source_target_pairs={{0,24},{8,0},{16,8},{24,16},{32,56},{40,32},{48,40},{56,48},{64,88... | collective-permute-start | bytes 393224 | tf_op jit(solution)/shard_map/ppermute | solution.py:349
  92.3 1.9 %collective-permute-done.20 = bf16[8,4,16,128]{3,2,1,0:T(8,128)(2,1)S(1)} collective-permute-done((bf16[8,4,16,128]{3,2,1,0:T(8,128)(2,1)S(1)}, bf16[8,4,16,128]{3,2,1,0:T(8,128)(2,1)S(1)}, u32[]{:S(2)}, u32[]{:S(2)}) %collective-permute-start.20) | collective-permute-done | bytes 131104 | tf_op jit(solution)/shard_map/ppermute | solution.py:349
  94.2 1.1 collective-permute-done.21
  95.7 11.5 %all_to_all.17 = bf16[8,4,16,128]{3,2,1,0:T(8,128)(2,1)S(1)} all-to-all(bf16[8,4,16,128]{3,2,1,0:T(8,128)(2,1)S(1)} %add_convert_fusion), channel_id=1, replica_groups={{0,32,64,96,128,160,192,224},{8,40,72,104,136,168,200,232},{16,48,80,11..., dimensions={0} | all-to-all | bytes 262144 | tf_op jit(solution)/shard_map/all_to_all | solution.py:366
  107.1 0.6 convert_reduce_fusion
  (34 shorter events, 2.7 us)
Async XLA Ops:
  0.6 10.4 %copy-start = (bf16[1,512,128]{2,1,0:T(8,128)(2,1)S(1)}, bf16[1,512,128]{2,1,0:T(8,128)(2,1)}, u32[]{:S(2)}) copy-start(bf16[1,512,128]{2,1,0:T(8,128)(2,1)} %rest_0_.2) | copy-start | bytes 393220
  0.6 9.8 %collective-permute-start.2 = (bf16[1,512,128]{2,1,0:T(8,128)(2,1)}, bf16[1,512,128]{2,1,0:T(8,128)(2,1)S(1)}, u32[]{:S(2)}, u32[]{:S(2)}) collective-permute-start(bf16[1,512,128]{2,1,0:T(8,128)(2,1)} %rest_0_.2), channel_id=1, source_target_pairs={{0,2},{1,3},{2,4},{3,5},{4,6},{5,7},{6,0},{7,1},{8,10},{9,11},{10,... | collective-permute-start | bytes 393224 | tf_op jit(solution)/shard_map/ppermute | solution.py:353
  2.2 8.2 %collective-permute-start.3 = (bf16[1,512,128]{2,1,0:T(8,128)(2,1)}, bf16[1,512,128]{2,1,0:T(8,128)(2,1)S(1)}, u32[]{:S(2)}, u32[]{:S(2)}) collective-permute-start(bf16[1,512,128]{2,1,0:T(8,128)(2,1)} %rest_0_.2), channel_id=1, source_target_pairs={{0,6},{1,7},{2,0},{3,1},{4,2},{5,3},{6,4},{7,5},{8,14},{9,15},{10,... | collective-permute-start | bytes 393224 | tf_op jit(solution)/shard_map/ppermute | solution.py:353
  4.0 9.9 %collective-permute-start = (bf16[1,512,128]{2,1,0:T(8,128)(2,1)}, bf16[1,512,128]{2,1,0:T(8,128)(2,1)S(1)}, u32[]{:S(2)}, u32[]{:S(2)}) collective-permute-start(bf16[1,512,128]{2,1,0:T(8,128)(2,1)} %rest_0_.3), channel_id=1, source_target_pairs={{0,2},{1,3},{2,4},{3,5},{4,6},{5,7},{6,0},{7,1},{8,10},{9,11},{10,... | collective-permute-start | bytes 393224 | tf_op jit(solution)/shard_map/ppermute | solution.py:353
  4.2 9.7 %collective-permute-start.1 = (bf16[1,512,128]{2,1,0:T(8,128)(2,1)}, bf16[1,512,128]{2,1,0:T(8,128)(2,1)S(1)}, u32[]{:S(2)}, u32[]{:S(2)}) collective-permute-start(bf16[1,512,128]{2,1,0:T(8,128)(2,1)} %rest_0_.3), channel_id=1, source_target_pairs={{0,6},{1,7},{2,0},{3,1},{4,2},{5,3},{6,4},{7,5},{8,14},{9,15},{10,... | collective-permute-start | bytes 393224 | tf_op jit(solution)/shard_map/ppermute | solution.py:353
  10.4 5.0 %collective-permute-start.4 = (bf16[1,512,128]{2,1,0:T(8,128)(2,1)S(1)}, bf16[1,512,128]{2,1,0:T(8,128)(2,1)S(1)}, u32[]{:S(2)}, u32[]{:S(2)}) collective-permute-start(bf16[1,512,128]{2,1,0:T(8,128)(2,1)S(1)} %collective-permute-done.3.rest_2_), channel_id=1, source_target_pairs={{0,6},{1,7},{2,0},{3,1},{4,2},{5,3},{6,4},{7,5},{8,14},{9,15},{10,... | collective-permute-start | bytes 393224 | tf_op jit(solution)/shard_map/ppermute | solution.py:353
  11.0 4.9 %collective-permute-start.6 = (bf16[1,512,128]{2,1,0:T(8,128)(2,1)S(1)}, bf16[1,512,128]{2,1,0:T(8,128)(2,1)S(1)}, u32[]{:S(2)}, u32[]{:S(2)}) collective-permute-start(bf16[1,512,128]{2,1,0:T(8,128)(2,1)S(1)} %copy-done), channel_id=1, source_target_pairs={{0,1},{1,0},{2,3},{3,2},{4,5},{5,4},{6,7},{7,6},{8,9},{9,8},{10,11... | collective-permute-start | bytes 393224 | tf_op jit(solution)/shard_map/ppermute | solution.py:357
  11.0 5.1 %collective-permute-start.8 = (bf16[1,512,128]{2,1,0:T(8,128)(2,1)S(1)}, bf16[1,512,128]{2,1,0:T(8,128)(2,1)S(1)}, u32[]{:S(2)}, u32[]{:S(2)}) collective-permute-start(bf16[1,512,128]{2,1,0:T(8,128)(2,1)S(1)} %collective-permute-done.3.rest_2_), channel_id=1, source_target_pairs={{0,1},{1,0},{2,3},{3,2},{4,5},{5,4},{6,7},{7,6},{8,9},{9,8},{10,11... | collective-permute-start | bytes 393224 | tf_op jit(solution)/shard_map/ppermute | solution.py:357
  11.5 4.4 %copy-start.1 = (bf16[1,512,128]{2,1,0:T(8,128)(2,1)S(1)}, bf16[1,512,128]{2,1,0:T(8,128)(2,1)}, u32[]{:S(2)}) copy-start(bf16[1,512,128]{2,1,0:T(8,128)(2,1)} %rest_0_.3) | copy-start | bytes 393220
  13.8 2.6 %collective-permute-start.7 = (bf16[1,512,128]{2,1,0:T(8,128)(2,1)S(1)}, bf16[1,512,128]{2,1,0:T(8,128)(2,1)S(1)}, u32[]{:S(2)}, u32[]{:S(2)}) collective-permute-start(bf16[1,512,128]{2,1,0:T(8,128)(2,1)S(1)} %collective-permute-done.2.rest_1_), channel_id=1, source_target_pairs={{0,1},{1,0},{2,3},{3,2},{4,5},{5,4},{6,7},{7,6},{8,9},{9,8},{10,11... | collective-permute-start | bytes 393224 | tf_op jit(solution)/shard_map/ppermute | solution.py:357
  15.5 1.3 %collective-permute-start.9 = (bf16[1,512,128]{2,1,0:T(8,128)(2,1)S(1)}, bf16[1,512,128]{2,1,0:T(8,128)(2,1)S(1)}, u32[]{:S(2)}, u32[]{:S(2)}) collective-permute-start(bf16[1,512,128]{2,1,0:T(8,128)(2,1)S(1)} %collective-permute-done.4.rest_3_), channel_id=1, source_target_pairs={{0,1},{1,0},{2,3},{3,2},{4,5},{5,4},{6,7},{7,6},{8,9},{9,8},{10,11... | collective-permute-start | bytes 393224 | tf_op jit(solution)/shard_map/ppermute | solution.py:357
  15.5 7.1 %collective-permute-start.5 = (bf16[1,512,128]{2,1,0:T(8,128)(2,1)S(1)}, bf16[1,512,128]{2,1,0:T(8,128)(2,1)S(1)}, u32[]{:S(2)}, u32[]{:S(2)}) collective-permute-start(bf16[1,512,128]{2,1,0:T(8,128)(2,1)S(1)} %collective-permute-done.rest_1_), channel_id=1, source_target_pairs={{0,2},{1,3},{2,4},{3,5},{4,6},{5,7},{6,0},{7,1},{8,10},{9,11},{10,... | collective-permute-start | bytes 393224 | tf_op jit(solution)/shard_map/ppermute | solution.py:353
  15.9 6.7 %collective-permute-start.10 = (bf16[1,512,128]{2,1,0:T(8,128)(2,1)S(1)}, bf16[1,512,128]{2,1,0:T(8,128)(2,1)S(1)}, u32[]{:S(2)}, u32[]{:S(2)}) collective-permute-start(bf16[1,512,128]{2,1,0:T(8,128)(2,1)S(1)} %copy-done.1), channel_id=1, source_target_pairs={{0,1},{1,0},{2,3},{3,2},{4,5},{5,4},{6,7},{7,6},{8,9},{9,8},{10,11... | collective-permute-start | bytes 393224 | tf_op jit(solution)/shard_map/ppermute | solution.py:357
  16.1 6.5 %collective-permute-start.11 = (bf16[1,512,128]{2,1,0:T(8,128)(2,1)S(1)}, bf16[1,512,128]{2,1,0:T(8,128)(2,1)S(1)}, u32[]{:S(2)}, u32[]{:S(2)}) collective-permute-start(bf16[1,512,128]{2,1,0:T(8,128)(2,1)S(1)} %collective-permute-done.rest_1_), channel_id=1, source_target_pairs={{0,1},{1,0},{2,3},{3,2},{4,5},{5,4},{6,7},{7,6},{8,9},{9,8},{10,11... | collective-permute-start | bytes 393224 | tf_op jit(solution)/shard_map/ppermute | solution.py:357
  16.4 6.2 %collective-permute-start.12 = (bf16[1,512,128]{2,1,0:T(8,128)(2,1)S(1)}, bf16[1,512,128]{2,1,0:T(8,128)(2,1)S(1)}, u32[]{:S(2)}, u32[]{:S(2)}) collective-permute-start(bf16[1,512,128]{2,1,0:T(8,128)(2,1)S(1)} %collective-permute-done.1.rest_2_), channel_id=1, source_target_pairs={{0,1},{1,0},{2,3},{3,2},{4,5},{5,4},{6,7},{7,6},{8,9},{9,8},{10,11... | collective-permute-start | bytes 393224 | tf_op jit(solution)/shard_map/ppermute | solution.py:357
  22.6 1.3 %collective-permute-start.13 = (bf16[1,512,128]{2,1,0:T(8,128)(2,1)S(1)}, bf16[1,512,128]{2,1,0:T(8,128)(2,1)S(1)}, u32[]{:S(2)}, u32[]{:S(2)}) collective-permute-start(bf16[1,512,128]{2,1,0:T(8,128)(2,1)S(1)} %collective-permute-done.5.rest_3_), channel_id=1, source_target_pairs={{0,1},{1,0},{2,3},{3,2},{4,5},{5,4},{6,7},{7,6},{8,9},{9,8},{10,11... | collective-permute-start | bytes 393224 | tf_op jit(solution)/shard_map/ppermute | solution.py:357
  25.5 7.9 %collective-permute-start.14 = (bf16[512,128]{1,0:T(8,128)(2,1)S(1)}, bf16[512,128]{1,0:T(8,128)(2,1)S(1)}, u32[]{:S(2)}, u32[]{:S(2)}) collective-permute-start(bf16[512,128]{1,0:T(8,128)(2,1)S(1)} %get-tuple-element.50), channel_id=1, source_target_pairs={{0,16},{8,24},{16,0},{24,8},{32,48},{40,56},{48,32},{56,40},{64,80... | collective-permute-start | bytes 393224 | tf_op jit(solution)/shard_map/ppermute | solution.py:349
  27.8 7.8 %collective-permute-start.15 = (bf16[512,128]{1,0:T(8,128)(2,1)S(1)}, bf16[512,128]{1,0:T(8,128)(2,1)S(1)}, u32[]{:S(2)}, u32[]{:S(2)}) collective-permute-start(bf16[512,128]{1,0:T(8,128)(2,1)S(1)} %get-tuple-element.51), channel_id=1, source_target_pairs={{0,8},{8,16},{16,24},{24,0},{32,40},{40,48},{48,56},{56,32},{64,72... | collective-permute-start | bytes 393224 | tf_op jit(solution)/shard_map/ppermute | solution.py:349
  29.2 6.3 %collective-permute-start.16 = (bf16[512,128]{1,0:T(8,128)(2,1)S(1)}, bf16[512,128]{1,0:T(8,128)(2,1)S(1)}, u32[]{:S(2)}, u32[]{:S(2)}) collective-permute-start(bf16[512,128]{1,0:T(8,128)(2,1)S(1)} %get-tuple-element.52), channel_id=1, source_target_pairs={{0,24},{8,0},{16,8},{24,16},{32,56},{40,32},{48,40},{56,48},{64,88... | collective-permute-start | bytes 393224 | tf_op jit(solution)/shard_map/ppermute | solution.py:349
  76.8 7.0 %collective-permute-start.17 = (bf16[544,128]{1,0:T(8,128)(2,1)S(1)}, bf16[544,128]{1,0:T(8,128)(2,1)S(1)}, u32[]{:S(2)}, u32[]{:S(2)}) collective-permute-start(bf16[544,128]{1,0:T(8,128)(2,1)S(1)} %get-tuple-element.56), channel_id=1, source_target_pairs={{0,16},{8,24},{16,0},{24,8},{32,48},{40,56},{48,32},{56,40},{64,80... | collective-permute-start | bytes 417800 | tf_op jit(solution)/shard_map/ppermute | solution.py:349
  78.6 5.2 %collective-permute-start.18 = (bf16[544,128]{1,0:T(8,128)(2,1)S(1)}, bf16[544,128]{1,0:T(8,128)(2,1)S(1)}, u32[]{:S(2)}, u32[]{:S(2)}) collective-permute-start(bf16[544,128]{1,0:T(8,128)(2,1)S(1)} %get-tuple-element.57), channel_id=1, source_target_pairs={{0,8},{8,16},{16,24},{24,0},{32,40},{40,48},{48,56},{56,32},{64,72... | collective-permute-start | bytes 417800 | tf_op jit(solution)/shard_map/ppermute | solution.py:349
  78.6 6.3 %collective-permute-start.19 = (bf16[544,128]{1,0:T(8,128)(2,1)S(1)}, bf16[544,128]{1,0:T(8,128)(2,1)S(1)}, u32[]{:S(2)}, u32[]{:S(2)}) collective-permute-start(bf16[544,128]{1,0:T(8,128)(2,1)S(1)} %get-tuple-element.58), channel_id=1, source_target_pairs={{0,24},{8,0},{16,8},{24,16},{32,56},{40,32},{48,40},{56,48},{64,88... | collective-permute-start | bytes 417800 | tf_op jit(solution)/shard_map/ppermute | solution.py:349
  87.7 6.5 %collective-permute-start.20 = (bf16[8,4,16,128]{3,2,1,0:T(8,128)(2,1)S(1)}, bf16[8,4,16,128]{3,2,1,0:T(8,128)(2,1)S(1)}, u32[]{:S(2)}, u32[]{:S(2)}) collective-permute-start(bf16[8,4,16,128]{3,2,1,0:T(8,128)(2,1)S(1)} %get-tuple-element.61), channel_id=1, source_target_pairs={{0,16},{8,24},{16,0},{24,8},{32,48},{40,56},{48,32},{56,40},{64,80... | collective-permute-start | bytes 393224 | tf_op jit(solution)/shard_map/ppermute | solution.py:349
  90.3 5.0 %collective-permute-start.21 = (bf16[8,4,16,128]{3,2,1,0:T(8,128)(2,1)S(1)}, bf16[8,4,16,128]{3,2,1,0:T(8,128)(2,1)S(1)}, u32[]{:S(2)}, u32[]{:S(2)}) collective-permute-start(bf16[8,4,16,128]{3,2,1,0:T(8,128)(2,1)S(1)} %get-tuple-element.62), channel_id=1, source_target_pairs={{0,8},{8,16},{16,24},{24,0},{32,40},{40,48},{48,56},{56,32},{64,72... | collective-permute-start | bytes 393224 | tf_op jit(solution)/shard_map/ppermute | solution.py:349
  90.3 5.3 %collective-permute-start.22 = (bf16[8,4,16,128]{3,2,1,0:T(8,128)(2,1)S(1)}, bf16[8,4,16,128]{3,2,1,0:T(8,128)(2,1)S(1)}, u32[]{:S(2)}, u32[]{:S(2)}) collective-permute-start(bf16[8,4,16,128]{3,2,1,0:T(8,128)(2,1)S(1)} %get-tuple-element.63), channel_id=1, source_target_pairs={{0,24},{8,0},{16,8},{24,16},{32,56},{40,32},{48,40},{56,48},{64,88... | collective-permute-start | bytes 393224 | tf_op jit(solution)/shard_map/ppermute | solution.py:349
